TPU v7x, 32 devices: a whole 2x2x4 slice. The times are simulated.
32 devices in a mesh: section: 4 (over y, x), ctx: 8 (over z, core).
Axes of the slice: x: 2, y: 2, z: 4, core: 2. Of those that a mesh axis runs over, the one named last changes fastest.
Arguments:
- resid: bfloat16 [4, 1024, 6144], P('section', 'ctx'), may hold values from -6 to 6
- queries: bfloat16 [4, 1024, 6144], P('section', 'ctx'), may hold values from -6 to 6
- keys: bfloat16 [4, 1024, 6144], P('section', 'ctx'), may hold values from -6 to 6
- values: bfloat16 [4, 1024, 6144], P('section', 'ctx'), may hold values from -6 to 6
- log_decay: float32 [4, 1024, 48], P('section', 'ctx'), may hold values from -3 to 0
- attn_gain: float32 [4, 6144], P('section'), may hold values from 0.25 to 1.75
- moe_gain: float32 [4, 6144], P('section'), may hold values from 0.25 to 1.75
- experts: int32 [4, 1024, 2], P('section', 'ctx'), may hold values from 0 to 31, all different within a row; in each aligned block of 128 rows (0 to 127, 128 to 255, ..., all dimensions but the last counted through in order) at most 16 rows name the same one
- combine_weight: float32 [4, 1024, 2], P('section', 'ctx'), may hold values from 0.2 to 1
- w_up: bfloat16 [4, 6144, 5120], P('section', None, 'ctx'), may hold values from -0.078125 to 0.078125
- w_down: bfloat16 [4, 5120, 6144], P('section', 'ctx'), may hold values from -0.078125 to 0.078125
Outputs:
- received: bfloat16 [4, 1024, 6144], P('section', 'ctx')
Inputs may be any that keep to these rules, and one draw needn't show every extreme that they name: In the rows of one device each expert is named at most 16 times, and the two experts of a token differ.
All inputs are finite; a program needn't handle non-finite values.
Results may differ from a plain program's by a relative error of at most 0.002.
Values may be sent and summed in bfloat16 or wider, within the bound.
No kernel may reach another device: no remote copies, remote signals or barrier semaphores. Data moves between devices by JAX's collectives and lax.ppermute only.
A program may use at most 256 MiB of HBM per device.

v0:
```python
import jax
import jax.numpy as jnp
from jax import lax
from jax.sharding import PartitionSpec as P

D = 6144
LINEAR_HEADS = 48
HEAD = 128
EXPERTS = 32
SHARDS = 8
CAP_SRC = 16


HIGH = lax.Precision.HIGHEST


def prefix_2(part, axis, combine, identity):
    place = lax.axis_index(axis)
    gathered = jax.tree.map(lambda a: lax.all_gather(a, axis), part)
    state = jax.tree.map(lambda a, e: jnp.zeros_like(a) + jnp.asarray(e, a.dtype), part, identity)

    def one(step, state):
        return combine(
            state, jax.tree.map(lambda a: lax.dynamic_index_in_dim(a, step, 0, False), gathered)
        )

    return lax.fori_loop(0, place, one, state)


def passed_along(value, axis, steps):
    count = lax.axis_size(axis)
    pairs = [(source, (source + steps) % count) for source in range(count)]
    return lax.ppermute(value, axis, pairs)


def rms_scale(values_in, gain):
    return (
        values_in
        * lax.rsqrt(jnp.mean(values_in * values_in, axis=-1, keepdims=True) + 1e-06)
        * gain
    )


def slots_of(chosen):
    onehot = (chosen[:, None] == jnp.arange(EXPERTS)[None, :]).astype(jnp.int32)
    before = jnp.cumsum(onehot, axis=0) - onehot
    return jnp.sum(before * onehot, axis=1)


def join_states(earlier, later):
    return (earlier[0] * later[0], later[0][:, None, None] * earlier[1] + later[1])


def local(
    resid,
    queries,
    keys,
    values,
    log_decay,
    attn_gain,
    moe_gain,
    experts,
    combine_weight,
    w_up,
    w_down,
):
    length = queries.shape[1]
    query = queries[0].astype(jnp.float32).reshape(length, LINEAR_HEADS, HEAD)
    keyrows = keys[0].astype(jnp.float32).reshape(length, LINEAR_HEADS, HEAD)
    valrows = values[0].astype(jnp.float32).reshape(length, LINEAR_HEADS, HEAD)
    log_rate = log_decay[0]
    cumul = jnp.cumsum(log_rate, axis=0)
    scores = jnp.einsum("thd,shd->hts", query, keyrows, precision=HIGH)
    spread = cumul.T[:, :, None] - cumul.T[:, None, :]
    lower = jnp.arange(length)[:, None] >= jnp.arange(length)[None, :]
    weights = jnp.exp(jnp.where(lower[None], spread, -1e30))
    intra = jnp.einsum("hts,shd->thd", scores * weights, valrows, precision=HIGH)
    tail_decay = jnp.exp(cumul[-1][None, :] - cumul)
    state = jnp.einsum("thd,the->hde", keyrows * tail_decay[:, :, None], valrows, precision=HIGH)
    identity = (
        jnp.ones((LINEAR_HEADS,), jnp.float32),
        jnp.zeros((LINEAR_HEADS, HEAD, HEAD), jnp.float32),
    )
    prefix = prefix_2((jnp.exp(cumul[-1]), state), "ctx", join_states, identity)
    inter = jnp.exp(cumul)[:, :, None] * jnp.einsum(
        "thd,hde->the", query, prefix[1], precision=HIGH
    )
    attn_raw = (intra + inter).reshape(length, D)
    hres = resid[0].astype(jnp.float32) + rms_scale(attn_raw, attn_gain[0])
    normed = rms_scale(hres, moe_gain[0]).astype(jnp.bfloat16)
    ctx_count = lax.axis_size("ctx")
    flying = ctx_count // SHARDS
    my_expert = lax.axis_index("ctx") // SHARDS
    chosen = experts[0].reshape(-1)
    slot = slots_of(chosen)
    target = chosen * CAP_SRC + slot
    in_window = chosen < flying
    select = (
        (target[None, :] == jnp.arange(flying * CAP_SRC)[:, None]) & in_window[None, :]
    ).astype(jnp.bfloat16)
    doubled = jnp.repeat(normed, 2, axis=0)
    outbox = jnp.dot(select, doubled, preferred_element_type=jnp.float32).astype(jnp.bfloat16)
    outbox = outbox.reshape(flying, CAP_SRC, D)
    up_local = w_up[0]
    down_local = w_down[0]
    mine = lax.dynamic_index_in_dim(
        lax.all_gather(outbox[None], "ctx", axis=0, tiled=True), my_expert, 1, False
    )
    count = mine.shape[0]
    hidden = jax.nn.gelu(
        jnp.dot(mine.reshape(count * CAP_SRC, D), up_local, preferred_element_type=jnp.float32),
        approximate=True,
    ).astype(jnp.bfloat16)
    partial_value = (
        jnp.dot(hidden, down_local, preferred_element_type=jnp.float32)
        .astype(jnp.bfloat16)
        .reshape(count, CAP_SRC, D)
    )
    returned = lax.all_to_all(partial_value, "ctx", split_axis=0, concat_axis=0, tiled=True)
    summed = returned.reshape(flying, SHARDS, CAP_SRC, D).astype(jnp.float32).sum(axis=1)
    summed = summed.reshape(flying * CAP_SRC, D)
    picked = jnp.take(summed, jnp.clip(target, 0, flying * CAP_SRC - 1), axis=0)
    picked = jnp.where(in_window[:, None], picked, 0.0) * combine_weight[0].reshape(-1)[:, None]
    mixed = picked.reshape(length, 2, D).sum(axis=1)
    layer_out = (hres + mixed).astype(jnp.bfloat16)
    return passed_along(layer_out[None], "section", 1)


def solution(mesh):
    return jax.shard_map(
        local,
        mesh=mesh,
        in_specs=(
            P("section", "ctx", None),
            P("section", "ctx", None),
            P("section", "ctx", None),
            P("section", "ctx", None),
            P("section", "ctx", None),
            P("section", None),
            P("section", None),
            P("section", "ctx", None),
            P("section", "ctx", None),
            P("section", None, "ctx"),
            P("section", "ctx", None),
        ),
        out_specs=P("section", "ctx", None),
        check_vma=False,
    )
```

profile of v0, /device:TPU:0, one launch (start us, length us, event | category | flops | bytes accessed | tf_op | source)
XLA Modules:
  0.0 450.4 jit_solution(3672909860523334791)
XLA Ops:
  6.5 0.9 copy.47
  7.5 0.2 reduce_window_sum.26
  7.7 0.1 copy.53
  7.8 1.9 copy.66
  9.7 0.4 copy.69
  10.1 1.2 copy-done.2
  11.3 3.6 fusion.11
  15.1 0.6 copy-done.11
  15.7 0.1 copy.59
  15.8 0.1 reshape_squeeze.3
  15.9 0.1 eq.39
  16.1 0.1 copy.51
  16.1 1.8 copy.68
  17.9 0.1 copy.48
  18.0 0.6 reduce-window.6
  18.6 0.2 slice_reduce_fusion
  18.8 13.5 %all-gather.2 = f32[8,1,48]{2,1,0:T(1,128)S(1)} all-gather(f32[1,1,48]{2,1,0:T(1,128)S(1)} %get-tuple-element.63), channel_id=1, replica_groups=mesh['section'=4,'ctx'=8] {'ctx'}, dimensions={0}, use_global_device_ids=true | all-gather | bytes 1728 | tf_op jit(solution)/shard_map/all_gather | solution.py:19
  32.3 0.1 fusion.50
  32.4 0.6 fusion.27
  33.0 0.9 copy-done.3
  34.0 5.5 %fusion.14 = f32[48,128,128]{1,2,0:T(8,128)} fusion(f32[48,128,128]{2,1,0:T(8,128)S(1)} %fusion.27, f32[48,128]{1,0:T(8,128)S(1)} %copy.48, pred[128,128]{1,0:T(8,128)(4,1)S(1)} %iota_compare_fusion, bf16[128,48,128]{2,1,0:T(8,128)(2,1)S(1)} %bitcast.101), kind=kOutput, calls=%fused_computation.24 | convolution fusion | flops 1210318848 | bytes 7905280 | tf_op jit(solution)/shard_map/hts,shd->thd/dot_general | solution.py:77
  39.4 198.3 %all-gather.6.cloned.1.call-done = f32[384,128,128]{2,1,0:T(8,128)} async-done(((f32[48,128,128]{2,1,0:T(8,128)}), f32[384,128,128]{2,1,0:T(8,128)}) %all-gather.6.cloned.1.call-update) | async-done | bytes 25165840 | tf_op jit(solution)/shard_map/all_gather | solution.py:19
  237.7 0.4 broadcast_in_dim.60
  238.1 0.2 while.12
  238.3 6.8 %multiply_reduce_fusion.2 = (f32[128]{0:T(128)S(1)}, f32[128,48,128]{0,2,1:T(8,128)}) fusion(f32[48,128,128]{2,1,0:T(8,128)S(1)} %get-tuple-element.49, bf16[128,48,128]{2,1,0:T(8,128)(2,1)} %bitcast.97, f32[128,48]{0,1:T(8,128)S(1)} %copy.51, f32[48,128,128]{1,2,0:T(8,128)} %fusion.14), kind=kOutput, calls=%fused_computation.20 | convolution fusion | flops 1211105152 | bytes 11035136 | tf_op jit(solution)/shard_map/thd,hde->the/dot_general | solution.py:85
  245.1 2.4 copy.63
  247.5 2.3 multiply_reduce_fusion.1
  249.8 1.9 multiply_convert_fusion
  251.7 5.0 %broadcast_in_dim.63 = bf16[128,2,6144]{2,1,0:T(2,128)(2,1)} broadcast(bf16[128,6144]{1,0:T(8,128)(2,1)} %multiply_convert_fusion), dimensions={0,2} | broadcast | bytes 4718592 | tf_op jit(solution)/shard_map/broadcast_in_dim | solution.py:101
  256.7 6.2 %reshape.246 = bf16[256,6144]{1,0:T(8,128)(2,1)S(1)} reshape(bf16[128,2,6144]{2,1,0:T(2,128)(2,1)} %broadcast_in_dim.63) | data formatting | bytes 6291456 | tf_op jit(solution)/shard_map/reshape | solution.py:101
  262.9 1.2 convolution_convert_fusion
  264.1 40.8 %all-gather.8.cloned.1.call-done = bf16[128,6144]{1,0:T(8,128)(2,1)} async-done(((bf16[16,6144]{1,0:T(8,128)(2,1)}), bf16[128,6144]{1,0:T(8,128)(2,1)}) %all-gather.8.cloned.1.call-update) | async-done | bytes 1572880 | tf_op jit(solution)/shard_map/all_gather | solution.py:107
  304.9 9.8 %fusion.4 = bf16[128,6144]{1,0:T(8,128)(2,1)} fusion(bf16[1,640,6144]{2,1,0:T(8,128)(2,1)} %param.23, bf16[128,6144]{1,0:T(8,128)(2,1)} %all-gather.8.cloned.1.call-done, bf16[1,6144,640]{2,1,0:T(8,128)(2,1)} %param.22), kind=kOutput, calls=%fused_computation.7 | convolution fusion | flops 2014789632 | bytes 18874368 | tf_op jit(solution)/shard_map/dot_general | solution.py:115
  314.7 4.8 %all-to-all-start = ((bf16[8,16,6144]{2,1,0:T(8,128)(2,1)}), bf16[8,16,6144]{2,1,0:T(8,128)(2,1)}, u32[]{:S(2)}, u32[]{:S(2)}) async-start(bf16[8,16,6144]{2,1,0:T(8,128)(2,1)} %bitcast.103), calls=%async_computation | async-start | bytes 3145728 | tf_op jit(solution)/shard_map/all_to_all | solution.py:119
  319.4 0.1 reduce_sum.53
  319.6 0.1 mul.203
  319.7 0.1 copy.64
  319.9 0.1 copy.58
  320.1 2.4 copy.57
  322.5 34.6 %all-to-all-done = bf16[8,16,6144]{2,1,0:T(8,128)(2,1)} async-done(((bf16[8,16,6144]{2,1,0:T(8,128)(2,1)}), bf16[8,16,6144]{2,1,0:T(8,128)(2,1)}, u32[]{:S(2)}, u32[]{:S(2)}) %all-to-all-start) | async-done | bytes 1572896 | tf_op jit(solution)/shard_map/all_to_all | solution.py:119
  357.0 1.7 convert_reduce_fusion
  358.7 5.1 %gather_fusion = f32[256,6144]{1,0:T(8,128)} fusion(f32[16,6144]{1,0:T(8,128)S(1)} %convert_reduce_fusion, s32[1024]{0:T(1024)S(1)} %pad_clamp_fusion), kind=kCustom, calls=%fused_computation | custom fusion | bytes 12583936 | tf_op jit(solution)/shard_map/jit(_take)/gather | solution.py:122
  363.8 8.1 %gather.7 = f32[128,2,6144]{2,1,0:T(2,128)} reshape(f32[256,6144]{1,0:T(8,128)} %gather_fusion) | data formatting | bytes 12582912 | tf_op jit(solution)/shard_map/jit(_take)/gather | solution.py:122
  372.0 32.9 %multiply_reduce_fusion = f32[128,6144]{1,0:T(8,128)S(1)} fusion(f32[128,2,6144]{2,1,0:T(2,128)} %gather.7, pred[128,2]{1,0:T(8,128)(4,1)S(1)} %compare_and_fusion, pred[128,2]{1,0:T(8,128)(4,1)S(1)} %copy.58, f32[128,2]{1,0:T(8,128)S(1)} %copy.64), kind=kLoop, calls=%fused_computation.9 | loop fusion | flops 5505024 | bytes 9438720 | tf_op jit(solution)/shard_map/reduce_sum | solution.py:124
  404.9 0.7 fusion.8
  405.6 1.5 collective-permute-start
  407.1 35.3 %collective-permute-done = bf16[1,128,6144]{2,1,0:T(8,128)(2,1)S(1)} collective-permute-done((bf16[1,128,6144]{2,1,0:T(8,128)(2,1)S(1)}, bf16[1,128,6144]{2,1,0:T(8,128)(2,1)S(1)}, u32[]{:S(2)}, u32[]{:S(2)}) %collective-permute-start) | collective-permute-done | bytes 1572896 | tf_op jit(solution)/shard_map/ppermute | solution.py:33
  442.4 1.1 copy.88
  (40 shorter events, 0.3 us)
Async XLA Ops:
  6.5 3.2 copy-start.7
  6.5 231.2 %all-gather.6.cloned.1.call-start = ((), (), s32[]{:S(2)}) async-start(), calls=%async_computation.1 | async-start | bytes 28311552 | tf_op jit(solution)/shard_map/all_gather | solution.py:19
  10.1 1.2 copy-start.2
  15.0 0.7 copy-start.11
  15.0 289.9 %all-gather.8.cloned.1.call-start = ((), (), s32[]{:S(2)}) async-start(), calls=%async_computation.2 | async-start | bytes 1769472 | tf_op jit(solution)/shard_map/all_gather | solution.py:107
  17.9 15.1 %copy-start.1 = (bf16[16,8,48,128]{3,2,1,0:T(8,128)(2,1)}, bf16[16,8,48,128]{3,2,1,0:T(8,128)(2,1)S(1)}, u32[]{:S(2)}) copy-start(bf16[16,8,48,128]{3,2,1,0:T(8,128)(2,1)S(1)} %copy.68) | copy-start | bytes 4718596
  32.4 1.5 copy-start.3
  245.1 2.4 copy-start.8
  247.5 2.4 copy-start.4
  247.5 2.3 copy-start.9
  314.7 5.1 %copy-start.10 = (f32[1,128,2]{1,2,0:T(2,128)S(1)}, f32[1,128,2]{1,2,0:T(2,128)}, u32[]{:S(2)}) copy-start(f32[1,128,2]{1,2,0:T(2,128)} %param.21) | copy-start | bytes 3076
  314.7 5.4 %copy-start = (f32[128,48,128]{0,2,1:T(8,128)S(1)}, f32[128,48,128]{0,2,1:T(8,128)}, u32[]{:S(2)}) copy-start(f32[128,48,128]{0,2,1:T(8,128)} %get-tuple-element.65) | copy-start | bytes 9437188
  314.7 42.4 %all-to-all-start = ((bf16[8,16,6144]{2,1,0:T(8,128)(2,1)}), bf16[8,16,6144]{2,1,0:T(8,128)(2,1)}, u32[]{:S(2)}, u32[]{:S(2)}) async-start(bf16[8,16,6144]{2,1,0:T(8,128)(2,1)} %bitcast.103), calls=%async_computation | async-start | bytes 3145728 | tf_op jit(solution)/shard_map/all_to_all | solution.py:119
  372.0 32.9 %copy-start.5 = (bf16[1,128,6144]{2,1,0:T(8,128)(2,1)S(1)}, bf16[1,128,6144]{2,1,0:T(8,128)(2,1)}, u32[]{:S(2)}) copy-start(bf16[1,128,6144]{2,1,0:T(8,128)(2,1)} %param.13) | copy-start | bytes 4718596
  372.0 32.9 %copy-start.6 = (f32[1,128,6144]{2,1,0:T(8,128)S(1)}, f32[1,128,6144]{2,1,0:T(8,128)}, u32[]{:S(2)}) copy-start(f32[1,128,6144]{2,1,0:T(8,128)} %copy.57) | copy-start | bytes 9437188
  405.6 36.8 %collective-permute-start = (bf16[1,128,6144]{2,1,0:T(8,128)(2,1)S(1)}, bf16[1,128,6144]{2,1,0:T(8,128)(2,1)S(1)}, u32[]{:S(2)}, u32[]{:S(2)}) collective-permute-start(bf16[1,128,6144]{2,1,0:T(8,128)(2,1)S(1)} %fusion.8), channel_id=1, source_target_pairs={{0,8},{8,16},{16,24},{24,0},{1,9},{9,17},{17,25},{25,1},{2,10},{10... | collective-permute-start | bytes 4718600 | tf_op jit(solution)/shard_map/ppermute | solution.py:33
Sparse Core Ops, SparseCore 0:
  15.1 222.5 all-gather.5
  264.2 40.6 all-gather.7
where the time goes:
time: 451 us; the launch traced here: 450 us
  waiting for transfers between devices  309 us (69%)
  other arithmetic  40.5 us (9%)
  local copies, waits for them, and re-layouts  39.8 us (9%)
  matrix products  27.4 us (6%)
  between operations  13.7 us (3%)
  blocking collectives  13.5 us (3%)
  starting transfers between devices  6.34 us (1%)
    all_gather x1, waiting for transfers between devices, prefix_2(): gathered = jax.tree.map(lambda a: lax.all_gather(a, axis), part)  198 us
    all_gather x1, waiting for transfers between devices, local(): lax.all_gather(outbox[None], 'ctx', axis=0, tiled=True)  40.8 us
    ppermute x1, waiting for transfers between devices, passed_along(): return lax.ppermute(value, axis, pairs)  35.3 us
    all_to_all x1, waiting for transfers between devices, local(): lax.all_to_all(partial_value, 'ctx', split_axis=0, concat_axis=0, tiled=T...  34.6 us
    reduce_sum x1, other arithmetic, local(): mixed = picked.reshape(length, 2, D).sum(axis=1)  32.9 us
    all_gather x1, blocking collectives, prefix_2(): gathered = jax.tree.map(lambda a: lax.all_gather(a, axis), part)  13.5 us
    gather x2, local copies, waits for them, and re-layouts, local(): picked = jnp.take(summed, jnp.clip(target, 0, flying * CAP_SRC - 1), axis=0)  13.3 us
    dot_general x1, matrix products, local(): jnp.dot(hidden, down_local, preferred_element_type=jnp.float32)  9.77 us
  transfers between devices with their start and end apart: 4, of which 4 were waited for; matrix products, arithmetic and copies ran while one was open for 3% of the time, Pallas kernels for 0%

commit v1 on v0

v1 whole, which is shorter than its diff:
```python
import jax
import jax.numpy as jnp
from jax import lax
from jax.experimental import pallas as pl
from jax.experimental.pallas import tpu as pltpu
from jax.sharding import PartitionSpec as P

HEAD = 128
SHARDS = 8
CAP_SRC = 16
GROUP = 8
CHUNKS = 4

F32, BF16 = jnp.float32, jnp.bfloat16


def dot(a, b, dims=((1,), (0,))):
    return lax.dot_general(a, b, (dims, ((), ())), preferred_element_type=F32)


def split(a):
    hi = a.astype(BF16)
    return hi, (a - hi.astype(F32)).astype(BF16)


def cumul_rows(rate, cum_ref):
    length = rate.shape[0]
    upper = (
        lax.broadcasted_iota(jnp.int32, (length, length), 0)
        <= lax.broadcasted_iota(jnp.int32, (length, length), 1)
    ).astype(F32)
    cum_ref[...] = lax.dot_general(
        rate, upper, (((0,), (0,)), ((), ())), precision=lax.Precision.HIGHEST,
        preferred_element_type=F32,
    )


def state_kernel(half_ref, rate_ref, k_ref, v_ref, state_ref, decay_ref, cum_ref):
    step = pl.program_id(0)
    length = rate_ref.shape[0]

    @pl.when(step == 0)
    def _():
        cumul_rows(rate_ref[...], cum_ref)
        last = cum_ref[:, length - 1 :]
        decay_ref[...] = jnp.broadcast_to(jnp.exp(last), decay_ref.shape)

    row = (half_ref[0] * pl.num_programs(0) + step) * GROUP
    cum = cum_ref[pl.ds(pl.multiple_of(row, GROUP), GROUP), :]
    tail = jnp.exp(cum[:, length - 1 :] - cum)
    for j in range(GROUP):
        cols = slice(j * HEAD, (j + 1) * HEAD)
        turned = k_ref[:, cols].astype(F32).T * tail[j : j + 1, :]
        hi, lo = split(turned)
        v = v_ref[:, cols]
        state_ref[j] = dot(hi, v) + dot(lo, v)


def half_state(half, rate, keys, values):
    length, width = keys.shape
    heads = width // HEAD
    steps = heads // 2 // GROUP
    block = pl.BlockSpec((length, GROUP * HEAD), lambda i, h: (0, h[0] * steps + i))
    return pl.pallas_call(
        state_kernel,
        grid_spec=pltpu.PrefetchScalarGridSpec(
            num_scalar_prefetch=1,
            grid=(steps,),
            in_specs=[pl.BlockSpec((length, heads), lambda i, h: (0, 0)), block, block],
            out_specs=[
                pl.BlockSpec((GROUP, HEAD, HEAD), lambda i, h: (i, 0, 0)),
                pl.BlockSpec((heads, HEAD), lambda i, h: (0, 0)),
            ],
            scratch_shapes=[pltpu.VMEM((heads, length), F32)],
        ),
        out_shape=[
            jax.ShapeDtypeStruct((heads // 2, HEAD, HEAD), F32),
            jax.ShapeDtypeStruct((heads, HEAD), F32),
        ],
        name="half_state",
    )(half, rate, keys, values)


def intra_kernel(rate_ref, q_ref, k_ref, v_ref, out_ref, cum_ref):
    step = pl.program_id(0)
    length = rate_ref.shape[0]

    @pl.when(step == 0)
    def _():
        cumul_rows(rate_ref[...], cum_ref)

    lower = lax.broadcasted_iota(jnp.int32, (length, length), 0) >= lax.broadcasted_iota(
        jnp.int32, (length, length), 1
    )
    cum = cum_ref[pl.ds(pl.multiple_of(step * GROUP, GROUP), GROUP), :]
    for j in range(GROUP):
        cols = slice(j * HEAD, (j + 1) * HEAD)
        across = jnp.broadcast_to(cum[j : j + 1, :], (length, length))
        weights = jnp.exp(jnp.where(lower, across.T - across, -1e30))
        scores = dot(q_ref[:, cols], k_ref[:, cols], ((1,), (1,)))
        hi, lo = split(scores * weights)
        v = v_ref[:, cols]
        out_ref[:, cols] = dot(hi, v) + dot(lo, v)


def intra_attention(rate, queries, keys, values):
    length, width = keys.shape
    heads = width // HEAD
    block = pl.BlockSpec((length, GROUP * HEAD), lambda i: (0, i))
    return pl.pallas_call(
        intra_kernel,
        grid=(heads // GROUP,),
        in_specs=[pl.BlockSpec((length, heads), lambda i: (0, 0)), block, block, block],
        out_specs=block,
        out_shape=jax.ShapeDtypeStruct((length, width), F32),
        scratch_shapes=[pltpu.VMEM((heads, length), F32)],
        name="intra_attention",
    )(rate, queries, keys, values)


def finish_kernel(
    core_ref, rate_ref, q_ref, intra_ref, keep_ref, got_ref, resid_ref, again_ref, mgain_ref,
    experts_ref, weight_ref, early_ref, outbox_ref, picked_ref, wcol_ref, place_ref,
    cum_ref, attn_ref, normed_ref,
):
    step = pl.program_id(0)
    steps = pl.num_programs(0)
    length, width = resid_ref.shape

    @pl.when(step == 0)
    def _():
        cumul_rows(rate_ref[...], cum_ref)

    place = lax.rem(step + core_ref[0] * (steps // 2), steps)
    cum = cum_ref[pl.ds(pl.multiple_of(place * GROUP, GROUP), GROUP), :]

    def inter(prefix_ref):
        for j in range(GROUP):
            cols = slice(j * HEAD, (j + 1) * HEAD)
            across = jnp.broadcast_to(jnp.exp(cum[j : j + 1, :]), (length, length))
            hi, lo = split(prefix_ref[j])
            q = q_ref[:, cols]
            value = intra_ref[:, cols] + across.T * (dot(q, hi) + dot(q, lo))
            column = pl.multiple_of(place * (GROUP * HEAD) + j * HEAD, HEAD)
            attn_ref[:, pl.ds(column, HEAD)] = value

    @pl.when(step < steps // 2)
    def _():
        inter(keep_ref)

    @pl.when(step >= steps // 2)
    def _():
        inter(got_ref)

    @pl.when(step == steps - 1)
    def _():
        rows = 16

        def norm(r, carry):
            at = pl.ds(pl.multiple_of(r * rows, rows), rows)
            x = attn_ref[at, :]
            scale = lax.rsqrt(jnp.mean(x * x, axis=-1, keepdims=True) + 1e-06)
            hres = resid_ref[at, :].astype(F32) + x * scale * again_ref[...]
            attn_ref[at, :] = hres
            early_ref[at, :] = hres.astype(BF16)
            scale = lax.rsqrt(jnp.mean(hres * hres, axis=-1, keepdims=True) + 1e-06)
            normed_ref[at, :] = (hres * scale * mgain_ref[...]).astype(BF16)
            return carry

        lax.fori_loop(0, length // rows, norm, 0)
        slots = outbox_ref.shape[0]
        before = (
            lax.broadcasted_iota(jnp.int32, (length, length), 0)
            < lax.broadcasted_iota(jnp.int32, (length, length), 1)
        ).astype(BF16)
        named = experts_ref[...] == 0
        taken = jnp.max(named.astype(F32), axis=0, keepdims=True)
        slot = dot(jnp.broadcast_to(taken, (8, length)).astype(BF16), before)[0:1, :]
        slot = jnp.where(taken > 0, slot, -1.0)
        place_ref[...] = jnp.broadcast_to(slot, place_ref.shape)
        hot = lax.broadcasted_iota(jnp.int32, (slots, length), 0).astype(F32) == slot
        weight = jnp.sum(jnp.where(named, weight_ref[...], 0.0), axis=0, keepdims=True)
        weight = jnp.sum(jnp.where(hot, weight, 0.0), axis=1, keepdims=True)
        wcol_ref[...] = jnp.broadcast_to(weight, wcol_ref.shape)
        hot = hot.astype(BF16)
        outbox_ref[...] = dot(hot, normed_ref[...]).astype(BF16)
        for c in range(width // 512):
            cols = slice(c * 512, (c + 1) * 512)
            x = attn_ref[:, cols]
            hi, rest = x.astype(BF16), None
            rest = x - hi.astype(F32)
            mid, low = split(rest)
            picked_ref[:, cols] = dot(hot, hi) + dot(hot, mid) + dot(hot, low)


def finish(core, rate, queries, intra, keep, got, resid, attn_gain, moe_gain, experts, weight):
    length, width = queries.shape
    heads = width // HEAD
    steps = heads // GROUP
    half = steps // 2

    def whole(shape):
        return pl.BlockSpec(shape, lambda i, c: (0,) * len(shape))

    block = pl.BlockSpec((length, GROUP * HEAD), lambda i, c: (0, lax.rem(i + c[0] * half, steps)))
    states = (GROUP, HEAD, HEAD)
    outs = [
        ((length, width), BF16),
        ((CAP_SRC, width), BF16),
        ((CAP_SRC, width), F32),
        ((CAP_SRC, 128), F32),
        ((8, length), F32),
    ]
    return pl.pallas_call(
        finish_kernel,
        grid_spec=pltpu.PrefetchScalarGridSpec(
            num_scalar_prefetch=1,
            grid=(steps,),
            in_specs=[
                whole((length, heads)),
                block,
                block,
                pl.BlockSpec(states, lambda i, c: (jnp.minimum(i, half - 1), 0, 0)),
                pl.BlockSpec(states, lambda i, c: (jnp.maximum(i - half, 0), 0, 0)),
                whole((length, width)),
                whole((1, width)),
                whole((1, width)),
                whole((2, length)),
                whole((2, length)),
            ],
            out_specs=[whole(shape) for shape, _ in outs],
            scratch_shapes=[
                pltpu.VMEM((heads, length), F32),
                pltpu.VMEM((length, width), F32),
                pltpu.VMEM((length, width), BF16),
            ],
        ),
        out_shape=[jax.ShapeDtypeStruct(*out) for out in outs],
        name="finish",
    )(core, rate, queries, intra, keep, got, resid, attn_gain, moe_gain, experts, weight)


def expert_kernel(count, *refs):
    row_refs, (up_ref, down_ref, mine_ref, other_ref, acc_ref, hidden_ref) = refs[:count], refs[count:]
    step = pl.program_id(0)
    steps = pl.num_programs(0) // 2
    block = up_ref.shape[0]

    @pl.when(step < steps)
    def _():
        cols = pl.ds(pl.multiple_of(step * block, block), block)
        rows = jnp.concatenate([ref[:, cols] for ref in row_refs], axis=0)
        part = dot(rows, up_ref[...])

        @pl.when(step == 0)
        def _():
            acc_ref[...] = part

        @pl.when(step > 0)
        def _():
            acc_ref[...] += part

    @pl.when(step == steps - 1)
    def _():
        hidden_ref[...] = jax.nn.gelu(acc_ref[...], approximate=True).astype(BF16)

    @pl.when(step >= steps)
    def _():
        half = hidden_ref.shape[0] // 2
        part = dot(hidden_ref[...], down_ref[...]).astype(BF16)
        mine_ref[...] = part[:half]
        other_ref[...] = part[half:]


def expert_rows(rows, up, down):
    width, units = up.shape
    steps = 4
    block = width // steps
    total = sum(r.shape[0] for r in rows)

    def part(i):
        return jnp.maximum(i - steps, 0)

    out = pl.BlockSpec((total // 2, block), lambda i: (0, part(i)))
    return pl.pallas_call(
        lambda *refs: expert_kernel(len(rows), *refs),
        grid=(2 * steps,),
        in_specs=[pl.BlockSpec(r.shape, lambda i: (0, 0)) for r in rows]
        + [
            pl.BlockSpec((block, units), lambda i: (jnp.minimum(i, steps - 1), 0)),
            pl.BlockSpec((units, block), lambda i: (0, part(i))),
        ],
        out_specs=[out, out],
        out_shape=[jax.ShapeDtypeStruct((total // 2, width), BF16)] * 2,
        scratch_shapes=[pltpu.VMEM((total, units), F32), pltpu.VMEM((total, units), BF16)],
        name="expert_rows",
    )(*rows, up, down)


def passed_along(value, axis, steps):
    count = lax.axis_size(axis)
    pairs = [(source, (source + steps) % count) for source in range(count)]
    return lax.ppermute(value, axis, pairs)


def swapped(value):
    count = lax.axis_size("ctx")
    return lax.ppermute(value, "ctx", [(i, i ^ 1) for i in range(count)])


def chain_prefix(total, decay, chip, chips, scale):
    heads = total.shape[0]
    per = heads // CHUNKS
    received = []
    for step in range(CHUNKS + chips - 2):
        place = jnp.clip(step - chip, 0, CHUNKS - 1) * per
        gone = lax.dynamic_slice_in_dim(total, place, per, 0) * scale
        if step >= 1:
            before = received[step - 1].astype(F32)
            gone = lax.dynamic_slice_in_dim(decay, place, per, 0)[:, None, :] * before + gone
        pairs = [
            (2 * z + core, 2 * z + 2 + core)
            for z in range(chips - 1)
            if 0 <= step - z < CHUNKS
            for core in range(2)
        ]
        received.append(lax.ppermute(gone.astype(jnp.float16), "ctx", pairs))
    row = jnp.concatenate(received, axis=0)
    first = jnp.maximum(chip - 1, 0) * per
    mine = lax.dynamic_slice_in_dim(row, first, heads, 0).astype(F32) * (1.0 / scale)
    return jnp.where(chip > 0, mine, 0.0)


def local(
    resid,
    queries,
    keys,
    values,
    log_decay,
    attn_gain,
    moe_gain,
    experts,
    combine_weight,
    w_up,
    w_down,
):
    return layer(
        resid[0], queries[0], keys[0], values[0], log_decay[0], attn_gain, moe_gain,
        experts[0], combine_weight[0], w_up[0], w_down[0],
    )


def layer(resid, queries, keys, values, rate, attn_gain, moe_gain, experts, weight, up, down):
    length, width = queries.shape
    count = lax.axis_size("ctx")
    me = lax.axis_index("ctx")
    chips, chip, core = count // 2, me // 2, me % 2
    half = width // HEAD // 2
    first = core == 0
    core1 = core.astype(jnp.int32)[None]

    other, decay = half_state(1 - core1, rate, keys, values)
    partner = swapped(other)
    decay_partner = swapped(decay)
    mine, _ = half_state(core1, rate, keys, values)
    decay = lax.dynamic_slice_in_dim(decay, core * half, half, 0)
    decay_partner = lax.dynamic_slice_in_dim(decay_partner, core * half, half, 0)
    state0, state1 = jnp.where(first, mine, partner), jnp.where(first, partner, mine)
    decay0, decay1 = (
        jnp.where(first, decay, decay_partner),
        jnp.where(first, decay_partner, decay),
    )
    scale = 1.0
    while 36.0 * count * length * scale > 65000.0:
        scale = scale / 2
    total = decay1[:, None, :] * state0 + state1
    prefix = chain_prefix(total, decay0 * decay1, chip, chips, scale)
    after0 = decay0[:, None, :] * prefix + state0
    keep = jnp.where(first, prefix, after0)
    got = swapped(jnp.where(first, after0, prefix))
    intra = intra_attention(rate, queries, keys, values)
    flying = count // SHARDS
    if flying > 1:
        prefix = jnp.where(first, jnp.concatenate([keep, got]), jnp.concatenate([got, keep]))
        return many_experts(
            flying, rate, queries, intra, prefix, resid, attn_gain, moe_gain, experts, weight, up, down
        )
    early, outbox, picked, wcol, place = finish(
        core1, rate, queries, intra, keep, got, resid, attn_gain, moe_gain, experts.T, weight.T
    )
    early = passed_along(early, "section", 1)
    place = passed_along(place, "section", 1)
    own = [outbox] + [
        lax.ppermute(outbox, "ctx", [(i, (i + 2 * d) % count) for i in range(count)])
        for d in range(1, chips)
    ]
    others = [swapped(r) for r in own]
    mine, other = expert_rows(own + others, up, down)
    pair = (mine.astype(F32) + swapped(other).astype(F32)).astype(BF16)
    pair = pair.reshape(chips, CAP_SRC, width)
    summed = pair[0].astype(F32)
    for d in range(1, chips):
        back = lax.ppermute(pair[d], "ctx", [(i, (i - 2 * d) % count) for i in range(count)])
        summed = summed + back.astype(F32)
    late = (picked + wcol[:, :1] * summed).astype(BF16)
    late = passed_along(late, "section", 1)
    found = (place[:1] == jnp.arange(CAP_SRC, dtype=F32)[:, None]).astype(BF16)
    rows = lax.dot_general(
        found, late, (((0,), (0,)), ((), ())), preferred_element_type=F32
    ).astype(BF16)
    return jnp.where(place[0][:, None] >= 0, rows, early)[None]


def rms_scale(values_in, gain):
    return (
        values_in
        * lax.rsqrt(jnp.mean(values_in * values_in, axis=-1, keepdims=True) + 1e-06)
        * gain
    )


def many_experts(
    flying, rate, queries, intra, prefix, resid, attn_gain, moe_gain, experts, weight, up, down
):
    length, width = queries.shape
    heads = width // HEAD
    count = lax.axis_size("ctx")
    inter = jnp.exp(jnp.cumsum(rate, axis=0))[:, :, None] * jnp.einsum(
        "thd,hde->the",
        queries.astype(F32).reshape(length, heads, HEAD),
        prefix,
        precision=lax.Precision.HIGHEST,
    )
    hres = resid.astype(F32) + rms_scale(intra + inter.reshape(length, width), attn_gain)
    normed = rms_scale(hres, moe_gain).astype(BF16)
    slots = flying * CAP_SRC
    chosen = experts.reshape(-1)
    onehot = (chosen[:, None] == jnp.arange(flying)[None, :]).astype(jnp.int32)
    slot = jnp.sum((jnp.cumsum(onehot, axis=0) - onehot) * onehot, axis=1)
    target = jnp.where(chosen < flying, chosen * CAP_SRC + slot, -1)
    hot = (target[None, :] == jnp.arange(slots)[:, None]).reshape(slots, length, 2)
    outbox = dot(hot.any(axis=2).astype(BF16), normed).astype(BF16)
    outbox = outbox.reshape(1, flying, CAP_SRC, width)
    mine = lax.dynamic_index_in_dim(
        lax.all_gather(outbox, "ctx", axis=0, tiled=True), lax.axis_index("ctx") // SHARDS, 1, False
    )
    hidden = jax.nn.gelu(dot(mine.reshape(count * CAP_SRC, width), up), approximate=True)
    part = dot(hidden.astype(BF16), down).astype(BF16).reshape(count, CAP_SRC, width)
    returned = lax.all_to_all(part, "ctx", split_axis=0, concat_axis=0, tiled=True)
    summed = returned.reshape(flying, SHARDS, CAP_SRC, width).astype(F32).sum(axis=1)
    mixed = lax.dot_general(
        jnp.where(hot, weight[None], 0.0).sum(axis=2),
        summed.reshape(slots, width),
        (((0,), (0,)), ((), ())),
        precision=lax.Precision.HIGHEST,
    )
    return passed_along((hres + mixed).astype(BF16)[None], "section", 1)


def solution(mesh):
    return jax.shard_map(
        local,
        mesh=mesh,
        in_specs=(
            P("section", "ctx", None),
            P("section", "ctx", None),
            P("section", "ctx", None),
            P("section", "ctx", None),
            P("section", "ctx", None),
            P("section", None),
            P("section", None),
            P("section", "ctx", None),
            P("section", "ctx", None),
            P("section", None, "ctx"),
            P("section", "ctx", None),
        ),
        out_specs=P("section", "ctx", None),
        check_vma=False,
    )
```

time: 451 us -> 163 us (0.36)
  waiting for transfers between devices: 309 us -> 61.3 us
  starting transfers between devices: 6.34 us -> 46.4 us
  Pallas kernels: 0 us -> 39.2 us
  local copies, waits for them, and re-layouts: 39.8 us -> 6.07 us
  other arithmetic: 40.5 us -> 7.51 us
  matrix products: 27.4 us -> 1.77 us
  blocking collectives: 13.5 us -> 0 us
  between operations: 13.7 us -> 0.32 us
    all_gather x2 -> x0, waiting for transfers between devices: 239 us -> none  [the longest x1 198 us: prefix_2(): gathered = jax.tree.map(lambda a: lax.all_gather(a, axis), part)]
    ppermute x0 -> x20, waiting for transfers between devices: none -> 45.6 us  [the longest x3 15.9 us: layer(): lax.ppermute(outbox, 'ctx', [(i, (i + 2 * d) % count) for i in range(coun...]
    ppermute x0 -> x20, starting transfers between devices: none -> 41.9 us  [the longest x6 20.3 us: chain_prefix(): received.append(lax.ppermute(gone.astype(jnp.float16), 'ctx', pairs))]
    pallas_call x0 -> x5, Pallas kernels: none -> 39.2 us  [the longest x1 11.9 us: finish(): pl.pallas_call(finish_kernel, grid_spec=pltpu.PrefetchScalarGridSpec(num_...]
    reduce_sum x4 -> x0, other arithmetic: 36.9 us -> none  [the longest x1 32.9 us: local(): mixed = picked.reshape(length, 2, D).sum(axis=1)]
    all_to_all x1 -> x0, waiting for transfers between devices: 34.6 us -> none  [local(): lax.all_to_all(partial_value, 'ctx', split_axis=0, concat_axis=0, tiled=T...]
    dot_general x6 -> x1, matrix products: 27.4 us -> 1.77 us  [layer(): lax.dot_general(found, late, (((0,), (0,)), ((), ())), preferred_element_...]
    ppermute x1 -> x3, waiting for transfers between devices: 35.3 us -> 15.8 us  [passed_along(): return lax.ppermute(value, axis, pairs)]
  transfers between devices with their start and end apart: 4 -> 23, of which waited for: 4 -> 13; matrix products, arithmetic and copies ran while one was open for 3% -> 3% of each run, Pallas kernels for 0% -> 7%
where the time goes in v1:
time: 163 us
  waiting for transfers between devices  61.3 us (38%)
  starting transfers between devices  46.4 us (28%)
  Pallas kernels  39.2 us (24%)
  other arithmetic  7.51 us (5%)
  local copies, waits for them, and re-layouts  6.07 us (4%)
  matrix products  1.77 us (1%)
    ppermute x6, starting transfers between devices, chain_prefix(): received.append(lax.ppermute(gone.astype(jnp.float16), 'ctx', pairs))  20.3 us
    ppermute x3, waiting for transfers between devices, layer(): lax.ppermute(outbox, 'ctx', [(i, (i + 2 * d) % count) for i in range(coun...  15.9 us
    ppermute x3, waiting for transfers between devices, passed_along(): return lax.ppermute(value, axis, pairs)  15.8 us
    ppermute x3, waiting for transfers between devices, layer(): lax.ppermute(pair[d], 'ctx', [(i, (i - 2 * d) % count) for i in range(cou...  15.5 us
    ppermute x3, starting transfers between devices, layer(): lax.ppermute(outbox, 'ctx', [(i, (i + 2 * d) % count) for i in range(coun...  14.9 us
    ppermute x6, waiting for transfers between devices, chain_prefix(): received.append(lax.ppermute(gone.astype(jnp.float16), 'ctx', pairs))  13 us
    pallas_call x1, Pallas kernels, finish(): pl.pallas_call(finish_kernel, grid_spec=pltpu.PrefetchScalarGridSpec(num_...  11.9 us
    pallas_call x1, Pallas kernels, expert_rows(): pl.pallas_call(lambda *refs: expert_kernel(len(rows), *refs), grid=(2 * s...  11.5 us
  transfers between devices with their start and end apart: 23, of which 13 were waited for; matrix products, arithmetic and copies ran while one was open for 3% of the time, Pallas kernels for 7%

profile of v1, /device:TPU:0, one launch (start us, length us, event | category | flops | bytes accessed | tf_op | source)
XLA Modules:
  0.0 162.6 jit_solution(12114888496580661953)
XLA Ops:
  0.0 1.5 copy.13
  1.5 4.2 %half_state.2 = (f32[24,128,128]{2,1,0:T(8,128)}, f32[48,128]{1,0:T(8,128)}) custom-call(s32[1]{0:T(128)S(6)} %sub.29.half_ref, f32[128,48]{1,0:T(8,128)} %bitcast.31, bf16[128,6144]{1,0:T(8,128)(2,1)} %bitcast.21, bf16[128,6144]{1,0:T(8,128)(2,1)} %bitcast.24), custom_call_target="tpu_custom_call" | custom-call | tf_op jit(solution)/shard_map/half_state/pallas_call | solution.py:64
  5.7 0.5 collective-permute-start.1
  6.2 4.2 %half_state.3 = (f32[24,128,128]{2,1,0:T(8,128)}, f32[48,128]{1,0:T(8,128)}) custom-call(s32[1]{0:T(128)} %bitcast.half_ref.core_ref, f32[128,48]{1,0:T(8,128)} %bitcast.32, bf16[128,6144]{1,0:T(8,128)(2,1)} %bitcast.22, bf16[128,6144]{1,0:T(8,128)(2,1)} %bitcast.25), custom_call_target="tpu_custom_call" | custom-call | tf_op jit(solution)/shard_map/half_state/pallas_call | solution.py:64
  10.4 0.6 fusion.3
  11.0 1.7 %select_add_fusion = f32[24,128,128]{2,1,0:T(8,128)S(1)} fusion(f32[24,128,128]{2,1,0:T(8,128)S(1)} %collective-permute-done.1, f32[24,128,128]{2,1,0:T(8,128)} %get-tuple-element.16, f32[24,128]{1,0:T(8,128)S(1)} %get-tuple-element.26, pred[]{:T(512)S(6)} %eq.18), kind=kLoop, calls=%fused_computation.7 | loop fusion | flops 1572864 | bytes 4730881 | tf_op jit(solution)/shard_map/add | solution.py:376
  12.7 5.0 %collective-permute-start.2 = (f16[6,128,128]{2,1,0:T(8,128)(2,1)S(1)}, f16[6,128,128]{2,1,0:T(8,128)(2,1)S(1)}, u32[]{:S(2)}, u32[]{:S(2)}) collective-permute-start(f16[6,128,128]{2,1,0:T(8,128)(2,1)S(1)} %dynamic-slice_convert_fusion), channel_id=1, source_target_pairs={{0,2},{1,3},{8,10},{9,11},{16,18},{17,19},{24,26},{25,27}} | collective-permute-start | bytes 589832 | tf_op jit(solution)/shard_map/ppermute | solution.py:327
  17.8 0.6 constant_dynamic-slice_fusion
  18.4 3.6 %collective-permute-done.2 = f16[6,128,128]{2,1,0:T(8,128)(2,1)S(1)} collective-permute-done((f16[6,128,128]{2,1,0:T(8,128)(2,1)S(1)}, f16[6,128,128]{2,1,0:T(8,128)(2,1)S(1)}, u32[]{:S(2)}, u32[]{:S(2)}) %collective-permute-start.2) | collective-permute-done | bytes 196640 | tf_op jit(solution)/shard_map/ppermute | solution.py:327
  22.1 4.4 %collective-permute-start.3 = (f16[6,128,128]{2,1,0:T(8,128)(2,1)S(1)}, f16[6,128,128]{2,1,0:T(8,128)(2,1)S(1)}, u32[]{:S(2)}, u32[]{:S(2)}) collective-permute-start(f16[6,128,128]{2,1,0:T(8,128)(2,1)S(1)} %add_convert_fusion.6), channel_id=1, source_target_pairs={{0,2},{1,3},{2,4},{3,5},{8,10},{9,11},{10,12},{11,13},{16,18},{17,... | collective-permute-start | bytes 589832 | tf_op jit(solution)/shard_map/ppermute | solution.py:327
  26.5 3.4 %collective-permute-done.3 = f16[6,128,128]{2,1,0:T(8,128)(2,1)S(1)} collective-permute-done((f16[6,128,128]{2,1,0:T(8,128)(2,1)S(1)}, f16[6,128,128]{2,1,0:T(8,128)(2,1)S(1)}, u32[]{:S(2)}, u32[]{:S(2)}) %collective-permute-start.3) | collective-permute-done | bytes 196640 | tf_op jit(solution)/shard_map/ppermute | solution.py:327
  30.0 4.4 %collective-permute-start.4 = (f16[6,128,128]{2,1,0:T(8,128)(2,1)S(1)}, f16[6,128,128]{2,1,0:T(8,128)(2,1)S(1)}, u32[]{:S(2)}, u32[]{:S(2)}) collective-permute-start(f16[6,128,128]{2,1,0:T(8,128)(2,1)S(1)} %add_convert_fusion.5), channel_id=1, source_target_pairs={{0,2},{1,3},{2,4},{3,5},{4,6},{5,7},{8,10},{9,11},{10,12},{11,13},... | collective-permute-start | bytes 589832 | tf_op jit(solution)/shard_map/ppermute | solution.py:327
  34.4 3.2 %collective-permute-done.4 = f16[6,128,128]{2,1,0:T(8,128)(2,1)S(1)} collective-permute-done((f16[6,128,128]{2,1,0:T(8,128)(2,1)S(1)}, f16[6,128,128]{2,1,0:T(8,128)(2,1)S(1)}, u32[]{:S(2)}, u32[]{:S(2)}) %collective-permute-start.4) | collective-permute-done | bytes 196640 | tf_op jit(solution)/shard_map/ppermute | solution.py:327
  37.5 0.7 copy-done.2
  38.2 0.8 add_convert_fusion.4
  39.0 5.1 %collective-permute-start.5 = (f16[6,128,128]{2,1,0:T(8,128)(2,1)}, f16[6,128,128]{2,1,0:T(8,128)(2,1)}, u32[]{:S(2)}, u32[]{:S(2)}) collective-permute-start(f16[6,128,128]{2,1,0:T(8,128)(2,1)} %add_convert_fusion.4), channel_id=1, source_target_pairs={{0,2},{1,3},{2,4},{3,5},{4,6},{5,7},{8,10},{9,11},{10,12},{11,13},... | collective-permute-start | bytes 589832 | tf_op jit(solution)/shard_map/ppermute | solution.py:327
  44.1 2.8 %collective-permute-done.5 = f16[6,128,128]{2,1,0:T(8,128)(2,1)} collective-permute-done((f16[6,128,128]{2,1,0:T(8,128)(2,1)}, f16[6,128,128]{2,1,0:T(8,128)(2,1)}, u32[]{:S(2)}, u32[]{:S(2)}) %collective-permute-start.5) | collective-permute-done | bytes 196640 | tf_op jit(solution)/shard_map/ppermute | solution.py:327
  46.8 1.0 add_convert_fusion.3
  47.9 0.8 collective-permute-start.6
  48.9 0.7 collective-permute-start.7
  49.6 1.0 constant_dynamic-update-slice_fusion.2
  50.7 1.7 %fusion = (f32[24,128,128]{2,1,0:T(8,128)S(1)}, f32[24,128,128]{2,1,0:T(8,128)}) fusion(f32[24,128]{1,0:T(8,128)S(1)} %copy-done.12, pred[]{:T(512)S(6)} %gt.3, pred[]{:T(512)S(6)} %eq.18, f32[24,128,128]{2,1,0:T(8,128)S(1)} %copy-done, f32[24,128,128]{2,1,0:T(8,128)S(1)} %collective-permute-done.1, ...), kind=kLoop, calls=%fused_computation.4 | loop fusion | flops 2752512 | bytes 7090182 | tf_op jit(solution)/shard_map/jit(_where)/select_n | solution.py:380
  52.4 7.3 %intra_attention.1.intra_ref = f32[128,6144]{1,0:T(8,128)} custom-call(f32[128,48]{1,0:T(8,128)} %bitcast.33, bf16[128,6144]{1,0:T(8,128)(2,1)} %bitcast.29, bf16[128,6144]{1,0:T(8,128)(2,1)} %bitcast.23, bf16[128,6144]{1,0:T(8,128)(2,1)} %bitcast.26), custom_call_target="tpu_custom_call" | custom-call | tf_op jit(solution)/shard_map/intra_attention/pallas_call | solution.py:110
  59.8 1.2 copy-done.1
  61.0 11.9 %finish.1 = (bf16[128,6144]{1,0:T(8,128)(2,1)}, bf16[16,6144]{1,0:T(8,128)(2,1)}, f32[16,6144]{1,0:T(8,128)}, f32[16,128]{1,0:T(8,128)}, f32[8,128]{1,0:T(8,128)}) custom-call(s32[1]{0:T(128)} %bitcast.half_ref.core_ref, f32[128,48]{1,0:T(8,128)} %bitcast.34, bf16[128,6144]{1,0:T(8,128)(2,1)} %bitcast.30, f32[128,6144]{1,0:T(8,128)} %intra_attention.1.intra_ref, ...), custom_call_target="tpu_custom_call" | custom-call | tf_op jit(solution)/shard_map/finish/pallas_call | solution.py:214
  72.9 14.3 %collective-permute-start.12 = (bf16[16,6144]{1,0:T(8,128)(2,1)}, bf16[16,6144]{1,0:T(8,128)(2,1)S(1)}, u32[]{:S(2)}, u32[]{:S(2)}) collective-permute-start(bf16[16,6144]{1,0:T(8,128)(2,1)} %get-tuple-element.21.refs_0_), channel_id=1, source_target_pairs={{0,6},{1,7},{2,0},{3,1},{4,2},{5,3},{6,4},{7,5},{8,14},{9,15},{10,... | collective-permute-start | bytes 589832 | tf_op jit(solution)/shard_map/ppermute | solution.py:394
  87.2 0.6 collective-permute-start.10
  87.8 5.1 %collective-permute-done.12.refs_3_ = bf16[16,6144]{1,0:T(8,128)(2,1)S(1)} collective-permute-done((bf16[16,6144]{1,0:T(8,128)(2,1)}, bf16[16,6144]{1,0:T(8,128)(2,1)S(1)}, u32[]{:S(2)}, u32[]{:S(2)}) %collective-permute-start.12) | collective-permute-done | bytes 196640 | tf_op jit(solution)/shard_map/ppermute | solution.py:394
  92.9 10.9 %collective-permute-done.11.refs_2_ = bf16[16,6144]{1,0:T(8,128)(2,1)S(1)} collective-permute-done((bf16[16,6144]{1,0:T(8,128)(2,1)}, bf16[16,6144]{1,0:T(8,128)(2,1)S(1)}, u32[]{:S(2)}, u32[]{:S(2)}) %collective-permute-start.11) | collective-permute-done | bytes 196640 | tf_op jit(solution)/shard_map/ppermute | solution.py:394
  103.8 0.5 collective-permute-start.14
  104.3 0.9 collective-permute-done.15.refs_6_
  105.2 0.3 collective-permute-done.14.refs_5_
  105.5 0.4 copy-done.10
  105.9 0.3 copy-done.11
  106.2 11.5 %expert_rows.1 = (bf16[64,6144]{1,0:T(8,128)(2,1)}, bf16[64,6144]{1,0:T(8,128)(2,1)}) custom-call(bf16[16,6144]{1,0:T(8,128)(2,1)} %get-tuple-element.21.refs_0_, bf16[16,6144]{1,0:T(8,128)(2,1)} %copy-done.7, bf16[16,6144]{1,0:T(8,128)(2,1)} %copy-done.6, bf16[16,6144]{1,0:T(8,128)(2,1)} %copy-done.5, bf16[16,6144]{1,0:T(8,128)(2,1)} %copy-done.8, ...), custom_call_target="tpu_custom_call" | custom-call | tf_op jit(solution)/shard_map/expert_rows/pallas_call | solution.py:285
  117.9 1.5 collective-permute-start.9
  119.4 1.5 collective-permute-start.22
  121.0 1.4 add_convert_fusion
  122.5 0.9 collective-permute-start.18
  123.4 1.2 collective-permute-start.20
  124.5 3.3 %collective-permute-start.19 = (bf16[16,6144]{1,0:T(8,128)(2,1)S(1)}, bf16[16,6144]{1,0:T(8,128)(2,1)S(1)}, u32[]{:S(2)}, u32[]{:S(2)}) collective-permute-start(bf16[16,6144]{1,0:T(8,128)(2,1)S(1)} %get-tuple-element.32), channel_id=1, source_target_pairs={{0,4},{1,5},{2,6},{3,7},{4,0},{5,1},{6,2},{7,3},{8,12},{9,13},{10,... | collective-permute-start | bytes 589832 | tf_op jit(solution)/shard_map/ppermute | solution.py:403
  127.9 1.1 collective-permute-done.18
  129.0 8.3 %collective-permute-done.20 = bf16[16,6144]{1,0:T(8,128)(2,1)S(1)} collective-permute-done((bf16[16,6144]{1,0:T(8,128)(2,1)S(1)}, bf16[16,6144]{1,0:T(8,128)(2,1)S(1)}, u32[]{:S(2)}, u32[]{:S(2)}) %collective-permute-start.20) | collective-permute-done | bytes 196640 | tf_op jit(solution)/shard_map/ppermute | solution.py:403
  137.4 6.0 %collective-permute-done.19 = bf16[16,6144]{1,0:T(8,128)(2,1)S(1)} collective-permute-done((bf16[16,6144]{1,0:T(8,128)(2,1)S(1)}, bf16[16,6144]{1,0:T(8,128)(2,1)S(1)}, u32[]{:S(2)}, u32[]{:S(2)}) %collective-permute-start.19) | collective-permute-done | bytes 196640 | tf_op jit(solution)/shard_map/ppermute | solution.py:403
  143.5 1.5 collective-permute-start.21
  145.0 12.5 %collective-permute-done.22 = bf16[128,6144]{1,0:T(8,128)(2,1)S(1)} collective-permute-done((bf16[128,6144]{1,0:T(8,128)(2,1)S(1)}, bf16[128,6144]{1,0:T(8,128)(2,1)S(1)}, u32[]{:S(2)}, u32[]{:S(2)}) %collective-permute-start.22) | collective-permute-done | bytes 1572896 | tf_op jit(solution)/shard_map/ppermute | solution.py:303
  157.6 3.2 %collective-permute-done.21 = bf16[16,6144]{1,0:T(8,128)(2,1)S(1)} collective-permute-done((bf16[16,6144]{1,0:T(8,128)(2,1)S(1)}, bf16[16,6144]{1,0:T(8,128)(2,1)S(1)}, u32[]{:S(2)}, u32[]{:S(2)}) %collective-permute-start.21) | collective-permute-done | bytes 196640 | tf_op jit(solution)/shard_map/ppermute | solution.py:303
  160.8 1.8 %select_bitcast_fusion = bf16[1,128,6144]{2,1,0:T(8,128)(2,1)} fusion(bf16[128,6144]{1,0:T(8,128)(2,1)S(1)} %collective-permute-done.22, pred[128]{0:T(512)(128)(4,1)S(1)} %broadcast_compare_fusion, bf16[16,6144]{1,0:T(8,128)(2,1)S(1)} %collective-permute-done.21, f32[128]{0:T(128)S(1)} %slice_bitcast_fusion), kind=kOutput, calls=%fused_computation.1 | convolution fusion | flops 26740736 | bytes 3342976 | tf_op jit(solution)/shard_map/dot_general | solution.py:408
  (63 shorter events, 1.2 us)
Async XLA Ops:
  5.7 5.3 %collective-permute-start.1 = (f32[24,128,128]{2,1,0:T(8,128)}, f32[24,128,128]{2,1,0:T(8,128)S(1)}, u32[]{:S(2)}, u32[]{:S(2)}) collective-permute-start(f32[24,128,128]{2,1,0:T(8,128)} %get-tuple-element.17), channel_id=1, source_target_pairs={{0,1},{1,0},{2,3},{3,2},{4,5},{5,4},{6,7},{7,6},{8,9},{9,8},{10,11... | collective-permute-start | bytes 4718600 | tf_op jit(solution)/shard_map/ppermute | solution.py:308
  6.2 4.2 %collective-permute-start = (f32[48,128]{1,0:T(8,128)}, f32[48,128]{1,0:T(8,128)S(1)}, u32[]{:S(2)}, u32[]{:S(2)}) collective-permute-start(f32[48,128]{1,0:T(8,128)} %get-tuple-element.15), channel_id=1, source_target_pairs={{0,1},{1,0},{2,3},{3,2},{4,5},{5,4},{6,7},{7,6},{8,9},{9,8},{10,11... | collective-permute-start | bytes 73736 | tf_op jit(solution)/shard_map/ppermute | solution.py:308
  6.2 4.2 %copy-start.15 = (f32[48,128]{1,0:T(8,128)S(1)}, f32[48,128]{1,0:T(8,128)}, u32[]{:S(2)}) copy-start(f32[48,128]{1,0:T(8,128)} %get-tuple-element.15) | copy-start | bytes 73732
  12.7 9.3 %collective-permute-start.2 = (f16[6,128,128]{2,1,0:T(8,128)(2,1)S(1)}, f16[6,128,128]{2,1,0:T(8,128)(2,1)S(1)}, u32[]{:S(2)}, u32[]{:S(2)}) collective-permute-start(f16[6,128,128]{2,1,0:T(8,128)(2,1)S(1)} %dynamic-slice_convert_fusion), channel_id=1, source_target_pairs={{0,2},{1,3},{8,10},{9,11},{16,18},{17,19},{24,26},{25,27}} | collective-permute-start | bytes 589832 | tf_op jit(solution)/shard_map/ppermute | solution.py:327
  18.4 28.5 %copy-start.13 = (f32[6,128]{1,0:T(8,128)S(1)}, f32[6,128]{1,0:T(8,128)}, u32[]{:S(2)}) copy-start(f32[6,128]{1,0:T(8,128)} %get-tuple-element.34) | copy-start | bytes 9220
  22.1 7.8 %collective-permute-start.3 = (f16[6,128,128]{2,1,0:T(8,128)(2,1)S(1)}, f16[6,128,128]{2,1,0:T(8,128)(2,1)S(1)}, u32[]{:S(2)}, u32[]{:S(2)}) collective-permute-start(f16[6,128,128]{2,1,0:T(8,128)(2,1)S(1)} %add_convert_fusion.6), channel_id=1, source_target_pairs={{0,2},{1,3},{2,4},{3,5},{8,10},{9,11},{10,12},{11,13},{16,18},{17,... | collective-permute-start | bytes 589832 | tf_op jit(solution)/shard_map/ppermute | solution.py:327
  30.0 7.6 %collective-permute-start.4 = (f16[6,128,128]{2,1,0:T(8,128)(2,1)S(1)}, f16[6,128,128]{2,1,0:T(8,128)(2,1)S(1)}, u32[]{:S(2)}, u32[]{:S(2)}) collective-permute-start(f16[6,128,128]{2,1,0:T(8,128)(2,1)S(1)} %add_convert_fusion.5), channel_id=1, source_target_pairs={{0,2},{1,3},{2,4},{3,5},{4,6},{5,7},{8,10},{9,11},{10,12},{11,13},... | collective-permute-start | bytes 589832 | tf_op jit(solution)/shard_map/ppermute | solution.py:327
  37.5 0.7 copy-start.2
  39.0 7.9 %collective-permute-start.5 = (f16[6,128,128]{2,1,0:T(8,128)(2,1)}, f16[6,128,128]{2,1,0:T(8,128)(2,1)}, u32[]{:S(2)}, u32[]{:S(2)}) collective-permute-start(f16[6,128,128]{2,1,0:T(8,128)(2,1)} %add_convert_fusion.4), channel_id=1, source_target_pairs={{0,2},{1,3},{2,4},{3,5},{4,6},{5,7},{8,10},{9,11},{10,12},{11,13},... | collective-permute-start | bytes 589832 | tf_op jit(solution)/shard_map/ppermute | solution.py:327
  44.0 4.7 %copy-start.3 = (f16[6,128,128]{2,1,0:T(8,128)(2,1)S(1)}, f16[6,128,128]{2,1,0:T(8,128)(2,1)}, u32[]{:S(2)}) copy-start(f16[6,128,128]{2,1,0:T(8,128)(2,1)} %copy-done.2) | copy-start | bytes 589828
  47.8 2.9 %copy-start = (f32[24,128,128]{2,1,0:T(8,128)S(1)}, f32[24,128,128]{2,1,0:T(8,128)}, u32[]{:S(2)}) copy-start(f32[24,128,128]{2,1,0:T(8,128)} %get-tuple-element.16) | copy-start | bytes 4718596
  47.8 2.9 %copy-start.12 = (f32[24,128]{1,0:T(8,128)S(1)}, f32[24,128]{1,0:T(8,128)}, u32[]{:S(2)}) copy-start(f32[24,128]{1,0:T(8,128)} %get-tuple-element.27) | copy-start | bytes 36868
  47.9 1.0 collective-permute-start.6
  48.9 1.7 %collective-permute-start.7 = (f16[6,128,128]{2,1,0:T(8,128)(2,1)S(1)}, f16[6,128,128]{2,1,0:T(8,128)(2,1)S(1)}, u32[]{:S(2)}, u32[]{:S(2)}) collective-permute-start(f16[6,128,128]{2,1,0:T(8,128)(2,1)S(1)} %add_convert_fusion.2), channel_id=1, source_target_pairs={{4,6},{5,7},{12,14},{13,15},{20,22},{21,23},{28,30},{29,31}} | collective-permute-start | bytes 589832 | tf_op jit(solution)/shard_map/ppermute | solution.py:327
  52.4 7.4 %collective-permute-start.8 = (f32[24,128,128]{2,1,0:T(8,128)S(1)}, f32[24,128,128]{2,1,0:T(8,128)S(1)}, u32[]{:S(2)}, u32[]{:S(2)}) collective-permute-start(f32[24,128,128]{2,1,0:T(8,128)S(1)} %get-tuple-element.28), channel_id=1, source_target_pairs={{0,1},{1,0},{2,3},{3,2},{4,5},{5,4},{6,7},{7,6},{8,9},{9,8},{10,11... | collective-permute-start | bytes 4718600 | tf_op jit(solution)/shard_map/ppermute | solution.py:308
  59.8 1.2 copy-start.1
  72.9 20.0 %collective-permute-start.12 = (bf16[16,6144]{1,0:T(8,128)(2,1)}, bf16[16,6144]{1,0:T(8,128)(2,1)S(1)}, u32[]{:S(2)}, u32[]{:S(2)}) collective-permute-start(bf16[16,6144]{1,0:T(8,128)(2,1)} %get-tuple-element.21.refs_0_), channel_id=1, source_target_pairs={{0,6},{1,7},{2,0},{3,1},{4,2},{5,3},{6,4},{7,5},{8,14},{9,15},{10,... | collective-permute-start | bytes 589832 | tf_op jit(solution)/shard_map/ppermute | solution.py:394
  87.2 16.6 %collective-permute-start.11 = (bf16[16,6144]{1,0:T(8,128)(2,1)}, bf16[16,6144]{1,0:T(8,128)(2,1)S(1)}, u32[]{:S(2)}, u32[]{:S(2)}) collective-permute-start(bf16[16,6144]{1,0:T(8,128)(2,1)} %get-tuple-element.21.refs_0_), channel_id=1, source_target_pairs={{0,4},{1,5},{2,6},{3,7},{4,0},{5,1},{6,2},{7,3},{8,12},{9,13},{10,... | collective-permute-start | bytes 589832 | tf_op jit(solution)/shard_map/ppermute | solution.py:394
  87.2 16.6 %collective-permute-start.10 = (bf16[16,6144]{1,0:T(8,128)(2,1)}, bf16[16,6144]{1,0:T(8,128)(2,1)S(1)}, u32[]{:S(2)}, u32[]{:S(2)}) collective-permute-start(bf16[16,6144]{1,0:T(8,128)(2,1)} %get-tuple-element.21.refs_0_), channel_id=1, source_target_pairs={{0,2},{1,3},{2,4},{3,5},{4,6},{5,7},{6,0},{7,1},{8,10},{9,11},{10,... | collective-permute-start | bytes 589832 | tf_op jit(solution)/shard_map/ppermute | solution.py:394
  87.8 16.4 %collective-permute-start.13 = (bf16[16,6144]{1,0:T(8,128)(2,1)}, bf16[16,6144]{1,0:T(8,128)(2,1)S(1)}, u32[]{:S(2)}, u32[]{:S(2)}) collective-permute-start(bf16[16,6144]{1,0:T(8,128)(2,1)} %get-tuple-element.21.refs_0_), channel_id=1, source_target_pairs={{0,1},{1,0},{2,3},{3,2},{4,5},{5,4},{6,7},{7,6},{8,9},{9,8},{10,11... | collective-permute-start | bytes 589832 | tf_op jit(solution)/shard_map/ppermute | solution.py:308
  92.9 12.6 %copy-start.5 = (bf16[16,6144]{1,0:T(8,128)(2,1)}, bf16[16,6144]{1,0:T(8,128)(2,1)S(1)}, u32[]{:S(2)}) copy-start(bf16[16,6144]{1,0:T(8,128)(2,1)S(1)} %collective-permute-done.12.refs_3_) | copy-start | bytes 589828
  92.9 11.4 %collective-permute-start.16 = (bf16[16,6144]{1,0:T(8,128)(2,1)S(1)}, bf16[16,6144]{1,0:T(8,128)(2,1)S(1)}, u32[]{:S(2)}, u32[]{:S(2)}) collective-permute-start(bf16[16,6144]{1,0:T(8,128)(2,1)S(1)} %collective-permute-done.12.refs_3_), channel_id=1, source_target_pairs={{0,1},{1,0},{2,3},{3,2},{4,5},{5,4},{6,7},{7,6},{8,9},{9,8},{10,11... | collective-permute-start | bytes 589832 | tf_op jit(solution)/shard_map/ppermute | solution.py:308
  103.7 1.7 %copy-start.6 = (bf16[16,6144]{1,0:T(8,128)(2,1)}, bf16[16,6144]{1,0:T(8,128)(2,1)S(1)}, u32[]{:S(2)}) copy-start(bf16[16,6144]{1,0:T(8,128)(2,1)S(1)} %collective-permute-done.11.refs_2_) | copy-start | bytes 589828
  103.7 1.4 collective-permute-start.15
  103.8 1.7 %copy-start.7 = (bf16[16,6144]{1,0:T(8,128)(2,1)}, bf16[16,6144]{1,0:T(8,128)(2,1)S(1)}, u32[]{:S(2)}) copy-start(bf16[16,6144]{1,0:T(8,128)(2,1)S(1)} %collective-permute-done.10.refs_1_) | copy-start | bytes 589828
  103.8 1.7 %collective-permute-start.14 = (bf16[16,6144]{1,0:T(8,128)(2,1)S(1)}, bf16[16,6144]{1,0:T(8,128)(2,1)S(1)}, u32[]{:S(2)}, u32[]{:S(2)}) collective-permute-start(bf16[16,6144]{1,0:T(8,128)(2,1)S(1)} %collective-permute-done.10.refs_1_), channel_id=1, source_target_pairs={{0,1},{1,0},{2,3},{3,2},{4,5},{5,4},{6,7},{7,6},{8,9},{9,8},{10,11... | collective-permute-start | bytes 589832 | tf_op jit(solution)/shard_map/ppermute | solution.py:308
  104.3 1.2 copy-start.8
  104.3 1.2 copy-start.9
  105.2 0.7 copy-start.10
  105.5 0.7 copy-start.11
  106.1 11.8 %copy-start.17 = (f32[8,128]{1,0:T(8,128)S(1)}, f32[8,128]{1,0:T(8,128)}, u32[]{:S(2)}) copy-start(f32[8,128]{1,0:T(8,128)} %get-tuple-element.18) | copy-start | bytes 12292
  106.1 13.3 %copy-start.16 = (bf16[128,6144]{1,0:T(8,128)(2,1)S(1)}, bf16[128,6144]{1,0:T(8,128)(2,1)}, u32[]{:S(2)}) copy-start(bf16[128,6144]{1,0:T(8,128)(2,1)} %get-tuple-element.24) | copy-start | bytes 4718596
  106.2 14.8 %copy-start.14 = (f32[16,128]{1,0:T(8,128)S(1)}, f32[16,128]{1,0:T(8,128)}, u32[]{:S(2)}) copy-start(f32[16,128]{1,0:T(8,128)} %get-tuple-element.20) | copy-start | bytes 24580
  117.7 3.3 %collective-permute-start.17 = (bf16[64,6144]{1,0:T(8,128)(2,1)}, bf16[64,6144]{1,0:T(8,128)(2,1)S(1)}, u32[]{:S(2)}, u32[]{:S(2)}) collective-permute-start(bf16[64,6144]{1,0:T(8,128)(2,1)} %get-tuple-element.23), channel_id=1, source_target_pairs={{0,1},{1,0},{2,3},{3,2},{4,5},{5,4},{6,7},{7,6},{8,9},{9,8},{10,11... | collective-permute-start | bytes 2359304 | tf_op jit(solution)/shard_map/ppermute | solution.py:308
  117.9 10.0 %collective-permute-start.9 = (f32[8,128]{1,0:T(8,128)S(1)}, f32[8,128]{1,0:T(8,128)S(1)}, u32[]{:S(2)}, u32[]{:S(2)}) collective-permute-start(f32[8,128]{1,0:T(8,128)S(1)} %copy-done.17), channel_id=1, source_target_pairs={{0,8},{8,16},{16,24},{24,0},{1,9},{9,17},{17,25},{25,1},{2,10},{10... | collective-permute-start | bytes 12296 | tf_op jit(solution)/shard_map/ppermute | solution.py:303
  119.4 38.2 %collective-permute-start.22 = (bf16[128,6144]{1,0:T(8,128)(2,1)S(1)}, bf16[128,6144]{1,0:T(8,128)(2,1)S(1)}, u32[]{:S(2)}, u32[]{:S(2)}) collective-permute-start(bf16[128,6144]{1,0:T(8,128)(2,1)S(1)} %copy-done.16), channel_id=1, source_target_pairs={{0,8},{8,16},{16,24},{24,0},{1,9},{9,17},{17,25},{25,1},{2,10},{10... | collective-permute-start | bytes 4718600 | tf_op jit(solution)/shard_map/ppermute | solution.py:303
  121.0 22.3 %copy-start.4 = (f32[16,6144]{1,0:T(8,128)S(1)}, f32[16,6144]{1,0:T(8,128)}, u32[]{:S(2)}) copy-start(f32[16,6144]{1,0:T(8,128)} %get-tuple-element.19) | copy-start | bytes 1179652
  122.5 6.6 %collective-permute-start.18 = (bf16[16,6144]{1,0:T(8,128)(2,1)S(1)}, bf16[16,6144]{1,0:T(8,128)(2,1)S(1)}, u32[]{:S(2)}, u32[]{:S(2)}) collective-permute-start(bf16[16,6144]{1,0:T(8,128)(2,1)S(1)} %get-tuple-element.30), channel_id=1, source_target_pairs={{0,6},{1,7},{2,0},{3,1},{4,2},{5,3},{6,4},{7,5},{8,14},{9,15},{10,... | collective-permute-start | bytes 589832 | tf_op jit(solution)/shard_map/ppermute | solution.py:403
  123.4 14.0 %collective-permute-start.20 = (bf16[16,6144]{1,0:T(8,128)(2,1)S(1)}, bf16[16,6144]{1,0:T(8,128)(2,1)S(1)}, u32[]{:S(2)}, u32[]{:S(2)}) collective-permute-start(bf16[16,6144]{1,0:T(8,128)(2,1)S(1)} %get-tuple-element.31), channel_id=1, source_target_pairs={{0,2},{1,3},{2,4},{3,5},{4,6},{5,7},{6,0},{7,1},{8,10},{9,11},{10,... | collective-permute-start | bytes 589832 | tf_op jit(solution)/shard_map/ppermute | solution.py:403
  124.5 18.8 %collective-permute-start.19 = (bf16[16,6144]{1,0:T(8,128)(2,1)S(1)}, bf16[16,6144]{1,0:T(8,128)(2,1)S(1)}, u32[]{:S(2)}, u32[]{:S(2)}) collective-permute-start(bf16[16,6144]{1,0:T(8,128)(2,1)S(1)} %get-tuple-element.32), channel_id=1, source_target_pairs={{0,4},{1,5},{2,6},{3,7},{4,0},{5,1},{6,2},{7,3},{8,12},{9,13},{10,... | collective-permute-start | bytes 589832 | tf_op jit(solution)/shard_map/ppermute | solution.py:403
  143.5 17.3 %collective-permute-start.21 = (bf16[16,6144]{1,0:T(8,128)(2,1)S(1)}, bf16[16,6144]{1,0:T(8,128)(2,1)S(1)}, u32[]{:S(2)}, u32[]{:S(2)}) collective-permute-start(bf16[16,6144]{1,0:T(8,128)(2,1)S(1)} %add_convert_fusion.1), channel_id=1, source_target_pairs={{0,8},{8,16},{16,24},{24,0},{1,9},{9,17},{17,25},{25,1},{2,10},{10... | collective-permute-start | bytes 589832 | tf_op jit(solution)/shard_map/ppermute | solution.py:303

commit v2 on v1

v2 whole, which is shorter than its diff:
```python
import jax
import jax.numpy as jnp
from jax import lax
from jax.experimental import pallas as pl
from jax.experimental.pallas import tpu as pltpu
from jax.sharding import PartitionSpec as P

HEAD = 128
SHARDS = 8
CAP_SRC = 16
GROUP = 8
CHUNKS = 4
PARTS = 3

F32, BF16 = jnp.float32, jnp.bfloat16


def dot(a, b, dims=((1,), (0,))):
    return lax.dot_general(a, b, (dims, ((), ())), preferred_element_type=F32)


def split(a):
    hi = a.astype(BF16)
    return hi, (a - hi.astype(F32)).astype(BF16)


def cumul_rows(rate_ref):
    length = rate_ref.shape[1]
    upper = (
        lax.broadcasted_iota(jnp.int32, (length, length), 0)
        <= lax.broadcasted_iota(jnp.int32, (length, length), 1)
    ).astype(F32)
    return lax.dot_general(
        rate_ref[...], upper, (((1,), (0,)), ((), ())), precision=lax.Precision.HIGHEST,
        preferred_element_type=F32,
    )


def in_vmem(x):
    return pltpu.with_memory_space_constraint(x, pltpu.VMEM)


VMEM_SPEC = pl.BlockSpec(memory_space=pltpu.VMEM)
HBM_SPEC = pl.BlockSpec(memory_space=pltpu.HBM)
ANY_SPEC = pl.BlockSpec(memory_space=pl.ANY)
SMEM_SPEC = pl.BlockSpec(memory_space=pltpu.SMEM)


def state_kernel(
    half_ref, rate_ref, k_hbm, v_hbm, state_hbm, decay_ref, k_ref, v_ref, state_ref, cum_ref, sems
):
    groups = sems.shape[1]
    length = rate_ref.shape[1]
    span = GROUP * HEAD

    def fetch(kind, g):
        source, target = ((k_hbm, k_ref), (v_hbm, v_ref))[kind]
        column = pl.multiple_of((half_ref[0] * groups + g) * span, span)
        return pltpu.make_async_copy(
            source.at[:, pl.ds(column, span)], target.at[g], sems.at[kind, g]
        )

    def store(g):
        at = pl.ds(g * GROUP, GROUP)
        return pltpu.make_async_copy(state_ref.at[at], state_hbm.at[at], sems.at[2, g])

    for g in range(groups):
        for kind in range(2):
            fetch(kind, g).start()
    cum_ref[...] = cumul_rows(rate_ref)
    decay_ref[...] = jnp.broadcast_to(jnp.exp(cum_ref[:, length - 1 :]), decay_ref.shape)
    for g in range(groups):
        row = pl.multiple_of((half_ref[0] * groups + g) * GROUP, GROUP)
        cum = cum_ref[pl.ds(row, GROUP), :]
        tail = jnp.exp(cum[:, length - 1 :] - cum)
        for kind in range(2):
            fetch(kind, g).wait()
        for j in range(GROUP):
            cols = slice(j * HEAD, (j + 1) * HEAD)
            turned = k_ref[g, :, cols].astype(F32).T * tail[j : j + 1, :]
            hi, lo = split(turned)
            v = v_ref[g, :, cols]
            state_ref[g * GROUP + j] = dot(hi, v) + dot(lo, v)
        store(g).start()
    for g in range(groups):
        store(g).wait()


def half_state(half, rate, keys, values):
    length, width = keys.shape
    heads = width // HEAD
    groups = heads // 2 // GROUP
    return pl.pallas_call(
        state_kernel,
        in_specs=[SMEM_SPEC, VMEM_SPEC, HBM_SPEC, HBM_SPEC],
        out_specs=[HBM_SPEC, VMEM_SPEC],
        out_shape=[
            jax.ShapeDtypeStruct((heads // 2, HEAD, HEAD), F32),
            jax.ShapeDtypeStruct((heads, HEAD), F32),
        ],
        scratch_shapes=[
            pltpu.VMEM((groups, length, GROUP * HEAD), BF16),
            pltpu.VMEM((groups, length, GROUP * HEAD), BF16),
            pltpu.VMEM((heads // 2, HEAD, HEAD), F32),
            pltpu.VMEM((heads, length), F32),
            pltpu.SemaphoreType.DMA((3, groups)),
        ],
        name="half_state",
    )(half, rate, keys, values)


def intra_kernel(first, rate_ref, q_hbm, k_hbm, v_hbm, out_hbm, q_ref, k_ref, v_ref, out_ref, sems):
    groups = sems.shape[1]
    length = rate_ref.shape[1]
    span = GROUP * HEAD

    def fetch(kind, g):
        source, target = ((q_hbm, q_ref), (k_hbm, k_ref), (v_hbm, v_ref))[kind]
        return pltpu.make_async_copy(
            source.at[:, pl.ds((first + g) * span, span)], target.at[g], sems.at[kind, g]
        )

    def store(g):
        at = pl.ds(g * span, span)
        return pltpu.make_async_copy(out_ref.at[g], out_hbm.at[:, at], sems.at[3, g])

    for g in range(groups):
        for kind in range(3):
            fetch(kind, g).start()
    cumul = cumul_rows(rate_ref)
    lower = lax.broadcasted_iota(jnp.int32, (length, length), 0) >= lax.broadcasted_iota(
        jnp.int32, (length, length), 1
    )
    for g in range(groups):
        for kind in range(3):
            fetch(kind, g).wait()
        for j in range(GROUP):
            head = (first + g) * GROUP + j
            cols = slice(j * HEAD, (j + 1) * HEAD)
            across = jnp.broadcast_to(cumul[head : head + 1, :], (length, length))
            weights = jnp.exp(jnp.where(lower, across.T - across, -1e30))
            scores = dot(q_ref[g, :, cols], k_ref[g, :, cols], ((1,), (1,)))
            hi, lo = split(scores * weights)
            v = v_ref[g, :, cols]
            out_ref[g, :, cols] = dot(hi, v) + dot(lo, v)
        store(g).start()
    for g in range(groups):
        store(g).wait()


def intra_attention(part, parts, rate, queries, keys, values):
    length, width = keys.shape
    groups = width // HEAD // GROUP // parts
    piece = (groups, length, GROUP * HEAD)
    return pl.pallas_call(
        lambda *refs: intra_kernel(part * groups, *refs),
        in_specs=[VMEM_SPEC] + [HBM_SPEC] * 3,
        out_specs=HBM_SPEC,
        out_shape=jax.ShapeDtypeStruct((length, width // parts), F32),
        scratch_shapes=[pltpu.VMEM(piece, BF16)] * 3
        + [pltpu.VMEM(piece, F32), pltpu.SemaphoreType.DMA((4, groups))],
        name="intra_attention",
    )(rate, queries, keys, values)


def finish_kernel(parts, core_ref, rate_ref, q_hbm, *refs):
    intra_hbm = refs[:parts]
    (
        keep_hbm, got_hbm, resid_hbm, again_ref, mgain_ref, experts_ref, weight_ref,
        early_ref, outbox_ref, picked_ref, wcol_ref, place_ref,
        attn_ref, normed_ref, q_ref, intra_ref, state_ref, resid_ref, scale_ref, sems,
    ) = refs[parts:]
    length, width = resid_ref.shape
    heads = width // HEAD
    groups = heads // GROUP
    span = GROUP * HEAD

    def copies(g):
        at = pl.ds(g * span, span)
        part, place = divmod(g * parts, groups)
        place = place // parts
        return [
            pltpu.make_async_copy(q_hbm.at[:, at], q_ref.at[g], sems.at[0, g]),
            pltpu.make_async_copy(
                intra_hbm[part].at[:, pl.ds(place * span, span)], intra_ref.at[g], sems.at[1, g]
            ),
        ]

    half = heads // 2
    for g in range(groups):
        for copy in copies(g):
            copy.start()

    def states(n):
        place = pl.multiple_of(lax.rem(core_ref[0] + n, 2) * half, half)
        return pltpu.make_async_copy(
            (keep_hbm, got_hbm)[n], state_ref.at[pl.ds(place, half)], sems.at[2, n]
        )

    states(0).start()
    states(1).start()
    rest = pltpu.make_async_copy(resid_hbm, resid_ref, sems.at[2, 2])
    rest.start()
    growth = jnp.exp(cumul_rows(rate_ref))
    for head in range(heads):
        across = jnp.broadcast_to(growth[head : head + 1, :], (length, length))
        scale_ref[:, head * HEAD : (head + 1) * HEAD] = across.T
    states(0).wait()
    states(1).wait()
    for g in range(groups):
        for copy in copies(g):
            copy.wait()
        for j in range(GROUP):
            head = g * GROUP + j
            mine = slice(j * HEAD, (j + 1) * HEAD)
            cols = slice(head * HEAD, (head + 1) * HEAD)
            hi, lo = split(state_ref[head])
            q = q_ref[g, :, mine]
            value = dot(q, hi) + dot(q, lo)
            attn_ref[:, cols] = intra_ref[g, :, mine] + scale_ref[:, cols] * value
    rest.wait()

    rows = 16

    def norm(r, carry):
        at = pl.ds(pl.multiple_of(r * rows, rows), rows)
        x = attn_ref[at, :]
        scale = lax.rsqrt(jnp.mean(x * x, axis=-1, keepdims=True) + 1e-06)
        hres = resid_ref[at, :].astype(F32) + x * scale * again_ref[...]
        attn_ref[at, :] = hres
        early_ref[at, :] = hres.astype(BF16)
        scale = lax.rsqrt(jnp.mean(hres * hres, axis=-1, keepdims=True) + 1e-06)
        normed_ref[at, :] = (hres * scale * mgain_ref[...]).astype(BF16)
        return carry

    lax.fori_loop(0, length // rows, norm, 0)
    slots = outbox_ref.shape[0]
    before = (
        lax.broadcasted_iota(jnp.int32, (length, length), 0)
        < lax.broadcasted_iota(jnp.int32, (length, length), 1)
    ).astype(BF16)
    named = experts_ref[...] == 0
    taken = jnp.max(named.astype(F32), axis=0, keepdims=True)
    slot = dot(jnp.broadcast_to(taken, (8, length)).astype(BF16), before)[0:1, :]
    slot = jnp.where(taken > 0, slot, -1.0)
    place_ref[...] = jnp.broadcast_to(slot, place_ref.shape)
    hot = lax.broadcasted_iota(jnp.int32, (slots, length), 0).astype(F32) == slot
    weight = jnp.sum(jnp.where(named, weight_ref[...], 0.0), axis=0, keepdims=True)
    weight = jnp.sum(jnp.where(hot, weight, 0.0), axis=1, keepdims=True)
    wcol_ref[...] = jnp.broadcast_to(weight, wcol_ref.shape)
    hot = hot.astype(BF16)
    outbox_ref[...] = dot(hot, normed_ref[...]).astype(BF16)
    for c in range(width // 512):
        cols = slice(c * 512, (c + 1) * 512)
        x = attn_ref[:, cols]
        hi = x.astype(BF16)
        mid, low = split(x - hi.astype(F32))
        picked_ref[:, cols] = dot(hot, hi) + dot(hot, mid) + dot(hot, low)


def finish(core, rate, queries, intra, keep, got, resid, attn_gain, moe_gain, experts, weight):
    length, width = queries.shape
    heads = width // HEAD
    groups = heads // GROUP
    parts = len(intra)
    args = [rate, queries, *intra, keep, got, resid, attn_gain, moe_gain, experts, weight]
    return pl.pallas_call(
        lambda *refs: finish_kernel(parts, *refs),
        in_specs=[SMEM_SPEC, VMEM_SPEC]
        + [HBM_SPEC] * (1 + parts)
        + [ANY_SPEC] * 2
        + [HBM_SPEC]
        + [VMEM_SPEC] * 4,
        out_specs=[VMEM_SPEC] * 5,
        out_shape=[
            pltpu.VMEM((length, width), BF16),
            pltpu.VMEM((CAP_SRC, width), BF16),
            pltpu.VMEM((CAP_SRC, width), F32),
            pltpu.VMEM((CAP_SRC, 128), F32),
            pltpu.VMEM((8, length), F32),
        ],
        scratch_shapes=[
            pltpu.VMEM((length, width), F32),
            pltpu.VMEM((length, width), BF16),
            pltpu.VMEM((groups, length, GROUP * HEAD), BF16),
            pltpu.VMEM((groups, length, GROUP * HEAD), F32),
            pltpu.VMEM((heads, HEAD, HEAD), F32),
            pltpu.VMEM((length, width), BF16),
            pltpu.VMEM((length, width), F32),
            pltpu.SemaphoreType.DMA((3, groups)),
        ],
        compiler_params=pltpu.CompilerParams(vmem_limit_bytes=32 << 20),
        name="finish",
    )(core, *args)


def expert_kernel(count, *refs):
    row_refs = refs[:count]
    (
        up_hbm, down_hbm, mine_ref, other_ref,
        up_ref, down_ref, rows_ref, hidden_ref, sems,
    ) = refs[count:]
    parts = sems.shape[1]
    depth, length = up_ref.shape[0] // parts, down_ref.shape[1] // parts
    half = mine_ref.shape[0]

    def fetch(kind, i):
        if kind == 0:
            at = pl.ds(i * depth, depth)
            return pltpu.make_async_copy(up_hbm.at[at], up_ref.at[at], sems.at[0, i])
        at = pl.ds(i * length, length)
        return pltpu.make_async_copy(down_hbm.at[:, at], down_ref.at[:, at], sems.at[1, i])

    for kind in range(2):
        for i in range(parts):
            fetch(kind, i).start()
    each = row_refs[0].shape[0]
    for n, ref in enumerate(row_refs):
        rows_ref[n * each : (n + 1) * each, :] = ref[...]
    acc = None
    for i in range(parts):
        fetch(0, i).wait()
        at = slice(i * depth, (i + 1) * depth)
        part = dot(rows_ref[:, at], up_ref[at, :])
        acc = part if acc is None else acc + part
    hidden_ref[...] = jax.nn.gelu(acc, approximate=True).astype(BF16)
    for i in range(parts):
        fetch(1, i).wait()
        at = slice(i * length, (i + 1) * length)
        part = dot(hidden_ref[...], down_ref[:, at]).astype(BF16)
        mine_ref[:, at] = part[:half]
        other_ref[:, at] = part[half:]


def expert_rows(rows, up, down):
    width, units = up.shape
    parts = 6
    total = sum(r.shape[0] for r in rows)
    return pl.pallas_call(
        lambda *refs: expert_kernel(len(rows), *refs),
        in_specs=[VMEM_SPEC] * len(rows) + [HBM_SPEC] * 2,
        out_specs=[VMEM_SPEC] * 2,
        out_shape=[pltpu.VMEM((total // 2, width), BF16)] * 2,
        scratch_shapes=[
            pltpu.VMEM((width, units), BF16),
            pltpu.VMEM((units, width), BF16),
            pltpu.VMEM((total, width), BF16),
            pltpu.VMEM((total, units), BF16),
            pltpu.SemaphoreType.DMA((2, parts)),
        ],
        compiler_params=pltpu.CompilerParams(vmem_limit_bytes=32 << 20),
        name="expert_rows",
    )(*[in_vmem(r) for r in rows], up, down)


def expert_kernel(count, *refs):
    row_refs = refs[:count]
    up_ref, down_ref, mine_ref, other_ref, rows_ref, hidden_ref = refs[count:]
    half = mine_ref.shape[0]
    each = row_refs[0].shape[0]
    for n, ref in enumerate(row_refs):
        rows_ref[n * each : (n + 1) * each, :] = ref[...]
    hidden = dot(rows_ref[...], up_ref[...])
    hidden_ref[...] = jax.nn.gelu(hidden, approximate=True).astype(BF16)
    parts = 4
    length = down_ref.shape[1] // parts
    for i in range(parts):
        at = slice(i * length, (i + 1) * length)
        part = dot(hidden_ref[...], down_ref[:, at]).astype(BF16)
        mine_ref[:, at] = part[:half]
        other_ref[:, at] = part[half:]


def expert_rows(rows, up, down):
    width, units = up.shape
    total = sum(r.shape[0] for r in rows)
    return pl.pallas_call(
        lambda *refs: expert_kernel(len(rows), *refs),
        in_specs=[VMEM_SPEC] * (len(rows) + 2),
        out_specs=[VMEM_SPEC] * 2,
        out_shape=[pltpu.VMEM((total // 2, width), BF16)] * 2,
        scratch_shapes=[pltpu.VMEM((total, width), BF16), pltpu.VMEM((total, units), BF16)],
        compiler_params=pltpu.CompilerParams(vmem_limit_bytes=12 << 20),
        name="expert_rows",
    )(*[in_vmem(r) for r in rows], in_vmem(up), in_vmem(down))


def passed_along(value, axis, steps):
    count = lax.axis_size(axis)
    pairs = [(source, (source + steps) % count) for source in range(count)]
    return lax.ppermute(value, axis, pairs)


def swapped(value):
    count = lax.axis_size("ctx")
    return lax.ppermute(value, "ctx", [(i, i ^ 1) for i in range(count)])


def chain_prefix(total, decay, chip, chips, scale):
    heads = total.shape[0]
    per = heads // CHUNKS
    received = []
    for step in range(CHUNKS + chips - 2):
        place = jnp.clip(step - chip, 0, CHUNKS - 1) * per
        gone = lax.dynamic_slice_in_dim(total, place, per, 0) * scale
        if step >= 1:
            before = received[step - 1].astype(F32)
            gone = lax.dynamic_slice_in_dim(decay, place, per, 0)[:, None, :] * before + gone
        pairs = [
            (2 * z + core, 2 * z + 2 + core)
            for z in range(chips - 1)
            if 0 <= step - z < CHUNKS
            for core in range(2)
        ]
        received.append(lax.ppermute(gone.astype(jnp.float16), "ctx", pairs))
    row = jnp.concatenate(received, axis=0)
    first = jnp.maximum(chip - 1, 0) * per
    mine = lax.dynamic_slice_in_dim(row, first, heads, 0).astype(F32) * (1.0 / scale)
    return jnp.where(chip > 0, mine, 0.0)


def local(
    resid,
    queries,
    keys,
    values,
    log_decay,
    attn_gain,
    moe_gain,
    experts,
    combine_weight,
    w_up,
    w_down,
):
    return layer(
        resid[0], queries[0], keys[0], values[0], log_decay[0], attn_gain, moe_gain,
        experts[0], combine_weight[0], w_up[0], w_down[0],
    )


def layer(resid, queries, keys, values, rate, attn_gain, moe_gain, experts, weight, up, down):
    length, width = queries.shape
    count = lax.axis_size("ctx")
    me = lax.axis_index("ctx")
    chips, chip, core = count // 2, me // 2, me % 2
    half = width // HEAD // 2
    first = core == 0
    core1 = core.astype(jnp.int32)[None]
    turned = rate.T

    other, decay = half_state(1 - core1, turned, keys, values)
    partner = swapped(other)
    decay_partner = swapped(decay)
    mine, _ = half_state(core1, turned, keys, values)
    decay = lax.dynamic_slice_in_dim(decay, core * half, half, 0)
    decay_partner = lax.dynamic_slice_in_dim(decay_partner, core * half, half, 0)
    state0, state1 = jnp.where(first, mine, partner), jnp.where(first, partner, mine)
    decay0, decay1 = (
        jnp.where(first, decay, decay_partner),
        jnp.where(first, decay_partner, decay),
    )
    scale = 1.0
    while 36.0 * count * length * scale > 65000.0:
        scale = scale / 2
    total = decay1[:, None, :] * state0 + state1
    prefix = chain_prefix(total, decay0 * decay1, chip, chips, scale)
    after0 = decay0[:, None, :] * prefix + state0
    keep = jnp.where(first, prefix, after0)
    got = swapped(jnp.where(first, after0, prefix))
    intra = []
    for part in range(PARTS):
        intra.append(intra_attention(part, PARTS, turned, queries, keys, values))
    flying = count // SHARDS
    if flying > 1:
        prefix = jnp.where(first, jnp.concatenate([keep, got]), jnp.concatenate([got, keep]))
        return many_experts(
            flying, rate, queries, jnp.concatenate(intra, axis=1), prefix, resid, attn_gain, moe_gain, experts, weight, up, down
        )
    early, outbox, picked, wcol, place = finish(
        core1, turned, queries, intra, keep, got, resid, attn_gain, moe_gain, experts.T, weight.T
    )
    early = passed_along(early, "section", 1)
    place = passed_along(place, "section", 1)
    own = [outbox] + [
        lax.ppermute(outbox, "ctx", [(i, (i + 2 * d) % count) for i in range(count)])
        for d in range(1, chips)
    ]
    others = [swapped(r) for r in own]
    mine, other = expert_rows(own + others, up, down)
    pair = (mine.astype(F32) + swapped(other).astype(F32)).astype(BF16)
    pair = pair.reshape(chips, CAP_SRC, width)
    summed = pair[0].astype(F32)
    for d in range(1, chips):
        back = lax.ppermute(pair[d], "ctx", [(i, (i - 2 * d) % count) for i in range(count)])
        summed = summed + back.astype(F32)
    late = (picked + wcol[:, :1] * summed).astype(BF16)
    late = passed_along(late, "section", 1)
    found = (place[:1] == jnp.arange(CAP_SRC, dtype=F32)[:, None]).astype(BF16)
    rows = lax.dot_general(
        found, late, (((0,), (0,)), ((), ())), preferred_element_type=F32
    ).astype(BF16)
    return jnp.where(place[0][:, None] >= 0, rows, early)[None]


def rms_scale(values_in, gain):
    return (
        values_in
        * lax.rsqrt(jnp.mean(values_in * values_in, axis=-1, keepdims=True) + 1e-06)
        * gain
    )


def many_experts(
    flying, rate, queries, intra, prefix, resid, attn_gain, moe_gain, experts, weight, up, down
):
    length, width = queries.shape
    heads = width // HEAD
    count = lax.axis_size("ctx")
    inter = jnp.exp(jnp.cumsum(rate, axis=0))[:, :, None] * jnp.einsum(
        "thd,hde->the",
        queries.astype(F32).reshape(length, heads, HEAD),
        prefix,
        precision=lax.Precision.HIGHEST,
    )
    hres = resid.astype(F32) + rms_scale(intra + inter.reshape(length, width), attn_gain)
    normed = rms_scale(hres, moe_gain).astype(BF16)
    slots = flying * CAP_SRC
    chosen = experts.reshape(-1)
    onehot = (chosen[:, None] == jnp.arange(flying)[None, :]).astype(jnp.int32)
    slot = jnp.sum((jnp.cumsum(onehot, axis=0) - onehot) * onehot, axis=1)
    target = jnp.where(chosen < flying, chosen * CAP_SRC + slot, -1)
    hot = (target[None, :] == jnp.arange(slots)[:, None]).reshape(slots, length, 2)
    outbox = dot(hot.any(axis=2).astype(BF16), normed).astype(BF16)
    outbox = outbox.reshape(1, flying, CAP_SRC, width)
    mine = lax.dynamic_index_in_dim(
        lax.all_gather(outbox, "ctx", axis=0, tiled=True), lax.axis_index("ctx") // SHARDS, 1, False
    )
    hidden = jax.nn.gelu(dot(mine.reshape(count * CAP_SRC, width), up), approximate=True)
    part = dot(hidden.astype(BF16), down).astype(BF16).reshape(count, CAP_SRC, width)
    returned = lax.all_to_all(part, "ctx", split_axis=0, concat_axis=0, tiled=True)
    summed = returned.reshape(flying, SHARDS, CAP_SRC, width).astype(F32).sum(axis=1)
    mixed = lax.dot_general(
        jnp.where(hot, weight[None], 0.0).sum(axis=2),
        summed.reshape(slots, width),
        (((0,), (0,)), ((), ())),
        precision=lax.Precision.HIGHEST,
    )
    return passed_along((hres + mixed).astype(BF16)[None], "section", 1)


def solution(mesh):
    return jax.shard_map(
        local,
        mesh=mesh,
        in_specs=(
            P("section", "ctx", None),
            P("section", "ctx", None),
            P("section", "ctx", None),
            P("section", "ctx", None),
            P("section", "ctx", None),
            P("section", None),
            P("section", None),
            P("section", "ctx", None),
            P("section", "ctx", None),
            P("section", None, "ctx"),
            P("section", "ctx", None),
        ),
        out_specs=P("section", "ctx", None),
        check_vma=False,
    )
```

time: 163 us -> 163 us (level)
  Pallas kernels: 39.2 us -> 31.8 us
  local copies, waits for them, and re-layouts: 6.07 us -> 12.1 us
  other arithmetic: 7.51 us -> 4.64 us
  waiting for transfers between devices: 61.3 us -> 63.2 us
    ppermute x3, waiting for transfers between devices: 15.8 us -> 34.9 us  [passed_along(): return lax.ppermute(value, axis, pairs)]
    ppermute x3, waiting for transfers between devices: 15.5 us -> 0.01 us  [layer(): lax.ppermute(pair[d], 'ctx', [(i, (i - 2 * d) % count) for i in range(cou...]
    pallas_call x5 -> x7, Pallas kernels: 39.2 us -> 31.8 us  [the longest x3 12.2 us: intra_attention(): pl.pallas_call(lambda *refs: intra_kernel(part * groups, *refs), in_specs...]
    unnamed x42 -> x37, local copies, waits for them, and re-layouts: 5.25 us -> 11.9 us
    ppermute x3, waiting for transfers between devices: 15.9 us -> 13.1 us  [layer(): lax.ppermute(outbox, 'ctx', [(i, (i + 2 * d) % count) for i in range(coun...]
    convert_element_type x6, other arithmetic: 2.02 us -> 0.39 us  [chain_prefix(): received.append(lax.ppermute(gone.astype(jnp.float16), 'ctx', pairs))]
  transfers between devices with their start and end apart: 23 -> 23, of which waited for: 13 -> 10; matrix products, arithmetic and copies ran while one was open for 3% -> 1% of each run, Pallas kernels for 7% -> 10%
where the time goes in v2:
time: 163 us; the launch traced here: 161 us
  waiting for transfers between devices  63.2 us (39%)
  starting transfers between devices  46.9 us (29%)
  Pallas kernels  31.8 us (20%)
  local copies, waits for them, and re-layouts  12.1 us (7%)
  other arithmetic  4.64 us (3%)
  matrix products  1.77 us (1%)
    ppermute x3, waiting for transfers between devices, passed_along(): return lax.ppermute(value, axis, pairs)  34.9 us
    ppermute x6, starting transfers between devices, chain_prefix(): received.append(lax.ppermute(gone.astype(jnp.float16), 'ctx', pairs))  19.6 us
    ppermute x3, starting transfers between devices, layer(): lax.ppermute(outbox, 'ctx', [(i, (i + 2 * d) % count) for i in range(coun...  16.4 us
    ppermute x6, waiting for transfers between devices, chain_prefix(): received.append(lax.ppermute(gone.astype(jnp.float16), 'ctx', pairs))  14.1 us
    ppermute x3, waiting for transfers between devices, layer(): lax.ppermute(outbox, 'ctx', [(i, (i + 2 * d) % count) for i in range(coun...  13.1 us
    pallas_call x3, Pallas kernels, intra_attention(): pl.pallas_call(lambda *refs: intra_kernel(part * groups, *refs), in_specs...  12.2 us
    unnamed x37, local copies, waits for them, and re-layouts  11.9 us
    pallas_call x2, Pallas kernels, half_state(): pl.pallas_call(state_kernel, in_specs=[SMEM_SPEC, VMEM_SPEC, HBM_SPEC, HB...  8.81 us
  transfers between devices with their start and end apart: 23, of which 10 were waited for; matrix products, arithmetic and copies ran while one was open for 1% of the time, Pallas kernels for 10%

profile of v2, /device:TPU:0, one launch (start us, length us, event | category | flops | bytes accessed | tf_op | source)
XLA Modules:
  0.0 161.0 jit_solution(4174061260011711867)
XLA Ops:
  0.0 4.4 %half_state.2 = (f32[24,128,128]{2,1,0:T(8,128)}, f32[48,128]{1,0:T(8,128)}) custom-call(s32[1]{0:T(128)S(6)} %sub.29.half_ref, f32[48,128]{1,0:T(8,128)} %bitcast.30, bf16[128,6144]{1,0:T(8,128)(2,1)} %bitcast.38, bf16[128,6144]{1,0:T(8,128)(2,1)} %bitcast.43), custom_call_target="tpu_custom_call" | custom-call | tf_op jit(solution)/shard_map/half_state/pallas_call | solution.py:93
  4.4 0.6 collective-permute-start.1
  5.0 0.1 collective-permute-start
  5.0 4.4 %half_state.3 = (f32[24,128,128]{2,1,0:T(8,128)}, f32[48,128]{1,0:T(8,128)}) custom-call(s32[1]{0:T(128)} %bitcast.half_ref.refs_0_, f32[48,128]{1,0:T(8,128)} %bitcast.31, bf16[128,6144]{1,0:T(8,128)(2,1)} %bitcast.39, bf16[128,6144]{1,0:T(8,128)(2,1)} %bitcast.44), custom_call_target="tpu_custom_call" | custom-call | tf_op jit(solution)/shard_map/half_state/pallas_call | solution.py:93
  9.6 2.3 %select_add_fusion = f32[24,128,128]{2,1,0:T(8,128)S(1)} fusion(f32[24,128,128]{2,1,0:T(8,128)S(1)} %collective-permute-done.1, f32[24,128,128]{2,1,0:T(8,128)} %get-tuple-element.16, f32[24,128]{1,0:T(8,128)S(1)} %get-tuple-element.26, pred[]{:T(512)S(6)} %eq.18), kind=kLoop, calls=%fused_computation.7 | loop fusion | flops 1572864 | bytes 4730881 | tf_op jit(solution)/shard_map/add | solution.py:465
  11.9 4.9 %collective-permute-start.2 = (f16[6,128,128]{2,1,0:T(8,128)(2,1)S(1)}, f16[6,128,128]{2,1,0:T(8,128)(2,1)S(1)}, u32[]{:S(2)}, u32[]{:S(2)}) collective-permute-start(f16[6,128,128]{2,1,0:T(8,128)(2,1)S(1)} %dynamic-slice_convert_fusion), channel_id=1, source_target_pairs={{0,2},{1,3},{8,10},{9,11},{16,18},{17,19},{24,26},{25,27}} | collective-permute-start | bytes 589832 | tf_op jit(solution)/shard_map/ppermute | solution.py:415
  16.9 4.3 %collective-permute-done.2 = f16[6,128,128]{2,1,0:T(8,128)(2,1)S(1)} collective-permute-done((f16[6,128,128]{2,1,0:T(8,128)(2,1)S(1)}, f16[6,128,128]{2,1,0:T(8,128)(2,1)S(1)}, u32[]{:S(2)}, u32[]{:S(2)}) %collective-permute-start.2) | collective-permute-done | bytes 196640 | tf_op jit(solution)/shard_map/ppermute | solution.py:415
  21.2 4.4 %collective-permute-start.3 = (f16[6,128,128]{2,1,0:T(8,128)(2,1)S(1)}, f16[6,128,128]{2,1,0:T(8,128)(2,1)S(1)}, u32[]{:S(2)}, u32[]{:S(2)}) collective-permute-start(f16[6,128,128]{2,1,0:T(8,128)(2,1)S(1)} %add_convert_fusion.6), channel_id=1, source_target_pairs={{0,2},{1,3},{2,4},{3,5},{8,10},{9,11},{10,12},{11,13},{16,18},{17,... | collective-permute-start | bytes 589832 | tf_op jit(solution)/shard_map/ppermute | solution.py:415
  25.7 3.5 %collective-permute-done.3 = f16[6,128,128]{2,1,0:T(8,128)(2,1)S(1)} collective-permute-done((f16[6,128,128]{2,1,0:T(8,128)(2,1)S(1)}, f16[6,128,128]{2,1,0:T(8,128)(2,1)S(1)}, u32[]{:S(2)}, u32[]{:S(2)}) %collective-permute-start.3) | collective-permute-done | bytes 196640 | tf_op jit(solution)/shard_map/ppermute | solution.py:415
  29.2 4.4 %collective-permute-start.4 = (f16[6,128,128]{2,1,0:T(8,128)(2,1)S(1)}, f16[6,128,128]{2,1,0:T(8,128)(2,1)S(1)}, u32[]{:S(2)}, u32[]{:S(2)}) collective-permute-start(f16[6,128,128]{2,1,0:T(8,128)(2,1)S(1)} %add_convert_fusion.5), channel_id=1, source_target_pairs={{0,2},{1,3},{2,4},{3,5},{4,6},{5,7},{8,10},{9,11},{10,12},{11,13},... | collective-permute-start | bytes 589832 | tf_op jit(solution)/shard_map/ppermute | solution.py:415
  33.6 3.2 %collective-permute-done.4 = f16[6,128,128]{2,1,0:T(8,128)(2,1)S(1)} collective-permute-done((f16[6,128,128]{2,1,0:T(8,128)(2,1)S(1)}, f16[6,128,128]{2,1,0:T(8,128)(2,1)S(1)}, u32[]{:S(2)}, u32[]{:S(2)}) %collective-permute-start.4) | collective-permute-done | bytes 196640 | tf_op jit(solution)/shard_map/ppermute | solution.py:415
  36.9 4.4 %collective-permute-start.5 = (f16[6,128,128]{2,1,0:T(8,128)(2,1)S(1)}, f16[6,128,128]{2,1,0:T(8,128)(2,1)S(1)}, u32[]{:S(2)}, u32[]{:S(2)}) collective-permute-start(f16[6,128,128]{2,1,0:T(8,128)(2,1)S(1)} %add_convert_fusion.4), channel_id=1, source_target_pairs={{0,2},{1,3},{2,4},{3,5},{4,6},{5,7},{8,10},{9,11},{10,12},{11,13},... | collective-permute-start | bytes 589832 | tf_op jit(solution)/shard_map/ppermute | solution.py:415
  41.3 3.1 %collective-permute-done.5 = f16[6,128,128]{2,1,0:T(8,128)(2,1)S(1)} collective-permute-done((f16[6,128,128]{2,1,0:T(8,128)(2,1)S(1)}, f16[6,128,128]{2,1,0:T(8,128)(2,1)S(1)}, u32[]{:S(2)}, u32[]{:S(2)}) %collective-permute-start.5) | collective-permute-done | bytes 196640 | tf_op jit(solution)/shard_map/ppermute | solution.py:415
  44.5 0.8 collective-permute-start.6
  45.5 0.1 add_convert_fusion.2
  45.6 0.7 collective-permute-start.7
  46.5 1.6 %fusion = (f32[24,128,128]{2,1,0:T(8,128)}, f32[24,128,128]{2,1,0:T(8,128)S(1)}) fusion(f32[24,128]{1,0:T(8,128)S(1)} %get-tuple-element.27, pred[]{:T(512)S(6)} %gt.3, pred[]{:T(512)S(6)} %eq.18, f32[24,128,128]{2,1,0:T(8,128)S(1)} %copy-done.14, f32[24,128,128]{2,1,0:T(8,128)S(1)} %copy-done.13, ...), kind=kLoop, calls=%fused_computation.4 | loop fusion | flops 2752512 | bytes 7090182 | tf_op jit(solution)/shard_map/jit(_where)/select_n | solution.py:469
  48.1 4.1 %intra_attention.3.refs_3_ = f32[128,2048]{1,0:T(8,128)} custom-call(f32[48,128]{1,0:T(8,128)} %bitcast.32, bf16[128,6144]{1,0:T(8,128)(2,1)} %bitcast.23, bf16[128,6144]{1,0:T(8,128)(2,1)} %bitcast.40, bf16[128,6144]{1,0:T(8,128)(2,1)} %bitcast.45), custom_call_target="tpu_custom_call" | custom-call | tf_op jit(solution)/shard_map/intra_attention/pallas_call | solution.py:155
  52.2 4.0 %intra_attention.4.refs_4_ = f32[128,2048]{1,0:T(8,128)} custom-call(f32[48,128]{1,0:T(8,128)} %bitcast.33, bf16[128,6144]{1,0:T(8,128)(2,1)} %bitcast.24, bf16[128,6144]{1,0:T(8,128)(2,1)} %bitcast.41, bf16[128,6144]{1,0:T(8,128)(2,1)} %bitcast.46), custom_call_target="tpu_custom_call" | custom-call | tf_op jit(solution)/shard_map/intra_attention/pallas_call | solution.py:155
  56.3 4.1 %intra_attention.5.refs_5_ = f32[128,2048]{1,0:T(8,128)} custom-call(f32[48,128]{1,0:T(8,128)} %bitcast.34, bf16[128,6144]{1,0:T(8,128)(2,1)} %bitcast.25, bf16[128,6144]{1,0:T(8,128)(2,1)} %bitcast.42, bf16[128,6144]{1,0:T(8,128)(2,1)} %bitcast.47), custom_call_target="tpu_custom_call" | custom-call | tf_op jit(solution)/shard_map/intra_attention/pallas_call | solution.py:155
  60.5 1.2 copy-done.3
  61.7 1.2 copy-done.4
  63.0 1.2 copy-done.5
  64.2 1.4 copy-done.6
  65.6 8.0 %finish.1 = (bf16[128,6144]{1,0:T(8,128)(2,1)S(1)}, bf16[16,6144]{1,0:T(8,128)(2,1)S(1)}, f32[16,6144]{1,0:T(8,128)S(1)}, f32[16,128]{1,0:T(8,128)S(1)}, f32[8,128]{1,0:T(8,128)S(1)}) custom-call(s32[1]{0:T(128)} %bitcast.half_ref.refs_0_, f32[48,128]{1,0:T(8,128)S(1)} %bitcast.35, bf16[128,6144]{1,0:T(8,128)(2,1)S(1)} %bitcast.26, ...), custom_call_target="tpu_custom_call" | custom-call | tf_op jit(solution)/shard_map/finish/pallas_call | solution.py:267
  73.6 7.2 %collective-permute-start.10 = (bf16[16,6144]{1,0:T(8,128)(2,1)S(1)}, bf16[16,6144]{1,0:T(8,128)(2,1)S(1)}, u32[]{:S(2)}, u32[]{:S(2)}) collective-permute-start(bf16[16,6144]{1,0:T(8,128)(2,1)S(1)} %get-tuple-element.21.refs_0_), channel_id=1, source_target_pairs={{0,2},{1,3},{2,4},{3,5},{4,6},{5,7},{6,0},{7,1},{8,10},{9,11},{10,... | collective-permute-start | bytes 589832 | tf_op jit(solution)/shard_map/ppermute | solution.py:485
  80.8 8.7 %collective-permute-start.11 = (bf16[16,6144]{1,0:T(8,128)(2,1)S(1)}, bf16[16,6144]{1,0:T(8,128)(2,1)S(1)}, u32[]{:S(2)}, u32[]{:S(2)}) collective-permute-start(bf16[16,6144]{1,0:T(8,128)(2,1)S(1)} %get-tuple-element.21.refs_0_), channel_id=1, source_target_pairs={{0,4},{1,5},{2,6},{3,7},{4,0},{5,1},{6,2},{7,3},{8,12},{9,13},{10,... | collective-permute-start | bytes 589832 | tf_op jit(solution)/shard_map/ppermute | solution.py:485
  89.6 0.4 collective-permute-start.12
  90.0 4.9 %collective-permute-done.10.refs_1_ = bf16[16,6144]{1,0:T(8,128)(2,1)S(1)} collective-permute-done((bf16[16,6144]{1,0:T(8,128)(2,1)S(1)}, bf16[16,6144]{1,0:T(8,128)(2,1)S(1)}, u32[]{:S(2)}, u32[]{:S(2)}) %collective-permute-start.10) | collective-permute-done | bytes 196640 | tf_op jit(solution)/shard_map/ppermute | solution.py:485
  94.9 8.2 %collective-permute-done.11.refs_2_ = bf16[16,6144]{1,0:T(8,128)(2,1)S(1)} collective-permute-done((bf16[16,6144]{1,0:T(8,128)(2,1)S(1)}, bf16[16,6144]{1,0:T(8,128)(2,1)S(1)}, u32[]{:S(2)}, u32[]{:S(2)}) %collective-permute-start.11) | collective-permute-done | bytes 196640 | tf_op jit(solution)/shard_map/ppermute | solution.py:485
  103.1 0.5 collective-permute-start.16
  103.6 0.9 collective-permute-done.15.refs_6_
  104.5 0.3 collective-permute-done.16.refs_7_
  104.8 3.2 %copy-done.1 = bf16[1,6144,640]{2,1,0:T(8,128)(2,1)S(1)} copy-done((bf16[1,6144,640]{2,1,0:T(8,128)(2,1)S(1)}, bf16[1,6144,640]{2,1,0:T(8,128)(2,1)}, u32[]{:S(2)}) %copy-start.1) | copy-done | bytes 7864344
  108.1 3.2 %copy-done.2 = bf16[1,640,6144]{2,1,0:T(8,128)(2,1)S(1)} copy-done((bf16[1,640,6144]{2,1,0:T(8,128)(2,1)S(1)}, bf16[1,640,6144]{2,1,0:T(8,128)(2,1)}, u32[]{:S(2)}) %copy-start.2) | copy-done | bytes 7864344
  111.3 2.7 %expert_rows.1 = (bf16[64,6144]{1,0:T(8,128)(2,1)S(1)}, bf16[64,6144]{1,0:T(8,128)(2,1)S(1)}) custom-call(bf16[16,6144]{1,0:T(8,128)(2,1)S(1)} %get-tuple-element.21.refs_0_, bf16[16,6144]{1,0:T(8,128)(2,1)S(1)} %collective-permute-done.10.refs_1_, bf16[16,6144]{1,0:T(8,128)(2,1)S(1)} %collective-permute-done.11.refs_2_, ...), custom_call_target="tpu_custom_call" | custom-call | tf_op jit(solution)/shard_map/expert_rows/pallas_call | solution.py:377
  114.0 0.3 collective-permute-start.17
  114.3 1.5 collective-permute-start.22
  115.8 1.5 collective-permute-start.9
  117.3 0.1 slice_reduce_fusion
  117.4 0.2 add_convert_fusion
  117.7 4.9 %collective-permute-start.18 = (bf16[16,6144]{1,0:T(8,128)(2,1)S(1)}, bf16[16,6144]{1,0:T(8,128)(2,1)S(1)}, u32[]{:S(2)}, u32[]{:S(2)}) collective-permute-start(bf16[16,6144]{1,0:T(8,128)(2,1)S(1)} %get-tuple-element.30), channel_id=1, source_target_pairs={{0,6},{1,7},{2,0},{3,1},{4,2},{5,3},{6,4},{7,5},{8,14},{9,15},{10,... | collective-permute-start | bytes 589832 | tf_op jit(solution)/shard_map/ppermute | solution.py:494
  122.6 1.0 collective-permute-start.19
  123.5 28.3 %collective-permute-done.9 = f32[8,128]{1,0:T(8,128)S(1)} collective-permute-done((f32[8,128]{1,0:T(8,128)S(1)}, f32[8,128]{1,0:T(8,128)S(1)}, u32[]{:S(2)}, u32[]{:S(2)}) %collective-permute-start.9) | collective-permute-done | bytes 4128 | tf_op jit(solution)/shard_map/ppermute | solution.py:391
  151.9 0.1 add_convert_fusion.1
  152.0 0.7 collective-permute-start.21
  152.7 6.5 %collective-permute-done.21 = bf16[16,6144]{1,0:T(8,128)(2,1)S(1)} collective-permute-done((bf16[16,6144]{1,0:T(8,128)(2,1)S(1)}, bf16[16,6144]{1,0:T(8,128)(2,1)S(1)}, u32[]{:S(2)}, u32[]{:S(2)}) %collective-permute-start.21) | collective-permute-done | bytes 196640 | tf_op jit(solution)/shard_map/ppermute | solution.py:391
  159.2 1.8 %select_bitcast_fusion = bf16[1,128,6144]{2,1,0:T(8,128)(2,1)} fusion(bf16[128,6144]{1,0:T(8,128)(2,1)S(1)} %collective-permute-done.22, pred[128]{0:T(512)(128)(4,1)S(1)} %broadcast_compare_fusion, bf16[16,6144]{1,0:T(8,128)(2,1)S(1)} %collective-permute-done.21, f32[128]{0:T(128)S(1)} %slice_bitcast_fusion), kind=kOutput, calls=%fused_computation.1 | convolution fusion | flops 26740736 | bytes 3342976 | tf_op jit(solution)/shard_map/dot_general | solution.py:499
  (60 shorter events, 0.9 us)
Async XLA Ops:
  4.4 5.2 %collective-permute-start.1 = (f32[24,128,128]{2,1,0:T(8,128)}, f32[24,128,128]{2,1,0:T(8,128)S(1)}, u32[]{:S(2)}, u32[]{:S(2)}) collective-permute-start(f32[24,128,128]{2,1,0:T(8,128)} %get-tuple-element.17), channel_id=1, source_target_pairs={{0,1},{1,0},{2,3},{3,2},{4,5},{5,4},{6,7},{7,6},{8,9},{9,8},{10,11... | collective-permute-start | bytes 4718600 | tf_op jit(solution)/shard_map/ppermute | solution.py:396
  5.0 4.5 %collective-permute-start = (f32[48,128]{1,0:T(8,128)}, f32[48,128]{1,0:T(8,128)S(1)}, u32[]{:S(2)}, u32[]{:S(2)}) collective-permute-start(f32[48,128]{1,0:T(8,128)} %get-tuple-element.15), channel_id=1, source_target_pairs={{0,1},{1,0},{2,3},{3,2},{4,5},{5,4},{6,7},{7,6},{8,9},{9,8},{10,11... | collective-permute-start | bytes 73736 | tf_op jit(solution)/shard_map/ppermute | solution.py:396
  5.0 4.5 %copy-start.15 = (f32[48,128]{1,0:T(8,128)S(1)}, f32[48,128]{1,0:T(8,128)}, u32[]{:S(2)}) copy-start(f32[48,128]{1,0:T(8,128)} %get-tuple-element.15) | copy-start | bytes 73732
  9.6 2.3 %copy-start.12 = (f32[24,128,128]{2,1,0:T(8,128)}, f32[24,128,128]{2,1,0:T(8,128)S(1)}, u32[]{:S(2)}) copy-start(f32[24,128,128]{2,1,0:T(8,128)S(1)} %collective-permute-done.1) | copy-start | bytes 4718596
  11.9 9.3 %collective-permute-start.2 = (f16[6,128,128]{2,1,0:T(8,128)(2,1)S(1)}, f16[6,128,128]{2,1,0:T(8,128)(2,1)S(1)}, u32[]{:S(2)}, u32[]{:S(2)}) collective-permute-start(f16[6,128,128]{2,1,0:T(8,128)(2,1)S(1)} %dynamic-slice_convert_fusion), channel_id=1, source_target_pairs={{0,2},{1,3},{8,10},{9,11},{16,18},{17,19},{24,26},{25,27}} | collective-permute-start | bytes 589832 | tf_op jit(solution)/shard_map/ppermute | solution.py:415
  21.2 7.9 %collective-permute-start.3 = (f16[6,128,128]{2,1,0:T(8,128)(2,1)S(1)}, f16[6,128,128]{2,1,0:T(8,128)(2,1)S(1)}, u32[]{:S(2)}, u32[]{:S(2)}) collective-permute-start(f16[6,128,128]{2,1,0:T(8,128)(2,1)S(1)} %add_convert_fusion.6), channel_id=1, source_target_pairs={{0,2},{1,3},{2,4},{3,5},{8,10},{9,11},{10,12},{11,13},{16,18},{17,... | collective-permute-start | bytes 589832 | tf_op jit(solution)/shard_map/ppermute | solution.py:415
  29.2 7.6 %collective-permute-start.4 = (f16[6,128,128]{2,1,0:T(8,128)(2,1)S(1)}, f16[6,128,128]{2,1,0:T(8,128)(2,1)S(1)}, u32[]{:S(2)}, u32[]{:S(2)}) collective-permute-start(f16[6,128,128]{2,1,0:T(8,128)(2,1)S(1)} %add_convert_fusion.5), channel_id=1, source_target_pairs={{0,2},{1,3},{2,4},{3,5},{4,6},{5,7},{8,10},{9,11},{10,12},{11,13},... | collective-permute-start | bytes 589832 | tf_op jit(solution)/shard_map/ppermute | solution.py:415
  36.9 7.6 %collective-permute-start.5 = (f16[6,128,128]{2,1,0:T(8,128)(2,1)S(1)}, f16[6,128,128]{2,1,0:T(8,128)(2,1)S(1)}, u32[]{:S(2)}, u32[]{:S(2)}) collective-permute-start(f16[6,128,128]{2,1,0:T(8,128)(2,1)S(1)} %add_convert_fusion.4), channel_id=1, source_target_pairs={{0,2},{1,3},{2,4},{3,5},{4,6},{5,7},{8,10},{9,11},{10,12},{11,13},... | collective-permute-start | bytes 589832 | tf_op jit(solution)/shard_map/ppermute | solution.py:415
  44.4 2.0 %copy-start.14 = (f32[24,128,128]{2,1,0:T(8,128)S(1)}, f32[24,128,128]{2,1,0:T(8,128)}, u32[]{:S(2)}) copy-start(f32[24,128,128]{2,1,0:T(8,128)} %get-tuple-element.16) | copy-start | bytes 4718596
  44.5 2.0 %copy-start.13 = (f32[24,128,128]{2,1,0:T(8,128)S(1)}, f32[24,128,128]{2,1,0:T(8,128)}, u32[]{:S(2)}) copy-start(f32[24,128,128]{2,1,0:T(8,128)} %copy-done.12) | copy-start | bytes 4718596
  44.5 1.0 collective-permute-start.6
  45.6 0.8 collective-permute-start.7
  48.1 12.3 %collective-permute-start.8 = (f32[24,128,128]{2,1,0:T(8,128)}, f32[24,128,128]{2,1,0:T(8,128)}, u32[]{:S(2)}, u32[]{:S(2)}) collective-permute-start(f32[24,128,128]{2,1,0:T(8,128)} %get-tuple-element.28), channel_id=1, source_target_pairs={{0,1},{1,0},{2,3},{3,2},{4,5},{5,4},{6,7},{7,6},{8,9},{9,8},{10,11... | collective-permute-start | bytes 4718600 | tf_op jit(solution)/shard_map/ppermute | solution.py:396
  56.2 4.2 %copy-start = (bf16[1,128,6144]{2,1,0:T(8,128)(2,1)S(1)}, bf16[1,128,6144]{2,1,0:T(8,128)(2,1)}, u32[]{:S(2)}) copy-start(bf16[1,128,6144]{2,1,0:T(8,128)(2,1)} %param.12) | copy-start | bytes 4718596
  56.2 4.2 %copy-start.7 = (f32[1,128,48]{1,2,0:T(8,128)S(1)}, f32[1,128,48]{1,2,0:T(8,128)}, u32[]{:S(2)}) copy-start(f32[1,128,48]{1,2,0:T(8,128)} %param.15) | copy-start | bytes 73732
  56.3 4.2 %copy-start.8 = (f32[1,6144]{1,0:T(1,128)S(1)}, f32[1,6144]{1,0:T(1,128)}, u32[]{:S(2)}) copy-start(f32[1,6144]{1,0:T(1,128)} %refs_9_.1) | copy-start | bytes 73732
  56.3 4.2 %copy-start.9 = (f32[1,6144]{1,0:T(1,128)S(1)}, f32[1,6144]{1,0:T(1,128)}, u32[]{:S(2)}) copy-start(f32[1,6144]{1,0:T(1,128)} %refs_10_.1) | copy-start | bytes 73732
  56.3 4.2 %copy-start.10 = (s32[1,128,2]{1,2,0:T(2,128)S(1)}, s32[1,128,2]{1,2,0:T(2,128)}, u32[]{:S(2)}) copy-start(s32[1,128,2]{1,2,0:T(2,128)} %param.18) | copy-start | bytes 3076
  56.3 4.2 %copy-start.11 = (f32[1,128,2]{1,2,0:T(2,128)S(1)}, f32[1,128,2]{1,2,0:T(2,128)}, u32[]{:S(2)}) copy-start(f32[1,128,2]{1,2,0:T(2,128)} %param.19) | copy-start | bytes 3076
  60.5 1.2 copy-start.3
  61.7 1.2 copy-start.4
  63.0 1.2 copy-start.5
  64.2 1.4 copy-start.6
  73.6 21.3 %collective-permute-start.10 = (bf16[16,6144]{1,0:T(8,128)(2,1)S(1)}, bf16[16,6144]{1,0:T(8,128)(2,1)S(1)}, u32[]{:S(2)}, u32[]{:S(2)}) collective-permute-start(bf16[16,6144]{1,0:T(8,128)(2,1)S(1)} %get-tuple-element.21.refs_0_), channel_id=1, source_target_pairs={{0,2},{1,3},{2,4},{3,5},{4,6},{5,7},{6,0},{7,1},{8,10},{9,11},{10,... | collective-permute-start | bytes 589832 | tf_op jit(solution)/shard_map/ppermute | solution.py:485
  80.8 22.2 %collective-permute-start.11 = (bf16[16,6144]{1,0:T(8,128)(2,1)S(1)}, bf16[16,6144]{1,0:T(8,128)(2,1)S(1)}, u32[]{:S(2)}, u32[]{:S(2)}) collective-permute-start(bf16[16,6144]{1,0:T(8,128)(2,1)S(1)} %get-tuple-element.21.refs_0_), channel_id=1, source_target_pairs={{0,4},{1,5},{2,6},{3,7},{4,0},{5,1},{6,2},{7,3},{8,12},{9,13},{10,... | collective-permute-start | bytes 589832 | tf_op jit(solution)/shard_map/ppermute | solution.py:485
  89.6 13.6 %collective-permute-start.12 = (bf16[16,6144]{1,0:T(8,128)(2,1)S(1)}, bf16[16,6144]{1,0:T(8,128)(2,1)S(1)}, u32[]{:S(2)}, u32[]{:S(2)}) collective-permute-start(bf16[16,6144]{1,0:T(8,128)(2,1)S(1)} %get-tuple-element.21.refs_0_), channel_id=1, source_target_pairs={{0,6},{1,7},{2,0},{3,1},{4,2},{5,3},{6,4},{7,5},{8,14},{9,15},{10,... | collective-permute-start | bytes 589832 | tf_op jit(solution)/shard_map/ppermute | solution.py:485
  90.0 13.6 %collective-permute-start.13 = (bf16[16,6144]{1,0:T(8,128)(2,1)S(1)}, bf16[16,6144]{1,0:T(8,128)(2,1)S(1)}, u32[]{:S(2)}, u32[]{:S(2)}) collective-permute-start(bf16[16,6144]{1,0:T(8,128)(2,1)S(1)} %get-tuple-element.21.refs_0_), channel_id=1, source_target_pairs={{0,1},{1,0},{2,3},{3,2},{4,5},{5,4},{6,7},{7,6},{8,9},{9,8},{10,11... | collective-permute-start | bytes 589832 | tf_op jit(solution)/shard_map/ppermute | solution.py:396
  94.9 8.7 %collective-permute-start.14 = (bf16[16,6144]{1,0:T(8,128)(2,1)S(1)}, bf16[16,6144]{1,0:T(8,128)(2,1)S(1)}, u32[]{:S(2)}, u32[]{:S(2)}) collective-permute-start(bf16[16,6144]{1,0:T(8,128)(2,1)S(1)} %collective-permute-done.10.refs_1_), channel_id=1, source_target_pairs={{0,1},{1,0},{2,3},{3,2},{4,5},{5,4},{6,7},{7,6},{8,9},{9,8},{10,11... | collective-permute-start | bytes 589832 | tf_op jit(solution)/shard_map/ppermute | solution.py:396
  103.1 1.4 collective-permute-start.15
  103.1 1.7 %collective-permute-start.16 = (bf16[16,6144]{1,0:T(8,128)(2,1)S(1)}, bf16[16,6144]{1,0:T(8,128)(2,1)S(1)}, u32[]{:S(2)}, u32[]{:S(2)}) collective-permute-start(bf16[16,6144]{1,0:T(8,128)(2,1)S(1)} %collective-permute-done.12.refs_3_), channel_id=1, source_target_pairs={{0,1},{1,0},{2,3},{3,2},{4,5},{5,4},{6,7},{7,6},{8,9},{9,8},{10,11... | collective-permute-start | bytes 589832 | tf_op jit(solution)/shard_map/ppermute | solution.py:396
  104.8 3.2 %copy-start.1 = (bf16[1,6144,640]{2,1,0:T(8,128)(2,1)S(1)}, bf16[1,6144,640]{2,1,0:T(8,128)(2,1)}, u32[]{:S(2)}) copy-start(bf16[1,6144,640]{2,1,0:T(8,128)(2,1)} %param.20) | copy-start | bytes 23592964
  108.0 3.2 %copy-start.2 = (bf16[1,640,6144]{2,1,0:T(8,128)(2,1)S(1)}, bf16[1,640,6144]{2,1,0:T(8,128)(2,1)}, u32[]{:S(2)}) copy-start(bf16[1,640,6144]{2,1,0:T(8,128)(2,1)} %param.21) | copy-start | bytes 23592964
  114.0 3.4 %collective-permute-start.17 = (bf16[64,6144]{1,0:T(8,128)(2,1)S(1)}, bf16[64,6144]{1,0:T(8,128)(2,1)S(1)}, u32[]{:S(2)}, u32[]{:S(2)}) collective-permute-start(bf16[64,6144]{1,0:T(8,128)(2,1)S(1)} %get-tuple-element.23), channel_id=1, source_target_pairs={{0,1},{1,0},{2,3},{3,2},{4,5},{5,4},{6,7},{7,6},{8,9},{9,8},{10,11... | collective-permute-start | bytes 2359304 | tf_op jit(solution)/shard_map/ppermute | solution.py:396
  114.3 38.4 %collective-permute-start.22 = (bf16[128,6144]{1,0:T(8,128)(2,1)S(1)}, bf16[128,6144]{1,0:T(8,128)(2,1)S(1)}, u32[]{:S(2)}, u32[]{:S(2)}) collective-permute-start(bf16[128,6144]{1,0:T(8,128)(2,1)S(1)} %get-tuple-element.24), channel_id=1, source_target_pairs={{0,8},{8,16},{16,24},{24,0},{1,9},{9,17},{17,25},{25,1},{2,10},{10... | collective-permute-start | bytes 4718600 | tf_op jit(solution)/shard_map/ppermute | solution.py:391
  115.8 36.1 %collective-permute-start.9 = (f32[8,128]{1,0:T(8,128)S(1)}, f32[8,128]{1,0:T(8,128)S(1)}, u32[]{:S(2)}, u32[]{:S(2)}) collective-permute-start(f32[8,128]{1,0:T(8,128)S(1)} %get-tuple-element.18), channel_id=1, source_target_pairs={{0,8},{8,16},{16,24},{24,0},{1,9},{9,17},{17,25},{25,1},{2,10},{10... | collective-permute-start | bytes 12296 | tf_op jit(solution)/shard_map/ppermute | solution.py:391
  117.7 34.2 %collective-permute-start.18 = (bf16[16,6144]{1,0:T(8,128)(2,1)S(1)}, bf16[16,6144]{1,0:T(8,128)(2,1)S(1)}, u32[]{:S(2)}, u32[]{:S(2)}) collective-permute-start(bf16[16,6144]{1,0:T(8,128)(2,1)S(1)} %get-tuple-element.30), channel_id=1, source_target_pairs={{0,6},{1,7},{2,0},{3,1},{4,2},{5,3},{6,4},{7,5},{8,14},{9,15},{10,... | collective-permute-start | bytes 589832 | tf_op jit(solution)/shard_map/ppermute | solution.py:494
  122.6 29.3 %collective-permute-start.19 = (bf16[16,6144]{1,0:T(8,128)(2,1)S(1)}, bf16[16,6144]{1,0:T(8,128)(2,1)S(1)}, u32[]{:S(2)}, u32[]{:S(2)}) collective-permute-start(bf16[16,6144]{1,0:T(8,128)(2,1)S(1)} %get-tuple-element.32), channel_id=1, source_target_pairs={{0,4},{1,5},{2,6},{3,7},{4,0},{5,1},{6,2},{7,3},{8,12},{9,13},{10,... | collective-permute-start | bytes 589832 | tf_op jit(solution)/shard_map/ppermute | solution.py:494
  123.5 28.4 %collective-permute-start.20 = (bf16[16,6144]{1,0:T(8,128)(2,1)S(1)}, bf16[16,6144]{1,0:T(8,128)(2,1)S(1)}, u32[]{:S(2)}, u32[]{:S(2)}) collective-permute-start(bf16[16,6144]{1,0:T(8,128)(2,1)S(1)} %get-tuple-element.31), channel_id=1, source_target_pairs={{0,2},{1,3},{2,4},{3,5},{4,6},{5,7},{6,0},{7,1},{8,10},{9,11},{10,... | collective-permute-start | bytes 589832 | tf_op jit(solution)/shard_map/ppermute | solution.py:494
  152.0 7.2 %collective-permute-start.21 = (bf16[16,6144]{1,0:T(8,128)(2,1)S(1)}, bf16[16,6144]{1,0:T(8,128)(2,1)S(1)}, u32[]{:S(2)}, u32[]{:S(2)}) collective-permute-start(bf16[16,6144]{1,0:T(8,128)(2,1)S(1)} %add_convert_fusion.1), channel_id=1, source_target_pairs={{0,8},{8,16},{16,24},{24,0},{1,9},{9,17},{17,25},{25,1},{2,10},{10... | collective-permute-start | bytes 589832 | tf_op jit(solution)/shard_map/ppermute | solution.py:391

commit v3 on v2

--- a/solution.py
+++ b/solution.py
@@ -11,6 +11,7 @@
 GROUP = 8
 CHUNKS = 4
 PARTS = 3
+FETCH_MIB = 42
 
 F32, BF16 = jnp.float32, jnp.bfloat16
 
@@ -67,6 +68,10 @@
     for g in range(groups):
         for kind in range(2):
             fetch(kind, g).start()
+    eye = (
+        lax.broadcasted_iota(jnp.int32, (HEAD, HEAD), 0)
+        == lax.broadcasted_iota(jnp.int32, (HEAD, HEAD), 1)
+    ).astype(BF16)
     cum_ref[...] = cumul_rows(rate_ref)
     decay_ref[...] = jnp.broadcast_to(jnp.exp(cum_ref[:, length - 1 :]), decay_ref.shape)
     for g in range(groups):
@@ -77,7 +82,7 @@
             fetch(kind, g).wait()
         for j in range(GROUP):
             cols = slice(j * HEAD, (j + 1) * HEAD)
-            turned = k_ref[g, :, cols].astype(F32).T * tail[j : j + 1, :]
+            turned = dot(eye, k_ref[g, :, cols], ((1,), (1,))) * tail[j : j + 1, :]
             hi, lo = split(turned)
             v = v_ref[g, :, cols]
             state_ref[g * GROUP + j] = dot(hi, v) + dot(lo, v)
@@ -163,78 +168,9 @@
     )(rate, queries, keys, values)
 
 
-def finish_kernel(parts, core_ref, rate_ref, q_hbm, *refs):
-    intra_hbm = refs[:parts]
-    (
-        keep_hbm, got_hbm, resid_hbm, again_ref, mgain_ref, experts_ref, weight_ref,
-        early_ref, outbox_ref, picked_ref, wcol_ref, place_ref,
-        attn_ref, normed_ref, q_ref, intra_ref, state_ref, resid_ref, scale_ref, sems,
-    ) = refs[parts:]
-    length, width = resid_ref.shape
-    heads = width // HEAD
-    groups = heads // GROUP
-    span = GROUP * HEAD
-
-    def copies(g):
-        at = pl.ds(g * span, span)
-        part, place = divmod(g * parts, groups)
-        place = place // parts
-        return [
-            pltpu.make_async_copy(q_hbm.at[:, at], q_ref.at[g], sems.at[0, g]),
-            pltpu.make_async_copy(
-                intra_hbm[part].at[:, pl.ds(place * span, span)], intra_ref.at[g], sems.at[1, g]
-            ),
-        ]
-
-    half = heads // 2
-    for g in range(groups):
-        for copy in copies(g):
-            copy.start()
-
-    def states(n):
-        place = pl.multiple_of(lax.rem(core_ref[0] + n, 2) * half, half)
-        return pltpu.make_async_copy(
-            (keep_hbm, got_hbm)[n], state_ref.at[pl.ds(place, half)], sems.at[2, n]
-        )
-
-    states(0).start()
-    states(1).start()
-    rest = pltpu.make_async_copy(resid_hbm, resid_ref, sems.at[2, 2])
-    rest.start()
-    growth = jnp.exp(cumul_rows(rate_ref))
-    for head in range(heads):
-        across = jnp.broadcast_to(growth[head : head + 1, :], (length, length))
-        scale_ref[:, head * HEAD : (head + 1) * HEAD] = across.T
-    states(0).wait()
-    states(1).wait()
-    for g in range(groups):
-        for copy in copies(g):
-            copy.wait()
-        for j in range(GROUP):
-            head = g * GROUP + j
-            mine = slice(j * HEAD, (j + 1) * HEAD)
-            cols = slice(head * HEAD, (head + 1) * HEAD)
-            hi, lo = split(state_ref[head])
-            q = q_ref[g, :, mine]
-            value = dot(q, hi) + dot(q, lo)
-            attn_ref[:, cols] = intra_ref[g, :, mine] + scale_ref[:, cols] * value
-    rest.wait()
-
-    rows = 16
-
-    def norm(r, carry):
-        at = pl.ds(pl.multiple_of(r * rows, rows), rows)
-        x = attn_ref[at, :]
-        scale = lax.rsqrt(jnp.mean(x * x, axis=-1, keepdims=True) + 1e-06)
-        hres = resid_ref[at, :].astype(F32) + x * scale * again_ref[...]
-        attn_ref[at, :] = hres
-        early_ref[at, :] = hres.astype(BF16)
-        scale = lax.rsqrt(jnp.mean(hres * hres, axis=-1, keepdims=True) + 1e-06)
-        normed_ref[at, :] = (hres * scale * mgain_ref[...]).astype(BF16)
-        return carry
-
-    lax.fori_loop(0, length // rows, norm, 0)
-    slots = outbox_ref.shape[0]
+def route_kernel(experts_ref, weight_ref, place_ref, wcol_ref, token_ref):
+    slots = wcol_ref.shape[0]
+    length = experts_ref.shape[1]
     before = (
         lax.broadcasted_iota(jnp.int32, (length, length), 0)
         < lax.broadcasted_iota(jnp.int32, (length, length), 1)
@@ -248,109 +184,162 @@
     weight = jnp.sum(jnp.where(named, weight_ref[...], 0.0), axis=0, keepdims=True)
     weight = jnp.sum(jnp.where(hot, weight, 0.0), axis=1, keepdims=True)
     wcol_ref[...] = jnp.broadcast_to(weight, wcol_ref.shape)
-    hot = hot.astype(BF16)
-    outbox_ref[...] = dot(hot, normed_ref[...]).astype(BF16)
-    for c in range(width // 512):
-        cols = slice(c * 512, (c + 1) * 512)
-        x = attn_ref[:, cols]
-        hi = x.astype(BF16)
-        mid, low = split(x - hi.astype(F32))
-        picked_ref[:, cols] = dot(hot, hi) + dot(hot, mid) + dot(hot, low)
-
-
-def finish(core, rate, queries, intra, keep, got, resid, attn_gain, moe_gain, experts, weight):
+    at = lax.broadcasted_iota(jnp.int32, (slots, length), 1).astype(F32)
+    token = jnp.sum(jnp.where(hot, at, 0.0), axis=1, keepdims=True)
+    token_ref[...] = jnp.broadcast_to(token, token_ref.shape).astype(jnp.int32)
+
+
+def route(experts, weight):
+    length = experts.shape[1]
+    return pl.pallas_call(
+        route_kernel,
+        in_specs=[VMEM_SPEC] * 2,
+        out_specs=[VMEM_SPEC] * 3,
+        out_shape=[
+            jax.ShapeDtypeStruct((8, length), F32),
+            jax.ShapeDtypeStruct((CAP_SRC, 128), F32),
+            jax.ShapeDtypeStruct((CAP_SRC, 128), jnp.int32),
+        ],
+        name="route",
+    )(experts, weight)
+
+
+def finish_kernel(parts, chunks, steps, core_ref, token_ref, rate_ref, q_hbm, *refs):
+    intra_hbm, refs = refs[:parts], refs[parts:]
+    keeps, gots, refs = refs[:steps], refs[steps : 2 * steps], refs[2 * steps :]
+    (
+        resid_hbm, again_ref, mgain_ref, early_ref, outbox_ref, picked_ref,
+        attn_ref, q_ref, intra_ref, state_ref, resid_ref, scale_ref, sems,
+    ) = refs
+    length, width = resid_ref.shape
+    heads = width // HEAD
+    groups = heads // GROUP
+    span = GROUP * HEAD
+
+    def copies(g):
+        at = pl.ds(g * span, span)
+        part, place = divmod(g * parts, groups)
+        place = place // parts
+        return [
+            pltpu.make_async_copy(q_hbm.at[:, at], q_ref.at[g], sems.at[0, g]),
+            pltpu.make_async_copy(
+                intra_hbm[part].at[:, pl.ds(place * span, span)], intra_ref.at[g], sems.at[1, g]
+            ),
+        ]
+
+    for g in range(groups):
+        for copy in copies(g):
+            copy.start()
+    half = heads // 2
+    per = half // chunks
+
+    def states(n, c, late):
+        place = pl.multiple_of(lax.rem(core_ref[0] + n, 2) * half + c * per, per)
+        source = (keeps, gots)[n][c + late]
+        return pltpu.make_async_copy(source, state_ref.at[pl.ds(place, per)], sems.at[2 + n, c])
+
+    for late in range(steps - chunks + 1):
+
+        @pl.when(core_ref[1] == late)
+        def _():
+            for c in range(chunks):
+                for n in range(2):
+                    states(n, c, late).start()
+
+    rest = pltpu.make_async_copy(resid_hbm, resid_ref, sems.at[4, 0])
+    rest.start()
+    growth = jnp.exp(cumul_rows(rate_ref))
+    for head in range(heads):
+        across = jnp.broadcast_to(growth[head : head + 1, :], (length, length))
+        scale_ref[:, head * HEAD : (head + 1) * HEAD] = across.T
+    for c in range(chunks):
+        for n in range(2):
+            states(n, c, 0).wait()
+    for g in range(groups):
+        for copy in copies(g):
+            copy.wait()
+        for j in range(GROUP):
+            head = g * GROUP + j
+            mine = slice(j * HEAD, (j + 1) * HEAD)
+            cols = slice(head * HEAD, (head + 1) * HEAD)
+            hi, lo = split(state_ref[head])
+            q = q_ref[g, :, mine]
+            value = dot(q, hi) + dot(q, lo)
+            attn_ref[:, cols] = intra_ref[g, :, mine] + scale_ref[:, cols] * value
+    rest.wait()
+    rows = 16
+
+    def norm(r, carry):
+        at = pl.ds(pl.multiple_of(r * rows, rows), rows)
+        x = attn_ref[at, :]
+        scale = lax.rsqrt(jnp.mean(x * x, axis=-1, keepdims=True) + 1e-06)
+        hres = resid_ref[at, :].astype(F32) + x * scale * again_ref[...]
+        attn_ref[at, :] = hres
+        early_ref[at, :] = hres.astype(BF16)
+        return carry
+
+    lax.fori_loop(0, length // rows, norm, 0)
+    for s in range(picked_ref.shape[0]):
+        picked_ref[s : s + 1, :] = attn_ref[pl.ds(token_ref[s], 1), :]
+    x = picked_ref[...]
+    scale = lax.rsqrt(jnp.mean(x * x, axis=-1, keepdims=True) + 1e-06)
+    outbox_ref[...] = (x * scale * mgain_ref[...]).astype(BF16)
+
+
+def finish(core, token, rate, queries, intra, keeps, gots, resid, attn_gain, moe_gain):
     length, width = queries.shape
     heads = width // HEAD
     groups = heads // GROUP
-    parts = len(intra)
-    args = [rate, queries, *intra, keep, got, resid, attn_gain, moe_gain, experts, weight]
+    parts, steps = len(intra), len(keeps)
+    args = [rate, queries, *intra, *keeps, *gots, resid, attn_gain, moe_gain]
     return pl.pallas_call(
-        lambda *refs: finish_kernel(parts, *refs),
-        in_specs=[SMEM_SPEC, VMEM_SPEC]
+        lambda *refs: finish_kernel(parts, CHUNKS, steps, *refs),
+        in_specs=[SMEM_SPEC, SMEM_SPEC, VMEM_SPEC]
         + [HBM_SPEC] * (1 + parts)
-        + [ANY_SPEC] * 2
+        + [ANY_SPEC] * (2 * steps)
         + [HBM_SPEC]
-        + [VMEM_SPEC] * 4,
-        out_specs=[VMEM_SPEC] * 5,
+        + [VMEM_SPEC] * 2,
+        out_specs=[VMEM_SPEC] * 3,
         out_shape=[
             pltpu.VMEM((length, width), BF16),
             pltpu.VMEM((CAP_SRC, width), BF16),
             pltpu.VMEM((CAP_SRC, width), F32),
-            pltpu.VMEM((CAP_SRC, 128), F32),
-            pltpu.VMEM((8, length), F32),
         ],
         scratch_shapes=[
             pltpu.VMEM((length, width), F32),
-            pltpu.VMEM((length, width), BF16),
             pltpu.VMEM((groups, length, GROUP * HEAD), BF16),
             pltpu.VMEM((groups, length, GROUP * HEAD), F32),
             pltpu.VMEM((heads, HEAD, HEAD), F32),
             pltpu.VMEM((length, width), BF16),
             pltpu.VMEM((length, width), F32),
-            pltpu.SemaphoreType.DMA((3, groups)),
+            pltpu.SemaphoreType.DMA((5, max(groups, CHUNKS))),
         ],
         compiler_params=pltpu.CompilerParams(vmem_limit_bytes=32 << 20),
         name="finish",
-    )(core, *args)
-
-
-def expert_kernel(count, *refs):
-    row_refs = refs[:count]
-    (
-        up_hbm, down_hbm, mine_ref, other_ref,
-        up_ref, down_ref, rows_ref, hidden_ref, sems,
-    ) = refs[count:]
-    parts = sems.shape[1]
-    depth, length = up_ref.shape[0] // parts, down_ref.shape[1] // parts
-    half = mine_ref.shape[0]
-
-    def fetch(kind, i):
-        if kind == 0:
-            at = pl.ds(i * depth, depth)
-            return pltpu.make_async_copy(up_hbm.at[at], up_ref.at[at], sems.at[0, i])
-        at = pl.ds(i * length, length)
-        return pltpu.make_async_copy(down_hbm.at[:, at], down_ref.at[:, at], sems.at[1, i])
-
-    for kind in range(2):
-        for i in range(parts):
-            fetch(kind, i).start()
-    each = row_refs[0].shape[0]
-    for n, ref in enumerate(row_refs):
-        rows_ref[n * each : (n + 1) * each, :] = ref[...]
-    acc = None
-    for i in range(parts):
-        fetch(0, i).wait()
-        at = slice(i * depth, (i + 1) * depth)
-        part = dot(rows_ref[:, at], up_ref[at, :])
-        acc = part if acc is None else acc + part
-    hidden_ref[...] = jax.nn.gelu(acc, approximate=True).astype(BF16)
-    for i in range(parts):
-        fetch(1, i).wait()
-        at = slice(i * length, (i + 1) * length)
-        part = dot(hidden_ref[...], down_ref[:, at]).astype(BF16)
-        mine_ref[:, at] = part[:half]
-        other_ref[:, at] = part[half:]
-
-
-def expert_rows(rows, up, down):
-    width, units = up.shape
-    parts = 6
-    total = sum(r.shape[0] for r in rows)
+    )(core, token, *args)
+
+
+def fetch_kernel(up_hbm, down_hbm, up_ref, down_ref, sems):
+    copies = [
+        pltpu.make_async_copy(up_hbm, up_ref, sems.at[0]),
+        pltpu.make_async_copy(down_hbm, down_ref, sems.at[1]),
+    ]
+    for copy in copies:
+        copy.start()
+    for copy in copies:
+        copy.wait()
+
+
+def fetch(up, down):
     return pl.pallas_call(
-        lambda *refs: expert_kernel(len(rows), *refs),
-        in_specs=[VMEM_SPEC] * len(rows) + [HBM_SPEC] * 2,
+        fetch_kernel,
+        in_specs=[HBM_SPEC] * 2,
         out_specs=[VMEM_SPEC] * 2,
-        out_shape=[pltpu.VMEM((total // 2, width), BF16)] * 2,
-        scratch_shapes=[
-            pltpu.VMEM((width, units), BF16),
-            pltpu.VMEM((units, width), BF16),
-            pltpu.VMEM((total, width), BF16),
-            pltpu.VMEM((total, units), BF16),
-            pltpu.SemaphoreType.DMA((2, parts)),
-        ],
-        compiler_params=pltpu.CompilerParams(vmem_limit_bytes=32 << 20),
-        name="expert_rows",
-    )(*[in_vmem(r) for r in rows], up, down)
+        out_shape=[pltpu.VMEM(up.shape, BF16), pltpu.VMEM(down.shape, BF16)],
+        scratch_shapes=[pltpu.SemaphoreType.DMA((2,))],
+        compiler_params=pltpu.CompilerParams(vmem_limit_bytes=FETCH_MIB << 20),
+        name="fetch",
+    )(up, down)
 
 
 def expert_kernel(count, *refs):
@@ -382,7 +371,7 @@
         scratch_shapes=[pltpu.VMEM((total, width), BF16), pltpu.VMEM((total, units), BF16)],
         compiler_params=pltpu.CompilerParams(vmem_limit_bytes=12 << 20),
         name="expert_rows",
-    )(*[in_vmem(r) for r in rows], in_vmem(up), in_vmem(down))
+    )(*[in_vmem(r) for r in rows], up, down)
 
 
 def passed_along(value, axis, steps):
@@ -396,27 +385,44 @@
     return lax.ppermute(value, "ctx", [(i, i ^ 1) for i in range(count)])
 
 
-def chain_prefix(total, decay, chip, chips, scale):
-    heads = total.shape[0]
+def chain_prefix(mine, partner, decay, decay_partner, chip, chips, first, scale):
+    heads = mine.shape[0]
     per = heads // CHUNKS
-    received = []
+    keeps, gots, before = [], [], None
+
+    def chunk(index):
+        place = jnp.clip(index, 0, CHUNKS - 1) * per
+        cut = [
+            lax.dynamic_slice_in_dim(a, place, per, 0)
+            for a in (mine, partner, decay, decay_partner)
+        ]
+        state0, state1 = jnp.where(first, cut[0], cut[1]), jnp.where(first, cut[1], cut[0])
+        decay0, decay1 = jnp.where(first, cut[2], cut[3]), jnp.where(first, cut[3], cut[2])
+        return state0, state1, decay0[:, None, :], decay1[:, None, :]
+
     for step in range(CHUNKS + chips - 2):
-        place = jnp.clip(step - chip, 0, CHUNKS - 1) * per
-        gone = lax.dynamic_slice_in_dim(total, place, per, 0) * scale
-        if step >= 1:
-            before = received[step - 1].astype(F32)
-            gone = lax.dynamic_slice_in_dim(decay, place, per, 0)[:, None, :] * before + gone
+        state0, state1, decay0, decay1 = chunk(step - chip)
+        gone = (decay1 * state0 + state1) * scale
+        if before is not None:
+            gone = (decay0 * decay1) * before.astype(F32) + gone
         pairs = [
             (2 * z + core, 2 * z + 2 + core)
             for z in range(chips - 1)
             if 0 <= step - z < CHUNKS
             for core in range(2)
         ]
-        received.append(lax.ppermute(gone.astype(jnp.float16), "ctx", pairs))
-    row = jnp.concatenate(received, axis=0)
-    first = jnp.maximum(chip - 1, 0) * per
-    mine = lax.dynamic_slice_in_dim(row, first, heads, 0).astype(F32) * (1.0 / scale)
-    return jnp.where(chip > 0, mine, 0.0)
+        before = lax.ppermute(gone.astype(jnp.float16), "ctx", pairs)
+        if step > 0:
+            before, keep, give = lax.optimization_barrier((before, keep, give))
+            keeps.append(keep)
+            gots.append(swapped(give))
+        state0, _, decay0, _ = chunk(step - jnp.maximum(chip - 1, 0))
+        prefix = lax.optimization_barrier(before).astype(F32) * (1.0 / scale)
+        after0 = decay0 * prefix + state0
+        keep, give = jnp.where(first, prefix, after0), jnp.where(first, after0, prefix)
+    keeps.append(keep)
+    gots.append(swapped(give))
+    return keeps, gots
 
 
 def local(
@@ -454,30 +460,31 @@
     mine, _ = half_state(core1, turned, keys, values)
     decay = lax.dynamic_slice_in_dim(decay, core * half, half, 0)
     decay_partner = lax.dynamic_slice_in_dim(decay_partner, core * half, half, 0)
-    state0, state1 = jnp.where(first, mine, partner), jnp.where(first, partner, mine)
-    decay0, decay1 = (
-        jnp.where(first, decay, decay_partner),
-        jnp.where(first, decay_partner, decay),
-    )
     scale = 1.0
     while 36.0 * count * length * scale > 65000.0:
         scale = scale / 2
-    total = decay1[:, None, :] * state0 + state1
-    prefix = chain_prefix(total, decay0 * decay1, chip, chips, scale)
-    after0 = decay0[:, None, :] * prefix + state0
-    keep = jnp.where(first, prefix, after0)
-    got = swapped(jnp.where(first, after0, prefix))
+    keeps, gots = chain_prefix(
+        mine, partner, decay, decay_partner, chip, chips, first, scale
+    )
+    late_by = jnp.maximum(chip - 1, 0)
     intra = []
     for part in range(PARTS):
         intra.append(intra_attention(part, PARTS, turned, queries, keys, values))
     flying = count // SHARDS
     if flying > 1:
+        keep, got = (
+            lax.dynamic_slice_in_dim(jnp.concatenate(a), late_by * (half // CHUNKS), half, 0)
+            for a in (keeps, gots)
+        )
         prefix = jnp.where(first, jnp.concatenate([keep, got]), jnp.concatenate([got, keep]))
         return many_experts(
-            flying, rate, queries, jnp.concatenate(intra, axis=1), prefix, resid, attn_gain, moe_gain, experts, weight, up, down
+            flying, rate, queries, jnp.concatenate(intra, axis=1), prefix, resid,
+            attn_gain, moe_gain, experts, weight, up, down,
         )
-    early, outbox, picked, wcol, place = finish(
-        core1, turned, queries, intra, keep, got, resid, attn_gain, moe_gain, experts.T, weight.T
+    place, wcol, token = route(experts.T, weight.T)
+    early, outbox, picked = finish(
+        jnp.stack([core, late_by]).astype(jnp.int32), token[:, 0], turned, queries, intra,
+        keeps, gots, resid, attn_gain, moe_gain,
     )
     early = passed_along(early, "section", 1)
     place = passed_along(place, "section", 1)
@@ -486,6 +493,7 @@
         for d in range(1, chips)
     ]
     others = [swapped(r) for r in own]
+    up, down = fetch(up, down)
     mine, other = expert_rows(own + others, up, down)
     pair = (mine.astype(F32) + swapped(other).astype(F32)).astype(BF16)
     pair = pair.reshape(chips, CAP_SRC, width)

time: 163 us -> 177 us (1.086)
  Pallas kernels: 31.8 us -> 39.6 us
  waiting for transfers between devices: 63.2 us -> 67.8 us
  other arithmetic: 4.64 us -> 8.16 us
    ppermute x3, waiting for transfers between devices: 0.01 us -> 14.5 us  [layer(): lax.ppermute(pair[d], 'ctx', [(i, (i - 2 * d) % count) for i in range(cou...]
    ppermute x3, waiting for transfers between devices: 34.9 us -> 23.3 us  [passed_along(): return lax.ppermute(value, axis, pairs)]
    pallas_call x1 -> x3, Pallas kernels: 8.04 us -> 14.4 us  [the longest x1 7.41 us: finish(): pl.pallas_call(lambda *refs: finish_kernel(parts, CHUNKS, steps, *refs),...]
    select_n x1 -> x7, other arithmetic: 1.64 us -> 6.69 us  [the longest x6 6.57 us: chain_prefix(): jnp.where(first, after0, prefix)]
    add x1 -> x0, other arithmetic: 2.27 us -> none  [layer(): total = decay1[:, None, :] * state0 + state1]
    unnamed x37 -> x36, local copies, waits for them, and re-layouts: 11.9 us -> 9.66 us
    ppermute x3, waiting for transfers between devices: 13.1 us -> 15.2 us  [layer(): lax.ppermute(outbox, 'ctx', [(i, (i + 2 * d) % count) for i in range(coun...]
  transfers between devices with their start and end apart: 23 -> 28, of which waited for: 10 -> 11; matrix products, arithmetic and copies ran while one was open for 1% -> 1% of each run, Pallas kernels for 10% -> 14%
where the time goes in v3:
time: 177 us; the launch traced here: 176 us
  waiting for transfers between devices  67.8 us (38%)
  starting transfers between devices  47.4 us (27%)
  Pallas kernels  39.6 us (22%)
  local copies, waits for them, and re-layouts  10.6 us (6%)
  other arithmetic  8.16 us (5%)
  matrix products  1.77 us (1%)
    ppermute x3, waiting for transfers between devices, passed_along(): return lax.ppermute(value, axis, pairs)  23.3 us
    ppermute x6, starting transfers between devices, chain_prefix(): before = lax.ppermute(gone.astype(jnp.float16), 'ctx', pairs)  19.5 us
    ppermute x3, waiting for transfers between devices, layer(): lax.ppermute(outbox, 'ctx', [(i, (i + 2 * d) % count) for i in range(coun...  15.2 us
    ppermute x3, starting transfers between devices, layer(): lax.ppermute(outbox, 'ctx', [(i, (i + 2 * d) % count) for i in range(coun...  15 us
    ppermute x3, waiting for transfers between devices, layer(): lax.ppermute(pair[d], 'ctx', [(i, (i - 2 * d) % count) for i in range(cou...  14.5 us
    ppermute x6, waiting for transfers between devices, chain_prefix(): before = lax.ppermute(gone.astype(jnp.float16), 'ctx', pairs)  14.2 us
    pallas_call x3, Pallas kernels, intra_attention(): pl.pallas_call(lambda *refs: intra_kernel(part * groups, *refs), in_specs...  12.3 us
    pallas_call x2, Pallas kernels, half_state(): pl.pallas_call(state_kernel, in_specs=[SMEM_SPEC, VMEM_SPEC, HBM_SPEC, HB...  10.2 us
  transfers between devices with their start and end apart: 28, of which 11 were waited for; matrix products, arithmetic and copies ran while one was open for 1% of the time, Pallas kernels for 14%

profile of v3, /device:TPU:0, one launch (start us, length us, event | category | flops | bytes accessed | tf_op | source)
XLA Modules:
  0.0 175.9 jit_solution(10197120255500425950)
XLA Ops:
  0.0 5.1 %half_state.2 = (f32[24,128,128]{2,1,0:T(8,128)}, f32[48,128]{1,0:T(8,128)}) custom-call(s32[1]{0:T(128)S(6)} %sub.54.half_ref, f32[48,128]{1,0:T(8,128)} %bitcast.29, bf16[128,6144]{1,0:T(8,128)(2,1)} %bitcast.35, bf16[128,6144]{1,0:T(8,128)(2,1)} %bitcast.40), custom_call_target="tpu_custom_call" | custom-call | tf_op jit(solution)/shard_map/half_state/pallas_call | solution.py:98
  5.8 5.1 %half_state.3 = (f32[24,128,128]{2,1,0:T(8,128)}, f32[48,128]{1,0:T(8,128)}) custom-call(s32[1]{0:T(128)} %bitcast.5.half_ref, f32[48,128]{1,0:T(8,128)} %bitcast.30, bf16[128,6144]{1,0:T(8,128)(2,1)} %bitcast.36, bf16[128,6144]{1,0:T(8,128)(2,1)} %bitcast.41), custom_call_target="tpu_custom_call" | custom-call | tf_op jit(solution)/shard_map/half_state/pallas_call | solution.py:98
  11.1 1.1 add_convert_fusion.7
  12.2 5.0 %collective-permute-start.3 = (f16[6,128,128]{2,1,0:T(8,128)(2,1)S(1)}, f16[6,128,128]{2,1,0:T(8,128)(2,1)S(1)}, u32[]{:S(2)}, u32[]{:S(2)}) collective-permute-start(f16[6,128,128]{2,1,0:T(8,128)(2,1)S(1)} %add_convert_fusion.7), channel_id=1, source_target_pairs={{0,2},{1,3},{8,10},{9,11},{16,18},{17,19},{24,26},{25,27}} | collective-permute-start | bytes 589832 | tf_op jit(solution)/shard_map/ppermute | solution.py:414
  17.3 4.4 %collective-permute-done.3 = f16[6,128,128]{2,1,0:T(8,128)(2,1)S(1)} collective-permute-done((f16[6,128,128]{2,1,0:T(8,128)(2,1)S(1)}, f16[6,128,128]{2,1,0:T(8,128)(2,1)S(1)}, u32[]{:S(2)}, u32[]{:S(2)}) %collective-permute-start.3) | collective-permute-done | bytes 196640 | tf_op jit(solution)/shard_map/ppermute | solution.py:414
  21.7 1.3 convert_select_fusion.10
  23.0 4.4 %collective-permute-start.4 = (f16[6,128,128]{2,1,0:T(8,128)(2,1)S(1)}, f16[6,128,128]{2,1,0:T(8,128)(2,1)S(1)}, u32[]{:S(2)}, u32[]{:S(2)}) collective-permute-start(f16[6,128,128]{2,1,0:T(8,128)(2,1)S(1)} %get-tuple-element.87), channel_id=1, source_target_pairs={{0,2},{1,3},{2,4},{3,5},{8,10},{9,11},{10,12},{11,13},{16,18},{17,... | collective-permute-start | bytes 589832 | tf_op jit(solution)/shard_map/ppermute | solution.py:414
  27.4 3.5 %collective-permute-done.4 = f16[6,128,128]{2,1,0:T(8,128)(2,1)S(1)} collective-permute-done((f16[6,128,128]{2,1,0:T(8,128)(2,1)S(1)}, f16[6,128,128]{2,1,0:T(8,128)(2,1)S(1)}, u32[]{:S(2)}, u32[]{:S(2)}) %collective-permute-start.4) | collective-permute-done | bytes 196640 | tf_op jit(solution)/shard_map/ppermute | solution.py:414
  30.9 1.1 convert_select_fusion.8
  32.0 4.4 %collective-permute-start.5 = (f16[6,128,128]{2,1,0:T(8,128)(2,1)S(1)}, f16[6,128,128]{2,1,0:T(8,128)(2,1)S(1)}, u32[]{:S(2)}, u32[]{:S(2)}) collective-permute-start(f16[6,128,128]{2,1,0:T(8,128)(2,1)S(1)} %get-tuple-element.86), channel_id=1, source_target_pairs={{0,2},{1,3},{2,4},{3,5},{4,6},{5,7},{8,10},{9,11},{10,12},{11,13},... | collective-permute-start | bytes 589832 | tf_op jit(solution)/shard_map/ppermute | solution.py:414
  36.4 3.2 %collective-permute-done.5 = f16[6,128,128]{2,1,0:T(8,128)(2,1)S(1)} collective-permute-done((f16[6,128,128]{2,1,0:T(8,128)(2,1)S(1)}, f16[6,128,128]{2,1,0:T(8,128)(2,1)S(1)}, u32[]{:S(2)}, u32[]{:S(2)}) %collective-permute-start.5) | collective-permute-done | bytes 196640 | tf_op jit(solution)/shard_map/ppermute | solution.py:414
  39.5 1.1 convert_select_fusion.6
  40.6 4.4 %collective-permute-start.6 = (f16[6,128,128]{2,1,0:T(8,128)(2,1)S(1)}, f16[6,128,128]{2,1,0:T(8,128)(2,1)S(1)}, u32[]{:S(2)}, u32[]{:S(2)}) collective-permute-start(f16[6,128,128]{2,1,0:T(8,128)(2,1)S(1)} %get-tuple-element.85), channel_id=1, source_target_pairs={{0,2},{1,3},{2,4},{3,5},{4,6},{5,7},{8,10},{9,11},{10,12},{11,13},... | collective-permute-start | bytes 589832 | tf_op jit(solution)/shard_map/ppermute | solution.py:414
  45.0 3.2 %collective-permute-done.6 = f16[6,128,128]{2,1,0:T(8,128)(2,1)S(1)} collective-permute-done((f16[6,128,128]{2,1,0:T(8,128)(2,1)S(1)}, f16[6,128,128]{2,1,0:T(8,128)(2,1)S(1)}, u32[]{:S(2)}, u32[]{:S(2)}) %collective-permute-start.6) | collective-permute-done | bytes 196640 | tf_op jit(solution)/shard_map/ppermute | solution.py:414
  48.2 1.1 convert_select_fusion.4
  50.0 1.1 convert_select_fusion.2
  52.8 0.9 convert_select_fusion
  53.8 0.8 copy-done.10
  55.0 4.0 %intra_attention.5.refs_6_ = f32[128,2048]{1,0:T(8,128)} custom-call(f32[48,128]{1,0:T(8,128)} %bitcast.31, bf16[128,6144]{1,0:T(8,128)(2,1)} %bitcast.24, bf16[128,6144]{1,0:T(8,128)(2,1)} %bitcast.37, bf16[128,6144]{1,0:T(8,128)(2,1)} %bitcast.42), custom_call_target="tpu_custom_call" | custom-call | tf_op jit(solution)/shard_map/intra_attention/pallas_call | solution.py:160
  59.1 4.1 %intra_attention.4.refs_5_ = f32[128,2048]{1,0:T(8,128)} custom-call(f32[48,128]{1,0:T(8,128)} %bitcast.32, bf16[128,6144]{1,0:T(8,128)(2,1)} %bitcast.25, bf16[128,6144]{1,0:T(8,128)(2,1)} %bitcast.38, bf16[128,6144]{1,0:T(8,128)(2,1)} %bitcast.43), custom_call_target="tpu_custom_call" | custom-call | tf_op jit(solution)/shard_map/intra_attention/pallas_call | solution.py:160
  63.2 4.2 %intra_attention.3.refs_4_ = f32[128,2048]{1,0:T(8,128)} custom-call(f32[48,128]{1,0:T(8,128)} %bitcast.33, bf16[128,6144]{1,0:T(8,128)(2,1)} %bitcast.26, bf16[128,6144]{1,0:T(8,128)(2,1)} %bitcast.39, bf16[128,6144]{1,0:T(8,128)(2,1)} %bitcast.44), custom_call_target="tpu_custom_call" | custom-call | tf_op jit(solution)/shard_map/intra_attention/pallas_call | solution.py:160
  67.3 1.5 route.1
  68.9 0.8 slice_reduce_fusion.1.refs_1_
  69.8 1.2 copy-done.2
  71.1 1.2 copy-done.3
  72.3 1.0 copy-done.4
  73.3 1.0 copy-done.5
  74.3 1.0 copy-done.6
  75.3 1.0 copy-done.7
  76.3 1.4 copy-done.8
  77.7 1.0 copy-done.11
  78.7 7.4 %finish.1 = (bf16[128,6144]{1,0:T(8,128)(2,1)S(1)}, bf16[16,6144]{1,0:T(8,128)(2,1)S(1)}, f32[16,6144]{1,0:T(8,128)S(1)}) custom-call(s32[2]{0:T(128)S(1)} %pad_add_fusion.refs_0_, s32[16]{0:T(128)S(1)} %slice_reduce_fusion.1.refs_1_, f32[48,128]{1,0:T(8,128)S(1)} %bitcast.34, bf16[128,6144]{1,0:T(8,128)(2,1)S(1)} %bitcast.27, f32[128,2048]{1,0:T(8,128)S(1)} %copy-done.3, ...), custom_call_target="tpu_custom_call" | custom-call | tf_op jit(solution)/shard_map/finish/pallas_call | solution.py:295
  86.1 14.4 %collective-permute-start.17 = (bf16[16,6144]{1,0:T(8,128)(2,1)S(1)}, bf16[16,6144]{1,0:T(8,128)(2,1)S(1)}, u32[]{:S(2)}, u32[]{:S(2)}) collective-permute-start(bf16[16,6144]{1,0:T(8,128)(2,1)S(1)} %get-tuple-element.55.refs_0_), channel_id=1, source_target_pairs={{0,6},{1,7},{2,0},{3,1},{4,2},{5,3},{6,4},{7,5},{8,14},{9,15},{10,... | collective-permute-start | bytes 589832 | tf_op jit(solution)/shard_map/ppermute | solution.py:492
  101.1 4.7 %collective-permute-done.17.refs_3_ = bf16[16,6144]{1,0:T(8,128)(2,1)S(1)} collective-permute-done((bf16[16,6144]{1,0:T(8,128)(2,1)S(1)}, bf16[16,6144]{1,0:T(8,128)(2,1)S(1)}, u32[]{:S(2)}, u32[]{:S(2)}) %collective-permute-start.17) | collective-permute-done | bytes 196640 | tf_op jit(solution)/shard_map/ppermute | solution.py:492
  105.8 10.5 %collective-permute-done.16.refs_2_ = bf16[16,6144]{1,0:T(8,128)(2,1)S(1)} collective-permute-done((bf16[16,6144]{1,0:T(8,128)(2,1)S(1)}, bf16[16,6144]{1,0:T(8,128)(2,1)S(1)}, u32[]{:S(2)}, u32[]{:S(2)}) %collective-permute-start.16) | collective-permute-done | bytes 196640 | tf_op jit(solution)/shard_map/ppermute | solution.py:492
  116.8 5.5 %fetch.1 = (bf16[6144,640]{1,0:T(8,128)(2,1)S(1)}, bf16[640,6144]{1,0:T(8,128)(2,1)S(1)}) custom-call(bf16[6144,640]{1,0:T(8,128)(2,1)} %bitcast.45, bf16[640,6144]{1,0:T(8,128)(2,1)} %bitcast.46), custom_call_target="tpu_custom_call" | custom-call | tf_op jit(solution)/shard_map/fetch/pallas_call | solution.py:334
  122.4 2.7 %expert_rows.1 = (bf16[64,6144]{1,0:T(8,128)(2,1)S(1)}, bf16[64,6144]{1,0:T(8,128)(2,1)S(1)}) custom-call(bf16[16,6144]{1,0:T(8,128)(2,1)S(1)} %get-tuple-element.55.refs_0_, bf16[16,6144]{1,0:T(8,128)(2,1)S(1)} %collective-permute-done.15.refs_1_, bf16[16,6144]{1,0:T(8,128)(2,1)S(1)} %collective-permute-done.16.refs_2_, ...), custom_call_target="tpu_custom_call" | custom-call | tf_op jit(solution)/shard_map/expert_rows/pallas_call | solution.py:366
  125.2 1.5 collective-permute-start
  127.7 1.4 collective-permute-start.23
  129.1 0.7 collective-permute-start.25
  129.8 3.3 %collective-permute-start.24 = (bf16[16,6144]{1,0:T(8,128)(2,1)S(1)}, bf16[16,6144]{1,0:T(8,128)(2,1)S(1)}, u32[]{:S(2)}, u32[]{:S(2)}) collective-permute-start(bf16[16,6144]{1,0:T(8,128)(2,1)S(1)} %get-tuple-element.90), channel_id=1, source_target_pairs={{0,4},{1,5},{2,6},{3,7},{4,0},{5,1},{6,2},{7,3},{8,12},{9,13},{10,... | collective-permute-start | bytes 589832 | tf_op jit(solution)/shard_map/ppermute | solution.py:502
  133.1 1.5 collective-permute-start.27
  134.7 7.9 %collective-permute-done.25 = bf16[16,6144]{1,0:T(8,128)(2,1)S(1)} collective-permute-done((bf16[16,6144]{1,0:T(8,128)(2,1)S(1)}, bf16[16,6144]{1,0:T(8,128)(2,1)S(1)}, u32[]{:S(2)}, u32[]{:S(2)}) %collective-permute-start.25) | collective-permute-done | bytes 196640 | tf_op jit(solution)/shard_map/ppermute | solution.py:502
  142.6 6.6 %collective-permute-done.24 = bf16[16,6144]{1,0:T(8,128)(2,1)S(1)} collective-permute-done((bf16[16,6144]{1,0:T(8,128)(2,1)S(1)}, bf16[16,6144]{1,0:T(8,128)(2,1)S(1)}, u32[]{:S(2)}, u32[]{:S(2)}) %collective-permute-start.24) | collective-permute-done | bytes 196640 | tf_op jit(solution)/shard_map/ppermute | solution.py:502
  149.3 1.5 collective-permute-start.26
  150.8 20.5 %collective-permute-done.27 = bf16[128,6144]{1,0:T(8,128)(2,1)S(1)} collective-permute-done((bf16[128,6144]{1,0:T(8,128)(2,1)S(1)}, bf16[128,6144]{1,0:T(8,128)(2,1)S(1)}, u32[]{:S(2)}, u32[]{:S(2)}) %collective-permute-start.27) | collective-permute-done | bytes 1572896 | tf_op jit(solution)/shard_map/ppermute | solution.py:380
  171.3 2.8 %collective-permute-done.26 = bf16[16,6144]{1,0:T(8,128)(2,1)S(1)} collective-permute-done((bf16[16,6144]{1,0:T(8,128)(2,1)S(1)}, bf16[16,6144]{1,0:T(8,128)(2,1)S(1)}, u32[]{:S(2)}, u32[]{:S(2)}) %collective-permute-start.26) | collective-permute-done | bytes 196640 | tf_op jit(solution)/shard_map/ppermute | solution.py:380
  174.1 1.8 %select_bitcast_fusion = bf16[1,128,6144]{2,1,0:T(8,128)(2,1)} fusion(bf16[128,6144]{1,0:T(8,128)(2,1)S(1)} %collective-permute-done.27, pred[128]{0:T(512)(128)(4,1)S(1)} %broadcast_compare_fusion, bf16[16,6144]{1,0:T(8,128)(2,1)S(1)} %collective-permute-done.26, f32[128]{0:T(128)S(1)} %slice_bitcast_fusion), kind=kOutput, calls=%fused_computation.1 | convolution fusion | flops 26740736 | bytes 3342976 | tf_op jit(solution)/shard_map/dot_general | solution.py:507
  (70 shorter events, 6.2 us)
Async XLA Ops:
  5.1 6.0 %collective-permute-start.2 = (f32[24,128,128]{2,1,0:T(8,128)}, f32[24,128,128]{2,1,0:T(8,128)S(1)}, u32[]{:S(2)}, u32[]{:S(2)}) collective-permute-start(f32[24,128,128]{2,1,0:T(8,128)} %get-tuple-element.37), channel_id=1, source_target_pairs={{0,1},{1,0},{2,3},{3,2},{4,5},{5,4},{6,7},{7,6},{8,9},{9,8},{10,11... | collective-permute-start | bytes 4718600 | tf_op jit(solution)/shard_map/ppermute | solution.py:385
  5.7 5.3 %collective-permute-start.1 = (f32[48,128]{1,0:T(8,128)}, f32[48,128]{1,0:T(8,128)S(1)}, u32[]{:S(2)}, u32[]{:S(2)}) collective-permute-start(f32[48,128]{1,0:T(8,128)} %get-tuple-element.35), channel_id=1, source_target_pairs={{0,1},{1,0},{2,3},{3,2},{4,5},{5,4},{6,7},{7,6},{8,9},{9,8},{10,11... | collective-permute-start | bytes 73736 | tf_op jit(solution)/shard_map/ppermute | solution.py:385
  5.8 5.2 %copy-start.15 = (f32[48,128]{1,0:T(8,128)S(1)}, f32[48,128]{1,0:T(8,128)}, u32[]{:S(2)}) copy-start(f32[48,128]{1,0:T(8,128)} %get-tuple-element.35) | copy-start | bytes 73732
  12.2 18.7 %copy-start.14 = (f32[24,128,128]{2,1,0:T(8,128)S(1)}, f32[24,128,128]{2,1,0:T(8,128)}, u32[]{:S(2)}) copy-start(f32[24,128,128]{2,1,0:T(8,128)} %get-tuple-element.36) | copy-start | bytes 4718596
  12.2 9.4 %collective-permute-start.3 = (f16[6,128,128]{2,1,0:T(8,128)(2,1)S(1)}, f16[6,128,128]{2,1,0:T(8,128)(2,1)S(1)}, u32[]{:S(2)}, u32[]{:S(2)}) collective-permute-start(f16[6,128,128]{2,1,0:T(8,128)(2,1)S(1)} %add_convert_fusion.7), channel_id=1, source_target_pairs={{0,2},{1,3},{8,10},{9,11},{16,18},{17,19},{24,26},{25,27}} | collective-permute-start | bytes 589832 | tf_op jit(solution)/shard_map/ppermute | solution.py:414
  23.0 7.9 %collective-permute-start.4 = (f16[6,128,128]{2,1,0:T(8,128)(2,1)S(1)}, f16[6,128,128]{2,1,0:T(8,128)(2,1)S(1)}, u32[]{:S(2)}, u32[]{:S(2)}) collective-permute-start(f16[6,128,128]{2,1,0:T(8,128)(2,1)S(1)} %get-tuple-element.87), channel_id=1, source_target_pairs={{0,2},{1,3},{2,4},{3,5},{8,10},{9,11},{10,12},{11,13},{16,18},{17,... | collective-permute-start | bytes 589832 | tf_op jit(solution)/shard_map/ppermute | solution.py:414
  32.0 7.6 %collective-permute-start.5 = (f16[6,128,128]{2,1,0:T(8,128)(2,1)S(1)}, f16[6,128,128]{2,1,0:T(8,128)(2,1)S(1)}, u32[]{:S(2)}, u32[]{:S(2)}) collective-permute-start(f16[6,128,128]{2,1,0:T(8,128)(2,1)S(1)} %get-tuple-element.86), channel_id=1, source_target_pairs={{0,2},{1,3},{2,4},{3,5},{4,6},{5,7},{8,10},{9,11},{10,12},{11,13},... | collective-permute-start | bytes 589832 | tf_op jit(solution)/shard_map/ppermute | solution.py:414
  40.6 7.6 %collective-permute-start.6 = (f16[6,128,128]{2,1,0:T(8,128)(2,1)S(1)}, f16[6,128,128]{2,1,0:T(8,128)(2,1)S(1)}, u32[]{:S(2)}, u32[]{:S(2)}) collective-permute-start(f16[6,128,128]{2,1,0:T(8,128)(2,1)S(1)} %get-tuple-element.85), channel_id=1, source_target_pairs={{0,2},{1,3},{2,4},{3,5},{4,6},{5,7},{8,10},{9,11},{10,12},{11,13},... | collective-permute-start | bytes 589832 | tf_op jit(solution)/shard_map/ppermute | solution.py:414
  49.3 0.7 collective-permute-start.7
  51.0 1.8 %collective-permute-start.8 = (f16[6,128,128]{2,1,0:T(8,128)(2,1)S(1)}, f16[6,128,128]{2,1,0:T(8,128)(2,1)S(1)}, u32[]{:S(2)}, u32[]{:S(2)}) collective-permute-start(f16[6,128,128]{2,1,0:T(8,128)(2,1)S(1)} %get-tuple-element.83), channel_id=1, source_target_pairs={{4,6},{5,7},{12,14},{13,15},{20,22},{21,23},{28,30},{29,31}} | collective-permute-start | bytes 589832 | tf_op jit(solution)/shard_map/ppermute | solution.py:414
  51.7 2.1 %collective-permute-start.9 = (f32[6,128,128]{2,1,0:T(8,128)S(1)}, f32[6,128,128]{2,1,0:T(8,128)S(1)}, u32[]{:S(2)}, u32[]{:S(2)}) collective-permute-start(f32[6,128,128]{2,1,0:T(8,128)S(1)} %get-tuple-element.48), channel_id=1, source_target_pairs={{0,1},{1,0},{2,3},{3,2},{4,5},{5,4},{6,7},{7,6},{8,9},{9,8},{10,11... | collective-permute-start | bytes 1179656 | tf_op jit(solution)/shard_map/ppermute | solution.py:385
  51.8 17.9 %collective-permute-start.10 = (f32[6,128,128]{2,1,0:T(8,128)}, f32[6,128,128]{2,1,0:T(8,128)}, u32[]{:S(2)}, u32[]{:S(2)}) collective-permute-start(f32[6,128,128]{2,1,0:T(8,128)} %get-tuple-element.49), channel_id=1, source_target_pairs={{0,1},{1,0},{2,3},{3,2},{4,5},{5,4},{6,7},{7,6},{8,9},{9,8},{10,11... | collective-permute-start | bytes 1179656 | tf_op jit(solution)/shard_map/ppermute | solution.py:385
  52.3 17.5 %collective-permute-start.11 = (f32[6,128,128]{2,1,0:T(8,128)}, f32[6,128,128]{2,1,0:T(8,128)}, u32[]{:S(2)}, u32[]{:S(2)}) collective-permute-start(f32[6,128,128]{2,1,0:T(8,128)} %get-tuple-element.50), channel_id=1, source_target_pairs={{0,1},{1,0},{2,3},{3,2},{4,5},{5,4},{6,7},{7,6},{8,9},{9,8},{10,11... | collective-permute-start | bytes 1179656 | tf_op jit(solution)/shard_map/ppermute | solution.py:385
  52.4 17.4 %collective-permute-start.12 = (f32[6,128,128]{2,1,0:T(8,128)}, f32[6,128,128]{2,1,0:T(8,128)}, u32[]{:S(2)}, u32[]{:S(2)}) collective-permute-start(f32[6,128,128]{2,1,0:T(8,128)} %get-tuple-element.51), channel_id=1, source_target_pairs={{0,1},{1,0},{2,3},{3,2},{4,5},{5,4},{6,7},{7,6},{8,9},{9,8},{10,11... | collective-permute-start | bytes 1179656 | tf_op jit(solution)/shard_map/ppermute | solution.py:385
  53.7 16.1 %collective-permute-start.14 = (f32[6,128,128]{2,1,0:T(8,128)}, f32[6,128,128]{2,1,0:T(8,128)}, u32[]{:S(2)}, u32[]{:S(2)}) collective-permute-start(f32[6,128,128]{2,1,0:T(8,128)} %get-tuple-element.71), channel_id=1, source_target_pairs={{0,1},{1,0},{2,3},{3,2},{4,5},{5,4},{6,7},{7,6},{8,9},{9,8},{10,11... | collective-permute-start | bytes 1179656 | tf_op jit(solution)/shard_map/ppermute | solution.py:385
  53.8 0.8 copy-start.10
  54.6 15.2 %collective-permute-start.13 = (f32[6,128,128]{2,1,0:T(8,128)}, f32[6,128,128]{2,1,0:T(8,128)}, u32[]{:S(2)}, u32[]{:S(2)}) collective-permute-start(f32[6,128,128]{2,1,0:T(8,128)} %get-tuple-element.52), channel_id=1, source_target_pairs={{0,1},{1,0},{2,3},{3,2},{4,5},{5,4},{6,7},{7,6},{8,9},{9,8},{10,11... | collective-permute-start | bytes 1179656 | tf_op jit(solution)/shard_map/ppermute | solution.py:385
  63.1 6.7 %copy-start = (bf16[1,128,6144]{2,1,0:T(8,128)(2,1)S(1)}, bf16[1,128,6144]{2,1,0:T(8,128)(2,1)}, u32[]{:S(2)}) copy-start(bf16[1,128,6144]{2,1,0:T(8,128)(2,1)} %param.12) | copy-start | bytes 4718596
  63.1 6.7 %copy-start.1 = (f32[128,2048]{1,0:T(8,128)S(1)}, f32[128,2048]{1,0:T(8,128)}, u32[]{:S(2)}) copy-start(f32[128,2048]{1,0:T(8,128)} %intra_attention.5.refs_6_) | copy-start | bytes 3145732
  63.1 6.7 %copy-start.9 = (f32[1,128,48]{1,2,0:T(8,128)S(1)}, f32[1,128,48]{1,2,0:T(8,128)}, u32[]{:S(2)}) copy-start(f32[1,128,48]{1,2,0:T(8,128)} %param.15) | copy-start | bytes 73732
  63.2 6.7 %copy-start.12 = (f32[1,6144]{1,0:T(1,128)S(1)}, f32[1,6144]{1,0:T(1,128)}, u32[]{:S(2)}) copy-start(f32[1,6144]{1,0:T(1,128)} %refs_20_.1) | copy-start | bytes 73732
  63.2 6.7 %copy-start.13 = (f32[1,6144]{1,0:T(1,128)S(1)}, f32[1,6144]{1,0:T(1,128)}, u32[]{:S(2)}) copy-start(f32[1,6144]{1,0:T(1,128)} %refs_21_.1) | copy-start | bytes 73732
  69.8 1.2 copy-start.2
  71.1 1.2 copy-start.3
  72.3 1.0 copy-start.4
  73.3 1.0 copy-start.5
  74.3 1.0 copy-start.6
  75.3 1.0 copy-start.7
  76.3 1.4 copy-start.8
  77.7 1.0 copy-start.11
  86.1 19.7 %collective-permute-start.17 = (bf16[16,6144]{1,0:T(8,128)(2,1)S(1)}, bf16[16,6144]{1,0:T(8,128)(2,1)S(1)}, u32[]{:S(2)}, u32[]{:S(2)}) collective-permute-start(bf16[16,6144]{1,0:T(8,128)(2,1)S(1)} %get-tuple-element.55.refs_0_), channel_id=1, source_target_pairs={{0,6},{1,7},{2,0},{3,1},{4,2},{5,3},{6,4},{7,5},{8,14},{9,15},{10,... | collective-permute-start | bytes 589832 | tf_op jit(solution)/shard_map/ppermute | solution.py:492
  100.5 15.8 %collective-permute-start.16 = (bf16[16,6144]{1,0:T(8,128)(2,1)S(1)}, bf16[16,6144]{1,0:T(8,128)(2,1)S(1)}, u32[]{:S(2)}, u32[]{:S(2)}) collective-permute-start(bf16[16,6144]{1,0:T(8,128)(2,1)S(1)} %get-tuple-element.55.refs_0_), channel_id=1, source_target_pairs={{0,4},{1,5},{2,6},{3,7},{4,0},{5,1},{6,2},{7,3},{8,12},{9,13},{10,... | collective-permute-start | bytes 589832 | tf_op jit(solution)/shard_map/ppermute | solution.py:492
  100.5 15.9 %collective-permute-start.15 = (bf16[16,6144]{1,0:T(8,128)(2,1)S(1)}, bf16[16,6144]{1,0:T(8,128)(2,1)S(1)}, u32[]{:S(2)}, u32[]{:S(2)}) collective-permute-start(bf16[16,6144]{1,0:T(8,128)(2,1)S(1)} %get-tuple-element.55.refs_0_), channel_id=1, source_target_pairs={{0,2},{1,3},{2,4},{3,5},{4,6},{5,7},{6,0},{7,1},{8,10},{9,11},{10,... | collective-permute-start | bytes 589832 | tf_op jit(solution)/shard_map/ppermute | solution.py:492
  101.1 21.2 %collective-permute-start.18 = (bf16[16,6144]{1,0:T(8,128)(2,1)S(1)}, bf16[16,6144]{1,0:T(8,128)(2,1)S(1)}, u32[]{:S(2)}, u32[]{:S(2)}) collective-permute-start(bf16[16,6144]{1,0:T(8,128)(2,1)S(1)} %get-tuple-element.55.refs_0_), channel_id=1, source_target_pairs={{0,1},{1,0},{2,3},{3,2},{4,5},{5,4},{6,7},{7,6},{8,9},{9,8},{10,11... | collective-permute-start | bytes 589832 | tf_op jit(solution)/shard_map/ppermute | solution.py:385
  105.8 16.5 %collective-permute-start.21 = (bf16[16,6144]{1,0:T(8,128)(2,1)S(1)}, bf16[16,6144]{1,0:T(8,128)(2,1)S(1)}, u32[]{:S(2)}, u32[]{:S(2)}) collective-permute-start(bf16[16,6144]{1,0:T(8,128)(2,1)S(1)} %collective-permute-done.17.refs_3_), channel_id=1, source_target_pairs={{0,1},{1,0},{2,3},{3,2},{4,5},{5,4},{6,7},{7,6},{8,9},{9,8},{10,11... | collective-permute-start | bytes 589832 | tf_op jit(solution)/shard_map/ppermute | solution.py:385
  116.3 6.0 %collective-permute-start.20 = (bf16[16,6144]{1,0:T(8,128)(2,1)S(1)}, bf16[16,6144]{1,0:T(8,128)(2,1)S(1)}, u32[]{:S(2)}, u32[]{:S(2)}) collective-permute-start(bf16[16,6144]{1,0:T(8,128)(2,1)S(1)} %collective-permute-done.16.refs_2_), channel_id=1, source_target_pairs={{0,1},{1,0},{2,3},{3,2},{4,5},{5,4},{6,7},{7,6},{8,9},{9,8},{10,11... | collective-permute-start | bytes 589832 | tf_op jit(solution)/shard_map/ppermute | solution.py:385
  116.3 6.0 %collective-permute-start.19 = (bf16[16,6144]{1,0:T(8,128)(2,1)S(1)}, bf16[16,6144]{1,0:T(8,128)(2,1)S(1)}, u32[]{:S(2)}, u32[]{:S(2)}) collective-permute-start(bf16[16,6144]{1,0:T(8,128)(2,1)S(1)} %collective-permute-done.15.refs_1_), channel_id=1, source_target_pairs={{0,1},{1,0},{2,3},{3,2},{4,5},{5,4},{6,7},{7,6},{8,9},{9,8},{10,11... | collective-permute-start | bytes 589832 | tf_op jit(solution)/shard_map/ppermute | solution.py:385
  122.4 2.8 %copy-start.17 = (f32[8,128]{1,0:T(8,128)S(1)}, f32[8,128]{1,0:T(8,128)}, u32[]{:S(2)}) copy-start(f32[8,128]{1,0:T(8,128)} %get-tuple-element.33) | copy-start | bytes 12292
  122.4 4.4 %copy-start.16 = (f32[16,128]{1,0:T(8,128)S(1)}, f32[16,128]{1,0:T(8,128)}, u32[]{:S(2)}) copy-start(f32[16,128]{1,0:T(8,128)} %get-tuple-element.54) | copy-start | bytes 24580
  125.1 2.4 %collective-permute-start.22 = (bf16[64,6144]{1,0:T(8,128)(2,1)S(1)}, bf16[64,6144]{1,0:T(8,128)(2,1)S(1)}, u32[]{:S(2)}, u32[]{:S(2)}) collective-permute-start(bf16[64,6144]{1,0:T(8,128)(2,1)S(1)} %get-tuple-element.59), channel_id=1, source_target_pairs={{0,1},{1,0},{2,3},{3,2},{4,5},{5,4},{6,7},{7,6},{8,9},{9,8},{10,11... | collective-permute-start | bytes 2359304 | tf_op jit(solution)/shard_map/ppermute | solution.py:385
  125.2 7.9 %collective-permute-start = (f32[8,128]{1,0:T(8,128)S(1)}, f32[8,128]{1,0:T(8,128)S(1)}, u32[]{:S(2)}, u32[]{:S(2)}) collective-permute-start(f32[8,128]{1,0:T(8,128)S(1)} %copy-done.17), channel_id=1, source_target_pairs={{0,8},{8,16},{16,24},{24,0},{1,9},{9,17},{17,25},{25,1},{2,10},{10... | collective-permute-start | bytes 12296 | tf_op jit(solution)/shard_map/ppermute | solution.py:380
  127.7 7.0 %collective-permute-start.23 = (bf16[16,6144]{1,0:T(8,128)(2,1)S(1)}, bf16[16,6144]{1,0:T(8,128)(2,1)S(1)}, u32[]{:S(2)}, u32[]{:S(2)}) collective-permute-start(bf16[16,6144]{1,0:T(8,128)(2,1)S(1)} %get-tuple-element.88), channel_id=1, source_target_pairs={{0,6},{1,7},{2,0},{3,1},{4,2},{5,3},{6,4},{7,5},{8,14},{9,15},{10,... | collective-permute-start | bytes 589832 | tf_op jit(solution)/shard_map/ppermute | solution.py:502
  129.1 13.5 %collective-permute-start.25 = (bf16[16,6144]{1,0:T(8,128)(2,1)S(1)}, bf16[16,6144]{1,0:T(8,128)(2,1)S(1)}, u32[]{:S(2)}, u32[]{:S(2)}) collective-permute-start(bf16[16,6144]{1,0:T(8,128)(2,1)S(1)} %get-tuple-element.89), channel_id=1, source_target_pairs={{0,2},{1,3},{2,4},{3,5},{4,6},{5,7},{6,0},{7,1},{8,10},{9,11},{10,... | collective-permute-start | bytes 589832 | tf_op jit(solution)/shard_map/ppermute | solution.py:502
  129.8 19.4 %collective-permute-start.24 = (bf16[16,6144]{1,0:T(8,128)(2,1)S(1)}, bf16[16,6144]{1,0:T(8,128)(2,1)S(1)}, u32[]{:S(2)}, u32[]{:S(2)}) collective-permute-start(bf16[16,6144]{1,0:T(8,128)(2,1)S(1)} %get-tuple-element.90), channel_id=1, source_target_pairs={{0,4},{1,5},{2,6},{3,7},{4,0},{5,1},{6,2},{7,3},{8,12},{9,13},{10,... | collective-permute-start | bytes 589832 | tf_op jit(solution)/shard_map/ppermute | solution.py:502
  133.1 38.2 %collective-permute-start.27 = (bf16[128,6144]{1,0:T(8,128)(2,1)S(1)}, bf16[128,6144]{1,0:T(8,128)(2,1)S(1)}, u32[]{:S(2)}, u32[]{:S(2)}) collective-permute-start(bf16[128,6144]{1,0:T(8,128)(2,1)S(1)} %get-tuple-element.60), channel_id=1, source_target_pairs={{0,8},{8,16},{16,24},{24,0},{1,9},{9,17},{17,25},{25,1},{2,10},{10... | collective-permute-start | bytes 4718600 | tf_op jit(solution)/shard_map/ppermute | solution.py:380
  149.3 24.8 %collective-permute-start.26 = (bf16[16,6144]{1,0:T(8,128)(2,1)S(1)}, bf16[16,6144]{1,0:T(8,128)(2,1)S(1)}, u32[]{:S(2)}, u32[]{:S(2)}) collective-permute-start(bf16[16,6144]{1,0:T(8,128)(2,1)S(1)} %add_convert_fusion.1), channel_id=1, source_target_pairs={{0,8},{8,16},{16,24},{24,0},{1,9},{9,17},{17,25},{25,1},{2,10},{10... | collective-permute-start | bytes 589832 | tf_op jit(solution)/shard_map/ppermute | solution.py:380

commit v4 on v3

--- a/solution.py
+++ b/solution.py
@@ -48,11 +48,14 @@
 
 
 def state_kernel(
-    half_ref, rate_ref, k_hbm, v_hbm, state_hbm, decay_ref, k_ref, v_ref, state_ref, cum_ref, sems
+    half_ref, rate_hbm, k_hbm, v_hbm, state_hbm, decay_hbm,
+    rate_ref, k_ref, v_ref, state_ref, decay_ref, cum_ref, sems,
 ):
-    groups = sems.shape[1]
+    groups = k_ref.shape[0]
     length = rate_ref.shape[1]
     span = GROUP * HEAD
+    rates = pltpu.make_async_copy(rate_hbm, rate_ref, sems.at[3, 0])
+    rates.start()
 
     def fetch(kind, g):
         source, target = ((k_hbm, k_ref), (v_hbm, v_ref))[kind]
@@ -68,12 +71,11 @@
     for g in range(groups):
         for kind in range(2):
             fetch(kind, g).start()
-    eye = (
-        lax.broadcasted_iota(jnp.int32, (HEAD, HEAD), 0)
-        == lax.broadcasted_iota(jnp.int32, (HEAD, HEAD), 1)
-    ).astype(BF16)
+    rates.wait()
     cum_ref[...] = cumul_rows(rate_ref)
     decay_ref[...] = jnp.broadcast_to(jnp.exp(cum_ref[:, length - 1 :]), decay_ref.shape)
+    decays = pltpu.make_async_copy(decay_ref, decay_hbm, sems.at[3, 1])
+    decays.start()
     for g in range(groups):
         row = pl.multiple_of((half_ref[0] * groups + g) * GROUP, GROUP)
         cum = cum_ref[pl.ds(row, GROUP), :]
@@ -82,13 +84,14 @@
             fetch(kind, g).wait()
         for j in range(GROUP):
             cols = slice(j * HEAD, (j + 1) * HEAD)
-            turned = dot(eye, k_ref[g, :, cols], ((1,), (1,))) * tail[j : j + 1, :]
+            turned = k_ref[g, :, cols].T.astype(F32) * tail[j : j + 1, :]
             hi, lo = split(turned)
             v = v_ref[g, :, cols]
             state_ref[g * GROUP + j] = dot(hi, v) + dot(lo, v)
         store(g).start()
     for g in range(groups):
         store(g).wait()
+    decays.wait()
 
 
 def half_state(half, rate, keys, values):
@@ -97,18 +100,20 @@
     groups = heads // 2 // GROUP
     return pl.pallas_call(
         state_kernel,
-        in_specs=[SMEM_SPEC, VMEM_SPEC, HBM_SPEC, HBM_SPEC],
-        out_specs=[HBM_SPEC, VMEM_SPEC],
+        in_specs=[SMEM_SPEC, HBM_SPEC, HBM_SPEC, HBM_SPEC],
+        out_specs=[HBM_SPEC, HBM_SPEC],
         out_shape=[
             jax.ShapeDtypeStruct((heads // 2, HEAD, HEAD), F32),
             jax.ShapeDtypeStruct((heads, HEAD), F32),
         ],
         scratch_shapes=[
+            pltpu.VMEM((heads, length), F32),
             pltpu.VMEM((groups, length, GROUP * HEAD), BF16),
             pltpu.VMEM((groups, length, GROUP * HEAD), BF16),
             pltpu.VMEM((heads // 2, HEAD, HEAD), F32),
+            pltpu.VMEM((heads, HEAD), F32),
             pltpu.VMEM((heads, length), F32),
-            pltpu.SemaphoreType.DMA((3, groups)),
+            pltpu.SemaphoreType.DMA((4, max(groups, 2))),
         ],
         name="half_state",
     )(half, rate, keys, values)
@@ -168,7 +173,11 @@
     )(rate, queries, keys, values)
 
 
-def route_kernel(experts_ref, weight_ref, place_ref, wcol_ref, token_ref):
+def select_kernel(
+    parts, experts_ref, weight_ref, rate_ref, q_ref, resid_ref, *refs
+):
+    intra_refs = refs[:parts]
+    wcol_ref, token_ref, growth_ref, q_out, resid_out, intra_out, at_ref, at_smem, sem = refs[parts:]
     slots = wcol_ref.shape[0]
     length = experts_ref.shape[1]
     before = (
@@ -179,37 +188,129 @@
     taken = jnp.max(named.astype(F32), axis=0, keepdims=True)
     slot = dot(jnp.broadcast_to(taken, (8, length)).astype(BF16), before)[0:1, :]
     slot = jnp.where(taken > 0, slot, -1.0)
-    place_ref[...] = jnp.broadcast_to(slot, place_ref.shape)
     hot = lax.broadcasted_iota(jnp.int32, (slots, length), 0).astype(F32) == slot
     weight = jnp.sum(jnp.where(named, weight_ref[...], 0.0), axis=0, keepdims=True)
     weight = jnp.sum(jnp.where(hot, weight, 0.0), axis=1, keepdims=True)
     wcol_ref[...] = jnp.broadcast_to(weight, wcol_ref.shape)
-    at = lax.broadcasted_iota(jnp.int32, (slots, length), 1).astype(F32)
-    token = jnp.sum(jnp.where(hot, at, 0.0), axis=1, keepdims=True)
-    token_ref[...] = jnp.broadcast_to(token, token_ref.shape).astype(jnp.int32)
-
-
-def route(experts, weight):
-    length = experts.shape[1]
-    return pl.pallas_call(
-        route_kernel,
-        in_specs=[VMEM_SPEC] * 2,
-        out_specs=[VMEM_SPEC] * 3,
+    at = lax.broadcasted_iota(jnp.int32, (slots, length), 1).astype(F32) + 1.0
+    token = jnp.sum(jnp.where(hot, at, 0.0), axis=1, keepdims=True) - 1.0
+    token_ref[...] = jnp.broadcast_to(token, token_ref.shape)
+    at_ref[...] = jnp.broadcast_to(jnp.maximum(token, 0.0), at_ref.shape).astype(jnp.int32)
+    known = pltpu.make_async_copy(at_ref, at_smem, sem)
+    known.start()
+    growth_ref[...] = lax.dot_general(
+        hot.astype(F32), jnp.exp(cumul_rows(rate_ref)), (((1,), (1,)), ((), ())),
+        precision=lax.Precision.HIGHEST, preferred_element_type=F32,
+    )
+    hot = hot.astype(BF16)
+    q_out[...] = dot(hot, q_ref[...]).astype(BF16)
+    resid_out[...] = dot(hot, resid_ref[...])
+    known.wait()
+    for s in range(slots):
+        row = pl.ds(at_smem[s, 0], 1)
+        for part, ref in enumerate(intra_refs):
+            cols = slice(part * ref.shape[1], (part + 1) * ref.shape[1])
+            intra_out[s : s + 1, cols] = ref[row, :]
+
+
+def select(experts, weight, rate, queries, resid, intra):
+    _, width = queries.shape
+    heads = width // HEAD
+    parts = len(intra)
+    return pl.pallas_call(
+        lambda *refs: select_kernel(parts, *refs),
+        in_specs=[VMEM_SPEC] * (5 + parts),
+        out_specs=[VMEM_SPEC] * 6,
         out_shape=[
-            jax.ShapeDtypeStruct((8, length), F32),
             jax.ShapeDtypeStruct((CAP_SRC, 128), F32),
-            jax.ShapeDtypeStruct((CAP_SRC, 128), jnp.int32),
+            jax.ShapeDtypeStruct((CAP_SRC, 128), F32),
+            jax.ShapeDtypeStruct((CAP_SRC, heads), F32),
+            jax.ShapeDtypeStruct((CAP_SRC, width), BF16),
+            jax.ShapeDtypeStruct((CAP_SRC, width), F32),
+            jax.ShapeDtypeStruct((CAP_SRC, width), F32),
         ],
-        name="route",
-    )(experts, weight)
-
-
-def finish_kernel(parts, chunks, steps, core_ref, token_ref, rate_ref, q_hbm, *refs):
+        scratch_shapes=[
+            pltpu.VMEM((CAP_SRC, 128), jnp.int32),
+            pltpu.SMEM((CAP_SRC, 128), jnp.int32),
+            pltpu.SemaphoreType.DMA,
+        ],
+        name="select",
+    )(experts, weight, rate, queries, resid, *intra)
+
+
+def prefix_copies(core_ref, keeps, gots, state_ref, sems, chunks):
+    steps = len(keeps)
+    half = state_ref.shape[0] // 2
+    per = half // chunks
+
+    def states(n, c, late):
+        place = pl.multiple_of(lax.rem(core_ref[0] + n, 2) * half + c * per, per)
+        source = (keeps, gots)[n][c + late]
+        return pltpu.make_async_copy(source, state_ref.at[pl.ds(place, per)], sems.at[n, c])
+
+    for late in range(steps - chunks + 1):
+
+        @pl.when(core_ref[1] == late)
+        def _():
+            for c in range(chunks):
+                for n in range(2):
+                    states(n, c, late).start()
+
+    def wait(c):
+        for n in range(2):
+            states(n, c, 0).wait()
+
+    return wait
+
+
+def rows_kernel(chunks, steps, core_ref, growth_ref, q_ref, resid_ref, intra_ref, *refs):
+    keeps, gots, refs = refs[:steps], refs[steps : 2 * steps], refs[2 * steps :]
+    again_ref, mgain_ref, outbox_ref, picked_ref, state_ref, sems = refs
+    _, width = picked_ref.shape
+    heads = width // HEAD
+    half = heads // 2
+    per = half // chunks
+    wait = prefix_copies(core_ref, keeps, gots, state_ref, sems, chunks)
+    for c in range(chunks):
+        wait(c)
+        for head in [n * half + c * per + j for n in range(2) for j in range(per)]:
+            cols = slice(head * HEAD, (head + 1) * HEAD)
+            hi, lo = split(state_ref[head])
+            q = q_ref[:, cols]
+            value = growth_ref[:, head : head + 1] * (dot(q, hi) + dot(q, lo))
+            picked_ref[:, cols] = intra_ref[:, cols] + value
+    x = picked_ref[...]
+    scale = lax.rsqrt(jnp.mean(x * x, axis=-1, keepdims=True) + 1e-06)
+    hres = resid_ref[...] + x * scale * again_ref[...]
+    picked_ref[...] = hres
+    scale = lax.rsqrt(jnp.mean(hres * hres, axis=-1, keepdims=True) + 1e-06)
+    outbox_ref[...] = (hres * scale * mgain_ref[...]).astype(BF16)
+
+
+def selected_rows(core, growth, queries, resid, intra, keeps, gots, attn_gain, moe_gain):
+    slots, width = queries.shape
+    heads = width // HEAD
+    steps = len(keeps)
+    return pl.pallas_call(
+        lambda *refs: rows_kernel(CHUNKS, steps, *refs),
+        in_specs=[SMEM_SPEC] + [VMEM_SPEC] * 4 + [ANY_SPEC] * (2 * steps) + [VMEM_SPEC] * 2,
+        out_specs=[VMEM_SPEC] * 2,
+        out_shape=[pltpu.VMEM((slots, width), BF16), pltpu.VMEM((slots, width), F32)],
+        scratch_shapes=[
+            pltpu.VMEM((heads, HEAD, HEAD), F32),
+            pltpu.SemaphoreType.DMA((2, CHUNKS)),
+        ],
+        compiler_params=pltpu.CompilerParams(vmem_limit_bytes=16 << 20),
+        name="selected_rows",
+    )(core, growth, queries, resid, intra, *keeps, *gots, attn_gain, moe_gain)
+
+
+def finish_kernel(parts, chunks, steps, core_ref, rate_ref, q_hbm, *refs):
     intra_hbm, refs = refs[:parts], refs[parts:]
     keeps, gots, refs = refs[:steps], refs[steps : 2 * steps], refs[2 * steps :]
     (
-        resid_hbm, again_ref, mgain_ref, early_ref, outbox_ref, picked_ref,
-        attn_ref, q_ref, intra_ref, state_ref, resid_ref, scale_ref, sems,
+        resid_hbm, again_ref, early_ref,
+        attn_ref, q_ref, intra_ref, state_ref, resid_ref, scale_ref, sems, state_sems,
     ) = refs
     length, width = resid_ref.shape
     heads = width // HEAD
@@ -230,31 +331,15 @@
     for g in range(groups):
         for copy in copies(g):
             copy.start()
-    half = heads // 2
-    per = half // chunks
-
-    def states(n, c, late):
-        place = pl.multiple_of(lax.rem(core_ref[0] + n, 2) * half + c * per, per)
-        source = (keeps, gots)[n][c + late]
-        return pltpu.make_async_copy(source, state_ref.at[pl.ds(place, per)], sems.at[2 + n, c])
-
-    for late in range(steps - chunks + 1):
-
-        @pl.when(core_ref[1] == late)
-        def _():
-            for c in range(chunks):
-                for n in range(2):
-                    states(n, c, late).start()
-
-    rest = pltpu.make_async_copy(resid_hbm, resid_ref, sems.at[4, 0])
+    wait = prefix_copies(core_ref, keeps, gots, state_ref, state_sems, chunks)
+    rest = pltpu.make_async_copy(resid_hbm, resid_ref, sems.at[2, 0])
     rest.start()
     growth = jnp.exp(cumul_rows(rate_ref))
     for head in range(heads):
         across = jnp.broadcast_to(growth[head : head + 1, :], (length, length))
         scale_ref[:, head * HEAD : (head + 1) * HEAD] = across.T
     for c in range(chunks):
-        for n in range(2):
-            states(n, c, 0).wait()
+        wait(c)
     for g in range(groups):
         for copy in copies(g):
             copy.wait()
@@ -274,37 +359,26 @@
         x = attn_ref[at, :]
         scale = lax.rsqrt(jnp.mean(x * x, axis=-1, keepdims=True) + 1e-06)
         hres = resid_ref[at, :].astype(F32) + x * scale * again_ref[...]
-        attn_ref[at, :] = hres
         early_ref[at, :] = hres.astype(BF16)
         return carry
 
     lax.fori_loop(0, length // rows, norm, 0)
-    for s in range(picked_ref.shape[0]):
-        picked_ref[s : s + 1, :] = attn_ref[pl.ds(token_ref[s], 1), :]
-    x = picked_ref[...]
-    scale = lax.rsqrt(jnp.mean(x * x, axis=-1, keepdims=True) + 1e-06)
-    outbox_ref[...] = (x * scale * mgain_ref[...]).astype(BF16)
-
-
-def finish(core, token, rate, queries, intra, keeps, gots, resid, attn_gain, moe_gain):
+
+
+def finish(core, rate, queries, intra, keeps, gots, resid, attn_gain):
     length, width = queries.shape
     heads = width // HEAD
     groups = heads // GROUP
     parts, steps = len(intra), len(keeps)
-    args = [rate, queries, *intra, *keeps, *gots, resid, attn_gain, moe_gain]
+    args = [rate, queries, *intra, *keeps, *gots, resid, attn_gain]
     return pl.pallas_call(
         lambda *refs: finish_kernel(parts, CHUNKS, steps, *refs),
-        in_specs=[SMEM_SPEC, SMEM_SPEC, VMEM_SPEC]
+        in_specs=[SMEM_SPEC, VMEM_SPEC]
         + [HBM_SPEC] * (1 + parts)
         + [ANY_SPEC] * (2 * steps)
-        + [HBM_SPEC]
-        + [VMEM_SPEC] * 2,
-        out_specs=[VMEM_SPEC] * 3,
-        out_shape=[
-            pltpu.VMEM((length, width), BF16),
-            pltpu.VMEM((CAP_SRC, width), BF16),
-            pltpu.VMEM((CAP_SRC, width), F32),
-        ],
+        + [HBM_SPEC, VMEM_SPEC],
+        out_specs=VMEM_SPEC,
+        out_shape=pltpu.VMEM((length, width), BF16),
         scratch_shapes=[
             pltpu.VMEM((length, width), F32),
             pltpu.VMEM((groups, length, GROUP * HEAD), BF16),
@@ -312,11 +386,70 @@
             pltpu.VMEM((heads, HEAD, HEAD), F32),
             pltpu.VMEM((length, width), BF16),
             pltpu.VMEM((length, width), F32),
-            pltpu.SemaphoreType.DMA((5, max(groups, CHUNKS))),
+            pltpu.SemaphoreType.DMA((3, groups)),
+            pltpu.SemaphoreType.DMA((2, CHUNKS)),
         ],
         compiler_params=pltpu.CompilerParams(vmem_limit_bytes=32 << 20),
         name="finish",
-    )(core, token, *args)
+    )(core, *args)
+
+
+def late_kernel(count, picked_ref, wcol_ref, token_ref, *refs):
+    parts, out_ref = refs[:count], refs[count]
+    width = picked_ref.shape[1]
+    total = parts[0][...].astype(F32)
+    for part in parts[1:]:
+        total = total + part[...].astype(F32)
+    out_ref[:, :width] = (picked_ref[...] + wcol_ref[:, :1] * total).astype(BF16)
+    out_ref[:, width:] = token_ref[...].astype(BF16)
+
+
+def late_rows(picked, wcol, token, parts):
+    slots, width = picked.shape
+    return pl.pallas_call(
+        lambda *refs: late_kernel(len(parts), *refs),
+        in_specs=[VMEM_SPEC] * (3 + len(parts)),
+        out_specs=VMEM_SPEC,
+        out_shape=pltpu.VMEM((slots, width + 128), BF16),
+        compiler_params=pltpu.CompilerParams(vmem_limit_bytes=8 << 20),
+        name="late_rows",
+    )(in_vmem(picked), wcol, token, *[in_vmem(p) for p in parts])
+
+
+def merge_kernel(early_ref, late_ref, out_hbm, out_ref, sems):
+    length, width = early_ref.shape
+    slots = late_ref.shape[0]
+    parts = sems.shape[0]
+    span = width // parts
+    token = late_ref[:, width:].astype(F32)
+    found = token == lax.broadcasted_iota(jnp.int32, (slots, length), 1).astype(F32)
+    found = found.astype(BF16)
+    down = ((0,), (0,))
+    hit = dot(found, jnp.ones((slots, 128), BF16), down)[:, :1] > 0.5
+
+    def store(i):
+        at = pl.ds(i * span, span)
+        return pltpu.make_async_copy(out_ref.at[:, at], out_hbm.at[:, at], sems.at[i])
+
+    for i in range(parts):
+        at = slice(i * span, (i + 1) * span)
+        rows = dot(found, late_ref[:, at], down)
+        out_ref[:, at] = jnp.where(hit, rows, early_ref[:, at].astype(F32)).astype(BF16)
+        store(i).start()
+    for i in range(parts):
+        store(i).wait()
+
+
+def merged(early, late):
+    return pl.pallas_call(
+        merge_kernel,
+        in_specs=[VMEM_SPEC] * 2,
+        out_specs=HBM_SPEC,
+        out_shape=jax.ShapeDtypeStruct(early.shape, BF16),
+        scratch_shapes=[pltpu.VMEM(early.shape, BF16), pltpu.SemaphoreType.DMA((4,))],
+        compiler_params=pltpu.CompilerParams(vmem_limit_bytes=8 << 20),
+        name="merged",
+    )(in_vmem(early), in_vmem(late))
 
 
 def fetch_kernel(up_hbm, down_hbm, up_ref, down_ref, sems):
@@ -388,7 +521,7 @@
 def chain_prefix(mine, partner, decay, decay_partner, chip, chips, first, scale):
     heads = mine.shape[0]
     per = heads // CHUNKS
-    keeps, gots, before = [], [], None
+    keeps, gives, before = [], [], None
 
     def chunk(index):
         place = jnp.clip(index, 0, CHUNKS - 1) * per
@@ -411,18 +544,16 @@
             if 0 <= step - z < CHUNKS
             for core in range(2)
         ]
-        before = lax.ppermute(gone.astype(jnp.float16), "ctx", pairs)
-        if step > 0:
-            before, keep, give = lax.optimization_barrier((before, keep, give))
-            keeps.append(keep)
-            gots.append(swapped(give))
+        gone = gone.astype(jnp.float16)
+        if step >= 2:
+            gone, keeps[-1], gives[-1] = lax.optimization_barrier((gone, keeps[-1], gives[-1]))
+        before = lax.ppermute(gone, "ctx", pairs)
         state0, _, decay0, _ = chunk(step - jnp.maximum(chip - 1, 0))
         prefix = lax.optimization_barrier(before).astype(F32) * (1.0 / scale)
         after0 = decay0 * prefix + state0
-        keep, give = jnp.where(first, prefix, after0), jnp.where(first, after0, prefix)
-    keeps.append(keep)
-    gots.append(swapped(give))
-    return keeps, gots
+        keeps.append(jnp.where(first, prefix, after0))
+        gives.append(jnp.where(first, after0, prefix))
+    return keeps, [swapped(give) for give in gives]
 
 
 def local(
@@ -481,33 +612,30 @@
             flying, rate, queries, jnp.concatenate(intra, axis=1), prefix, resid,
             attn_gain, moe_gain, experts, weight, up, down,
         )
-    place, wcol, token = route(experts.T, weight.T)
-    early, outbox, picked = finish(
-        jnp.stack([core, late_by]).astype(jnp.int32), token[:, 0], turned, queries, intra,
-        keeps, gots, resid, attn_gain, moe_gain,
-    )
-    early = passed_along(early, "section", 1)
-    place = passed_along(place, "section", 1)
+    where = jnp.stack([core, late_by]).astype(jnp.int32)
+    wcol, token, growth, q_rows, resid_rows, intra_rows = select(
+        experts.T, weight.T, turned, queries, resid, intra
+    )
+    outbox, picked = selected_rows(
+        where, growth, q_rows, resid_rows, intra_rows, keeps, gots, attn_gain, moe_gain
+    )
     own = [outbox] + [
         lax.ppermute(outbox, "ctx", [(i, (i + 2 * d) % count) for i in range(count)])
         for d in range(1, chips)
     ]
+    early = finish(where, turned, queries, intra, keeps, gots, resid, attn_gain)
+    early = passed_along(early, "section", 1)
+    up, down = fetch(up, down)
     others = [swapped(r) for r in own]
-    up, down = fetch(up, down)
     mine, other = expert_rows(own + others, up, down)
     pair = (mine.astype(F32) + swapped(other).astype(F32)).astype(BF16)
     pair = pair.reshape(chips, CAP_SRC, width)
-    summed = pair[0].astype(F32)
-    for d in range(1, chips):
-        back = lax.ppermute(pair[d], "ctx", [(i, (i - 2 * d) % count) for i in range(count)])
-        summed = summed + back.astype(F32)
-    late = (picked + wcol[:, :1] * summed).astype(BF16)
-    late = passed_along(late, "section", 1)
-    found = (place[:1] == jnp.arange(CAP_SRC, dtype=F32)[:, None]).astype(BF16)
-    rows = lax.dot_general(
-        found, late, (((0,), (0,)), ((), ())), preferred_element_type=F32
-    ).astype(BF16)
-    return jnp.where(place[0][:, None] >= 0, rows, early)[None]
+    backs = [
+        lax.ppermute(pair[d], "ctx", [(i, (i - 2 * d) % count) for i in range(count)])
+        for d in range(1, chips)
+    ]
+    late = passed_along(late_rows(picked, wcol, token, [pair[0], *backs]), "section", 1)
+    return merged(early, late)[None]
 
 
 def rms_scale(values_in, gain):

time: 177 us -> 168 us (0.949)
  waiting for transfers between devices: 67.8 us -> 61.4 us
  local copies, waits for them, and re-layouts: 10.6 us -> 5.2 us
  Pallas kernels: 39.6 us -> 43.9 us
  matrix products: 1.77 us -> 0 us
    unnamed x36, local copies, waits for them, and re-layouts: 9.66 us -> 5.14 us
    pallas_call x3 -> x6, Pallas kernels: 11.7 us -> 16.2 us  [the longest x2 6 us: half_state(): pl.pallas_call(state_kernel, in_specs=[SMEM_SPEC, HBM_SPEC, HBM_SPEC, HBM...]
    ppermute x3, waiting for transfers between devices: 14.5 us -> 10.8 us  [layer(): lax.ppermute(pair[d], 'ctx', [(i, (i - 2 * d) % count) for i in range(cou...]
    ppermute x3 -> x2, waiting for transfers between devices: 23.3 us -> 21 us  [passed_along(): return lax.ppermute(value, axis, pairs)]
    dot_general x1 -> x0, matrix products: 1.77 us -> none  [layer(): lax.dot_general(found, late, (((0,), (0,)), ((), ())), preferred_element_...]
    ppermute x3 -> x2, starting transfers between devices: 4.62 us -> 3.08 us  [passed_along(): return lax.ppermute(value, axis, pairs)]
    select_n x6 -> x5, other arithmetic: 6.57 us -> 5.36 us  [chain_prefix(): gives.append(jnp.where(first, after0, prefix))]
  transfers between devices with their start and end apart: 28 -> 27, of which waited for: 11 -> 11; matrix products, arithmetic and copies ran while one was open for 1% -> 2% of each run, Pallas kernels for 14% -> 20%
where the time goes in v4:
time: 168 us; the launch traced here: 167 us
  waiting for transfers between devices  61.4 us (37%)
  starting transfers between devices  47 us (28%)
  Pallas kernels  43.9 us (26%)
  other arithmetic  8.5 us (5%)
  local copies, waits for them, and re-layouts  5.2 us (3%)
    ppermute x2, waiting for transfers between devices, passed_along(): return lax.ppermute(value, axis, pairs)  21 us
    ppermute x6, starting transfers between devices, chain_prefix(): before = lax.ppermute(gone, 'ctx', pairs)  19.4 us
    ppermute x3, waiting for transfers between devices, layer(): lax.ppermute(outbox, 'ctx', [(i, (i + 2 * d) % count) for i in range(coun...  15.3 us
    ppermute x3, starting transfers between devices, layer(): lax.ppermute(outbox, 'ctx', [(i, (i + 2 * d) % count) for i in range(coun...  15 us
    ppermute x6, waiting for transfers between devices, chain_prefix(): before = lax.ppermute(gone, 'ctx', pairs)  14.2 us
    pallas_call x3, Pallas kernels, intra_attention(): pl.pallas_call(lambda *refs: intra_kernel(part * groups, *refs), in_specs...  12 us
    ppermute x3, waiting for transfers between devices, layer(): lax.ppermute(pair[d], 'ctx', [(i, (i - 2 * d) % count) for i in range(cou...  10.8 us
    pallas_call x1, Pallas kernels, finish(): pl.pallas_call(lambda *refs: finish_kernel(parts, CHUNKS, steps, *refs),...  7.35 us
  transfers between devices with their start and end apart: 27, of which 11 were waited for; matrix products, arithmetic and copies ran while one was open for 2% of the time, Pallas kernels for 20%

profile of v4, /device:TPU:0, one launch (start us, length us, event | category | flops | bytes accessed | tf_op | source)
XLA Modules:
  0.0 166.6 jit_solution(10336481662379861329)
XLA Ops:
  0.0 3.0 %half_state.2 = (f32[24,128,128]{2,1,0:T(8,128)}, f32[48,128]{1,0:T(8,128)}) custom-call(s32[1]{0:T(128)S(6)} %sub.54.half_ref, f32[48,128]{1,0:T(8,128)} %bitcast.25, bf16[128,6144]{1,0:T(8,128)(2,1)} %bitcast.32, bf16[128,6144]{1,0:T(8,128)(2,1)} %bitcast.37), custom_call_target="tpu_custom_call" | custom-call | tf_op jit(solution)/shard_map/half_state/pallas_call | solution.py:101
  3.0 0.6 collective-permute-start.1
  3.6 3.0 %half_state.3 = (f32[24,128,128]{2,1,0:T(8,128)}, f32[48,128]{1,0:T(8,128)}) custom-call(s32[1]{0:T(128)} %bitcast.half_ref, f32[48,128]{1,0:T(8,128)} %bitcast.26, bf16[128,6144]{1,0:T(8,128)(2,1)} %bitcast.33, bf16[128,6144]{1,0:T(8,128)(2,1)} %bitcast.38), custom_call_target="tpu_custom_call" | custom-call | tf_op jit(solution)/shard_map/half_state/pallas_call | solution.py:101
  6.9 1.7 %add_convert_fusion.6 = f16[6,128,128]{2,1,0:T(8,128)(2,1)S(1)} fusion(f32[24,128,128]{2,1,0:T(8,128)S(1)} %collective-permute-done.1, s32[]{:T(128)S(6)} %select_n.313, f32[24,128,128]{2,1,0:T(8,128)} %get-tuple-element.33, f32[6,128]{1,0:T(8,128)S(1)} %get-tuple-element.107, pred[]{:T(512)S(6)} %eq.5), kind=kLoop, calls=%fused_computation.36 | loop fusion | flops 491520 | bytes 986117 | tf_op jit(solution)/shard_map/convert_element_type | solution.py:547
  8.6 4.9 %collective-permute-start.2 = (f16[6,128,128]{2,1,0:T(8,128)(2,1)S(1)}, f16[6,128,128]{2,1,0:T(8,128)(2,1)S(1)}, u32[]{:S(2)}, u32[]{:S(2)}) collective-permute-start(f16[6,128,128]{2,1,0:T(8,128)(2,1)S(1)} %add_convert_fusion.6), channel_id=1, source_target_pairs={{0,2},{1,3},{8,10},{9,11},{16,18},{17,19},{24,26},{25,27}} | collective-permute-start | bytes 589832 | tf_op jit(solution)/shard_map/ppermute | solution.py:550
  13.5 4.4 %collective-permute-done.2 = f16[6,128,128]{2,1,0:T(8,128)(2,1)S(1)} collective-permute-done((f16[6,128,128]{2,1,0:T(8,128)(2,1)S(1)}, f16[6,128,128]{2,1,0:T(8,128)(2,1)S(1)}, u32[]{:S(2)}, u32[]{:S(2)}) %collective-permute-start.2) | collective-permute-done | bytes 196640 | tf_op jit(solution)/shard_map/ppermute | solution.py:550
  17.9 1.1 add_convert_fusion.5
  19.1 4.4 %collective-permute-start.3 = (f16[6,128,128]{2,1,0:T(8,128)(2,1)S(1)}, f16[6,128,128]{2,1,0:T(8,128)(2,1)S(1)}, u32[]{:S(2)}, u32[]{:S(2)}) collective-permute-start(f16[6,128,128]{2,1,0:T(8,128)(2,1)S(1)} %add_convert_fusion.5), channel_id=1, source_target_pairs={{0,2},{1,3},{2,4},{3,5},{8,10},{9,11},{10,12},{11,13},{16,18},{17,... | collective-permute-start | bytes 589832 | tf_op jit(solution)/shard_map/ppermute | solution.py:550
  23.5 3.5 %collective-permute-done.3 = f16[6,128,128]{2,1,0:T(8,128)(2,1)S(1)} collective-permute-done((f16[6,128,128]{2,1,0:T(8,128)(2,1)S(1)}, f16[6,128,128]{2,1,0:T(8,128)(2,1)S(1)}, u32[]{:S(2)}, u32[]{:S(2)}) %collective-permute-start.3) | collective-permute-done | bytes 196640 | tf_op jit(solution)/shard_map/ppermute | solution.py:550
  27.2 4.4 %collective-permute-start.4 = (f16[6,128,128]{2,1,0:T(8,128)(2,1)S(1)}, f16[6,128,128]{2,1,0:T(8,128)(2,1)S(1)}, u32[]{:S(2)}, u32[]{:S(2)}) collective-permute-start(f16[6,128,128]{2,1,0:T(8,128)(2,1)S(1)} %get-tuple-element.36), channel_id=1, source_target_pairs={{0,2},{1,3},{2,4},{3,5},{4,6},{5,7},{8,10},{9,11},{10,12},{11,13},... | collective-permute-start | bytes 589832 | tf_op jit(solution)/shard_map/ppermute | solution.py:550
  31.6 3.2 %collective-permute-done.4 = f16[6,128,128]{2,1,0:T(8,128)(2,1)S(1)} collective-permute-done((f16[6,128,128]{2,1,0:T(8,128)(2,1)S(1)}, f16[6,128,128]{2,1,0:T(8,128)(2,1)S(1)}, u32[]{:S(2)}, u32[]{:S(2)}) %collective-permute-start.4) | collective-permute-done | bytes 196640 | tf_op jit(solution)/shard_map/ppermute | solution.py:550
  34.8 1.0 convert_select_fusion.6
  35.7 4.4 %collective-permute-start.5 = (f16[6,128,128]{2,1,0:T(8,128)(2,1)S(1)}, f16[6,128,128]{2,1,0:T(8,128)(2,1)S(1)}, u32[]{:S(2)}, u32[]{:S(2)}) collective-permute-start(f16[6,128,128]{2,1,0:T(8,128)(2,1)S(1)} %get-tuple-element.38), channel_id=1, source_target_pairs={{0,2},{1,3},{2,4},{3,5},{4,6},{5,7},{8,10},{9,11},{10,12},{11,13},... | collective-permute-start | bytes 589832 | tf_op jit(solution)/shard_map/ppermute | solution.py:550
  40.1 3.2 %collective-permute-done.5 = f16[6,128,128]{2,1,0:T(8,128)(2,1)S(1)} collective-permute-done((f16[6,128,128]{2,1,0:T(8,128)(2,1)S(1)}, f16[6,128,128]{2,1,0:T(8,128)(2,1)S(1)}, u32[]{:S(2)}, u32[]{:S(2)}) %collective-permute-start.5) | collective-permute-done | bytes 196640 | tf_op jit(solution)/shard_map/ppermute | solution.py:550
  43.3 1.0 convert_select_fusion.4
  44.2 0.7 collective-permute-start.6
  44.9 1.0 convert_select_fusion.2
  45.9 0.7 collective-permute-start.7
  47.6 2.3 %convert_select_fusion = (f32[6,128,128]{2,1,0:T(8,128)}, f32[6,128,128]{2,1,0:T(8,128)S(1)}, f32[6,128,128]{2,1,0:T(8,128)S(1)}, f32[6,128,128]{2,1,0:T(8,128)}) fusion(f16[6,128,128]{2,1,0:T(8,128)(2,1)S(1)} %collective-permute-done.7, f32[6,128]{1,0:T(8,128)S(1)} %get-tuple-element.91, pred[]{:T(512)S(6)} %eq.5, f32[24,128,128]{2,1,0:T(8,128)} %copy-done.15, ...), kind=kLoop, calls=%fused_computation.1 | loop fusion | flops 1179648 | bytes 3545097 | tf_op jit(solution)/shard_map/jit(_where)/select_n | solution.py:555
  50.4 4.0 %intra_attention.5.refs_5_.refs_7_ = f32[128,2048]{1,0:T(8,128)} custom-call(f32[48,128]{1,0:T(8,128)} %bitcast.27, bf16[128,6144]{1,0:T(8,128)(2,1)} %bitcast.18, bf16[128,6144]{1,0:T(8,128)(2,1)} %bitcast.34, bf16[128,6144]{1,0:T(8,128)(2,1)} %bitcast.39), custom_call_target="tpu_custom_call" | custom-call | tf_op jit(solution)/shard_map/intra_attention/pallas_call | solution.py:165
  54.4 4.0 %intra_attention.4.refs_4_.refs_6_ = f32[128,2048]{1,0:T(8,128)} custom-call(f32[48,128]{1,0:T(8,128)} %bitcast.28, bf16[128,6144]{1,0:T(8,128)(2,1)} %bitcast.19, bf16[128,6144]{1,0:T(8,128)(2,1)} %bitcast.35, bf16[128,6144]{1,0:T(8,128)(2,1)} %bitcast.40), custom_call_target="tpu_custom_call" | custom-call | tf_op jit(solution)/shard_map/intra_attention/pallas_call | solution.py:165
  58.5 4.0 %intra_attention.3.refs_3_.refs_5_ = f32[128,2048]{1,0:T(8,128)} custom-call(f32[48,128]{1,0:T(8,128)} %bitcast.29, bf16[128,6144]{1,0:T(8,128)(2,1)} %bitcast.20, bf16[128,6144]{1,0:T(8,128)(2,1)} %bitcast.36, bf16[128,6144]{1,0:T(8,128)(2,1)} %bitcast.41), custom_call_target="tpu_custom_call" | custom-call | tf_op jit(solution)/shard_map/intra_attention/pallas_call | solution.py:165
  62.5 4.9 %select.7 = (f32[16,128]{1,0:T(8,128)}, f32[16,128]{1,0:T(8,128)}, f32[16,48]{1,0:T(8,128)}, bf16[16,6144]{1,0:T(8,128)(2,1)}, f32[16,6144]{1,0:T(8,128)}, /*index=5*/f32[16,6144]{1,0:T(8,128)}) custom-call(s32[2,128]{1,0:T(2,128)} %bitcast.44, f32[2,128]{1,0:T(2,128)} %bitcast.45, f32[48,128]{1,0:T(8,128)} %bitcast.30, bf16[128,6144]{1,0:T(8,128)(2,1)} %bitcast.21, ...), custom_call_target="tpu_custom_call" | custom-call | tf_op jit(solution)/shard_map/select/pallas_call | solution.py:220
  67.5 1.0 copy-done.6
  68.5 1.0 copy-done.7
  69.5 0.9 copy-done.8
  70.4 0.7 copy-done.9
  71.1 0.7 copy-done.11
  71.9 0.7 copy-done.14
  72.6 3.6 %selected_rows.1 = (bf16[16,6144]{1,0:T(8,128)(2,1)S(1)}, f32[16,6144]{1,0:T(8,128)S(1)}) custom-call(s32[2]{0:T(128)S(1)} %pad_add_fusion.refs_0_, f32[16,48]{1,0:T(8,128)S(1)} %copy-done.14, bf16[16,6144]{1,0:T(8,128)(2,1)S(1)} %copy-done.8, f32[16,6144]{1,0:T(8,128)S(1)} %copy-done.6, f32[16,6144]{1,0:T(8,128)S(1)} %copy-done.7, ...), custom_call_target="tpu_custom_call" | custom-call | tf_op jit(solution)/shard_map/selected_rows/pallas_call | solution.py:294
  76.2 14.4 %collective-permute-start.17 = (bf16[16,6144]{1,0:T(8,128)(2,1)S(1)}, bf16[16,6144]{1,0:T(8,128)(2,1)S(1)}, u32[]{:S(2)}, u32[]{:S(2)}) collective-permute-start(bf16[16,6144]{1,0:T(8,128)(2,1)S(1)} %get-tuple-element.54.refs_0_), channel_id=1, source_target_pairs={{0,6},{1,7},{2,0},{3,1},{4,2},{5,3},{6,4},{7,5},{8,14},{9,15},{10,... | collective-permute-start | bytes 589832 | tf_op jit(solution)/shard_map/ppermute | solution.py:623
  90.6 0.6 collective-permute-start.15
  91.2 4.7 %collective-permute-done.17.refs_3_ = bf16[16,6144]{1,0:T(8,128)(2,1)S(1)} collective-permute-done((bf16[16,6144]{1,0:T(8,128)(2,1)S(1)}, bf16[16,6144]{1,0:T(8,128)(2,1)S(1)}, u32[]{:S(2)}, u32[]{:S(2)}) %collective-permute-start.17) | collective-permute-done | bytes 196640 | tf_op jit(solution)/shard_map/ppermute | solution.py:623
  96.0 10.5 %collective-permute-done.16.refs_2_ = bf16[16,6144]{1,0:T(8,128)(2,1)S(1)} collective-permute-done((bf16[16,6144]{1,0:T(8,128)(2,1)S(1)}, bf16[16,6144]{1,0:T(8,128)(2,1)S(1)}, u32[]{:S(2)}, u32[]{:S(2)}) %collective-permute-start.16) | collective-permute-done | bytes 196640 | tf_op jit(solution)/shard_map/ppermute | solution.py:623
  106.5 0.5 collective-permute-start.19
  107.0 5.5 %fetch.1 = (bf16[6144,640]{1,0:T(8,128)(2,1)S(1)}, bf16[640,6144]{1,0:T(8,128)(2,1)S(1)}) custom-call(bf16[6144,640]{1,0:T(8,128)(2,1)} %bitcast.42, bf16[640,6144]{1,0:T(8,128)(2,1)} %bitcast.43), custom_call_target="tpu_custom_call" | custom-call | tf_op jit(solution)/shard_map/fetch/pallas_call | solution.py:467
  112.6 2.8 %expert_rows.1 = (bf16[64,6144]{1,0:T(8,128)(2,1)S(1)}, bf16[64,6144]{1,0:T(8,128)(2,1)S(1)}) custom-call(bf16[16,6144]{1,0:T(8,128)(2,1)S(1)} %get-tuple-element.54.refs_0_, bf16[16,6144]{1,0:T(8,128)(2,1)S(1)} %collective-permute-done.15.refs_1_, bf16[16,6144]{1,0:T(8,128)(2,1)S(1)} %collective-permute-done.16.refs_2_, ...), custom_call_target="tpu_custom_call" | custom-call | tf_op jit(solution)/shard_map/expert_rows/pallas_call | solution.py:499
  115.6 7.3 %finish.1 = bf16[128,6144]{1,0:T(8,128)(2,1)S(1)} custom-call(s32[2]{0:T(128)S(1)} %pad_add_fusion.refs_0_, f32[48,128]{1,0:T(8,128)S(1)} %bitcast.31, bf16[128,6144]{1,0:T(8,128)(2,1)S(1)} %bitcast.22, f32[128,2048]{1,0:T(8,128)S(1)} %copy-done.3, f32[128,2048]{1,0:T(8,128)S(1)} %copy-done.2, f32[128,2048]{1,0:T(8,128)S(1)} %copy-done.1, ...), custom_call_target="tpu_custom_call" | custom-call | tf_op jit(solution)/shard_map/finish/pallas_call | solution.py:374
  123.0 1.5 collective-permute-start.14
  124.8 1.8 %collective-permute-start.25 = (bf16[16,6144]{1,0:T(8,128)(2,1)S(1)}, bf16[16,6144]{1,0:T(8,128)(2,1)S(1)}, u32[]{:S(2)}, u32[]{:S(2)}) collective-permute-start(bf16[16,6144]{1,0:T(8,128)(2,1)S(1)} %get-tuple-element.87), channel_id=1, source_target_pairs={{0,2},{1,3},{2,4},{3,5},{4,6},{5,7},{6,0},{7,1},{8,10},{9,11},{10,... | collective-permute-start | bytes 589832 | tf_op jit(solution)/shard_map/ppermute | solution.py:634
  126.6 2.0 %collective-permute-start.24 = (bf16[16,6144]{1,0:T(8,128)(2,1)S(1)}, bf16[16,6144]{1,0:T(8,128)(2,1)S(1)}, u32[]{:S(2)}, u32[]{:S(2)}) collective-permute-start(bf16[16,6144]{1,0:T(8,128)(2,1)S(1)} %get-tuple-element.88), channel_id=1, source_target_pairs={{0,4},{1,5},{2,6},{3,7},{4,0},{5,1},{6,2},{7,3},{8,12},{9,13},{10,... | collective-permute-start | bytes 589832 | tf_op jit(solution)/shard_map/ppermute | solution.py:634
  128.6 2.8 %collective-permute-start.23 = (bf16[16,6144]{1,0:T(8,128)(2,1)S(1)}, bf16[16,6144]{1,0:T(8,128)(2,1)S(1)}, u32[]{:S(2)}, u32[]{:S(2)}) collective-permute-start(bf16[16,6144]{1,0:T(8,128)(2,1)S(1)} %get-tuple-element.89), channel_id=1, source_target_pairs={{0,6},{1,7},{2,0},{3,1},{4,2},{5,3},{6,4},{7,5},{8,14},{9,15},{10,... | collective-permute-start | bytes 589832 | tf_op jit(solution)/shard_map/ppermute | solution.py:634
  131.4 3.1 %collective-permute-done.25.refs_6_ = bf16[16,6144]{1,0:T(8,128)(2,1)S(1)} collective-permute-done((bf16[16,6144]{1,0:T(8,128)(2,1)S(1)}, bf16[16,6144]{1,0:T(8,128)(2,1)S(1)}, u32[]{:S(2)}, u32[]{:S(2)}) %collective-permute-start.25) | collective-permute-done | bytes 196640 | tf_op jit(solution)/shard_map/ppermute | solution.py:634
  134.5 7.6 %collective-permute-done.24.refs_5_ = bf16[16,6144]{1,0:T(8,128)(2,1)S(1)} collective-permute-done((bf16[16,6144]{1,0:T(8,128)(2,1)S(1)}, bf16[16,6144]{1,0:T(8,128)(2,1)S(1)}, u32[]{:S(2)}, u32[]{:S(2)}) %collective-permute-start.24) | collective-permute-done | bytes 196640 | tf_op jit(solution)/shard_map/ppermute | solution.py:634
  142.4 1.6 collective-permute-start.26
  143.9 17.2 %collective-permute-done.14.early_ref = bf16[128,6144]{1,0:T(8,128)(2,1)S(1)} collective-permute-done((bf16[128,6144]{1,0:T(8,128)(2,1)S(1)}, bf16[128,6144]{1,0:T(8,128)(2,1)S(1)}, u32[]{:S(2)}, u32[]{:S(2)}) %collective-permute-start.14) | collective-permute-done | bytes 1572896 | tf_op jit(solution)/shard_map/ppermute | solution.py:513
  161.2 3.8 %collective-permute-done.26.late_ref = bf16[16,6272]{1,0:T(8,128)(2,1)S(1)} collective-permute-done((bf16[16,6272]{1,0:T(8,128)(2,1)S(1)}, bf16[16,6272]{1,0:T(8,128)(2,1)S(1)}, u32[]{:S(2)}, u32[]{:S(2)}) %collective-permute-start.26) | collective-permute-done | bytes 200736 | tf_op jit(solution)/shard_map/ppermute | solution.py:513
  165.0 1.5 merged.1
  (65 shorter events, 2.7 us)
Async XLA Ops:
  3.0 3.9 %collective-permute-start.1 = (f32[24,128,128]{2,1,0:T(8,128)}, f32[24,128,128]{2,1,0:T(8,128)S(1)}, u32[]{:S(2)}, u32[]{:S(2)}) collective-permute-start(f32[24,128,128]{2,1,0:T(8,128)} %get-tuple-element.34), channel_id=1, source_target_pairs={{0,1},{1,0},{2,3},{3,2},{4,5},{5,4},{6,7},{7,6},{8,9},{9,8},{10,11... | collective-permute-start | bytes 4718600 | tf_op jit(solution)/shard_map/ppermute | solution.py:518
  3.6 3.3 %collective-permute-start = (f32[48,128]{1,0:T(8,128)}, f32[48,128]{1,0:T(8,128)S(1)}, u32[]{:S(2)}, u32[]{:S(2)}) collective-permute-start(f32[48,128]{1,0:T(8,128)} %get-tuple-element.32), channel_id=1, source_target_pairs={{0,1},{1,0},{2,3},{3,2},{4,5},{5,4},{6,7},{7,6},{8,9},{9,8},{10,11... | collective-permute-start | bytes 73736 | tf_op jit(solution)/shard_map/ppermute | solution.py:518
  3.6 3.2 %copy-start.17 = (f32[48,128]{1,0:T(8,128)S(1)}, f32[48,128]{1,0:T(8,128)}, u32[]{:S(2)}) copy-start(f32[48,128]{1,0:T(8,128)} %get-tuple-element.32) | copy-start | bytes 73732
  6.8 20.2 %copy-start.16 = (f32[24,128,128]{2,1,0:T(8,128)S(1)}, f32[24,128,128]{2,1,0:T(8,128)}, u32[]{:S(2)}) copy-start(f32[24,128,128]{2,1,0:T(8,128)} %get-tuple-element.33) | copy-start | bytes 4718596
  6.9 38.0 %copy-start.15 = (f32[24,128,128]{2,1,0:T(8,128)}, f32[24,128,128]{2,1,0:T(8,128)S(1)}, u32[]{:S(2)}) copy-start(f32[24,128,128]{2,1,0:T(8,128)S(1)} %collective-permute-done.1) | copy-start | bytes 4718596
  8.6 9.3 %collective-permute-start.2 = (f16[6,128,128]{2,1,0:T(8,128)(2,1)S(1)}, f16[6,128,128]{2,1,0:T(8,128)(2,1)S(1)}, u32[]{:S(2)}, u32[]{:S(2)}) collective-permute-start(f16[6,128,128]{2,1,0:T(8,128)(2,1)S(1)} %add_convert_fusion.6), channel_id=1, source_target_pairs={{0,2},{1,3},{8,10},{9,11},{16,18},{17,19},{24,26},{25,27}} | collective-permute-start | bytes 589832 | tf_op jit(solution)/shard_map/ppermute | solution.py:550
  19.1 7.9 %collective-permute-start.3 = (f16[6,128,128]{2,1,0:T(8,128)(2,1)S(1)}, f16[6,128,128]{2,1,0:T(8,128)(2,1)S(1)}, u32[]{:S(2)}, u32[]{:S(2)}) collective-permute-start(f16[6,128,128]{2,1,0:T(8,128)(2,1)S(1)} %add_convert_fusion.5), channel_id=1, source_target_pairs={{0,2},{1,3},{2,4},{3,5},{8,10},{9,11},{10,12},{11,13},{16,18},{17,... | collective-permute-start | bytes 589832 | tf_op jit(solution)/shard_map/ppermute | solution.py:550
  27.2 7.6 %collective-permute-start.4 = (f16[6,128,128]{2,1,0:T(8,128)(2,1)S(1)}, f16[6,128,128]{2,1,0:T(8,128)(2,1)S(1)}, u32[]{:S(2)}, u32[]{:S(2)}) collective-permute-start(f16[6,128,128]{2,1,0:T(8,128)(2,1)S(1)} %get-tuple-element.36), channel_id=1, source_target_pairs={{0,2},{1,3},{2,4},{3,5},{4,6},{5,7},{8,10},{9,11},{10,12},{11,13},... | collective-permute-start | bytes 589832 | tf_op jit(solution)/shard_map/ppermute | solution.py:550
  35.7 7.6 %collective-permute-start.5 = (f16[6,128,128]{2,1,0:T(8,128)(2,1)S(1)}, f16[6,128,128]{2,1,0:T(8,128)(2,1)S(1)}, u32[]{:S(2)}, u32[]{:S(2)}) collective-permute-start(f16[6,128,128]{2,1,0:T(8,128)(2,1)S(1)} %get-tuple-element.38), channel_id=1, source_target_pairs={{0,2},{1,3},{2,4},{3,5},{4,6},{5,7},{8,10},{9,11},{10,12},{11,13},... | collective-permute-start | bytes 589832 | tf_op jit(solution)/shard_map/ppermute | solution.py:550
  44.2 0.7 collective-permute-start.6
  45.9 1.8 %collective-permute-start.7 = (f16[6,128,128]{2,1,0:T(8,128)(2,1)S(1)}, f16[6,128,128]{2,1,0:T(8,128)(2,1)S(1)}, u32[]{:S(2)}, u32[]{:S(2)}) collective-permute-start(f16[6,128,128]{2,1,0:T(8,128)(2,1)S(1)} %get-tuple-element.42), channel_id=1, source_target_pairs={{4,6},{5,7},{12,14},{13,15},{20,22},{21,23},{28,30},{29,31}} | collective-permute-start | bytes 589832 | tf_op jit(solution)/shard_map/ppermute | solution.py:550
  46.5 3.4 %collective-permute-start.9 = (f32[6,128,128]{2,1,0:T(8,128)S(1)}, f32[6,128,128]{2,1,0:T(8,128)S(1)}, u32[]{:S(2)}, u32[]{:S(2)}) collective-permute-start(f32[6,128,128]{2,1,0:T(8,128)S(1)} %get-tuple-element.43), channel_id=1, source_target_pairs={{0,1},{1,0},{2,3},{3,2},{4,5},{5,4},{6,7},{7,6},{8,9},{9,8},{10,11... | collective-permute-start | bytes 1179656 | tf_op jit(solution)/shard_map/ppermute | solution.py:518
  46.6 20.8 %collective-permute-start.10 = (f32[6,128,128]{2,1,0:T(8,128)}, f32[6,128,128]{2,1,0:T(8,128)S(1)}, u32[]{:S(2)}, u32[]{:S(2)}) collective-permute-start(f32[6,128,128]{2,1,0:T(8,128)} %get-tuple-element.44), channel_id=1, source_target_pairs={{0,1},{1,0},{2,3},{3,2},{4,5},{5,4},{6,7},{7,6},{8,9},{9,8},{10,11... | collective-permute-start | bytes 1179656 | tf_op jit(solution)/shard_map/ppermute | solution.py:518
  47.1 20.3 %collective-permute-start.11 = (f32[6,128,128]{2,1,0:T(8,128)}, f32[6,128,128]{2,1,0:T(8,128)S(1)}, u32[]{:S(2)}, u32[]{:S(2)}) collective-permute-start(f32[6,128,128]{2,1,0:T(8,128)} %get-tuple-element.45), channel_id=1, source_target_pairs={{0,1},{1,0},{2,3},{3,2},{4,5},{5,4},{6,7},{7,6},{8,9},{9,8},{10,11... | collective-permute-start | bytes 1179656 | tf_op jit(solution)/shard_map/ppermute | solution.py:518
  47.2 20.2 %collective-permute-start.12 = (f32[6,128,128]{2,1,0:T(8,128)}, f32[6,128,128]{2,1,0:T(8,128)}, u32[]{:S(2)}, u32[]{:S(2)}) collective-permute-start(f32[6,128,128]{2,1,0:T(8,128)} %get-tuple-element.46), channel_id=1, source_target_pairs={{0,1},{1,0},{2,3},{3,2},{4,5},{5,4},{6,7},{7,6},{8,9},{9,8},{10,11... | collective-permute-start | bytes 1179656 | tf_op jit(solution)/shard_map/ppermute | solution.py:518
  49.9 17.5 %collective-permute-start.13 = (f32[6,128,128]{2,1,0:T(8,128)}, f32[6,128,128]{2,1,0:T(8,128)}, u32[]{:S(2)}, u32[]{:S(2)}) collective-permute-start(f32[6,128,128]{2,1,0:T(8,128)} %get-tuple-element.69), channel_id=1, source_target_pairs={{0,1},{1,0},{2,3},{3,2},{4,5},{5,4},{6,7},{7,6},{8,9},{9,8},{10,11... | collective-permute-start | bytes 1179656 | tf_op jit(solution)/shard_map/ppermute | solution.py:518
  50.0 17.5 %collective-permute-start.8 = (f32[6,128,128]{2,1,0:T(8,128)}, f32[6,128,128]{2,1,0:T(8,128)}, u32[]{:S(2)}, u32[]{:S(2)}) collective-permute-start(f32[6,128,128]{2,1,0:T(8,128)} %get-tuple-element.82), channel_id=1, source_target_pairs={{0,1},{1,0},{2,3},{3,2},{4,5},{5,4},{6,7},{7,6},{8,9},{9,8},{10,11... | collective-permute-start | bytes 1179656 | tf_op jit(solution)/shard_map/ppermute | solution.py:518
  67.5 1.0 copy-start.6
  68.5 1.0 copy-start.7
  69.5 0.9 copy-start.8
  70.4 0.7 copy-start.9
  71.1 0.7 copy-start.11
  71.9 0.7 copy-start.14
  76.2 19.8 %collective-permute-start.17 = (bf16[16,6144]{1,0:T(8,128)(2,1)S(1)}, bf16[16,6144]{1,0:T(8,128)(2,1)S(1)}, u32[]{:S(2)}, u32[]{:S(2)}) collective-permute-start(bf16[16,6144]{1,0:T(8,128)(2,1)S(1)} %get-tuple-element.54.refs_0_), channel_id=1, source_target_pairs={{0,6},{1,7},{2,0},{3,1},{4,2},{5,3},{6,4},{7,5},{8,14},{9,15},{10,... | collective-permute-start | bytes 589832 | tf_op jit(solution)/shard_map/ppermute | solution.py:623
  90.6 15.9 %collective-permute-start.16 = (bf16[16,6144]{1,0:T(8,128)(2,1)S(1)}, bf16[16,6144]{1,0:T(8,128)(2,1)S(1)}, u32[]{:S(2)}, u32[]{:S(2)}) collective-permute-start(bf16[16,6144]{1,0:T(8,128)(2,1)S(1)} %get-tuple-element.54.refs_0_), channel_id=1, source_target_pairs={{0,4},{1,5},{2,6},{3,7},{4,0},{5,1},{6,2},{7,3},{8,12},{9,13},{10,... | collective-permute-start | bytes 589832 | tf_op jit(solution)/shard_map/ppermute | solution.py:623
  90.6 15.9 %collective-permute-start.15 = (bf16[16,6144]{1,0:T(8,128)(2,1)S(1)}, bf16[16,6144]{1,0:T(8,128)(2,1)S(1)}, u32[]{:S(2)}, u32[]{:S(2)}) collective-permute-start(bf16[16,6144]{1,0:T(8,128)(2,1)S(1)} %get-tuple-element.54.refs_0_), channel_id=1, source_target_pairs={{0,2},{1,3},{2,4},{3,5},{4,6},{5,7},{6,0},{7,1},{8,10},{9,11},{10,... | collective-permute-start | bytes 589832 | tf_op jit(solution)/shard_map/ppermute | solution.py:623
  91.2 21.3 %collective-permute-start.18 = (bf16[16,6144]{1,0:T(8,128)(2,1)S(1)}, bf16[16,6144]{1,0:T(8,128)(2,1)S(1)}, u32[]{:S(2)}, u32[]{:S(2)}) collective-permute-start(bf16[16,6144]{1,0:T(8,128)(2,1)S(1)} %get-tuple-element.54.refs_0_), channel_id=1, source_target_pairs={{0,1},{1,0},{2,3},{3,2},{4,5},{5,4},{6,7},{7,6},{8,9},{9,8},{10,11... | collective-permute-start | bytes 589832 | tf_op jit(solution)/shard_map/ppermute | solution.py:518
  96.0 16.6 %collective-permute-start.21 = (bf16[16,6144]{1,0:T(8,128)(2,1)S(1)}, bf16[16,6144]{1,0:T(8,128)(2,1)S(1)}, u32[]{:S(2)}, u32[]{:S(2)}) collective-permute-start(bf16[16,6144]{1,0:T(8,128)(2,1)S(1)} %collective-permute-done.17.refs_3_), channel_id=1, source_target_pairs={{0,1},{1,0},{2,3},{3,2},{4,5},{5,4},{6,7},{7,6},{8,9},{9,8},{10,11... | collective-permute-start | bytes 589832 | tf_op jit(solution)/shard_map/ppermute | solution.py:518
  106.5 6.0 %collective-permute-start.20 = (bf16[16,6144]{1,0:T(8,128)(2,1)S(1)}, bf16[16,6144]{1,0:T(8,128)(2,1)S(1)}, u32[]{:S(2)}, u32[]{:S(2)}) collective-permute-start(bf16[16,6144]{1,0:T(8,128)(2,1)S(1)} %collective-permute-done.16.refs_2_), channel_id=1, source_target_pairs={{0,1},{1,0},{2,3},{3,2},{4,5},{5,4},{6,7},{7,6},{8,9},{9,8},{10,11... | collective-permute-start | bytes 589832 | tf_op jit(solution)/shard_map/ppermute | solution.py:518
  106.5 6.0 %collective-permute-start.19 = (bf16[16,6144]{1,0:T(8,128)(2,1)S(1)}, bf16[16,6144]{1,0:T(8,128)(2,1)S(1)}, u32[]{:S(2)}, u32[]{:S(2)}) collective-permute-start(bf16[16,6144]{1,0:T(8,128)(2,1)S(1)} %collective-permute-done.15.refs_1_), channel_id=1, source_target_pairs={{0,1},{1,0},{2,3},{3,2},{4,5},{5,4},{6,7},{7,6},{8,9},{9,8},{10,11... | collective-permute-start | bytes 589832 | tf_op jit(solution)/shard_map/ppermute | solution.py:518
  112.6 3.0 %copy-start = (bf16[1,128,6144]{2,1,0:T(8,128)(2,1)S(1)}, bf16[1,128,6144]{2,1,0:T(8,128)(2,1)}, u32[]{:S(2)}) copy-start(bf16[1,128,6144]{2,1,0:T(8,128)(2,1)} %param.12) | copy-start | bytes 4718596
  112.6 3.0 %copy-start.1 = (f32[128,2048]{1,0:T(8,128)S(1)}, f32[128,2048]{1,0:T(8,128)}, u32[]{:S(2)}) copy-start(f32[128,2048]{1,0:T(8,128)} %intra_attention.5.refs_5_.refs_7_) | copy-start | bytes 3145732
  112.6 3.0 %copy-start.2 = (f32[128,2048]{1,0:T(8,128)S(1)}, f32[128,2048]{1,0:T(8,128)}, u32[]{:S(2)}) copy-start(f32[128,2048]{1,0:T(8,128)} %intra_attention.4.refs_4_.refs_6_) | copy-start | bytes 3145732
  112.6 3.0 %copy-start.3 = (f32[128,2048]{1,0:T(8,128)S(1)}, f32[128,2048]{1,0:T(8,128)}, u32[]{:S(2)}) copy-start(f32[128,2048]{1,0:T(8,128)} %intra_attention.3.refs_3_.refs_5_) | copy-start | bytes 3145732
  112.6 3.0 %copy-start.4 = (bf16[1,128,6144]{2,1,0:T(8,128)(2,1)S(1)}, bf16[1,128,6144]{2,1,0:T(8,128)(2,1)}, u32[]{:S(2)}) copy-start(bf16[1,128,6144]{2,1,0:T(8,128)(2,1)} %param.11) | copy-start | bytes 4718596
  112.6 3.0 %copy-start.5 = (f32[1,128,48]{1,2,0:T(8,128)S(1)}, f32[1,128,48]{1,2,0:T(8,128)}, u32[]{:S(2)}) copy-start(f32[1,128,48]{1,2,0:T(8,128)} %param.15) | copy-start | bytes 73732
  112.6 3.0 %copy-start.10 = (f32[1,6144]{1,0:T(1,128)S(1)}, f32[1,6144]{1,0:T(1,128)}, u32[]{:S(2)}) copy-start(f32[1,6144]{1,0:T(1,128)} %refs_17_.1) | copy-start | bytes 73732
  115.5 9.0 %collective-permute-start.22 = (bf16[64,6144]{1,0:T(8,128)(2,1)S(1)}, bf16[64,6144]{1,0:T(8,128)(2,1)S(1)}, u32[]{:S(2)}, u32[]{:S(2)}) collective-permute-start(bf16[64,6144]{1,0:T(8,128)(2,1)S(1)} %get-tuple-element.58), channel_id=1, source_target_pairs={{0,1},{1,0},{2,3},{3,2},{4,5},{5,4},{6,7},{7,6},{8,9},{9,8},{10,11... | collective-permute-start | bytes 2359304 | tf_op jit(solution)/shard_map/ppermute | solution.py:518
  123.0 38.2 %collective-permute-start.14 = (bf16[128,6144]{1,0:T(8,128)(2,1)S(1)}, bf16[128,6144]{1,0:T(8,128)(2,1)S(1)}, u32[]{:S(2)}, u32[]{:S(2)}) collective-permute-start(bf16[128,6144]{1,0:T(8,128)(2,1)S(1)} %finish.1), channel_id=1, source_target_pairs={{0,8},{8,16},{16,24},{24,0},{1,9},{9,17},{17,25},{25,1},{2,10},{10... | collective-permute-start | bytes 4718600 | tf_op jit(solution)/shard_map/ppermute | solution.py:513
  124.5 17.7 %copy-start.12 = (f32[16,128]{1,0:T(8,128)S(1)}, f32[16,128]{1,0:T(8,128)}, u32[]{:S(2)}) copy-start(f32[16,128]{1,0:T(8,128)} %get-tuple-element.52.refs_1_) | copy-start | bytes 24580
  124.5 17.7 %copy-start.13 = (f32[16,128]{1,0:T(8,128)S(1)}, f32[16,128]{1,0:T(8,128)}, u32[]{:S(2)}) copy-start(f32[16,128]{1,0:T(8,128)} %get-tuple-element.53.refs_2_) | copy-start | bytes 24580
  124.8 9.8 %collective-permute-start.25 = (bf16[16,6144]{1,0:T(8,128)(2,1)S(1)}, bf16[16,6144]{1,0:T(8,128)(2,1)S(1)}, u32[]{:S(2)}, u32[]{:S(2)}) collective-permute-start(bf16[16,6144]{1,0:T(8,128)(2,1)S(1)} %get-tuple-element.87), channel_id=1, source_target_pairs={{0,2},{1,3},{2,4},{3,5},{4,6},{5,7},{6,0},{7,1},{8,10},{9,11},{10,... | collective-permute-start | bytes 589832 | tf_op jit(solution)/shard_map/ppermute | solution.py:634
  126.6 15.6 %collective-permute-start.24 = (bf16[16,6144]{1,0:T(8,128)(2,1)S(1)}, bf16[16,6144]{1,0:T(8,128)(2,1)S(1)}, u32[]{:S(2)}, u32[]{:S(2)}) collective-permute-start(bf16[16,6144]{1,0:T(8,128)(2,1)S(1)} %get-tuple-element.88), channel_id=1, source_target_pairs={{0,4},{1,5},{2,6},{3,7},{4,0},{5,1},{6,2},{7,3},{8,12},{9,13},{10,... | collective-permute-start | bytes 589832 | tf_op jit(solution)/shard_map/ppermute | solution.py:634
  128.6 13.6 %collective-permute-start.23 = (bf16[16,6144]{1,0:T(8,128)(2,1)S(1)}, bf16[16,6144]{1,0:T(8,128)(2,1)S(1)}, u32[]{:S(2)}, u32[]{:S(2)}) collective-permute-start(bf16[16,6144]{1,0:T(8,128)(2,1)S(1)} %get-tuple-element.89), channel_id=1, source_target_pairs={{0,6},{1,7},{2,0},{3,1},{4,2},{5,3},{6,4},{7,5},{8,14},{9,15},{10,... | collective-permute-start | bytes 589832 | tf_op jit(solution)/shard_map/ppermute | solution.py:634
  142.4 22.6 %collective-permute-start.26 = (bf16[16,6272]{1,0:T(8,128)(2,1)S(1)}, bf16[16,6272]{1,0:T(8,128)(2,1)S(1)}, u32[]{:S(2)}, u32[]{:S(2)}) collective-permute-start(bf16[16,6272]{1,0:T(8,128)(2,1)S(1)} %late_rows.1), channel_id=1, source_target_pairs={{0,8},{8,16},{16,24},{24,0},{1,9},{9,17},{17,25},{25,1},{2,10},{10... | collective-permute-start | bytes 602120 | tf_op jit(solution)/shard_map/ppermute | solution.py:513

commit v5 on v4

--- a/solution.py
+++ b/solution.py
@@ -238,16 +238,25 @@
     )(experts, weight, rate, queries, resid, *intra)
 
 
-def prefix_copies(core_ref, keeps, gots, state_ref, sems, chunks):
+def prefix_copies(core_ref, given, keeps, gots, state_ref, start_ref, sems, chunks):
+    decay_ref, partner, partner_mine = given
     steps = len(keeps)
     half = state_ref.shape[0] // 2
     per = half // chunks
+
+    def own(n, c):
+        place = pl.multiple_of(lax.rem(core_ref[0] + n, 2) * half + c * per, per)
+        source = (partner, partner_mine)[n].at[pl.ds(c * per, per)]
+        return pltpu.make_async_copy(source, start_ref.at[pl.ds(place, per)], sems.at[2 + n, c])
 
     def states(n, c, late):
         place = pl.multiple_of(lax.rem(core_ref[0] + n, 2) * half + c * per, per)
         source = (keeps, gots)[n][c + late]
         return pltpu.make_async_copy(source, state_ref.at[pl.ds(place, per)], sems.at[n, c])
 
+    for c in range(chunks):
+        for n in range(2):
+            own(n, c).start()
     for late in range(steps - chunks + 1):
 
         @pl.when(core_ref[1] == late)
@@ -258,24 +267,32 @@
 
     def wait(c):
         for n in range(2):
+            own(n, c).wait()
             states(n, c, 0).wait()
 
-    return wait
+    second = core_ref[0].astype(F32)
+    decays = jnp.where(core_ref[0] == 0, 1.0, decay_ref[...])
+
+    def prefix(head):
+        return decays[head : head + 1, :] * state_ref[head] + second * start_ref[head]
+
+    return wait, prefix
 
 
 def rows_kernel(chunks, steps, core_ref, growth_ref, q_ref, resid_ref, intra_ref, *refs):
+    given, refs = refs[:3], refs[3:]
     keeps, gots, refs = refs[:steps], refs[steps : 2 * steps], refs[2 * steps :]
-    again_ref, mgain_ref, outbox_ref, picked_ref, state_ref, sems = refs
+    again_ref, mgain_ref, outbox_ref, picked_ref, state_ref, start_ref, sems = refs
     _, width = picked_ref.shape
     heads = width // HEAD
     half = heads // 2
     per = half // chunks
-    wait = prefix_copies(core_ref, keeps, gots, state_ref, sems, chunks)
+    wait, prefix = prefix_copies(core_ref, given, keeps, gots, state_ref, start_ref, sems, chunks)
     for c in range(chunks):
         wait(c)
         for head in [n * half + c * per + j for n in range(2) for j in range(per)]:
             cols = slice(head * HEAD, (head + 1) * HEAD)
-            hi, lo = split(state_ref[head])
+            hi, lo = split(prefix(head))
             q = q_ref[:, cols]
             value = growth_ref[:, head : head + 1] * (dot(q, hi) + dot(q, lo))
             picked_ref[:, cols] = intra_ref[:, cols] + value
@@ -287,30 +304,34 @@
     outbox_ref[...] = (hres * scale * mgain_ref[...]).astype(BF16)
 
 
-def selected_rows(core, growth, queries, resid, intra, keeps, gots, attn_gain, moe_gain):
+def selected_rows(
+    core, growth, queries, resid, intra, given, keeps, gots, attn_gain, moe_gain
+):
     slots, width = queries.shape
     heads = width // HEAD
     steps = len(keeps)
     return pl.pallas_call(
         lambda *refs: rows_kernel(CHUNKS, steps, *refs),
-        in_specs=[SMEM_SPEC] + [VMEM_SPEC] * 4 + [ANY_SPEC] * (2 * steps) + [VMEM_SPEC] * 2,
+        in_specs=[SMEM_SPEC] + [VMEM_SPEC] * 5 + [ANY_SPEC] * (2 + 2 * steps) + [VMEM_SPEC] * 2,
         out_specs=[VMEM_SPEC] * 2,
         out_shape=[pltpu.VMEM((slots, width), BF16), pltpu.VMEM((slots, width), F32)],
         scratch_shapes=[
             pltpu.VMEM((heads, HEAD, HEAD), F32),
-            pltpu.SemaphoreType.DMA((2, CHUNKS)),
+            pltpu.VMEM((heads, HEAD, HEAD), F32),
+            pltpu.SemaphoreType.DMA((4, CHUNKS)),
         ],
         compiler_params=pltpu.CompilerParams(vmem_limit_bytes=16 << 20),
         name="selected_rows",
-    )(core, growth, queries, resid, intra, *keeps, *gots, attn_gain, moe_gain)
+    )(core, growth, queries, resid, intra, *given, *keeps, *gots, attn_gain, moe_gain)
 
 
 def finish_kernel(parts, chunks, steps, core_ref, rate_ref, q_hbm, *refs):
     intra_hbm, refs = refs[:parts], refs[parts:]
+    given, refs = refs[:3], refs[3:]
     keeps, gots, refs = refs[:steps], refs[steps : 2 * steps], refs[2 * steps :]
     (
         resid_hbm, again_ref, early_ref,
-        attn_ref, q_ref, intra_ref, state_ref, resid_ref, scale_ref, sems, state_sems,
+        attn_ref, q_ref, intra_ref, state_ref, start_ref, resid_ref, sems, state_sems,
     ) = refs
     length, width = resid_ref.shape
     heads = width // HEAD
@@ -328,18 +349,27 @@
             ),
         ]
 
+    wait, prefix = prefix_copies(
+        core_ref, given, keeps, gots, state_ref, start_ref, state_sems, chunks
+    )
     for g in range(groups):
         for copy in copies(g):
             copy.start()
-    wait = prefix_copies(core_ref, keeps, gots, state_ref, state_sems, chunks)
     rest = pltpu.make_async_copy(resid_hbm, resid_ref, sems.at[2, 0])
     rest.start()
-    growth = jnp.exp(cumul_rows(rate_ref))
-    for head in range(heads):
-        across = jnp.broadcast_to(growth[head : head + 1, :], (length, length))
-        scale_ref[:, head * HEAD : (head + 1) * HEAD] = across.T
+    lower = (
+        lax.broadcasted_iota(jnp.int32, (length, length), 0)
+        >= lax.broadcasted_iota(jnp.int32, (length, length), 1)
+    ).astype(F32)
+    growth = jnp.exp(
+        lax.dot_general(
+            lower, rate_ref[...], (((1,), (1,)), ((), ())), precision=lax.Precision.HIGHEST,
+            preferred_element_type=F32,
+        )
+    )
     for c in range(chunks):
         wait(c)
+    squares = jnp.zeros((length, HEAD), F32)
     for g in range(groups):
         for copy in copies(g):
             copy.wait()
@@ -347,35 +377,33 @@
             head = g * GROUP + j
             mine = slice(j * HEAD, (j + 1) * HEAD)
             cols = slice(head * HEAD, (head + 1) * HEAD)
-            hi, lo = split(state_ref[head])
+            hi, lo = split(prefix(head))
             q = q_ref[g, :, mine]
-            value = dot(q, hi) + dot(q, lo)
-            attn_ref[:, cols] = intra_ref[g, :, mine] + scale_ref[:, cols] * value
+            value = growth[:, head : head + 1] * (dot(q, hi) + dot(q, lo))
+            value = intra_ref[g, :, mine] + value
+            attn_ref[:, cols] = value
+            squares = squares + value * value
+    scale_all = lax.rsqrt(jnp.sum(squares, axis=1, keepdims=True) * (1.0 / width) + 1e-06)
     rest.wait()
     rows = 16
-
-    def norm(r, carry):
-        at = pl.ds(pl.multiple_of(r * rows, rows), rows)
-        x = attn_ref[at, :]
-        scale = lax.rsqrt(jnp.mean(x * x, axis=-1, keepdims=True) + 1e-06)
-        hres = resid_ref[at, :].astype(F32) + x * scale * again_ref[...]
+    for r in range(length // rows):
+        at = slice(r * rows, (r + 1) * rows)
+        hres = resid_ref[at, :].astype(F32) + attn_ref[at, :] * scale_all[at] * again_ref[...]
         early_ref[at, :] = hres.astype(BF16)
-        return carry
-
-    lax.fori_loop(0, length // rows, norm, 0)
-
-
-def finish(core, rate, queries, intra, keeps, gots, resid, attn_gain):
+
+
+def finish(core, rate, queries, intra, given, keeps, gots, resid, attn_gain):
     length, width = queries.shape
     heads = width // HEAD
     groups = heads // GROUP
     parts, steps = len(intra), len(keeps)
-    args = [rate, queries, *intra, *keeps, *gots, resid, attn_gain]
+    args = [rate, queries, *intra, *given, *keeps, *gots, resid, attn_gain]
     return pl.pallas_call(
         lambda *refs: finish_kernel(parts, CHUNKS, steps, *refs),
         in_specs=[SMEM_SPEC, VMEM_SPEC]
         + [HBM_SPEC] * (1 + parts)
-        + [ANY_SPEC] * (2 * steps)
+        + [VMEM_SPEC]
+        + [ANY_SPEC] * (2 + 2 * steps)
         + [HBM_SPEC, VMEM_SPEC],
         out_specs=VMEM_SPEC,
         out_shape=pltpu.VMEM((length, width), BF16),
@@ -384,10 +412,10 @@
             pltpu.VMEM((groups, length, GROUP * HEAD), BF16),
             pltpu.VMEM((groups, length, GROUP * HEAD), F32),
             pltpu.VMEM((heads, HEAD, HEAD), F32),
+            pltpu.VMEM((heads, HEAD, HEAD), F32),
             pltpu.VMEM((length, width), BF16),
-            pltpu.VMEM((length, width), F32),
             pltpu.SemaphoreType.DMA((3, groups)),
-            pltpu.SemaphoreType.DMA((2, CHUNKS)),
+            pltpu.SemaphoreType.DMA((4, CHUNKS)),
         ],
         compiler_params=pltpu.CompilerParams(vmem_limit_bytes=32 << 20),
         name="finish",
@@ -521,39 +549,28 @@
 def chain_prefix(mine, partner, decay, decay_partner, chip, chips, first, scale):
     heads = mine.shape[0]
     per = heads // CHUNKS
-    keeps, gives, before = [], [], None
-
-    def chunk(index):
-        place = jnp.clip(index, 0, CHUNKS - 1) * per
+    keeps, gots, before = [], [], None
+    for step in range(CHUNKS + chips - 2):
+        place = jnp.clip(step - chip, 0, CHUNKS - 1) * per
         cut = [
             lax.dynamic_slice_in_dim(a, place, per, 0)
             for a in (mine, partner, decay, decay_partner)
         ]
         state0, state1 = jnp.where(first, cut[0], cut[1]), jnp.where(first, cut[1], cut[0])
         decay0, decay1 = jnp.where(first, cut[2], cut[3]), jnp.where(first, cut[3], cut[2])
-        return state0, state1, decay0[:, None, :], decay1[:, None, :]
-
-    for step in range(CHUNKS + chips - 2):
-        state0, state1, decay0, decay1 = chunk(step - chip)
-        gone = (decay1 * state0 + state1) * scale
+        gone = (decay1[:, None, :] * state0 + state1) * scale
         if before is not None:
-            gone = (decay0 * decay1) * before.astype(F32) + gone
+            gone = (decay0 * decay1)[:, None, :] * before.astype(F32) + gone
         pairs = [
             (2 * z + core, 2 * z + 2 + core)
             for z in range(chips - 1)
             if 0 <= step - z < CHUNKS
             for core in range(2)
         ]
-        gone = gone.astype(jnp.float16)
-        if step >= 2:
-            gone, keeps[-1], gives[-1] = lax.optimization_barrier((gone, keeps[-1], gives[-1]))
-        before = lax.ppermute(gone, "ctx", pairs)
-        state0, _, decay0, _ = chunk(step - jnp.maximum(chip - 1, 0))
-        prefix = lax.optimization_barrier(before).astype(F32) * (1.0 / scale)
-        after0 = decay0 * prefix + state0
-        keeps.append(jnp.where(first, prefix, after0))
-        gives.append(jnp.where(first, after0, prefix))
-    return keeps, [swapped(give) for give in gives]
+        before = lax.ppermute(gone.astype(jnp.float16), "ctx", pairs)
+        keeps.append(before.astype(F32) * (1.0 / scale))
+        gots.append(swapped(before).astype(F32) * (1.0 / scale))
+    return keeps, gots
 
 
 def local(
@@ -589,6 +606,8 @@
     partner = swapped(other)
     decay_partner = swapped(decay)
     mine, _ = half_state(core1, turned, keys, values)
+    partner_mine = swapped(mine)
+    before_me = (decay_partner, partner, partner_mine)
     decay = lax.dynamic_slice_in_dim(decay, core * half, half, 0)
     decay_partner = lax.dynamic_slice_in_dim(decay_partner, core * half, half, 0)
     scale = 1.0
@@ -608,6 +627,8 @@
             for a in (keeps, gots)
         )
         prefix = jnp.where(first, jnp.concatenate([keep, got]), jnp.concatenate([got, keep]))
+        done = prefix * before_me[0][:, None, :] + jnp.concatenate([partner_mine, partner])
+        prefix = jnp.where(first, prefix, done)
         return many_experts(
             flying, rate, queries, jnp.concatenate(intra, axis=1), prefix, resid,
             attn_gain, moe_gain, experts, weight, up, down,
@@ -617,13 +638,13 @@
         experts.T, weight.T, turned, queries, resid, intra
     )
     outbox, picked = selected_rows(
-        where, growth, q_rows, resid_rows, intra_rows, keeps, gots, attn_gain, moe_gain
+        where, growth, q_rows, resid_rows, intra_rows, before_me, keeps, gots, attn_gain, moe_gain
     )
     own = [outbox] + [
         lax.ppermute(outbox, "ctx", [(i, (i + 2 * d) % count) for i in range(count)])
         for d in range(1, chips)
     ]
-    early = finish(where, turned, queries, intra, keeps, gots, resid, attn_gain)
+    early = finish(where, turned, queries, intra, before_me, keeps, gots, resid, attn_gain)
     early = passed_along(early, "section", 1)
     up, down = fetch(up, down)
     others = [swapped(r) for r in own]

time: 168 us -> 176 us (1.048)
  other arithmetic: 8.5 us -> 16 us
  Pallas kernels: 43.9 us -> 48.4 us
  local copies, waits for them, and re-layouts: 5.2 us -> 1.58 us
    convert_element_type x2 -> x18, other arithmetic: 2.83 us -> 15.7 us  [the longest x6 6.84 us: chain_prefix(): before = lax.ppermute(gone.astype(jnp.float16), 'ctx', pairs)]
    select_n x6 -> x0, other arithmetic: 5.41 us -> none  [the longest x5 5.36 us: chain_prefix(): gives.append(jnp.where(first, after0, prefix))]
    unnamed x36 -> x50, local copies, waits for them, and re-layouts: 5.14 us -> 1.52 us
    pallas_call x1, Pallas kernels: 3.65 us -> 6.51 us  [selected_rows(): pl.pallas_call(lambda *refs: rows_kernel(CHUNKS, steps, *refs), in_specs=...]
    ppermute x6, starting transfers between devices: 19.4 us -> 22.2 us  [chain_prefix(): before = lax.ppermute(gone.astype(jnp.float16), 'ctx', pairs)]
    ppermute x3, starting transfers between devices: 15 us -> 12.9 us  [layer(): lax.ppermute(outbox, 'ctx', [(i, (i + 2 * d) % count) for i in range(coun...]
  transfers between devices with their start and end apart: 27 -> 28, of which waited for: 11 -> 11; matrix products, arithmetic and copies ran while one was open for 2% -> 7% of each run, Pallas kernels for 20% -> 19%
where the time goes in v5:
time: 176 us; the launch traced here: 175 us
  waiting for transfers between devices  61.1 us (35%)
  Pallas kernels  48.4 us (28%)
  starting transfers between devices  47.5 us (27%)
  other arithmetic  16 us (9%)
    ppermute x6, starting transfers between devices, chain_prefix(): before = lax.ppermute(gone.astype(jnp.float16), 'ctx', pairs)  22.2 us
    ppermute x2, waiting for transfers between devices, passed_along(): return lax.ppermute(value, axis, pairs)  21 us
    ppermute x3, waiting for transfers between devices, layer(): lax.ppermute(outbox, 'ctx', [(i, (i + 2 * d) % count) for i in range(coun...  16.1 us
    ppermute x6, waiting for transfers between devices, chain_prefix(): before = lax.ppermute(gone.astype(jnp.float16), 'ctx', pairs)  12.9 us
    ppermute x3, starting transfers between devices, layer(): lax.ppermute(outbox, 'ctx', [(i, (i + 2 * d) % count) for i in range(coun...  12.9 us
    pallas_call x3, Pallas kernels, intra_attention(): pl.pallas_call(lambda *refs: intra_kernel(part * groups, *refs), in_specs...  12.1 us
    ppermute x3, waiting for transfers between devices, layer(): lax.ppermute(pair[d], 'ctx', [(i, (i - 2 * d) % count) for i in range(cou...  10.8 us
    pallas_call x1, Pallas kernels, finish(): pl.pallas_call(lambda *refs: finish_kernel(parts, CHUNKS, steps, *refs),...  7.33 us
  transfers between devices with their start and end apart: 28, of which 11 were waited for; matrix products, arithmetic and copies ran while one was open for 7% of the time, Pallas kernels for 19%

profile of v5, /device:TPU:0, one launch (start us, length us, event | category | flops | bytes accessed | tf_op | source)
XLA Modules:
  0.0 175.4 jit_solution(9804549938412686658)
XLA Ops:
  0.0 3.0 %half_state.2 = (f32[24,128,128]{2,1,0:T(8,128)}, f32[48,128]{1,0:T(8,128)}) custom-call(s32[1]{0:T(128)S(6)} %sub.30.half_ref, f32[48,128]{1,0:T(8,128)} %bitcast.25, bf16[128,6144]{1,0:T(8,128)(2,1)} %bitcast.32, bf16[128,6144]{1,0:T(8,128)(2,1)} %bitcast.37), custom_call_target="tpu_custom_call" | custom-call | tf_op jit(solution)/shard_map/half_state/pallas_call | solution.py:101
  3.6 3.0 %half_state.3 = (f32[24,128,128]{2,1,0:T(8,128)}, f32[48,128]{1,0:T(8,128)}) custom-call(s32[1]{0:T(128)} %bitcast.half_ref, f32[48,128]{1,0:T(8,128)} %bitcast.26, bf16[128,6144]{1,0:T(8,128)(2,1)} %bitcast.33, bf16[128,6144]{1,0:T(8,128)(2,1)} %bitcast.38), custom_call_target="tpu_custom_call" | custom-call | tf_op jit(solution)/shard_map/half_state/pallas_call | solution.py:101
  6.9 1.1 add_convert_fusion.6
  8.0 4.8 %collective-permute-start.3 = (f16[6,128,128]{2,1,0:T(8,128)(2,1)S(1)}, f16[6,128,128]{2,1,0:T(8,128)(2,1)S(1)}, u32[]{:S(2)}, u32[]{:S(2)}) collective-permute-start(f16[6,128,128]{2,1,0:T(8,128)(2,1)S(1)} %add_convert_fusion.6), channel_id=1, source_target_pairs={{0,2},{1,3},{8,10},{9,11},{16,18},{17,19},{24,26},{25,27}} | collective-permute-start | bytes 589832 | tf_op jit(solution)/shard_map/ppermute | solution.py:570
  12.8 4.4 %collective-permute-done.3 = f16[6,128,128]{2,1,0:T(8,128)(2,1)S(1)} collective-permute-done((f16[6,128,128]{2,1,0:T(8,128)(2,1)S(1)}, f16[6,128,128]{2,1,0:T(8,128)(2,1)S(1)}, u32[]{:S(2)}, u32[]{:S(2)}) %collective-permute-start.3) | collective-permute-done | bytes 196640 | tf_op jit(solution)/shard_map/ppermute | solution.py:570
  17.3 1.1 add_convert_fusion.5
  18.4 4.4 %collective-permute-start.4 = (f16[6,128,128]{2,1,0:T(8,128)(2,1)S(1)}, f16[6,128,128]{2,1,0:T(8,128)(2,1)S(1)}, u32[]{:S(2)}, u32[]{:S(2)}) collective-permute-start(f16[6,128,128]{2,1,0:T(8,128)(2,1)S(1)} %add_convert_fusion.5), channel_id=1, source_target_pairs={{0,2},{1,3},{2,4},{3,5},{8,10},{9,11},{10,12},{11,13},{16,18},{17,... | collective-permute-start | bytes 589832 | tf_op jit(solution)/shard_map/ppermute | solution.py:570
  22.8 3.6 %collective-permute-done.4 = f16[6,128,128]{2,1,0:T(8,128)(2,1)S(1)} collective-permute-done((f16[6,128,128]{2,1,0:T(8,128)(2,1)S(1)}, f16[6,128,128]{2,1,0:T(8,128)(2,1)S(1)}, u32[]{:S(2)}, u32[]{:S(2)}) %collective-permute-start.4) | collective-permute-done | bytes 196640 | tf_op jit(solution)/shard_map/ppermute | solution.py:570
  26.4 1.1 add_convert_fusion.4
  27.5 5.1 %collective-permute-start.5 = (f16[6,128,128]{2,1,0:T(8,128)(2,1)S(1)}, f16[6,128,128]{2,1,0:T(8,128)(2,1)}, u32[]{:S(2)}, u32[]{:S(2)}) collective-permute-start(f16[6,128,128]{2,1,0:T(8,128)(2,1)S(1)} %add_convert_fusion.4), channel_id=1, source_target_pairs={{0,2},{1,3},{2,4},{3,5},{4,6},{5,7},{8,10},{9,11},{10,12},{11,13},... | collective-permute-start | bytes 589832 | tf_op jit(solution)/shard_map/ppermute | solution.py:570
  32.6 2.5 %collective-permute-done.5 = f16[6,128,128]{2,1,0:T(8,128)(2,1)} collective-permute-done((f16[6,128,128]{2,1,0:T(8,128)(2,1)S(1)}, f16[6,128,128]{2,1,0:T(8,128)(2,1)}, u32[]{:S(2)}, u32[]{:S(2)}) %collective-permute-start.5) | collective-permute-done | bytes 196640 | tf_op jit(solution)/shard_map/ppermute | solution.py:570
  35.1 1.2 add_convert_fusion.3
  36.2 5.2 %collective-permute-start.6 = (f16[6,128,128]{2,1,0:T(8,128)(2,1)S(1)}, f16[6,128,128]{2,1,0:T(8,128)(2,1)}, u32[]{:S(2)}, u32[]{:S(2)}) collective-permute-start(f16[6,128,128]{2,1,0:T(8,128)(2,1)S(1)} %add_convert_fusion.3), channel_id=1, source_target_pairs={{0,2},{1,3},{2,4},{3,5},{4,6},{5,7},{8,10},{9,11},{10,12},{11,13},... | collective-permute-start | bytes 589832 | tf_op jit(solution)/shard_map/ppermute | solution.py:570
  41.4 2.5 %collective-permute-done.6 = f16[6,128,128]{2,1,0:T(8,128)(2,1)} collective-permute-done((f16[6,128,128]{2,1,0:T(8,128)(2,1)S(1)}, f16[6,128,128]{2,1,0:T(8,128)(2,1)}, u32[]{:S(2)}, u32[]{:S(2)}) %collective-permute-start.6) | collective-permute-done | bytes 196640 | tf_op jit(solution)/shard_map/ppermute | solution.py:570
  43.9 1.2 add_convert_fusion.2
  45.1 1.3 collective-permute-start.7
  46.9 1.2 add_convert_fusion.1
  48.1 1.4 collective-permute-start.8
  51.2 4.1 %intra_attention.5.refs_5_.refs_7_ = f32[128,2048]{1,0:T(8,128)} custom-call(f32[48,128]{1,0:T(8,128)} %bitcast.27, bf16[128,6144]{1,0:T(8,128)(2,1)} %bitcast.18, bf16[128,6144]{1,0:T(8,128)(2,1)} %bitcast.34, bf16[128,6144]{1,0:T(8,128)(2,1)} %bitcast.39), custom_call_target="tpu_custom_call" | custom-call | tf_op jit(solution)/shard_map/intra_attention/pallas_call | solution.py:165
  55.2 4.0 %intra_attention.4.refs_4_.refs_6_ = f32[128,2048]{1,0:T(8,128)} custom-call(f32[48,128]{1,0:T(8,128)} %bitcast.28, bf16[128,6144]{1,0:T(8,128)(2,1)} %bitcast.19, bf16[128,6144]{1,0:T(8,128)(2,1)} %bitcast.35, bf16[128,6144]{1,0:T(8,128)(2,1)} %bitcast.40), custom_call_target="tpu_custom_call" | custom-call | tf_op jit(solution)/shard_map/intra_attention/pallas_call | solution.py:165
  59.3 4.0 %intra_attention.3.refs_3_.refs_5_ = f32[128,2048]{1,0:T(8,128)} custom-call(f32[48,128]{1,0:T(8,128)} %bitcast.29, bf16[128,6144]{1,0:T(8,128)(2,1)} %bitcast.20, bf16[128,6144]{1,0:T(8,128)(2,1)} %bitcast.36, bf16[128,6144]{1,0:T(8,128)(2,1)} %bitcast.41), custom_call_target="tpu_custom_call" | custom-call | tf_op jit(solution)/shard_map/intra_attention/pallas_call | solution.py:165
  63.3 4.9 %select.7 = (f32[16,128]{1,0:T(8,128)}, f32[16,128]{1,0:T(8,128)}, f32[16,48]{1,0:T(8,128)}, bf16[16,6144]{1,0:T(8,128)(2,1)}, f32[16,6144]{1,0:T(8,128)}, /*index=5*/f32[16,6144]{1,0:T(8,128)}) custom-call(s32[2,128]{1,0:T(2,128)} %bitcast.44, f32[2,128]{1,0:T(2,128)} %bitcast.45, f32[48,128]{1,0:T(8,128)} %bitcast.30, bf16[128,6144]{1,0:T(8,128)(2,1)} %bitcast.21, ...), custom_call_target="tpu_custom_call" | custom-call | tf_op jit(solution)/shard_map/select/pallas_call | solution.py:220
  68.4 1.0 convert_element_type.80.refs_15_.refs_14_
  69.3 1.0 convert_element_type.73.refs_11_.refs_10_
  70.4 1.0 convert_element_type.75.refs_12_.refs_11_
  71.3 1.0 convert_element_type.82.refs_17_.refs_16_
  72.4 1.0 convert_element_type.77.refs_13_.refs_12_
  73.4 1.0 convert_element_type.83.refs_18_.refs_17_
  74.4 1.0 convert_element_type.79.refs_14_.refs_13_
  75.3 1.0 convert_element_type.84.refs_19_.refs_18_
  76.3 1.1 convert_element_type.85.refs_20_.refs_19_
  77.5 6.5 %selected_rows.1 = (bf16[16,6144]{1,0:T(8,128)(2,1)}, f32[16,6144]{1,0:T(8,128)S(1)}) custom-call(s32[2]{0:T(128)S(1)} %pad_add_fusion.refs_0_, f32[16,48]{1,0:T(8,128)S(1)} %copy-done.21, bf16[16,6144]{1,0:T(8,128)(2,1)S(1)} %copy-done.16, f32[16,6144]{1,0:T(8,128)S(1)} %copy-done.10, f32[16,6144]{1,0:T(8,128)S(1)} %copy-done.11, f32[48,128]{1,0:T(8,128)S(1)} %copy-done.15, ...), custom_call_target="tpu_custom_call" | custom-call | tf_op jit(solution)/shard_map/selected_rows/pallas_call | solution.py:313
  84.8 12.3 %collective-permute-start.18 = (bf16[16,6144]{1,0:T(8,128)(2,1)}, bf16[16,6144]{1,0:T(8,128)(2,1)}, u32[]{:S(2)}, u32[]{:S(2)}) collective-permute-start(bf16[16,6144]{1,0:T(8,128)(2,1)} %get-tuple-element.30.refs_0_), channel_id=1, source_target_pairs={{0,6},{1,7},{2,0},{3,1},{4,2},{5,3},{6,4},{7,5},{8,14},{9,15},{10,... | collective-permute-start | bytes 589832 | tf_op jit(solution)/shard_map/ppermute | solution.py:644
  97.7 5.1 %collective-permute-done.18.refs_3_ = bf16[16,6144]{1,0:T(8,128)(2,1)} collective-permute-done((bf16[16,6144]{1,0:T(8,128)(2,1)}, bf16[16,6144]{1,0:T(8,128)(2,1)}, u32[]{:S(2)}, u32[]{:S(2)}) %collective-permute-start.18) | collective-permute-done | bytes 196640 | tf_op jit(solution)/shard_map/ppermute | solution.py:644
  102.8 11.0 %collective-permute-done.17.refs_2_ = bf16[16,6144]{1,0:T(8,128)(2,1)} collective-permute-done((bf16[16,6144]{1,0:T(8,128)(2,1)}, bf16[16,6144]{1,0:T(8,128)(2,1)}, u32[]{:S(2)}, u32[]{:S(2)}) %collective-permute-start.17) | collective-permute-done | bytes 196640 | tf_op jit(solution)/shard_map/ppermute | solution.py:644
  114.3 5.5 %fetch.1 = (bf16[6144,640]{1,0:T(8,128)(2,1)S(1)}, bf16[640,6144]{1,0:T(8,128)(2,1)S(1)}) custom-call(bf16[6144,640]{1,0:T(8,128)(2,1)} %bitcast.42, bf16[640,6144]{1,0:T(8,128)(2,1)} %bitcast.43), custom_call_target="tpu_custom_call" | custom-call | tf_op jit(solution)/shard_map/fetch/pallas_call | solution.py:495
  119.9 4.3 %expert_rows.1 = (bf16[64,6144]{1,0:T(8,128)(2,1)S(1)}, bf16[64,6144]{1,0:T(8,128)(2,1)S(1)}) custom-call(bf16[16,6144]{1,0:T(8,128)(2,1)} %get-tuple-element.30.refs_0_, bf16[16,6144]{1,0:T(8,128)(2,1)} %collective-permute-done.16.refs_1_, bf16[16,6144]{1,0:T(8,128)(2,1)} %collective-permute-done.17.refs_2_, ...), custom_call_target="tpu_custom_call" | custom-call | tf_op jit(solution)/shard_map/expert_rows/pallas_call | solution.py:527
  124.4 7.3 %finish.1 = bf16[128,6144]{1,0:T(8,128)(2,1)S(1)} custom-call(s32[2]{0:T(128)S(1)} %pad_add_fusion.refs_0_, f32[48,128]{1,0:T(8,128)S(1)} %bitcast.31, bf16[128,6144]{1,0:T(8,128)(2,1)S(1)} %bitcast.22, f32[128,2048]{1,0:T(8,128)S(1)} %copy-done.3, f32[128,2048]{1,0:T(8,128)S(1)} %copy-done.2, f32[128,2048]{1,0:T(8,128)S(1)} %copy-done.1, ...), custom_call_target="tpu_custom_call" | custom-call | tf_op jit(solution)/shard_map/finish/pallas_call | solution.py:401
  131.7 1.5 collective-permute-start.15
  133.5 1.7 collective-permute-start.26
  135.2 2.0 %collective-permute-start.25 = (bf16[16,6144]{1,0:T(8,128)(2,1)S(1)}, bf16[16,6144]{1,0:T(8,128)(2,1)S(1)}, u32[]{:S(2)}, u32[]{:S(2)}) collective-permute-start(bf16[16,6144]{1,0:T(8,128)(2,1)S(1)} %get-tuple-element.46), channel_id=1, source_target_pairs={{0,4},{1,5},{2,6},{3,7},{4,0},{5,1},{6,2},{7,3},{8,12},{9,13},{10,... | collective-permute-start | bytes 589832 | tf_op jit(solution)/shard_map/ppermute | solution.py:655
  137.2 2.8 %collective-permute-start.24 = (bf16[16,6144]{1,0:T(8,128)(2,1)S(1)}, bf16[16,6144]{1,0:T(8,128)(2,1)S(1)}, u32[]{:S(2)}, u32[]{:S(2)}) collective-permute-start(bf16[16,6144]{1,0:T(8,128)(2,1)S(1)} %get-tuple-element.47), channel_id=1, source_target_pairs={{0,6},{1,7},{2,0},{3,1},{4,2},{5,3},{6,4},{7,5},{8,14},{9,15},{10,... | collective-permute-start | bytes 589832 | tf_op jit(solution)/shard_map/ppermute | solution.py:655
  140.1 3.2 %collective-permute-done.26.refs_6_ = bf16[16,6144]{1,0:T(8,128)(2,1)S(1)} collective-permute-done((bf16[16,6144]{1,0:T(8,128)(2,1)S(1)}, bf16[16,6144]{1,0:T(8,128)(2,1)S(1)}, u32[]{:S(2)}, u32[]{:S(2)}) %collective-permute-start.26) | collective-permute-done | bytes 196640 | tf_op jit(solution)/shard_map/ppermute | solution.py:655
  143.3 7.6 %collective-permute-done.25.refs_5_ = bf16[16,6144]{1,0:T(8,128)(2,1)S(1)} collective-permute-done((bf16[16,6144]{1,0:T(8,128)(2,1)S(1)}, bf16[16,6144]{1,0:T(8,128)(2,1)S(1)}, u32[]{:S(2)}, u32[]{:S(2)}) %collective-permute-start.25) | collective-permute-done | bytes 196640 | tf_op jit(solution)/shard_map/ppermute | solution.py:655
  151.2 1.5 collective-permute-start.27
  152.7 17.2 %collective-permute-done.15.early_ref = bf16[128,6144]{1,0:T(8,128)(2,1)S(1)} collective-permute-done((bf16[128,6144]{1,0:T(8,128)(2,1)S(1)}, bf16[128,6144]{1,0:T(8,128)(2,1)S(1)}, u32[]{:S(2)}, u32[]{:S(2)}) %collective-permute-start.15) | collective-permute-done | bytes 1572896 | tf_op jit(solution)/shard_map/ppermute | solution.py:541
  169.9 3.8 %collective-permute-done.27.late_ref = bf16[16,6272]{1,0:T(8,128)(2,1)S(1)} collective-permute-done((bf16[16,6272]{1,0:T(8,128)(2,1)S(1)}, bf16[16,6272]{1,0:T(8,128)(2,1)S(1)}, u32[]{:S(2)}, u32[]{:S(2)}) %collective-permute-start.27) | collective-permute-done | bytes 200736 | tf_op jit(solution)/shard_map/ppermute | solution.py:541
  173.7 1.5 merged.1
  (92 shorter events, 5.7 us)
Async XLA Ops:
  3.0 3.9 %collective-permute-start.1 = (f32[24,128,128]{2,1,0:T(8,128)}, f32[24,128,128]{2,1,0:T(8,128)S(1)}, u32[]{:S(2)}, u32[]{:S(2)}) collective-permute-start(f32[24,128,128]{2,1,0:T(8,128)} %get-tuple-element.21), channel_id=1, source_target_pairs={{0,1},{1,0},{2,3},{3,2},{4,5},{5,4},{6,7},{7,6},{8,9},{9,8},{10,11... | collective-permute-start | bytes 4718600 | tf_op jit(solution)/shard_map/ppermute | solution.py:546
  3.6 3.3 %collective-permute-start = (f32[48,128]{1,0:T(8,128)}, f32[48,128]{1,0:T(8,128)S(1)}, u32[]{:S(2)}, u32[]{:S(2)}) collective-permute-start(f32[48,128]{1,0:T(8,128)} %get-tuple-element.20), channel_id=1, source_target_pairs={{0,1},{1,0},{2,3},{3,2},{4,5},{5,4},{6,7},{7,6},{8,9},{9,8},{10,11... | collective-permute-start | bytes 73736 | tf_op jit(solution)/shard_map/ppermute | solution.py:546
  6.8 20.6 %copy-start.14 = (f32[48,128]{1,0:T(8,128)}, f32[48,128]{1,0:T(8,128)S(1)}, u32[]{:S(2)}) copy-start(f32[48,128]{1,0:T(8,128)S(1)} %collective-permute-done.refs_6_.refs_5_) | copy-start | bytes 73732
  8.0 9.3 %collective-permute-start.3 = (f16[6,128,128]{2,1,0:T(8,128)(2,1)S(1)}, f16[6,128,128]{2,1,0:T(8,128)(2,1)S(1)}, u32[]{:S(2)}, u32[]{:S(2)}) collective-permute-start(f16[6,128,128]{2,1,0:T(8,128)(2,1)S(1)} %add_convert_fusion.6), channel_id=1, source_target_pairs={{0,2},{1,3},{8,10},{9,11},{16,18},{17,19},{24,26},{25,27}} | collective-permute-start | bytes 589832 | tf_op jit(solution)/shard_map/ppermute | solution.py:570
  18.4 8.0 %collective-permute-start.4 = (f16[6,128,128]{2,1,0:T(8,128)(2,1)S(1)}, f16[6,128,128]{2,1,0:T(8,128)(2,1)S(1)}, u32[]{:S(2)}, u32[]{:S(2)}) collective-permute-start(f16[6,128,128]{2,1,0:T(8,128)(2,1)S(1)} %add_convert_fusion.5), channel_id=1, source_target_pairs={{0,2},{1,3},{2,4},{3,5},{8,10},{9,11},{10,12},{11,13},{16,18},{17,... | collective-permute-start | bytes 589832 | tf_op jit(solution)/shard_map/ppermute | solution.py:570
  27.5 7.6 %collective-permute-start.5 = (f16[6,128,128]{2,1,0:T(8,128)(2,1)S(1)}, f16[6,128,128]{2,1,0:T(8,128)(2,1)}, u32[]{:S(2)}, u32[]{:S(2)}) collective-permute-start(f16[6,128,128]{2,1,0:T(8,128)(2,1)S(1)} %add_convert_fusion.4), channel_id=1, source_target_pairs={{0,2},{1,3},{2,4},{3,5},{4,6},{5,7},{8,10},{9,11},{10,12},{11,13},... | collective-permute-start | bytes 589832 | tf_op jit(solution)/shard_map/ppermute | solution.py:570
  32.6 44.8 %collective-permute-start.2 = (f32[24,128,128]{2,1,0:T(8,128)}, f32[24,128,128]{2,1,0:T(8,128)S(1)}, u32[]{:S(2)}, u32[]{:S(2)}) collective-permute-start(f32[24,128,128]{2,1,0:T(8,128)} %get-tuple-element.22), channel_id=1, source_target_pairs={{0,1},{1,0},{2,3},{3,2},{4,5},{5,4},{6,7},{7,6},{8,9},{9,8},{10,11... | collective-permute-start | bytes 4718600 | tf_op jit(solution)/shard_map/ppermute | solution.py:546
  36.2 7.7 %collective-permute-start.6 = (f16[6,128,128]{2,1,0:T(8,128)(2,1)S(1)}, f16[6,128,128]{2,1,0:T(8,128)(2,1)}, u32[]{:S(2)}, u32[]{:S(2)}) collective-permute-start(f16[6,128,128]{2,1,0:T(8,128)(2,1)S(1)} %add_convert_fusion.3), channel_id=1, source_target_pairs={{0,2},{1,3},{2,4},{3,5},{4,6},{5,7},{8,10},{9,11},{10,12},{11,13},... | collective-permute-start | bytes 589832 | tf_op jit(solution)/shard_map/ppermute | solution.py:570
  45.1 1.9 %collective-permute-start.7 = (f16[6,128,128]{2,1,0:T(8,128)(2,1)S(1)}, f16[6,128,128]{2,1,0:T(8,128)(2,1)}, u32[]{:S(2)}, u32[]{:S(2)}) collective-permute-start(f16[6,128,128]{2,1,0:T(8,128)(2,1)S(1)} %add_convert_fusion.2), channel_id=1, source_target_pairs={{2,4},{3,5},{4,6},{5,7},{10,12},{11,13},{12,14},{13,15},{18,20},{1... | collective-permute-start | bytes 589832 | tf_op jit(solution)/shard_map/ppermute | solution.py:570
  46.4 3.1 %collective-permute-start.9 = (f16[6,128,128]{2,1,0:T(8,128)(2,1)S(1)}, f16[6,128,128]{2,1,0:T(8,128)(2,1)}, u32[]{:S(2)}, u32[]{:S(2)}) collective-permute-start(f16[6,128,128]{2,1,0:T(8,128)(2,1)S(1)} %collective-permute-done.3), channel_id=1, source_target_pairs={{0,1},{1,0},{2,3},{3,2},{4,5},{5,4},{6,7},{7,6},{8,9},{9,8},{10,11... | collective-permute-start | bytes 589832 | tf_op jit(solution)/shard_map/ppermute | solution.py:546
  46.4 3.6 %collective-permute-start.10 = (f16[6,128,128]{2,1,0:T(8,128)(2,1)S(1)}, f16[6,128,128]{2,1,0:T(8,128)(2,1)S(1)}, u32[]{:S(2)}, u32[]{:S(2)}) collective-permute-start(f16[6,128,128]{2,1,0:T(8,128)(2,1)S(1)} %collective-permute-done.4), channel_id=1, source_target_pairs={{0,1},{1,0},{2,3},{3,2},{4,5},{5,4},{6,7},{7,6},{8,9},{9,8},{10,11... | collective-permute-start | bytes 589832 | tf_op jit(solution)/shard_map/ppermute | solution.py:546
  48.1 2.6 %collective-permute-start.8 = (f16[6,128,128]{2,1,0:T(8,128)(2,1)S(1)}, f16[6,128,128]{2,1,0:T(8,128)(2,1)}, u32[]{:S(2)}, u32[]{:S(2)}) collective-permute-start(f16[6,128,128]{2,1,0:T(8,128)(2,1)S(1)} %add_convert_fusion.1), channel_id=1, source_target_pairs={{4,6},{5,7},{12,14},{13,15},{20,22},{21,23},{28,30},{29,31}} | collective-permute-start | bytes 589832 | tf_op jit(solution)/shard_map/ppermute | solution.py:570
  49.5 21.9 %collective-permute-start.11 = (f16[6,128,128]{2,1,0:T(8,128)(2,1)}, f16[6,128,128]{2,1,0:T(8,128)(2,1)}, u32[]{:S(2)}, u32[]{:S(2)}) collective-permute-start(f16[6,128,128]{2,1,0:T(8,128)(2,1)} %collective-permute-done.5), channel_id=1, source_target_pairs={{0,1},{1,0},{2,3},{3,2},{4,5},{5,4},{6,7},{7,6},{8,9},{9,8},{10,11... | collective-permute-start | bytes 589832 | tf_op jit(solution)/shard_map/ppermute | solution.py:546
  49.5 23.9 %collective-permute-start.12 = (f16[6,128,128]{2,1,0:T(8,128)(2,1)}, f16[6,128,128]{2,1,0:T(8,128)(2,1)}, u32[]{:S(2)}, u32[]{:S(2)}) collective-permute-start(f16[6,128,128]{2,1,0:T(8,128)(2,1)} %collective-permute-done.6), channel_id=1, source_target_pairs={{0,1},{1,0},{2,3},{3,2},{4,5},{5,4},{6,7},{7,6},{8,9},{9,8},{10,11... | collective-permute-start | bytes 589832 | tf_op jit(solution)/shard_map/ppermute | solution.py:546
  50.7 24.7 %collective-permute-start.13 = (f16[6,128,128]{2,1,0:T(8,128)(2,1)}, f16[6,128,128]{2,1,0:T(8,128)(2,1)}, u32[]{:S(2)}, u32[]{:S(2)}) collective-permute-start(f16[6,128,128]{2,1,0:T(8,128)(2,1)} %collective-permute-done.7), channel_id=1, source_target_pairs={{0,1},{1,0},{2,3},{3,2},{4,5},{5,4},{6,7},{7,6},{8,9},{9,8},{10,11... | collective-permute-start | bytes 589832 | tf_op jit(solution)/shard_map/ppermute | solution.py:546
  50.7 25.6 %collective-permute-start.14 = (f16[6,128,128]{2,1,0:T(8,128)(2,1)}, f16[6,128,128]{2,1,0:T(8,128)(2,1)}, u32[]{:S(2)}, u32[]{:S(2)}) collective-permute-start(f16[6,128,128]{2,1,0:T(8,128)(2,1)} %collective-permute-done.8), channel_id=1, source_target_pairs={{0,1},{1,0},{2,3},{3,2},{4,5},{5,4},{6,7},{7,6},{8,9},{9,8},{10,11... | collective-permute-start | bytes 589832 | tf_op jit(solution)/shard_map/ppermute | solution.py:546
  72.3 5.1 %copy-start.10 = (f32[16,6144]{1,0:T(8,128)S(1)}, f32[16,6144]{1,0:T(8,128)}, u32[]{:S(2)}) copy-start(f32[16,6144]{1,0:T(8,128)} %get-tuple-element.25.refs_3_) | copy-start | bytes 1179652
  72.3 5.1 %copy-start.11 = (f32[16,6144]{1,0:T(8,128)S(1)}, f32[16,6144]{1,0:T(8,128)}, u32[]{:S(2)}) copy-start(f32[16,6144]{1,0:T(8,128)} %get-tuple-element.26.refs_4_) | copy-start | bytes 1179652
  72.3 5.1 %copy-start.15 = (f32[48,128]{1,0:T(8,128)S(1)}, f32[48,128]{1,0:T(8,128)}, u32[]{:S(2)}) copy-start(f32[48,128]{1,0:T(8,128)} %copy-done.14) | copy-start | bytes 73732
  72.3 5.1 %copy-start.16 = (bf16[16,6144]{1,0:T(8,128)(2,1)S(1)}, bf16[16,6144]{1,0:T(8,128)(2,1)}, u32[]{:S(2)}) copy-start(bf16[16,6144]{1,0:T(8,128)(2,1)} %get-tuple-element.24.refs_2_) | copy-start | bytes 589828
  72.3 5.1 %copy-start.17 = (f32[1,6144]{1,0:T(1,128)S(1)}, f32[1,6144]{1,0:T(1,128)}, u32[]{:S(2)}) copy-start(f32[1,6144]{1,0:T(1,128)} %refs_20_.1) | copy-start | bytes 73732
  72.3 5.1 %copy-start.18 = (f32[1,6144]{1,0:T(1,128)S(1)}, f32[1,6144]{1,0:T(1,128)}, u32[]{:S(2)}) copy-start(f32[1,6144]{1,0:T(1,128)} %refs_21_.1) | copy-start | bytes 73732
  72.3 5.1 %copy-start.21 = (f32[16,48]{1,0:T(8,128)S(1)}, f32[16,48]{1,0:T(8,128)}, u32[]{:S(2)}) copy-start(f32[16,48]{1,0:T(8,128)} %get-tuple-element.23.refs_1_) | copy-start | bytes 9220
  76.3 7.7 %copy-start.5 = (f32[6,128,128]{2,1,0:T(8,128)}, f32[6,128,128]{2,1,0:T(8,128)S(1)}, u32[]{:S(2)}) copy-start(f32[6,128,128]{2,1,0:T(8,128)S(1)} %convert_element_type.84.refs_19_.refs_18_) | copy-start | bytes 1179652
  77.4 6.6 %copy-start.7 = (f32[6,128,128]{2,1,0:T(8,128)}, f32[6,128,128]{2,1,0:T(8,128)S(1)}, u32[]{:S(2)}) copy-start(f32[6,128,128]{2,1,0:T(8,128)S(1)} %convert_element_type.85.refs_20_.refs_19_) | copy-start | bytes 1179652
  84.8 18.0 %collective-permute-start.18 = (bf16[16,6144]{1,0:T(8,128)(2,1)}, bf16[16,6144]{1,0:T(8,128)(2,1)}, u32[]{:S(2)}, u32[]{:S(2)}) collective-permute-start(bf16[16,6144]{1,0:T(8,128)(2,1)} %get-tuple-element.30.refs_0_), channel_id=1, source_target_pairs={{0,6},{1,7},{2,0},{3,1},{4,2},{5,3},{6,4},{7,5},{8,14},{9,15},{10,... | collective-permute-start | bytes 589832 | tf_op jit(solution)/shard_map/ppermute | solution.py:644
  97.1 16.7 %collective-permute-start.17 = (bf16[16,6144]{1,0:T(8,128)(2,1)}, bf16[16,6144]{1,0:T(8,128)(2,1)}, u32[]{:S(2)}, u32[]{:S(2)}) collective-permute-start(bf16[16,6144]{1,0:T(8,128)(2,1)} %get-tuple-element.30.refs_0_), channel_id=1, source_target_pairs={{0,4},{1,5},{2,6},{3,7},{4,0},{5,1},{6,2},{7,3},{8,12},{9,13},{10,... | collective-permute-start | bytes 589832 | tf_op jit(solution)/shard_map/ppermute | solution.py:644
  97.1 16.7 %collective-permute-start.16 = (bf16[16,6144]{1,0:T(8,128)(2,1)}, bf16[16,6144]{1,0:T(8,128)(2,1)}, u32[]{:S(2)}, u32[]{:S(2)}) collective-permute-start(bf16[16,6144]{1,0:T(8,128)(2,1)} %get-tuple-element.30.refs_0_), channel_id=1, source_target_pairs={{0,2},{1,3},{2,4},{3,5},{4,6},{5,7},{6,0},{7,1},{8,10},{9,11},{10,... | collective-permute-start | bytes 589832 | tf_op jit(solution)/shard_map/ppermute | solution.py:644
  97.7 22.1 %collective-permute-start.19 = (bf16[16,6144]{1,0:T(8,128)(2,1)}, bf16[16,6144]{1,0:T(8,128)(2,1)}, u32[]{:S(2)}, u32[]{:S(2)}) collective-permute-start(bf16[16,6144]{1,0:T(8,128)(2,1)} %get-tuple-element.30.refs_0_), channel_id=1, source_target_pairs={{0,1},{1,0},{2,3},{3,2},{4,5},{5,4},{6,7},{7,6},{8,9},{9,8},{10,11... | collective-permute-start | bytes 589832 | tf_op jit(solution)/shard_map/ppermute | solution.py:546
  102.8 17.0 %collective-permute-start.22 = (bf16[16,6144]{1,0:T(8,128)(2,1)}, bf16[16,6144]{1,0:T(8,128)(2,1)}, u32[]{:S(2)}, u32[]{:S(2)}) collective-permute-start(bf16[16,6144]{1,0:T(8,128)(2,1)} %collective-permute-done.18.refs_3_), channel_id=1, source_target_pairs={{0,1},{1,0},{2,3},{3,2},{4,5},{5,4},{6,7},{7,6},{8,9},{9,8},{10,11... | collective-permute-start | bytes 589832 | tf_op jit(solution)/shard_map/ppermute | solution.py:546
  113.8 6.0 %collective-permute-start.21 = (bf16[16,6144]{1,0:T(8,128)(2,1)}, bf16[16,6144]{1,0:T(8,128)(2,1)}, u32[]{:S(2)}, u32[]{:S(2)}) collective-permute-start(bf16[16,6144]{1,0:T(8,128)(2,1)} %collective-permute-done.17.refs_2_), channel_id=1, source_target_pairs={{0,1},{1,0},{2,3},{3,2},{4,5},{5,4},{6,7},{7,6},{8,9},{9,8},{10,11... | collective-permute-start | bytes 589832 | tf_op jit(solution)/shard_map/ppermute | solution.py:546
  113.8 6.0 %collective-permute-start.20 = (bf16[16,6144]{1,0:T(8,128)(2,1)}, bf16[16,6144]{1,0:T(8,128)(2,1)}, u32[]{:S(2)}, u32[]{:S(2)}) collective-permute-start(bf16[16,6144]{1,0:T(8,128)(2,1)} %collective-permute-done.16.refs_1_), channel_id=1, source_target_pairs={{0,1},{1,0},{2,3},{3,2},{4,5},{5,4},{6,7},{7,6},{8,9},{9,8},{10,11... | collective-permute-start | bytes 589832 | tf_op jit(solution)/shard_map/ppermute | solution.py:546
  119.8 4.5 %copy-start = (bf16[1,128,6144]{2,1,0:T(8,128)(2,1)S(1)}, bf16[1,128,6144]{2,1,0:T(8,128)(2,1)}, u32[]{:S(2)}) copy-start(bf16[1,128,6144]{2,1,0:T(8,128)(2,1)} %param.12) | copy-start | bytes 4718596
  119.8 4.5 %copy-start.1 = (f32[128,2048]{1,0:T(8,128)S(1)}, f32[128,2048]{1,0:T(8,128)}, u32[]{:S(2)}) copy-start(f32[128,2048]{1,0:T(8,128)} %intra_attention.5.refs_5_.refs_7_) | copy-start | bytes 3145732
  119.8 4.5 %copy-start.2 = (f32[128,2048]{1,0:T(8,128)S(1)}, f32[128,2048]{1,0:T(8,128)}, u32[]{:S(2)}) copy-start(f32[128,2048]{1,0:T(8,128)} %intra_attention.4.refs_4_.refs_6_) | copy-start | bytes 3145732
  119.9 4.5 %copy-start.3 = (f32[128,2048]{1,0:T(8,128)S(1)}, f32[128,2048]{1,0:T(8,128)}, u32[]{:S(2)}) copy-start(f32[128,2048]{1,0:T(8,128)} %intra_attention.3.refs_3_.refs_5_) | copy-start | bytes 3145732
  119.9 4.5 %copy-start.4 = (bf16[1,128,6144]{2,1,0:T(8,128)(2,1)S(1)}, bf16[1,128,6144]{2,1,0:T(8,128)(2,1)}, u32[]{:S(2)}) copy-start(bf16[1,128,6144]{2,1,0:T(8,128)(2,1)} %param.11) | copy-start | bytes 4718596
  119.9 4.5 %copy-start.6 = (f32[6,128,128]{2,1,0:T(8,128)S(1)}, f32[6,128,128]{2,1,0:T(8,128)}, u32[]{:S(2)}) copy-start(f32[6,128,128]{2,1,0:T(8,128)} %copy-done.5) | copy-start | bytes 1179652
  119.9 4.5 %copy-start.8 = (f32[6,128,128]{2,1,0:T(8,128)S(1)}, f32[6,128,128]{2,1,0:T(8,128)}, u32[]{:S(2)}) copy-start(f32[6,128,128]{2,1,0:T(8,128)} %copy-done.7) | copy-start | bytes 1179652
  124.2 9.0 %collective-permute-start.23 = (bf16[64,6144]{1,0:T(8,128)(2,1)S(1)}, bf16[64,6144]{1,0:T(8,128)(2,1)S(1)}, u32[]{:S(2)}, u32[]{:S(2)}) collective-permute-start(bf16[64,6144]{1,0:T(8,128)(2,1)S(1)} %get-tuple-element.34), channel_id=1, source_target_pairs={{0,1},{1,0},{2,3},{3,2},{4,5},{5,4},{6,7},{7,6},{8,9},{9,8},{10,11... | collective-permute-start | bytes 2359304 | tf_op jit(solution)/shard_map/ppermute | solution.py:546
  131.7 38.2 %collective-permute-start.15 = (bf16[128,6144]{1,0:T(8,128)(2,1)S(1)}, bf16[128,6144]{1,0:T(8,128)(2,1)S(1)}, u32[]{:S(2)}, u32[]{:S(2)}) collective-permute-start(bf16[128,6144]{1,0:T(8,128)(2,1)S(1)} %finish.1), channel_id=1, source_target_pairs={{0,8},{8,16},{16,24},{24,0},{1,9},{9,17},{17,25},{25,1},{2,10},{10... | collective-permute-start | bytes 4718600 | tf_op jit(solution)/shard_map/ppermute | solution.py:541
  133.3 17.7 %copy-start.13 = (f32[16,6144]{1,0:T(8,128)S(1)}, f32[16,6144]{1,0:T(8,128)}, u32[]{:S(2)}) copy-start(f32[16,6144]{1,0:T(8,128)} %copy-done.12) | copy-start | bytes 1179652
  133.3 17.7 %copy-start.19 = (f32[16,128]{1,0:T(8,128)S(1)}, f32[16,128]{1,0:T(8,128)}, u32[]{:S(2)}) copy-start(f32[16,128]{1,0:T(8,128)} %get-tuple-element.28.refs_1_) | copy-start | bytes 24580
  133.3 17.7 %copy-start.20 = (f32[16,128]{1,0:T(8,128)S(1)}, f32[16,128]{1,0:T(8,128)}, u32[]{:S(2)}) copy-start(f32[16,128]{1,0:T(8,128)} %get-tuple-element.29.refs_2_) | copy-start | bytes 24580
  133.5 9.8 %collective-permute-start.26 = (bf16[16,6144]{1,0:T(8,128)(2,1)S(1)}, bf16[16,6144]{1,0:T(8,128)(2,1)S(1)}, u32[]{:S(2)}, u32[]{:S(2)}) collective-permute-start(bf16[16,6144]{1,0:T(8,128)(2,1)S(1)} %get-tuple-element.45), channel_id=1, source_target_pairs={{0,2},{1,3},{2,4},{3,5},{4,6},{5,7},{6,0},{7,1},{8,10},{9,11},{10,... | collective-permute-start | bytes 589832 | tf_op jit(solution)/shard_map/ppermute | solution.py:655
  135.2 15.7 %collective-permute-start.25 = (bf16[16,6144]{1,0:T(8,128)(2,1)S(1)}, bf16[16,6144]{1,0:T(8,128)(2,1)S(1)}, u32[]{:S(2)}, u32[]{:S(2)}) collective-permute-start(bf16[16,6144]{1,0:T(8,128)(2,1)S(1)} %get-tuple-element.46), channel_id=1, source_target_pairs={{0,4},{1,5},{2,6},{3,7},{4,0},{5,1},{6,2},{7,3},{8,12},{9,13},{10,... | collective-permute-start | bytes 589832 | tf_op jit(solution)/shard_map/ppermute | solution.py:655
  137.2 13.7 %collective-permute-start.24 = (bf16[16,6144]{1,0:T(8,128)(2,1)S(1)}, bf16[16,6144]{1,0:T(8,128)(2,1)S(1)}, u32[]{:S(2)}, u32[]{:S(2)}) collective-permute-start(bf16[16,6144]{1,0:T(8,128)(2,1)S(1)} %get-tuple-element.47), channel_id=1, source_target_pairs={{0,6},{1,7},{2,0},{3,1},{4,2},{5,3},{6,4},{7,5},{8,14},{9,15},{10,... | collective-permute-start | bytes 589832 | tf_op jit(solution)/shard_map/ppermute | solution.py:655
  151.2 22.6 %collective-permute-start.27 = (bf16[16,6272]{1,0:T(8,128)(2,1)S(1)}, bf16[16,6272]{1,0:T(8,128)(2,1)S(1)}, u32[]{:S(2)}, u32[]{:S(2)}) collective-permute-start(bf16[16,6272]{1,0:T(8,128)(2,1)S(1)} %late_rows.1), channel_id=1, source_target_pairs={{0,8},{8,16},{16,24},{24,0},{1,9},{9,17},{17,25},{25,1},{2,10},{10... | collective-permute-start | bytes 602120 | tf_op jit(solution)/shard_map/ppermute | solution.py:541
  (5 other events, 11.2 us)

commit v6 on v4

--- a/solution.py
+++ b/solution.py
@@ -73,7 +73,8 @@
             fetch(kind, g).start()
     rates.wait()
     cum_ref[...] = cumul_rows(rate_ref)
-    decay_ref[...] = jnp.broadcast_to(jnp.exp(cum_ref[:, length - 1 :]), decay_ref.shape)
+    rows = pl.ds(pl.multiple_of(half_ref[0] * groups * GROUP, GROUP), groups * GROUP)
+    decay_ref[...] = jnp.broadcast_to(jnp.exp(cum_ref[rows, length - 1 :]), decay_ref.shape)
     decays = pltpu.make_async_copy(decay_ref, decay_hbm, sems.at[3, 1])
     decays.start()
     for g in range(groups):
@@ -104,14 +105,14 @@
         out_specs=[HBM_SPEC, HBM_SPEC],
         out_shape=[
             jax.ShapeDtypeStruct((heads // 2, HEAD, HEAD), F32),
-            jax.ShapeDtypeStruct((heads, HEAD), F32),
+            jax.ShapeDtypeStruct((heads // 2, HEAD), F32),
         ],
         scratch_shapes=[
             pltpu.VMEM((heads, length), F32),
             pltpu.VMEM((groups, length, GROUP * HEAD), BF16),
             pltpu.VMEM((groups, length, GROUP * HEAD), BF16),
             pltpu.VMEM((heads // 2, HEAD, HEAD), F32),
-            pltpu.VMEM((heads, HEAD), F32),
+            pltpu.VMEM((heads // 2, HEAD), F32),
             pltpu.VMEM((heads, length), F32),
             pltpu.SemaphoreType.DMA((4, max(groups, 2))),
         ],
@@ -119,7 +120,8 @@
     )(half, rate, keys, values)
 
 
-def intra_kernel(first, rate_ref, q_hbm, k_hbm, v_hbm, out_hbm, q_ref, k_ref, v_ref, out_ref, sems):
+def intra_kernel(first, rate_ref, q_hbm, k_hbm, v_hbm, *refs):
+    out_hbm, q_ref, k_ref, v_ref, out_ref, sems = refs[-6:]
     groups = sems.shape[1]
     length = rate_ref.shape[1]
     span = GROUP * HEAD
@@ -131,7 +133,7 @@
         )
 
     def store(g):
-        at = pl.ds(g * span, span)
+        at = pl.ds((first + g) * span, span)
         return pltpu.make_async_copy(out_ref.at[g], out_hbm.at[:, at], sems.at[3, g])
 
     for g in range(groups):
@@ -158,26 +160,26 @@
         store(g).wait()
 
 
-def intra_attention(part, parts, rate, queries, keys, values):
+def intra_attention(part, parts, rate, queries, keys, values, out):
     length, width = keys.shape
     groups = width // HEAD // GROUP // parts
     piece = (groups, length, GROUP * HEAD)
     return pl.pallas_call(
         lambda *refs: intra_kernel(part * groups, *refs),
-        in_specs=[VMEM_SPEC] + [HBM_SPEC] * 3,
+        in_specs=[VMEM_SPEC] + [HBM_SPEC] * (3 + len(out)),
         out_specs=HBM_SPEC,
-        out_shape=jax.ShapeDtypeStruct((length, width // parts), F32),
+        out_shape=jax.ShapeDtypeStruct((length, width), F32),
         scratch_shapes=[pltpu.VMEM(piece, BF16)] * 3
         + [pltpu.VMEM(piece, F32), pltpu.SemaphoreType.DMA((4, groups))],
+        input_output_aliases={4: 0} if out else {},
         name="intra_attention",
-    )(rate, queries, keys, values)
+    )(rate, queries, keys, values, *out)
 
 
 def select_kernel(
-    parts, experts_ref, weight_ref, rate_ref, q_ref, resid_ref, *refs
+    experts_ref, weight_ref, rate_ref, q_ref, resid_ref, intra_ref,
+    wcol_ref, token_ref, growth_ref, q_out, resid_out, intra_out, at_ref, at_smem, sem,
 ):
-    intra_refs = refs[:parts]
-    wcol_ref, token_ref, growth_ref, q_out, resid_out, intra_out, at_ref, at_smem, sem = refs[parts:]
     slots = wcol_ref.shape[0]
     length = experts_ref.shape[1]
     before = (
@@ -198,33 +200,32 @@
     at_ref[...] = jnp.broadcast_to(jnp.maximum(token, 0.0), at_ref.shape).astype(jnp.int32)
     known = pltpu.make_async_copy(at_ref, at_smem, sem)
     known.start()
-    growth_ref[...] = lax.dot_general(
+    growth = lax.dot_general(
         hot.astype(F32), jnp.exp(cumul_rows(rate_ref)), (((1,), (1,)), ((), ())),
         precision=lax.Precision.HIGHEST, preferred_element_type=F32,
     )
+    for head in range(growth.shape[1]):
+        growth_ref[:, head * HEAD : (head + 1) * HEAD] = jnp.broadcast_to(
+            growth[:, head : head + 1], (slots, HEAD)
+        )
     hot = hot.astype(BF16)
     q_out[...] = dot(hot, q_ref[...]).astype(BF16)
     resid_out[...] = dot(hot, resid_ref[...])
     known.wait()
     for s in range(slots):
-        row = pl.ds(at_smem[s, 0], 1)
-        for part, ref in enumerate(intra_refs):
-            cols = slice(part * ref.shape[1], (part + 1) * ref.shape[1])
-            intra_out[s : s + 1, cols] = ref[row, :]
+        intra_out[s : s + 1, :] = intra_ref[pl.ds(at_smem[s, 0], 1), :]
 
 
 def select(experts, weight, rate, queries, resid, intra):
     _, width = queries.shape
-    heads = width // HEAD
-    parts = len(intra)
-    return pl.pallas_call(
-        lambda *refs: select_kernel(parts, *refs),
-        in_specs=[VMEM_SPEC] * (5 + parts),
+    return pl.pallas_call(
+        select_kernel,
+        in_specs=[VMEM_SPEC] * 6,
         out_specs=[VMEM_SPEC] * 6,
         out_shape=[
             jax.ShapeDtypeStruct((CAP_SRC, 128), F32),
             jax.ShapeDtypeStruct((CAP_SRC, 128), F32),
-            jax.ShapeDtypeStruct((CAP_SRC, heads), F32),
+            jax.ShapeDtypeStruct((CAP_SRC, width), F32),
             jax.ShapeDtypeStruct((CAP_SRC, width), BF16),
             jax.ShapeDtypeStruct((CAP_SRC, width), F32),
             jax.ShapeDtypeStruct((CAP_SRC, width), F32),
@@ -235,50 +236,34 @@
             pltpu.SemaphoreType.DMA,
         ],
         name="select",
-    )(experts, weight, rate, queries, resid, *intra)
-
-
-def prefix_copies(core_ref, keeps, gots, state_ref, sems, chunks):
-    steps = len(keeps)
-    half = state_ref.shape[0] // 2
-    per = half // chunks
-
-    def states(n, c, late):
-        place = pl.multiple_of(lax.rem(core_ref[0] + n, 2) * half + c * per, per)
-        source = (keeps, gots)[n][c + late]
-        return pltpu.make_async_copy(source, state_ref.at[pl.ds(place, per)], sems.at[n, c])
-
+    )(experts, weight, rate, queries, resid, intra)
+
+
+def each_state(core_ref, keeps, gots, chunks, use):
+    steps, per = len(keeps), keeps[0].shape[0]
+    half = chunks * per
     for late in range(steps - chunks + 1):
 
         @pl.when(core_ref[1] == late)
         def _():
-            for c in range(chunks):
-                for n in range(2):
-                    states(n, c, late).start()
-
-    def wait(c):
-        for n in range(2):
-            states(n, c, 0).wait()
-
-    return wait
+            for n in range(2):
+                start = lax.rem(core_ref[0] + n, 2) * half
+                for c in range(chunks):
+                    for j in range(per):
+                        column = pl.multiple_of((start + c * per + j) * HEAD, HEAD)
+                        use(pl.ds(column, HEAD), (keeps, gots)[n][c + late][j])
 
 
 def rows_kernel(chunks, steps, core_ref, growth_ref, q_ref, resid_ref, intra_ref, *refs):
     keeps, gots, refs = refs[:steps], refs[steps : 2 * steps], refs[2 * steps :]
-    again_ref, mgain_ref, outbox_ref, picked_ref, state_ref, sems = refs
-    _, width = picked_ref.shape
-    heads = width // HEAD
-    half = heads // 2
-    per = half // chunks
-    wait = prefix_copies(core_ref, keeps, gots, state_ref, sems, chunks)
-    for c in range(chunks):
-        wait(c)
-        for head in [n * half + c * per + j for n in range(2) for j in range(per)]:
-            cols = slice(head * HEAD, (head + 1) * HEAD)
-            hi, lo = split(state_ref[head])
-            q = q_ref[:, cols]
-            value = growth_ref[:, head : head + 1] * (dot(q, hi) + dot(q, lo))
-            picked_ref[:, cols] = intra_ref[:, cols] + value
+    again_ref, mgain_ref, outbox_ref, picked_ref = refs
+
+    def use(cols, state):
+        hi, lo = split(state)
+        q = q_ref[:, cols]
+        picked_ref[:, cols] = intra_ref[:, cols] + growth_ref[:, cols] * (dot(q, hi) + dot(q, lo))
+
+    each_state(core_ref, keeps, gots, chunks, use)
     x = picked_ref[...]
     scale = lax.rsqrt(jnp.mean(x * x, axis=-1, keepdims=True) + 1e-06)
     hres = resid_ref[...] + x * scale * again_ref[...]
@@ -289,69 +274,33 @@
 
 def selected_rows(core, growth, queries, resid, intra, keeps, gots, attn_gain, moe_gain):
     slots, width = queries.shape
-    heads = width // HEAD
     steps = len(keeps)
+    args = [growth, queries, resid, intra, *keeps, *gots, attn_gain, moe_gain]
     return pl.pallas_call(
         lambda *refs: rows_kernel(CHUNKS, steps, *refs),
-        in_specs=[SMEM_SPEC] + [VMEM_SPEC] * 4 + [ANY_SPEC] * (2 * steps) + [VMEM_SPEC] * 2,
+        in_specs=[SMEM_SPEC] + [VMEM_SPEC] * len(args),
         out_specs=[VMEM_SPEC] * 2,
         out_shape=[pltpu.VMEM((slots, width), BF16), pltpu.VMEM((slots, width), F32)],
-        scratch_shapes=[
-            pltpu.VMEM((heads, HEAD, HEAD), F32),
-            pltpu.SemaphoreType.DMA((2, CHUNKS)),
-        ],
-        compiler_params=pltpu.CompilerParams(vmem_limit_bytes=16 << 20),
+        compiler_params=pltpu.CompilerParams(vmem_limit_bytes=8 << 20),
         name="selected_rows",
-    )(core, growth, queries, resid, intra, *keeps, *gots, attn_gain, moe_gain)
-
-
-def finish_kernel(parts, chunks, steps, core_ref, rate_ref, q_hbm, *refs):
-    intra_hbm, refs = refs[:parts], refs[parts:]
+    )(core, *[in_vmem(a) for a in args])
+
+
+def finish_kernel(chunks, steps, core_ref, rate_ref, q_ref, intra_ref, *refs):
     keeps, gots, refs = refs[:steps], refs[steps : 2 * steps], refs[2 * steps :]
-    (
-        resid_hbm, again_ref, early_ref,
-        attn_ref, q_ref, intra_ref, state_ref, resid_ref, scale_ref, sems, state_sems,
-    ) = refs
+    resid_ref, again_ref, early_ref, attn_ref, scale_ref = refs
     length, width = resid_ref.shape
-    heads = width // HEAD
-    groups = heads // GROUP
-    span = GROUP * HEAD
-
-    def copies(g):
-        at = pl.ds(g * span, span)
-        part, place = divmod(g * parts, groups)
-        place = place // parts
-        return [
-            pltpu.make_async_copy(q_hbm.at[:, at], q_ref.at[g], sems.at[0, g]),
-            pltpu.make_async_copy(
-                intra_hbm[part].at[:, pl.ds(place * span, span)], intra_ref.at[g], sems.at[1, g]
-            ),
-        ]
-
-    for g in range(groups):
-        for copy in copies(g):
-            copy.start()
-    wait = prefix_copies(core_ref, keeps, gots, state_ref, state_sems, chunks)
-    rest = pltpu.make_async_copy(resid_hbm, resid_ref, sems.at[2, 0])
-    rest.start()
     growth = jnp.exp(cumul_rows(rate_ref))
-    for head in range(heads):
+    for head in range(width // HEAD):
         across = jnp.broadcast_to(growth[head : head + 1, :], (length, length))
         scale_ref[:, head * HEAD : (head + 1) * HEAD] = across.T
-    for c in range(chunks):
-        wait(c)
-    for g in range(groups):
-        for copy in copies(g):
-            copy.wait()
-        for j in range(GROUP):
-            head = g * GROUP + j
-            mine = slice(j * HEAD, (j + 1) * HEAD)
-            cols = slice(head * HEAD, (head + 1) * HEAD)
-            hi, lo = split(state_ref[head])
-            q = q_ref[g, :, mine]
-            value = dot(q, hi) + dot(q, lo)
-            attn_ref[:, cols] = intra_ref[g, :, mine] + scale_ref[:, cols] * value
-    rest.wait()
+
+    def use(cols, state):
+        hi, lo = split(state)
+        q = q_ref[:, cols]
+        attn_ref[:, cols] = intra_ref[:, cols] + scale_ref[:, cols] * (dot(q, hi) + dot(q, lo))
+
+    each_state(core_ref, keeps, gots, chunks, use)
     rows = 16
 
     def norm(r, carry):
@@ -367,31 +316,17 @@
 
 def finish(core, rate, queries, intra, keeps, gots, resid, attn_gain):
     length, width = queries.shape
-    heads = width // HEAD
-    groups = heads // GROUP
-    parts, steps = len(intra), len(keeps)
-    args = [rate, queries, *intra, *keeps, *gots, resid, attn_gain]
-    return pl.pallas_call(
-        lambda *refs: finish_kernel(parts, CHUNKS, steps, *refs),
-        in_specs=[SMEM_SPEC, VMEM_SPEC]
-        + [HBM_SPEC] * (1 + parts)
-        + [ANY_SPEC] * (2 * steps)
-        + [HBM_SPEC, VMEM_SPEC],
+    steps = len(keeps)
+    args = [rate, queries, intra, *keeps, *gots, resid, attn_gain]
+    return pl.pallas_call(
+        lambda *refs: finish_kernel(CHUNKS, steps, *refs),
+        in_specs=[SMEM_SPEC] + [VMEM_SPEC] * len(args),
         out_specs=VMEM_SPEC,
         out_shape=pltpu.VMEM((length, width), BF16),
-        scratch_shapes=[
-            pltpu.VMEM((length, width), F32),
-            pltpu.VMEM((groups, length, GROUP * HEAD), BF16),
-            pltpu.VMEM((groups, length, GROUP * HEAD), F32),
-            pltpu.VMEM((heads, HEAD, HEAD), F32),
-            pltpu.VMEM((length, width), BF16),
-            pltpu.VMEM((length, width), F32),
-            pltpu.SemaphoreType.DMA((3, groups)),
-            pltpu.SemaphoreType.DMA((2, CHUNKS)),
-        ],
-        compiler_params=pltpu.CompilerParams(vmem_limit_bytes=32 << 20),
+        scratch_shapes=[pltpu.VMEM((length, width), F32), pltpu.VMEM((length, width), F32)],
+        compiler_params=pltpu.CompilerParams(vmem_limit_bytes=14 << 20),
         name="finish",
-    )(core, *args)
+    )(core, *[in_vmem(a) for a in args])
 
 
 def late_kernel(count, picked_ref, wcol_ref, token_ref, *refs):
@@ -585,12 +520,9 @@
     core1 = core.astype(jnp.int32)[None]
     turned = rate.T
 
-    other, decay = half_state(1 - core1, turned, keys, values)
-    partner = swapped(other)
-    decay_partner = swapped(decay)
-    mine, _ = half_state(core1, turned, keys, values)
-    decay = lax.dynamic_slice_in_dim(decay, core * half, half, 0)
-    decay_partner = lax.dynamic_slice_in_dim(decay_partner, core * half, half, 0)
+    other, decay_other = half_state(1 - core1, turned, keys, values)
+    partner, decay_partner = swapped(other), swapped(decay_other)
+    mine, decay = half_state(core1, turned, keys, values)
     scale = 1.0
     while 36.0 * count * length * scale > 65000.0:
         scale = scale / 2
@@ -600,7 +532,8 @@
     late_by = jnp.maximum(chip - 1, 0)
     intra = []
     for part in range(PARTS):
-        intra.append(intra_attention(part, PARTS, turned, queries, keys, values))
+        intra = [intra_attention(part, PARTS, turned, queries, keys, values, intra)]
+    intra = intra[0]
     flying = count // SHARDS
     if flying > 1:
         keep, got = (
@@ -609,7 +542,7 @@
         )
         prefix = jnp.where(first, jnp.concatenate([keep, got]), jnp.concatenate([got, keep]))
         return many_experts(
-            flying, rate, queries, jnp.concatenate(intra, axis=1), prefix, resid,
+            flying, rate, queries, intra, prefix, resid,
             attn_gain, moe_gain, experts, weight, up, down,
         )
     where = jnp.stack([core, late_by]).astype(jnp.int32)

time: 168 us -> 166 us (0.988)
  Pallas kernels: 43.9 us -> 41.5 us
    unnamed x36 -> x30, local copies, waits for them, and re-layouts: 5.14 us -> 5.43 us
  transfers between devices with their start and end apart: 27 -> 27, of which waited for: 11 -> 11; matrix products, arithmetic and copies ran while one was open for 2% -> 2% of each run, Pallas kernels for 20% -> 19%
where the time goes in v6:
time: 166 us; the launch traced here: 165 us
  waiting for transfers between devices  61.5 us (37%)
  starting transfers between devices  47 us (28%)
  Pallas kernels  41.5 us (25%)
  other arithmetic  9.17 us (6%)
  local copies, waits for them, and re-layouts  5.48 us (3%)
    ppermute x2, waiting for transfers between devices, passed_along(): return lax.ppermute(value, axis, pairs)  21 us
    ppermute x6, starting transfers between devices, chain_prefix(): before = lax.ppermute(gone, 'ctx', pairs)  19.3 us
    ppermute x3, waiting for transfers between devices, layer(): lax.ppermute(outbox, 'ctx', [(i, (i + 2 * d) % count) for i in range(coun...  15.3 us
    ppermute x3, starting transfers between devices, layer(): lax.ppermute(outbox, 'ctx', [(i, (i + 2 * d) % count) for i in range(coun...  15.1 us
    ppermute x6, waiting for transfers between devices, chain_prefix(): before = lax.ppermute(gone, 'ctx', pairs)  14.3 us
    pallas_call x3, Pallas kernels, intra_attention(): pl.pallas_call(lambda *refs: intra_kernel(part * groups, *refs), in_specs...  12.2 us
    ppermute x3, waiting for transfers between devices, layer(): lax.ppermute(pair[d], 'ctx', [(i, (i - 2 * d) % count) for i in range(cou...  10.8 us
    ppermute x3, starting transfers between devices, layer(): lax.ppermute(pair[d], 'ctx', [(i, (i - 2 * d) % count) for i in range(cou...  6.66 us
  transfers between devices with their start and end apart: 27, of which 11 were waited for; matrix products, arithmetic and copies ran while one was open for 2% of the time, Pallas kernels for 19%

profile of v6, /device:TPU:0, one launch (start us, length us, event | category | flops | bytes accessed | tf_op | source)
XLA Modules:
  0.0 165.3 jit_solution(12497408251737374814)
XLA Ops:
  0.0 3.0 %half_state.2 = (f32[24,128,128]{2,1,0:T(8,128)}, f32[24,128]{1,0:T(8,128)}) custom-call(s32[1]{0:T(128)S(6)} %sub.54.half_ref, f32[48,128]{1,0:T(8,128)} %bitcast.25, bf16[128,6144]{1,0:T(8,128)(2,1)} %bitcast.32, bf16[128,6144]{1,0:T(8,128)(2,1)} %bitcast.37), custom_call_target="tpu_custom_call" | custom-call | tf_op jit(solution)/shard_map/half_state/pallas_call | solution.py:102
  3.0 0.6 collective-permute-start.1
  3.6 3.0 %half_state.3 = (f32[24,128,128]{2,1,0:T(8,128)}, f32[24,128]{1,0:T(8,128)}) custom-call(s32[1]{0:T(128)} %bitcast.half_ref, f32[48,128]{1,0:T(8,128)} %bitcast.26, bf16[128,6144]{1,0:T(8,128)(2,1)} %bitcast.33, bf16[128,6144]{1,0:T(8,128)(2,1)} %bitcast.38), custom_call_target="tpu_custom_call" | custom-call | tf_op jit(solution)/shard_map/half_state/pallas_call | solution.py:102
  6.8 1.0 fusion.11
  7.9 1.4 add_convert_fusion.6
  9.3 4.8 %collective-permute-start.2 = (f16[6,128,128]{2,1,0:T(8,128)(2,1)S(1)}, f16[6,128,128]{2,1,0:T(8,128)(2,1)S(1)}, u32[]{:S(2)}, u32[]{:S(2)}) collective-permute-start(f16[6,128,128]{2,1,0:T(8,128)(2,1)S(1)} %add_convert_fusion.6), channel_id=1, source_target_pairs={{0,2},{1,3},{8,10},{9,11},{16,18},{17,19},{24,26},{25,27}} | collective-permute-start | bytes 589832 | tf_op jit(solution)/shard_map/ppermute | solution.py:485
  14.1 4.4 %collective-permute-done.2 = f16[6,128,128]{2,1,0:T(8,128)(2,1)S(1)} collective-permute-done((f16[6,128,128]{2,1,0:T(8,128)(2,1)S(1)}, f16[6,128,128]{2,1,0:T(8,128)(2,1)S(1)}, u32[]{:S(2)}, u32[]{:S(2)}) %collective-permute-start.2) | collective-permute-done | bytes 196640 | tf_op jit(solution)/shard_map/ppermute | solution.py:485
  18.5 1.1 add_convert_fusion.5
  19.6 4.4 %collective-permute-start.3 = (f16[6,128,128]{2,1,0:T(8,128)(2,1)S(1)}, f16[6,128,128]{2,1,0:T(8,128)(2,1)S(1)}, u32[]{:S(2)}, u32[]{:S(2)}) collective-permute-start(f16[6,128,128]{2,1,0:T(8,128)(2,1)S(1)} %add_convert_fusion.5), channel_id=1, source_target_pairs={{0,2},{1,3},{2,4},{3,5},{8,10},{9,11},{10,12},{11,13},{16,18},{17,... | collective-permute-start | bytes 589832 | tf_op jit(solution)/shard_map/ppermute | solution.py:485
  24.1 3.5 %collective-permute-done.3 = f16[6,128,128]{2,1,0:T(8,128)(2,1)S(1)} collective-permute-done((f16[6,128,128]{2,1,0:T(8,128)(2,1)S(1)}, f16[6,128,128]{2,1,0:T(8,128)(2,1)S(1)}, u32[]{:S(2)}, u32[]{:S(2)}) %collective-permute-start.3) | collective-permute-done | bytes 196640 | tf_op jit(solution)/shard_map/ppermute | solution.py:485
  27.8 4.4 %collective-permute-start.4 = (f16[6,128,128]{2,1,0:T(8,128)(2,1)S(1)}, f16[6,128,128]{2,1,0:T(8,128)(2,1)S(1)}, u32[]{:S(2)}, u32[]{:S(2)}) collective-permute-start(f16[6,128,128]{2,1,0:T(8,128)(2,1)S(1)} %get-tuple-element.38), channel_id=1, source_target_pairs={{0,2},{1,3},{2,4},{3,5},{4,6},{5,7},{8,10},{9,11},{10,12},{11,13},... | collective-permute-start | bytes 589832 | tf_op jit(solution)/shard_map/ppermute | solution.py:485
  32.2 3.2 %collective-permute-done.4 = f16[6,128,128]{2,1,0:T(8,128)(2,1)S(1)} collective-permute-done((f16[6,128,128]{2,1,0:T(8,128)(2,1)S(1)}, f16[6,128,128]{2,1,0:T(8,128)(2,1)S(1)}, u32[]{:S(2)}, u32[]{:S(2)}) %collective-permute-start.4) | collective-permute-done | bytes 196640 | tf_op jit(solution)/shard_map/ppermute | solution.py:485
  35.4 1.0 convert_select_fusion.6
  36.3 4.4 %collective-permute-start.5 = (f16[6,128,128]{2,1,0:T(8,128)(2,1)S(1)}, f16[6,128,128]{2,1,0:T(8,128)(2,1)S(1)}, u32[]{:S(2)}, u32[]{:S(2)}) collective-permute-start(f16[6,128,128]{2,1,0:T(8,128)(2,1)S(1)} %get-tuple-element.40), channel_id=1, source_target_pairs={{0,2},{1,3},{2,4},{3,5},{4,6},{5,7},{8,10},{9,11},{10,12},{11,13},... | collective-permute-start | bytes 589832 | tf_op jit(solution)/shard_map/ppermute | solution.py:485
  40.7 3.2 %collective-permute-done.5 = f16[6,128,128]{2,1,0:T(8,128)(2,1)S(1)} collective-permute-done((f16[6,128,128]{2,1,0:T(8,128)(2,1)S(1)}, f16[6,128,128]{2,1,0:T(8,128)(2,1)S(1)}, u32[]{:S(2)}, u32[]{:S(2)}) %collective-permute-start.5) | collective-permute-done | bytes 196640 | tf_op jit(solution)/shard_map/ppermute | solution.py:485
  43.9 1.0 convert_select_fusion.4
  44.9 0.7 collective-permute-start.6
  45.6 1.0 convert_select_fusion.2
  46.5 0.7 collective-permute-start.7
  48.3 2.2 %convert_select_fusion = (f32[6,128,128]{2,1,0:T(8,128)}, f32[6,128,128]{2,1,0:T(8,128)S(1)}, f32[6,128,128]{2,1,0:T(8,128)S(1)}, f32[6,128,128]{2,1,0:T(8,128)}) fusion(f16[6,128,128]{2,1,0:T(8,128)(2,1)S(1)} %collective-permute-done.7, f32[6,128]{1,0:T(8,128)S(1)} %get-tuple-element.93, pred[]{:T(512)S(6)} %eq.5, f32[24,128,128]{2,1,0:T(8,128)} %copy-done.13, ...), kind=kLoop, calls=%fused_computation.1 | loop fusion | flops 1179648 | bytes 3545097 | tf_op jit(solution)/shard_map/jit(_where)/select_n | solution.py:490
  51.1 4.1 %intra_attention.3.refs_4_ = f32[128,6144]{1,0:T(8,128)} custom-call(f32[48,128]{1,0:T(8,128)} %bitcast.27, bf16[128,6144]{1,0:T(8,128)(2,1)} %bitcast.18, bf16[128,6144]{1,0:T(8,128)(2,1)} %bitcast.34, bf16[128,6144]{1,0:T(8,128)(2,1)} %bitcast.39), custom_call_target="tpu_custom_call" | custom-call | tf_op jit(solution)/shard_map/intra_attention/pallas_call | solution.py:167
  55.1 4.1 %intra_attention.4.refs_4_ = f32[128,6144]{1,0:T(8,128)} custom-call(f32[48,128]{1,0:T(8,128)} %bitcast.28, bf16[128,6144]{1,0:T(8,128)(2,1)} %bitcast.19, bf16[128,6144]{1,0:T(8,128)(2,1)} %bitcast.35, bf16[128,6144]{1,0:T(8,128)(2,1)} %bitcast.40, f32[128,6144]{1,0:T(8,128)} %intra_attention.3.refs_4_), custom_call_target="tpu_custom_call", output_to_operand_aliasing={{}: (4, {})} | custom-call | tf_op jit(solution)/shard_map/intra_attention/pallas_call | solution.py:167
  59.2 4.1 %intra_attention.5.refs_3_.intra_ref = f32[128,6144]{1,0:T(8,128)} custom-call(f32[48,128]{1,0:T(8,128)} %bitcast.29, bf16[128,6144]{1,0:T(8,128)(2,1)} %bitcast.20, bf16[128,6144]{1,0:T(8,128)(2,1)} %bitcast.36, bf16[128,6144]{1,0:T(8,128)(2,1)} %bitcast.41, f32[128,6144]{1,0:T(8,128)} %intra_attention.4.refs_4_), custom_call_target="tpu_custom_call", output_to_operand_aliasing={{}: (4, {})} | custom-call | tf_op jit(solution)/shard_map/intra_attention/pallas_call | solution.py:167
  63.3 5.0 %select.7 = (f32[16,128]{1,0:T(8,128)}, f32[16,128]{1,0:T(8,128)}, f32[16,6144]{1,0:T(8,128)}, bf16[16,6144]{1,0:T(8,128)(2,1)}, f32[16,6144]{1,0:T(8,128)}, /*index=5*/f32[16,6144]{1,0:T(8,128)}) custom-call(s32[2,128]{1,0:T(2,128)} %bitcast.44, f32[2,128]{1,0:T(2,128)} %bitcast.45, f32[48,128]{1,0:T(8,128)} %bitcast.30, bf16[128,6144]{1,0:T(8,128)(2,1)} %bitcast.21, ...), custom_call_target="tpu_custom_call" | custom-call | tf_op jit(solution)/shard_map/select/pallas_call | solution.py:221
  68.4 1.0 copy-done.4
  69.4 1.0 copy-done.5
  70.4 1.0 copy-done.6
  71.4 0.9 copy-done.7
  72.3 0.7 copy-done.8
  73.1 0.7 copy-done.10
  73.8 2.6 %selected_rows.1 = (bf16[16,6144]{1,0:T(8,128)(2,1)S(1)}, f32[16,6144]{1,0:T(8,128)S(1)}) custom-call(s32[2]{0:T(128)S(1)} %pad_add_fusion.refs_0_, f32[16,6144]{1,0:T(8,128)S(1)} %copy-done.4, bf16[16,6144]{1,0:T(8,128)(2,1)S(1)} %copy-done.7, f32[16,6144]{1,0:T(8,128)S(1)} %copy-done.5, f32[16,6144]{1,0:T(8,128)S(1)} %copy-done.6, ...), custom_call_target="tpu_custom_call" | custom-call | tf_op jit(solution)/shard_map/selected_rows/pallas_call | solution.py:279
  76.4 14.5 %collective-permute-start.17 = (bf16[16,6144]{1,0:T(8,128)(2,1)S(1)}, bf16[16,6144]{1,0:T(8,128)(2,1)S(1)}, u32[]{:S(2)}, u32[]{:S(2)}) collective-permute-start(bf16[16,6144]{1,0:T(8,128)(2,1)S(1)} %get-tuple-element.56.refs_0_), channel_id=1, source_target_pairs={{0,6},{1,7},{2,0},{3,1},{4,2},{5,3},{6,4},{7,5},{8,14},{9,15},{10,... | collective-permute-start | bytes 589832 | tf_op jit(solution)/shard_map/ppermute | solution.py:556
  90.8 0.6 collective-permute-start.15
  91.5 4.7 %collective-permute-done.17.refs_3_ = bf16[16,6144]{1,0:T(8,128)(2,1)S(1)} collective-permute-done((bf16[16,6144]{1,0:T(8,128)(2,1)S(1)}, bf16[16,6144]{1,0:T(8,128)(2,1)S(1)}, u32[]{:S(2)}, u32[]{:S(2)}) %collective-permute-start.17) | collective-permute-done | bytes 196640 | tf_op jit(solution)/shard_map/ppermute | solution.py:556
  96.2 10.5 %collective-permute-done.16.refs_2_ = bf16[16,6144]{1,0:T(8,128)(2,1)S(1)} collective-permute-done((bf16[16,6144]{1,0:T(8,128)(2,1)S(1)}, bf16[16,6144]{1,0:T(8,128)(2,1)S(1)}, u32[]{:S(2)}, u32[]{:S(2)}) %collective-permute-start.16) | collective-permute-done | bytes 196640 | tf_op jit(solution)/shard_map/ppermute | solution.py:556
  107.3 5.5 %fetch.1 = (bf16[6144,640]{1,0:T(8,128)(2,1)S(1)}, bf16[640,6144]{1,0:T(8,128)(2,1)S(1)}) custom-call(bf16[6144,640]{1,0:T(8,128)(2,1)} %bitcast.42, bf16[640,6144]{1,0:T(8,128)(2,1)} %bitcast.43), custom_call_target="tpu_custom_call" | custom-call | tf_op jit(solution)/shard_map/fetch/pallas_call | solution.py:402
  112.9 2.8 %expert_rows.1 = (bf16[64,6144]{1,0:T(8,128)(2,1)S(1)}, bf16[64,6144]{1,0:T(8,128)(2,1)S(1)}) custom-call(bf16[16,6144]{1,0:T(8,128)(2,1)S(1)} %get-tuple-element.56.refs_0_, bf16[16,6144]{1,0:T(8,128)(2,1)S(1)} %collective-permute-done.15.refs_1_, bf16[16,6144]{1,0:T(8,128)(2,1)S(1)} %collective-permute-done.16.refs_2_, ...), custom_call_target="tpu_custom_call" | custom-call | tf_op jit(solution)/shard_map/expert_rows/pallas_call | solution.py:434
  115.8 5.8 %finish.1 = bf16[128,6144]{1,0:T(8,128)(2,1)S(1)} custom-call(s32[2]{0:T(128)S(1)} %pad_add_fusion.refs_0_, f32[48,128]{1,0:T(8,128)S(1)} %bitcast.31, bf16[128,6144]{1,0:T(8,128)(2,1)S(1)} %bitcast.22, f32[128,6144]{1,0:T(8,128)S(1)} %copy-done, f32[6,128,128]{2,1,0:T(8,128)S(1)} %get-tuple-element.83.refs_4_.refs_5_, ...), custom_call_target="tpu_custom_call" | custom-call | tf_op jit(solution)/shard_map/finish/pallas_call | solution.py:321
  121.6 1.5 collective-permute-start.14
  123.4 1.8 %collective-permute-start.25 = (bf16[16,6144]{1,0:T(8,128)(2,1)S(1)}, bf16[16,6144]{1,0:T(8,128)(2,1)S(1)}, u32[]{:S(2)}, u32[]{:S(2)}) collective-permute-start(bf16[16,6144]{1,0:T(8,128)(2,1)S(1)} %get-tuple-element.89), channel_id=1, source_target_pairs={{0,2},{1,3},{2,4},{3,5},{4,6},{5,7},{6,0},{7,1},{8,10},{9,11},{10,... | collective-permute-start | bytes 589832 | tf_op jit(solution)/shard_map/ppermute | solution.py:567
  125.2 2.0 %collective-permute-start.24 = (bf16[16,6144]{1,0:T(8,128)(2,1)S(1)}, bf16[16,6144]{1,0:T(8,128)(2,1)S(1)}, u32[]{:S(2)}, u32[]{:S(2)}) collective-permute-start(bf16[16,6144]{1,0:T(8,128)(2,1)S(1)} %get-tuple-element.90), channel_id=1, source_target_pairs={{0,4},{1,5},{2,6},{3,7},{4,0},{5,1},{6,2},{7,3},{8,12},{9,13},{10,... | collective-permute-start | bytes 589832 | tf_op jit(solution)/shard_map/ppermute | solution.py:567
  127.2 2.8 %collective-permute-start.23 = (bf16[16,6144]{1,0:T(8,128)(2,1)S(1)}, bf16[16,6144]{1,0:T(8,128)(2,1)S(1)}, u32[]{:S(2)}, u32[]{:S(2)}) collective-permute-start(bf16[16,6144]{1,0:T(8,128)(2,1)S(1)} %get-tuple-element.91), channel_id=1, source_target_pairs={{0,6},{1,7},{2,0},{3,1},{4,2},{5,3},{6,4},{7,5},{8,14},{9,15},{10,... | collective-permute-start | bytes 589832 | tf_op jit(solution)/shard_map/ppermute | solution.py:567
  130.1 3.1 %collective-permute-done.25.refs_6_ = bf16[16,6144]{1,0:T(8,128)(2,1)S(1)} collective-permute-done((bf16[16,6144]{1,0:T(8,128)(2,1)S(1)}, bf16[16,6144]{1,0:T(8,128)(2,1)S(1)}, u32[]{:S(2)}, u32[]{:S(2)}) %collective-permute-start.25) | collective-permute-done | bytes 196640 | tf_op jit(solution)/shard_map/ppermute | solution.py:567
  133.2 7.6 %collective-permute-done.24.refs_5_ = bf16[16,6144]{1,0:T(8,128)(2,1)S(1)} collective-permute-done((bf16[16,6144]{1,0:T(8,128)(2,1)S(1)}, bf16[16,6144]{1,0:T(8,128)(2,1)S(1)}, u32[]{:S(2)}, u32[]{:S(2)}) %collective-permute-start.24) | collective-permute-done | bytes 196640 | tf_op jit(solution)/shard_map/ppermute | solution.py:567
  141.0 1.5 collective-permute-start.26
  142.6 17.2 %collective-permute-done.14.early_ref = bf16[128,6144]{1,0:T(8,128)(2,1)S(1)} collective-permute-done((bf16[128,6144]{1,0:T(8,128)(2,1)S(1)}, bf16[128,6144]{1,0:T(8,128)(2,1)S(1)}, u32[]{:S(2)}, u32[]{:S(2)}) %collective-permute-start.14) | collective-permute-done | bytes 1572896 | tf_op jit(solution)/shard_map/ppermute | solution.py:448
  159.8 3.8 %collective-permute-done.26.late_ref = bf16[16,6272]{1,0:T(8,128)(2,1)S(1)} collective-permute-done((bf16[16,6272]{1,0:T(8,128)(2,1)S(1)}, bf16[16,6272]{1,0:T(8,128)(2,1)S(1)}, u32[]{:S(2)}, u32[]{:S(2)}) %collective-permute-start.26) | collective-permute-done | bytes 200736 | tf_op jit(solution)/shard_map/ppermute | solution.py:448
  163.6 1.5 merged.1
  (59 shorter events, 3.2 us)
Async XLA Ops:
  3.0 4.9 %collective-permute-start.1 = (f32[24,128,128]{2,1,0:T(8,128)}, f32[24,128,128]{2,1,0:T(8,128)S(1)}, u32[]{:S(2)}, u32[]{:S(2)}) collective-permute-start(f32[24,128,128]{2,1,0:T(8,128)} %get-tuple-element.36), channel_id=1, source_target_pairs={{0,1},{1,0},{2,3},{3,2},{4,5},{5,4},{6,7},{7,6},{8,9},{9,8},{10,11... | collective-permute-start | bytes 4718600 | tf_op jit(solution)/shard_map/ppermute | solution.py:453
  3.6 3.3 %collective-permute-start = (f32[24,128]{1,0:T(8,128)}, f32[24,128]{1,0:T(8,128)S(1)}, u32[]{:S(2)}, u32[]{:S(2)}) collective-permute-start(f32[24,128]{1,0:T(8,128)} %get-tuple-element.33), channel_id=1, source_target_pairs={{0,1},{1,0},{2,3},{3,2},{4,5},{5,4},{6,7},{7,6},{8,9},{9,8},{10,11... | collective-permute-start | bytes 36872 | tf_op jit(solution)/shard_map/ppermute | solution.py:453
  6.7 20.9 %copy-start.14 = (f32[24,128,128]{2,1,0:T(8,128)S(1)}, f32[24,128,128]{2,1,0:T(8,128)}, u32[]{:S(2)}) copy-start(f32[24,128,128]{2,1,0:T(8,128)} %get-tuple-element.35) | copy-start | bytes 4718596
  7.9 37.7 %copy-start.13 = (f32[24,128,128]{2,1,0:T(8,128)}, f32[24,128,128]{2,1,0:T(8,128)S(1)}, u32[]{:S(2)}) copy-start(f32[24,128,128]{2,1,0:T(8,128)S(1)} %collective-permute-done.1) | copy-start | bytes 4718596
  9.3 9.3 %collective-permute-start.2 = (f16[6,128,128]{2,1,0:T(8,128)(2,1)S(1)}, f16[6,128,128]{2,1,0:T(8,128)(2,1)S(1)}, u32[]{:S(2)}, u32[]{:S(2)}) collective-permute-start(f16[6,128,128]{2,1,0:T(8,128)(2,1)S(1)} %add_convert_fusion.6), channel_id=1, source_target_pairs={{0,2},{1,3},{8,10},{9,11},{16,18},{17,19},{24,26},{25,27}} | collective-permute-start | bytes 589832 | tf_op jit(solution)/shard_map/ppermute | solution.py:485
  19.6 7.9 %collective-permute-start.3 = (f16[6,128,128]{2,1,0:T(8,128)(2,1)S(1)}, f16[6,128,128]{2,1,0:T(8,128)(2,1)S(1)}, u32[]{:S(2)}, u32[]{:S(2)}) collective-permute-start(f16[6,128,128]{2,1,0:T(8,128)(2,1)S(1)} %add_convert_fusion.5), channel_id=1, source_target_pairs={{0,2},{1,3},{2,4},{3,5},{8,10},{9,11},{10,12},{11,13},{16,18},{17,... | collective-permute-start | bytes 589832 | tf_op jit(solution)/shard_map/ppermute | solution.py:485
  27.8 7.6 %collective-permute-start.4 = (f16[6,128,128]{2,1,0:T(8,128)(2,1)S(1)}, f16[6,128,128]{2,1,0:T(8,128)(2,1)S(1)}, u32[]{:S(2)}, u32[]{:S(2)}) collective-permute-start(f16[6,128,128]{2,1,0:T(8,128)(2,1)S(1)} %get-tuple-element.38), channel_id=1, source_target_pairs={{0,2},{1,3},{2,4},{3,5},{4,6},{5,7},{8,10},{9,11},{10,12},{11,13},... | collective-permute-start | bytes 589832 | tf_op jit(solution)/shard_map/ppermute | solution.py:485
  36.3 7.6 %collective-permute-start.5 = (f16[6,128,128]{2,1,0:T(8,128)(2,1)S(1)}, f16[6,128,128]{2,1,0:T(8,128)(2,1)S(1)}, u32[]{:S(2)}, u32[]{:S(2)}) collective-permute-start(f16[6,128,128]{2,1,0:T(8,128)(2,1)S(1)} %get-tuple-element.40), channel_id=1, source_target_pairs={{0,2},{1,3},{2,4},{3,5},{4,6},{5,7},{8,10},{9,11},{10,12},{11,13},... | collective-permute-start | bytes 589832 | tf_op jit(solution)/shard_map/ppermute | solution.py:485
  44.9 0.7 collective-permute-start.6
  46.5 1.8 %collective-permute-start.7 = (f16[6,128,128]{2,1,0:T(8,128)(2,1)S(1)}, f16[6,128,128]{2,1,0:T(8,128)(2,1)S(1)}, u32[]{:S(2)}, u32[]{:S(2)}) collective-permute-start(f16[6,128,128]{2,1,0:T(8,128)(2,1)S(1)} %get-tuple-element.44), channel_id=1, source_target_pairs={{4,6},{5,7},{12,14},{13,15},{20,22},{21,23},{28,30},{29,31}} | collective-permute-start | bytes 589832 | tf_op jit(solution)/shard_map/ppermute | solution.py:485
  47.2 3.4 %collective-permute-start.9 = (f32[6,128,128]{2,1,0:T(8,128)S(1)}, f32[6,128,128]{2,1,0:T(8,128)S(1)}, u32[]{:S(2)}, u32[]{:S(2)}) collective-permute-start(f32[6,128,128]{2,1,0:T(8,128)S(1)} %get-tuple-element.45), channel_id=1, source_target_pairs={{0,1},{1,0},{2,3},{3,2},{4,5},{5,4},{6,7},{7,6},{8,9},{9,8},{10,11... | collective-permute-start | bytes 1179656 | tf_op jit(solution)/shard_map/ppermute | solution.py:453
  47.3 21.1 %collective-permute-start.10 = (f32[6,128,128]{2,1,0:T(8,128)}, f32[6,128,128]{2,1,0:T(8,128)S(1)}, u32[]{:S(2)}, u32[]{:S(2)}) collective-permute-start(f32[6,128,128]{2,1,0:T(8,128)} %get-tuple-element.46), channel_id=1, source_target_pairs={{0,1},{1,0},{2,3},{3,2},{4,5},{5,4},{6,7},{7,6},{8,9},{9,8},{10,11... | collective-permute-start | bytes 1179656 | tf_op jit(solution)/shard_map/ppermute | solution.py:453
  47.8 20.6 %collective-permute-start.11 = (f32[6,128,128]{2,1,0:T(8,128)}, f32[6,128,128]{2,1,0:T(8,128)S(1)}, u32[]{:S(2)}, u32[]{:S(2)}) collective-permute-start(f32[6,128,128]{2,1,0:T(8,128)} %get-tuple-element.47), channel_id=1, source_target_pairs={{0,1},{1,0},{2,3},{3,2},{4,5},{5,4},{6,7},{7,6},{8,9},{9,8},{10,11... | collective-permute-start | bytes 1179656 | tf_op jit(solution)/shard_map/ppermute | solution.py:453
  47.9 20.5 %collective-permute-start.12 = (f32[6,128,128]{2,1,0:T(8,128)}, f32[6,128,128]{2,1,0:T(8,128)}, u32[]{:S(2)}, u32[]{:S(2)}) collective-permute-start(f32[6,128,128]{2,1,0:T(8,128)} %get-tuple-element.48), channel_id=1, source_target_pairs={{0,1},{1,0},{2,3},{3,2},{4,5},{5,4},{6,7},{7,6},{8,9},{9,8},{10,11... | collective-permute-start | bytes 1179656 | tf_op jit(solution)/shard_map/ppermute | solution.py:453
  50.5 17.8 %collective-permute-start.13 = (f32[6,128,128]{2,1,0:T(8,128)}, f32[6,128,128]{2,1,0:T(8,128)}, u32[]{:S(2)}, u32[]{:S(2)}) collective-permute-start(f32[6,128,128]{2,1,0:T(8,128)} %get-tuple-element.71), channel_id=1, source_target_pairs={{0,1},{1,0},{2,3},{3,2},{4,5},{5,4},{6,7},{7,6},{8,9},{9,8},{10,11... | collective-permute-start | bytes 1179656 | tf_op jit(solution)/shard_map/ppermute | solution.py:453
  50.6 17.8 %collective-permute-start.8 = (f32[6,128,128]{2,1,0:T(8,128)}, f32[6,128,128]{2,1,0:T(8,128)}, u32[]{:S(2)}, u32[]{:S(2)}) collective-permute-start(f32[6,128,128]{2,1,0:T(8,128)} %get-tuple-element.84), channel_id=1, source_target_pairs={{0,1},{1,0},{2,3},{3,2},{4,5},{5,4},{6,7},{7,6},{8,9},{9,8},{10,11... | collective-permute-start | bytes 1179656 | tf_op jit(solution)/shard_map/ppermute | solution.py:453
  68.4 1.0 copy-start.4
  69.4 1.0 copy-start.5
  70.4 1.0 copy-start.6
  71.4 0.9 copy-start.7
  72.3 0.7 copy-start.8
  73.1 0.7 copy-start.10
  76.4 19.9 %collective-permute-start.17 = (bf16[16,6144]{1,0:T(8,128)(2,1)S(1)}, bf16[16,6144]{1,0:T(8,128)(2,1)S(1)}, u32[]{:S(2)}, u32[]{:S(2)}) collective-permute-start(bf16[16,6144]{1,0:T(8,128)(2,1)S(1)} %get-tuple-element.56.refs_0_), channel_id=1, source_target_pairs={{0,6},{1,7},{2,0},{3,1},{4,2},{5,3},{6,4},{7,5},{8,14},{9,15},{10,... | collective-permute-start | bytes 589832 | tf_op jit(solution)/shard_map/ppermute | solution.py:556
  90.8 15.9 %collective-permute-start.16 = (bf16[16,6144]{1,0:T(8,128)(2,1)S(1)}, bf16[16,6144]{1,0:T(8,128)(2,1)S(1)}, u32[]{:S(2)}, u32[]{:S(2)}) collective-permute-start(bf16[16,6144]{1,0:T(8,128)(2,1)S(1)} %get-tuple-element.56.refs_0_), channel_id=1, source_target_pairs={{0,4},{1,5},{2,6},{3,7},{4,0},{5,1},{6,2},{7,3},{8,12},{9,13},{10,... | collective-permute-start | bytes 589832 | tf_op jit(solution)/shard_map/ppermute | solution.py:556
  90.8 15.9 %collective-permute-start.15 = (bf16[16,6144]{1,0:T(8,128)(2,1)S(1)}, bf16[16,6144]{1,0:T(8,128)(2,1)S(1)}, u32[]{:S(2)}, u32[]{:S(2)}) collective-permute-start(bf16[16,6144]{1,0:T(8,128)(2,1)S(1)} %get-tuple-element.56.refs_0_), channel_id=1, source_target_pairs={{0,2},{1,3},{2,4},{3,5},{4,6},{5,7},{6,0},{7,1},{8,10},{9,11},{10,... | collective-permute-start | bytes 589832 | tf_op jit(solution)/shard_map/ppermute | solution.py:556
  91.5 21.3 %collective-permute-start.18 = (bf16[16,6144]{1,0:T(8,128)(2,1)S(1)}, bf16[16,6144]{1,0:T(8,128)(2,1)S(1)}, u32[]{:S(2)}, u32[]{:S(2)}) collective-permute-start(bf16[16,6144]{1,0:T(8,128)(2,1)S(1)} %get-tuple-element.56.refs_0_), channel_id=1, source_target_pairs={{0,1},{1,0},{2,3},{3,2},{4,5},{5,4},{6,7},{7,6},{8,9},{9,8},{10,11... | collective-permute-start | bytes 589832 | tf_op jit(solution)/shard_map/ppermute | solution.py:453
  96.2 16.6 %collective-permute-start.21 = (bf16[16,6144]{1,0:T(8,128)(2,1)S(1)}, bf16[16,6144]{1,0:T(8,128)(2,1)S(1)}, u32[]{:S(2)}, u32[]{:S(2)}) collective-permute-start(bf16[16,6144]{1,0:T(8,128)(2,1)S(1)} %collective-permute-done.17.refs_3_), channel_id=1, source_target_pairs={{0,1},{1,0},{2,3},{3,2},{4,5},{5,4},{6,7},{7,6},{8,9},{9,8},{10,11... | collective-permute-start | bytes 589832 | tf_op jit(solution)/shard_map/ppermute | solution.py:453
  106.8 6.0 %collective-permute-start.20 = (bf16[16,6144]{1,0:T(8,128)(2,1)S(1)}, bf16[16,6144]{1,0:T(8,128)(2,1)S(1)}, u32[]{:S(2)}, u32[]{:S(2)}) collective-permute-start(bf16[16,6144]{1,0:T(8,128)(2,1)S(1)} %collective-permute-done.16.refs_2_), channel_id=1, source_target_pairs={{0,1},{1,0},{2,3},{3,2},{4,5},{5,4},{6,7},{7,6},{8,9},{9,8},{10,11... | collective-permute-start | bytes 589832 | tf_op jit(solution)/shard_map/ppermute | solution.py:453
  106.8 6.0 %collective-permute-start.19 = (bf16[16,6144]{1,0:T(8,128)(2,1)S(1)}, bf16[16,6144]{1,0:T(8,128)(2,1)S(1)}, u32[]{:S(2)}, u32[]{:S(2)}) collective-permute-start(bf16[16,6144]{1,0:T(8,128)(2,1)S(1)} %collective-permute-done.15.refs_1_), channel_id=1, source_target_pairs={{0,1},{1,0},{2,3},{3,2},{4,5},{5,4},{6,7},{7,6},{8,9},{9,8},{10,11... | collective-permute-start | bytes 589832 | tf_op jit(solution)/shard_map/ppermute | solution.py:453
  112.8 3.0 %copy-start = (f32[128,6144]{1,0:T(8,128)S(1)}, f32[128,6144]{1,0:T(8,128)}, u32[]{:S(2)}) copy-start(f32[128,6144]{1,0:T(8,128)} %intra_attention.5.refs_3_.intra_ref) | copy-start | bytes 9437188
  112.8 3.0 %copy-start.1 = (bf16[1,128,6144]{2,1,0:T(8,128)(2,1)S(1)}, bf16[1,128,6144]{2,1,0:T(8,128)(2,1)}, u32[]{:S(2)}) copy-start(bf16[1,128,6144]{2,1,0:T(8,128)(2,1)} %param.12) | copy-start | bytes 4718596
  112.8 3.0 %copy-start.2 = (bf16[1,128,6144]{2,1,0:T(8,128)(2,1)S(1)}, bf16[1,128,6144]{2,1,0:T(8,128)(2,1)}, u32[]{:S(2)}) copy-start(bf16[1,128,6144]{2,1,0:T(8,128)(2,1)} %param.11) | copy-start | bytes 4718596
  112.8 3.0 %copy-start.3 = (f32[1,128,48]{1,2,0:T(8,128)S(1)}, f32[1,128,48]{1,2,0:T(8,128)}, u32[]{:S(2)}) copy-start(f32[1,128,48]{1,2,0:T(8,128)} %param.15) | copy-start | bytes 73732
  112.8 3.0 %copy-start.9 = (f32[1,6144]{1,0:T(1,128)S(1)}, f32[1,6144]{1,0:T(1,128)}, u32[]{:S(2)}) copy-start(f32[1,6144]{1,0:T(1,128)} %refs_17_.3) | copy-start | bytes 73732
  115.7 7.5 %collective-permute-start.22 = (bf16[64,6144]{1,0:T(8,128)(2,1)S(1)}, bf16[64,6144]{1,0:T(8,128)(2,1)S(1)}, u32[]{:S(2)}, u32[]{:S(2)}) collective-permute-start(bf16[64,6144]{1,0:T(8,128)(2,1)S(1)} %get-tuple-element.60), channel_id=1, source_target_pairs={{0,1},{1,0},{2,3},{3,2},{4,5},{5,4},{6,7},{7,6},{8,9},{9,8},{10,11... | collective-permute-start | bytes 2359304 | tf_op jit(solution)/shard_map/ppermute | solution.py:453
  121.6 38.2 %collective-permute-start.14 = (bf16[128,6144]{1,0:T(8,128)(2,1)S(1)}, bf16[128,6144]{1,0:T(8,128)(2,1)S(1)}, u32[]{:S(2)}, u32[]{:S(2)}) collective-permute-start(bf16[128,6144]{1,0:T(8,128)(2,1)S(1)} %finish.1), channel_id=1, source_target_pairs={{0,8},{8,16},{16,24},{24,0},{1,9},{9,17},{17,25},{25,1},{2,10},{10... | collective-permute-start | bytes 4718600 | tf_op jit(solution)/shard_map/ppermute | solution.py:448
  123.1 17.7 %copy-start.11 = (f32[16,128]{1,0:T(8,128)S(1)}, f32[16,128]{1,0:T(8,128)}, u32[]{:S(2)}) copy-start(f32[16,128]{1,0:T(8,128)} %get-tuple-element.54.refs_1_) | copy-start | bytes 24580
  123.1 17.7 %copy-start.12 = (f32[16,128]{1,0:T(8,128)S(1)}, f32[16,128]{1,0:T(8,128)}, u32[]{:S(2)}) copy-start(f32[16,128]{1,0:T(8,128)} %get-tuple-element.55.refs_2_) | copy-start | bytes 24580
  123.4 9.8 %collective-permute-start.25 = (bf16[16,6144]{1,0:T(8,128)(2,1)S(1)}, bf16[16,6144]{1,0:T(8,128)(2,1)S(1)}, u32[]{:S(2)}, u32[]{:S(2)}) collective-permute-start(bf16[16,6144]{1,0:T(8,128)(2,1)S(1)} %get-tuple-element.89), channel_id=1, source_target_pairs={{0,2},{1,3},{2,4},{3,5},{4,6},{5,7},{6,0},{7,1},{8,10},{9,11},{10,... | collective-permute-start | bytes 589832 | tf_op jit(solution)/shard_map/ppermute | solution.py:567
  125.2 15.6 %collective-permute-start.24 = (bf16[16,6144]{1,0:T(8,128)(2,1)S(1)}, bf16[16,6144]{1,0:T(8,128)(2,1)S(1)}, u32[]{:S(2)}, u32[]{:S(2)}) collective-permute-start(bf16[16,6144]{1,0:T(8,128)(2,1)S(1)} %get-tuple-element.90), channel_id=1, source_target_pairs={{0,4},{1,5},{2,6},{3,7},{4,0},{5,1},{6,2},{7,3},{8,12},{9,13},{10,... | collective-permute-start | bytes 589832 | tf_op jit(solution)/shard_map/ppermute | solution.py:567
  127.2 13.6 %collective-permute-start.23 = (bf16[16,6144]{1,0:T(8,128)(2,1)S(1)}, bf16[16,6144]{1,0:T(8,128)(2,1)S(1)}, u32[]{:S(2)}, u32[]{:S(2)}) collective-permute-start(bf16[16,6144]{1,0:T(8,128)(2,1)S(1)} %get-tuple-element.91), channel_id=1, source_target_pairs={{0,6},{1,7},{2,0},{3,1},{4,2},{5,3},{6,4},{7,5},{8,14},{9,15},{10,... | collective-permute-start | bytes 589832 | tf_op jit(solution)/shard_map/ppermute | solution.py:567
  141.0 22.6 %collective-permute-start.26 = (bf16[16,6272]{1,0:T(8,128)(2,1)S(1)}, bf16[16,6272]{1,0:T(8,128)(2,1)S(1)}, u32[]{:S(2)}, u32[]{:S(2)}) collective-permute-start(bf16[16,6272]{1,0:T(8,128)(2,1)S(1)} %late_rows.1), channel_id=1, source_target_pairs={{0,8},{8,16},{16,24},{24,0},{1,9},{9,17},{17,25},{25,1},{2,10},{10... | collective-permute-start | bytes 602120 | tf_op jit(solution)/shard_map/ppermute | solution.py:448

commit v7 on v6

--- a/solution.py
+++ b/solution.py
@@ -9,8 +9,8 @@
 SHARDS = 8
 CAP_SRC = 16
 GROUP = 8
-CHUNKS = 4
-PARTS = 3
+CHUNKS = 3
+PARTS = 1
 FETCH_MIB = 42
 
 F32, BF16 = jnp.float32, jnp.bfloat16
@@ -73,8 +73,7 @@
             fetch(kind, g).start()
     rates.wait()
     cum_ref[...] = cumul_rows(rate_ref)
-    rows = pl.ds(pl.multiple_of(half_ref[0] * groups * GROUP, GROUP), groups * GROUP)
-    decay_ref[...] = jnp.broadcast_to(jnp.exp(cum_ref[rows, length - 1 :]), decay_ref.shape)
+    decay_ref[...] = jnp.broadcast_to(jnp.exp(cum_ref[:, length - 1 :]), decay_ref.shape)
     decays = pltpu.make_async_copy(decay_ref, decay_hbm, sems.at[3, 1])
     decays.start()
     for g in range(groups):
@@ -105,14 +104,14 @@
         out_specs=[HBM_SPEC, HBM_SPEC],
         out_shape=[
             jax.ShapeDtypeStruct((heads // 2, HEAD, HEAD), F32),
-            jax.ShapeDtypeStruct((heads // 2, HEAD), F32),
+            jax.ShapeDtypeStruct((heads, HEAD), F32),
         ],
         scratch_shapes=[
             pltpu.VMEM((heads, length), F32),
             pltpu.VMEM((groups, length, GROUP * HEAD), BF16),
             pltpu.VMEM((groups, length, GROUP * HEAD), BF16),
             pltpu.VMEM((heads // 2, HEAD, HEAD), F32),
-            pltpu.VMEM((heads // 2, HEAD), F32),
+            pltpu.VMEM((heads, HEAD), F32),
             pltpu.VMEM((heads, length), F32),
             pltpu.SemaphoreType.DMA((4, max(groups, 2))),
         ],
@@ -520,9 +519,12 @@
     core1 = core.astype(jnp.int32)[None]
     turned = rate.T
 
-    other, decay_other = half_state(1 - core1, turned, keys, values)
-    partner, decay_partner = swapped(other), swapped(decay_other)
-    mine, decay = half_state(core1, turned, keys, values)
+    other, decay = half_state(1 - core1, turned, keys, values)
+    partner, decay_partner = swapped(other), swapped(decay)
+    mine, _ = half_state(core1, turned, keys, values)
+    decay, decay_partner = (
+        lax.dynamic_slice_in_dim(a, core * half, half, 0) for a in (decay, decay_partner)
+    )
     scale = 1.0
     while 36.0 * count * length * scale > 65000.0:
         scale = scale / 2
@@ -553,7 +555,7 @@
         where, growth, q_rows, resid_rows, intra_rows, keeps, gots, attn_gain, moe_gain
     )
     own = [outbox] + [
-        lax.ppermute(outbox, "ctx", [(i, (i + 2 * d) % count) for i in range(count)])
+        lax.ppermute(outbox, "ctx", [(i, i ^ (2 * d)) for i in range(count)])
         for d in range(1, chips)
     ]
     early = finish(where, turned, queries, intra, keeps, gots, resid, attn_gain)
@@ -564,7 +566,7 @@
     pair = (mine.astype(F32) + swapped(other).astype(F32)).astype(BF16)
     pair = pair.reshape(chips, CAP_SRC, width)
     backs = [
-        lax.ppermute(pair[d], "ctx", [(i, (i - 2 * d) % count) for i in range(count)])
+        lax.ppermute(pair[d], "ctx", [(i, i ^ (2 * d)) for i in range(count)])
         for d in range(1, chips)
     ]
     late = passed_along(late_rows(picked, wcol, token, [pair[0], *backs]), "section", 1)

time: 166 us -> 157 us (0.946)
  Pallas kernels: 41.5 us -> 36.6 us
  starting transfers between devices: 47 us -> 42.3 us
  waiting for transfers between devices: 61.5 us -> 64 us
    pallas_call x3 -> x1, Pallas kernels: 12.2 us -> 6.49 us  [intra_attention(): pl.pallas_call(lambda *refs: intra_kernel(part * groups, *refs), in_specs...]
    ppermute x6 -> x5, starting transfers between devices: 19.3 us -> 15 us  [chain_prefix(): before = lax.ppermute(gone, 'ctx', pairs)]
    ppermute x6, waiting for transfers between devices: 26 us -> 29.7 us  [the longest x3 15.1 us: layer(): lax.ppermute(outbox, 'ctx', [(i, i ^ 2 * d) for i in range(count)])]
    ppermute x6 -> x5, waiting for transfers between devices: 14.3 us -> 14.8 us  [chain_prefix(): before = lax.ppermute(gone, 'ctx', pairs)]
    select_n x5 -> x4, other arithmetic: 5.38 us -> 5.85 us  [chain_prefix(): gives.append(jnp.where(first, after0, prefix))]
  transfers between devices with their start and end apart: 27 -> 25, of which waited for: 11 -> 10; matrix products, arithmetic and copies ran while one was open for 2% -> 2% of each run, Pallas kernels for 19% -> 17%
where the time goes in v7:
time: 157 us
  waiting for transfers between devices  64 us (41%)
  starting transfers between devices  42.3 us (27%)
  Pallas kernels  36.6 us (23%)
  other arithmetic  9.17 us (6%)
  local copies, waits for them, and re-layouts  4.02 us (3%)
    ppermute x2, waiting for transfers between devices, passed_along(): return lax.ppermute(value, axis, pairs)  19.5 us
    ppermute x3, starting transfers between devices, layer(): lax.ppermute(outbox, 'ctx', [(i, i ^ 2 * d) for i in range(count)])  17.4 us
    ppermute x3, waiting for transfers between devices, layer(): lax.ppermute(outbox, 'ctx', [(i, i ^ 2 * d) for i in range(count)])  15.1 us
    ppermute x5, starting transfers between devices, chain_prefix(): before = lax.ppermute(gone, 'ctx', pairs)  15 us
    ppermute x5, waiting for transfers between devices, chain_prefix(): before = lax.ppermute(gone, 'ctx', pairs)  14.8 us
    ppermute x3, waiting for transfers between devices, layer(): lax.ppermute(pair[d], 'ctx', [(i, i ^ 2 * d) for i in range(count)])  14.5 us
    pallas_call x1, Pallas kernels, intra_attention(): pl.pallas_call(lambda *refs: intra_kernel(part * groups, *refs), in_specs...  6.49 us
    pallas_call x1, Pallas kernels, finish(): pl.pallas_call(lambda *refs: finish_kernel(CHUNKS, steps, *refs), in_spec...  6.03 us
  transfers between devices with their start and end apart: 25, of which 10 were waited for; matrix products, arithmetic and copies ran while one was open for 2% of the time, Pallas kernels for 17%

profile of v7, /device:TPU:0, one launch (start us, length us, event | category | flops | bytes accessed | tf_op | source)
XLA Modules:
  0.0 156.8 jit_solution(10718420279445711095)
XLA Ops:
  0.0 3.0 %half_state.2 = (f32[24,128,128]{2,1,0:T(8,128)}, f32[48,128]{1,0:T(8,128)}) custom-call(s32[1]{0:T(128)S(6)} %sub.47.half_ref, f32[48,128]{1,0:T(8,128)} %bitcast.23, bf16[128,6144]{1,0:T(8,128)(2,1)} %bitcast.28, bf16[128,6144]{1,0:T(8,128)(2,1)} %bitcast.31), custom_call_target="tpu_custom_call" | custom-call | tf_op jit(solution)/shard_map/half_state/pallas_call | solution.py:101
  3.0 0.6 collective-permute-start.1
  3.6 0.1 collective-permute-start
  3.6 3.0 %half_state.3 = (f32[24,128,128]{2,1,0:T(8,128)}, f32[48,128]{1,0:T(8,128)}) custom-call(s32[1]{0:T(128)} %bitcast.half_ref, f32[48,128]{1,0:T(8,128)} %bitcast.24, bf16[128,6144]{1,0:T(8,128)(2,1)} %bitcast.29, bf16[128,6144]{1,0:T(8,128)(2,1)} %bitcast.32), custom_call_target="tpu_custom_call" | custom-call | tf_op jit(solution)/shard_map/half_state/pallas_call | solution.py:101
  6.9 1.8 %add_convert_fusion.5 = f16[8,128,128]{2,1,0:T(8,128)(2,1)S(1)} fusion(f32[24,128,128]{2,1,0:T(8,128)S(1)} %collective-permute-done.1, s32[]{:T(128)S(6)} %select_n.265, f32[24,128,128]{2,1,0:T(8,128)} %get-tuple-element.30, f32[8,128]{1,0:T(8,128)S(1)} %get-tuple-element.93, pred[]{:T(512)S(6)} %eq.5), kind=kLoop, calls=%fused_computation.30 | loop fusion | flops 655360 | bytes 1314821 | tf_op jit(solution)/shard_map/convert_element_type | solution.py:481
  8.7 4.9 %collective-permute-start.2 = (f16[8,128,128]{2,1,0:T(8,128)(2,1)S(1)}, f16[8,128,128]{2,1,0:T(8,128)(2,1)S(1)}, u32[]{:S(2)}, u32[]{:S(2)}) collective-permute-start(f16[8,128,128]{2,1,0:T(8,128)(2,1)S(1)} %add_convert_fusion.5), channel_id=1, source_target_pairs={{0,2},{1,3},{8,10},{9,11},{16,18},{17,19},{24,26},{25,27}} | collective-permute-start | bytes 786440 | tf_op jit(solution)/shard_map/ppermute | solution.py:484
  13.6 5.8 %collective-permute-done.2 = f16[8,128,128]{2,1,0:T(8,128)(2,1)S(1)} collective-permute-done((f16[8,128,128]{2,1,0:T(8,128)(2,1)S(1)}, f16[8,128,128]{2,1,0:T(8,128)(2,1)S(1)}, u32[]{:S(2)}, u32[]{:S(2)}) %collective-permute-start.2) | collective-permute-done | bytes 262176 | tf_op jit(solution)/shard_map/ppermute | solution.py:484
  19.4 1.2 add_convert_fusion.4
  20.6 4.4 %collective-permute-start.3 = (f16[8,128,128]{2,1,0:T(8,128)(2,1)S(1)}, f16[8,128,128]{2,1,0:T(8,128)(2,1)S(1)}, u32[]{:S(2)}, u32[]{:S(2)}) collective-permute-start(f16[8,128,128]{2,1,0:T(8,128)(2,1)S(1)} %add_convert_fusion.4), channel_id=1, source_target_pairs={{0,2},{1,3},{2,4},{3,5},{8,10},{9,11},{10,12},{11,13},{16,18},{17,... | collective-permute-start | bytes 786440 | tf_op jit(solution)/shard_map/ppermute | solution.py:484
  25.0 4.9 %collective-permute-done.3 = f16[8,128,128]{2,1,0:T(8,128)(2,1)S(1)} collective-permute-done((f16[8,128,128]{2,1,0:T(8,128)(2,1)S(1)}, f16[8,128,128]{2,1,0:T(8,128)(2,1)S(1)}, u32[]{:S(2)}, u32[]{:S(2)}) %collective-permute-start.3) | collective-permute-done | bytes 262176 | tf_op jit(solution)/shard_map/ppermute | solution.py:484
  30.0 1.1 convert_select_fusion.6
  31.1 4.4 %collective-permute-start.4 = (f16[8,128,128]{2,1,0:T(8,128)(2,1)S(1)}, f16[8,128,128]{2,1,0:T(8,128)(2,1)S(1)}, u32[]{:S(2)}, u32[]{:S(2)}) collective-permute-start(f16[8,128,128]{2,1,0:T(8,128)(2,1)S(1)} %get-tuple-element.33), channel_id=1, source_target_pairs={{0,2},{1,3},{2,4},{3,5},{4,6},{5,7},{8,10},{9,11},{10,12},{11,13},... | collective-permute-start | bytes 786440 | tf_op jit(solution)/shard_map/ppermute | solution.py:484
  35.5 4.1 %collective-permute-done.4 = f16[8,128,128]{2,1,0:T(8,128)(2,1)S(1)} collective-permute-done((f16[8,128,128]{2,1,0:T(8,128)(2,1)S(1)}, f16[8,128,128]{2,1,0:T(8,128)(2,1)S(1)}, u32[]{:S(2)}, u32[]{:S(2)}) %collective-permute-start.4) | collective-permute-done | bytes 262176 | tf_op jit(solution)/shard_map/ppermute | solution.py:484
  39.5 1.1 convert_select_fusion.4
  40.6 0.7 collective-permute-start.5
  41.3 1.1 convert_select_fusion.2
  42.4 0.7 collective-permute-start.6
  43.1 0.5 collective-permute-start.9
  43.6 0.1 collective-permute-start.10
  43.7 2.6 %convert_select_fusion = (f32[8,128,128]{2,1,0:T(8,128)}, f32[8,128,128]{2,1,0:T(8,128)S(1)}, f32[8,128,128]{2,1,0:T(8,128)S(1)}, f32[8,128,128]{2,1,0:T(8,128)}) fusion(f16[8,128,128]{2,1,0:T(8,128)(2,1)S(1)} %collective-permute-done.6, f32[8,128]{1,0:T(8,128)S(1)} %get-tuple-element.80, pred[]{:T(512)S(6)} %eq.5, f32[24,128,128]{2,1,0:T(8,128)} %copy-done.12, ...), kind=kLoop, calls=%fused_computation.1 | loop fusion | flops 1572864 | bytes 4726793 | tf_op jit(solution)/shard_map/jit(_where)/select_n | solution.py:489
  46.3 0.4 collective-permute-start.11
  46.7 0.1 collective-permute-start.7
  46.8 6.5 %intra_attention.1.refs_3_.intra_ref = f32[128,6144]{1,0:T(8,128)} custom-call(f32[48,128]{1,0:T(8,128)} %bitcast.25, bf16[128,6144]{1,0:T(8,128)(2,1)} %bitcast.18, bf16[128,6144]{1,0:T(8,128)(2,1)} %bitcast.30, bf16[128,6144]{1,0:T(8,128)(2,1)} %bitcast.33), custom_call_target="tpu_custom_call" | custom-call | tf_op jit(solution)/shard_map/intra_attention/pallas_call | solution.py:166
  53.3 5.1 %select.7 = (f32[16,128]{1,0:T(8,128)}, f32[16,128]{1,0:T(8,128)}, f32[16,6144]{1,0:T(8,128)}, bf16[16,6144]{1,0:T(8,128)(2,1)}, f32[16,6144]{1,0:T(8,128)}, /*index=5*/f32[16,6144]{1,0:T(8,128)}) custom-call(s32[2,128]{1,0:T(2,128)} %bitcast.36, f32[2,128]{1,0:T(2,128)} %bitcast.37, f32[48,128]{1,0:T(8,128)} %bitcast.26, bf16[128,6144]{1,0:T(8,128)(2,1)} %bitcast.19, ...), custom_call_target="tpu_custom_call" | custom-call | tf_op jit(solution)/shard_map/select/pallas_call | solution.py:220
  58.5 1.0 copy-done.4
  59.5 1.0 copy-done.5
  60.5 1.0 copy-done.6
  61.5 0.9 copy-done.7
  62.4 3.0 %selected_rows.1 = (bf16[16,6144]{1,0:T(8,128)(2,1)S(1)}, f32[16,6144]{1,0:T(8,128)S(1)}) custom-call(s32[2]{0:T(128)S(1)} %pad_add_fusion.refs_0_, f32[16,6144]{1,0:T(8,128)S(1)} %copy-done.4, bf16[16,6144]{1,0:T(8,128)(2,1)S(1)} %copy-done.7, f32[16,6144]{1,0:T(8,128)S(1)} %copy-done.5, f32[16,6144]{1,0:T(8,128)S(1)} %copy-done.6, ...), custom_call_target="tpu_custom_call" | custom-call | tf_op jit(solution)/shard_map/selected_rows/pallas_call | solution.py:278
  65.4 16.8 %collective-permute-start.15 = (bf16[16,6144]{1,0:T(8,128)(2,1)S(1)}, bf16[16,6144]{1,0:T(8,128)(2,1)S(1)}, u32[]{:S(2)}, u32[]{:S(2)}) collective-permute-start(bf16[16,6144]{1,0:T(8,128)(2,1)S(1)} %get-tuple-element.48.refs_0_), channel_id=1, source_target_pairs={{0,6},{1,7},{2,4},{3,5},{4,2},{5,3},{6,0},{7,1},{8,14},{9,15},{10,... | collective-permute-start | bytes 589832 | tf_op jit(solution)/shard_map/ppermute | solution.py:558
  82.2 0.6 collective-permute-start.13
  82.9 5.3 %collective-permute-done.15.refs_3_ = bf16[16,6144]{1,0:T(8,128)(2,1)S(1)} collective-permute-done((bf16[16,6144]{1,0:T(8,128)(2,1)S(1)}, bf16[16,6144]{1,0:T(8,128)(2,1)S(1)}, u32[]{:S(2)}, u32[]{:S(2)}) %collective-permute-start.15) | collective-permute-done | bytes 196640 | tf_op jit(solution)/shard_map/ppermute | solution.py:558
  88.1 9.9 %collective-permute-done.14.refs_2_ = bf16[16,6144]{1,0:T(8,128)(2,1)S(1)} collective-permute-done((bf16[16,6144]{1,0:T(8,128)(2,1)S(1)}, bf16[16,6144]{1,0:T(8,128)(2,1)S(1)}, u32[]{:S(2)}, u32[]{:S(2)}) %collective-permute-start.14) | collective-permute-done | bytes 196640 | tf_op jit(solution)/shard_map/ppermute | solution.py:558
  98.0 0.5 collective-permute-start.17
  98.5 5.5 %fetch.1 = (bf16[6144,640]{1,0:T(8,128)(2,1)S(1)}, bf16[640,6144]{1,0:T(8,128)(2,1)S(1)}) custom-call(bf16[6144,640]{1,0:T(8,128)(2,1)} %bitcast.34, bf16[640,6144]{1,0:T(8,128)(2,1)} %bitcast.35), custom_call_target="tpu_custom_call" | custom-call | tf_op jit(solution)/shard_map/fetch/pallas_call | solution.py:401
  104.1 2.8 %expert_rows.1 = (bf16[64,6144]{1,0:T(8,128)(2,1)S(1)}, bf16[64,6144]{1,0:T(8,128)(2,1)S(1)}) custom-call(bf16[16,6144]{1,0:T(8,128)(2,1)S(1)} %get-tuple-element.48.refs_0_, bf16[16,6144]{1,0:T(8,128)(2,1)S(1)} %collective-permute-done.13.refs_1_, bf16[16,6144]{1,0:T(8,128)(2,1)S(1)} %collective-permute-done.14.refs_2_, ...), custom_call_target="tpu_custom_call" | custom-call | tf_op jit(solution)/shard_map/expert_rows/pallas_call | solution.py:433
  107.0 6.0 %finish.1 = bf16[128,6144]{1,0:T(8,128)(2,1)S(1)} custom-call(s32[2]{0:T(128)S(1)} %pad_add_fusion.refs_0_, f32[48,128]{1,0:T(8,128)S(1)} %bitcast.27, bf16[128,6144]{1,0:T(8,128)(2,1)S(1)} %bitcast.20, f32[128,6144]{1,0:T(8,128)S(1)} %copy-done, f32[8,128,128]{2,1,0:T(8,128)S(1)} %get-tuple-element.71.refs_4_.refs_5_, ...), custom_call_target="tpu_custom_call" | custom-call | tf_op jit(solution)/shard_map/finish/pallas_call | solution.py:320
  113.1 1.5 collective-permute-start.12
  114.6 0.2 add_convert_fusion
  114.9 2.7 %collective-permute-start.23 = (bf16[16,6144]{1,0:T(8,128)(2,1)S(1)}, bf16[16,6144]{1,0:T(8,128)(2,1)S(1)}, u32[]{:S(2)}, u32[]{:S(2)}) collective-permute-start(bf16[16,6144]{1,0:T(8,128)(2,1)S(1)} %get-tuple-element.76), channel_id=1, source_target_pairs={{0,6},{1,7},{2,4},{3,5},{4,2},{5,3},{6,0},{7,1},{8,14},{9,15},{10,... | collective-permute-start | bytes 589832 | tf_op jit(solution)/shard_map/ppermute | solution.py:569
  117.6 1.8 %collective-permute-start.21 = (bf16[16,6144]{1,0:T(8,128)(2,1)S(1)}, bf16[16,6144]{1,0:T(8,128)(2,1)S(1)}, u32[]{:S(2)}, u32[]{:S(2)}) collective-permute-start(bf16[16,6144]{1,0:T(8,128)(2,1)S(1)} %get-tuple-element.78), channel_id=1, source_target_pairs={{0,2},{1,3},{2,0},{3,1},{4,6},{5,7},{6,4},{7,5},{8,10},{9,11},{10,... | collective-permute-start | bytes 589832 | tf_op jit(solution)/shard_map/ppermute | solution.py:569
  119.3 5.3 %collective-permute-done.23.refs_6_ = bf16[16,6144]{1,0:T(8,128)(2,1)S(1)} collective-permute-done((bf16[16,6144]{1,0:T(8,128)(2,1)S(1)}, bf16[16,6144]{1,0:T(8,128)(2,1)S(1)}, u32[]{:S(2)}, u32[]{:S(2)}) %collective-permute-start.23) | collective-permute-done | bytes 196640 | tf_op jit(solution)/shard_map/ppermute | solution.py:569
  124.6 9.2 %collective-permute-done.22.refs_5_ = bf16[16,6144]{1,0:T(8,128)(2,1)S(1)} collective-permute-done((bf16[16,6144]{1,0:T(8,128)(2,1)S(1)}, bf16[16,6144]{1,0:T(8,128)(2,1)S(1)}, u32[]{:S(2)}, u32[]{:S(2)}) %collective-permute-start.22) | collective-permute-done | bytes 196640 | tf_op jit(solution)/shard_map/ppermute | solution.py:569
  133.8 0.2 late_rows.1
  134.1 1.5 collective-permute-start.24
  135.6 15.7 %collective-permute-done.12.early_ref = bf16[128,6144]{1,0:T(8,128)(2,1)S(1)} collective-permute-done((bf16[128,6144]{1,0:T(8,128)(2,1)S(1)}, bf16[128,6144]{1,0:T(8,128)(2,1)S(1)}, u32[]{:S(2)}, u32[]{:S(2)}) %collective-permute-start.12) | collective-permute-done | bytes 1572896 | tf_op jit(solution)/shard_map/ppermute | solution.py:447
  151.3 3.8 %collective-permute-done.24.late_ref = bf16[16,6272]{1,0:T(8,128)(2,1)S(1)} collective-permute-done((bf16[16,6272]{1,0:T(8,128)(2,1)S(1)}, bf16[16,6272]{1,0:T(8,128)(2,1)S(1)}, u32[]{:S(2)}, u32[]{:S(2)}) %collective-permute-start.24) | collective-permute-done | bytes 200736 | tf_op jit(solution)/shard_map/ppermute | solution.py:447
  155.1 1.5 merged.1
  (52 shorter events, 0.5 us)
Async XLA Ops:
  3.0 3.9 %collective-permute-start.1 = (f32[24,128,128]{2,1,0:T(8,128)}, f32[24,128,128]{2,1,0:T(8,128)S(1)}, u32[]{:S(2)}, u32[]{:S(2)}) collective-permute-start(f32[24,128,128]{2,1,0:T(8,128)} %get-tuple-element.31), channel_id=1, source_target_pairs={{0,1},{1,0},{2,3},{3,2},{4,5},{5,4},{6,7},{7,6},{8,9},{9,8},{10,11... | collective-permute-start | bytes 4718600 | tf_op jit(solution)/shard_map/ppermute | solution.py:452
  3.6 3.3 %collective-permute-start = (f32[48,128]{1,0:T(8,128)}, f32[48,128]{1,0:T(8,128)S(1)}, u32[]{:S(2)}, u32[]{:S(2)}) collective-permute-start(f32[48,128]{1,0:T(8,128)} %get-tuple-element.29), channel_id=1, source_target_pairs={{0,1},{1,0},{2,3},{3,2},{4,5},{5,4},{6,7},{7,6},{8,9},{9,8},{10,11... | collective-permute-start | bytes 73736 | tf_op jit(solution)/shard_map/ppermute | solution.py:452
  3.6 3.2 %copy-start.14 = (f32[48,128]{1,0:T(8,128)S(1)}, f32[48,128]{1,0:T(8,128)}, u32[]{:S(2)}) copy-start(f32[48,128]{1,0:T(8,128)} %get-tuple-element.29) | copy-start | bytes 73732
  6.8 23.2 %copy-start.13 = (f32[24,128,128]{2,1,0:T(8,128)S(1)}, f32[24,128,128]{2,1,0:T(8,128)}, u32[]{:S(2)}) copy-start(f32[24,128,128]{2,1,0:T(8,128)} %get-tuple-element.30) | copy-start | bytes 4718596
  6.9 34.4 %copy-start.12 = (f32[24,128,128]{2,1,0:T(8,128)}, f32[24,128,128]{2,1,0:T(8,128)S(1)}, u32[]{:S(2)}) copy-start(f32[24,128,128]{2,1,0:T(8,128)S(1)} %collective-permute-done.1) | copy-start | bytes 4718596
  8.7 10.7 %collective-permute-start.2 = (f16[8,128,128]{2,1,0:T(8,128)(2,1)S(1)}, f16[8,128,128]{2,1,0:T(8,128)(2,1)S(1)}, u32[]{:S(2)}, u32[]{:S(2)}) collective-permute-start(f16[8,128,128]{2,1,0:T(8,128)(2,1)S(1)} %add_convert_fusion.5), channel_id=1, source_target_pairs={{0,2},{1,3},{8,10},{9,11},{16,18},{17,19},{24,26},{25,27}} | collective-permute-start | bytes 786440 | tf_op jit(solution)/shard_map/ppermute | solution.py:484
  20.6 9.3 %collective-permute-start.3 = (f16[8,128,128]{2,1,0:T(8,128)(2,1)S(1)}, f16[8,128,128]{2,1,0:T(8,128)(2,1)S(1)}, u32[]{:S(2)}, u32[]{:S(2)}) collective-permute-start(f16[8,128,128]{2,1,0:T(8,128)(2,1)S(1)} %add_convert_fusion.4), channel_id=1, source_target_pairs={{0,2},{1,3},{2,4},{3,5},{8,10},{9,11},{10,12},{11,13},{16,18},{17,... | collective-permute-start | bytes 786440 | tf_op jit(solution)/shard_map/ppermute | solution.py:484
  31.1 8.5 %collective-permute-start.4 = (f16[8,128,128]{2,1,0:T(8,128)(2,1)S(1)}, f16[8,128,128]{2,1,0:T(8,128)(2,1)S(1)}, u32[]{:S(2)}, u32[]{:S(2)}) collective-permute-start(f16[8,128,128]{2,1,0:T(8,128)(2,1)S(1)} %get-tuple-element.33), channel_id=1, source_target_pairs={{0,2},{1,3},{2,4},{3,5},{4,6},{5,7},{8,10},{9,11},{10,12},{11,13},... | collective-permute-start | bytes 786440 | tf_op jit(solution)/shard_map/ppermute | solution.py:484
  40.6 0.7 collective-permute-start.5
  42.4 1.3 collective-permute-start.6
  43.1 15.4 %collective-permute-start.8 = (f32[8,128,128]{2,1,0:T(8,128)}, f32[8,128,128]{2,1,0:T(8,128)S(1)}, u32[]{:S(2)}, u32[]{:S(2)}) collective-permute-start(f32[8,128,128]{2,1,0:T(8,128)} %get-tuple-element.38), channel_id=1, source_target_pairs={{0,1},{1,0},{2,3},{3,2},{4,5},{5,4},{6,7},{7,6},{8,9},{9,8},{10,11... | collective-permute-start | bytes 1572872 | tf_op jit(solution)/shard_map/ppermute | solution.py:452
  43.1 15.3 %collective-permute-start.9 = (f32[8,128,128]{2,1,0:T(8,128)}, f32[8,128,128]{2,1,0:T(8,128)}, u32[]{:S(2)}, u32[]{:S(2)}) collective-permute-start(f32[8,128,128]{2,1,0:T(8,128)} %get-tuple-element.39), channel_id=1, source_target_pairs={{0,1},{1,0},{2,3},{3,2},{4,5},{5,4},{6,7},{7,6},{8,9},{9,8},{10,11... | collective-permute-start | bytes 1572872 | tf_op jit(solution)/shard_map/ppermute | solution.py:452
  43.6 14.8 %collective-permute-start.10 = (f32[8,128,128]{2,1,0:T(8,128)}, f32[8,128,128]{2,1,0:T(8,128)}, u32[]{:S(2)}, u32[]{:S(2)}) collective-permute-start(f32[8,128,128]{2,1,0:T(8,128)} %get-tuple-element.40), channel_id=1, source_target_pairs={{0,1},{1,0},{2,3},{3,2},{4,5},{5,4},{6,7},{7,6},{8,9},{9,8},{10,11... | collective-permute-start | bytes 1572872 | tf_op jit(solution)/shard_map/ppermute | solution.py:452
  46.3 12.2 %collective-permute-start.11 = (f32[8,128,128]{2,1,0:T(8,128)}, f32[8,128,128]{2,1,0:T(8,128)}, u32[]{:S(2)}, u32[]{:S(2)}) collective-permute-start(f32[8,128,128]{2,1,0:T(8,128)} %get-tuple-element.61), channel_id=1, source_target_pairs={{0,1},{1,0},{2,3},{3,2},{4,5},{5,4},{6,7},{7,6},{8,9},{9,8},{10,11... | collective-permute-start | bytes 1572872 | tf_op jit(solution)/shard_map/ppermute | solution.py:452
  46.7 11.8 %collective-permute-start.7 = (f32[8,128,128]{2,1,0:T(8,128)}, f32[8,128,128]{2,1,0:T(8,128)}, u32[]{:S(2)}, u32[]{:S(2)}) collective-permute-start(f32[8,128,128]{2,1,0:T(8,128)} %get-tuple-element.72), channel_id=1, source_target_pairs={{0,1},{1,0},{2,3},{3,2},{4,5},{5,4},{6,7},{7,6},{8,9},{9,8},{10,11... | collective-permute-start | bytes 1572872 | tf_op jit(solution)/shard_map/ppermute | solution.py:452
  53.3 5.2 %copy-start.8 = (f32[1,6144]{1,0:T(1,128)S(1)}, f32[1,6144]{1,0:T(1,128)}, u32[]{:S(2)}) copy-start(f32[1,6144]{1,0:T(1,128)} %refs_15_.3) | copy-start | bytes 73732
  53.3 5.2 %copy-start.9 = (f32[1,6144]{1,0:T(1,128)S(1)}, f32[1,6144]{1,0:T(1,128)}, u32[]{:S(2)}) copy-start(f32[1,6144]{1,0:T(1,128)} %refs_16_.1) | copy-start | bytes 73732
  58.5 1.0 copy-start.4
  59.5 1.0 copy-start.5
  60.5 1.0 copy-start.6
  61.5 0.9 copy-start.7
  65.4 22.7 %collective-permute-start.15 = (bf16[16,6144]{1,0:T(8,128)(2,1)S(1)}, bf16[16,6144]{1,0:T(8,128)(2,1)S(1)}, u32[]{:S(2)}, u32[]{:S(2)}) collective-permute-start(bf16[16,6144]{1,0:T(8,128)(2,1)S(1)} %get-tuple-element.48.refs_0_), channel_id=1, source_target_pairs={{0,6},{1,7},{2,4},{3,5},{4,2},{5,3},{6,0},{7,1},{8,14},{9,15},{10,... | collective-permute-start | bytes 589832 | tf_op jit(solution)/shard_map/ppermute | solution.py:558
  82.2 15.8 %collective-permute-start.14 = (bf16[16,6144]{1,0:T(8,128)(2,1)S(1)}, bf16[16,6144]{1,0:T(8,128)(2,1)S(1)}, u32[]{:S(2)}, u32[]{:S(2)}) collective-permute-start(bf16[16,6144]{1,0:T(8,128)(2,1)S(1)} %get-tuple-element.48.refs_0_), channel_id=1, source_target_pairs={{0,4},{1,5},{2,6},{3,7},{4,0},{5,1},{6,2},{7,3},{8,12},{9,13},{10,... | collective-permute-start | bytes 589832 | tf_op jit(solution)/shard_map/ppermute | solution.py:558
  82.2 15.8 %collective-permute-start.13 = (bf16[16,6144]{1,0:T(8,128)(2,1)S(1)}, bf16[16,6144]{1,0:T(8,128)(2,1)S(1)}, u32[]{:S(2)}, u32[]{:S(2)}) collective-permute-start(bf16[16,6144]{1,0:T(8,128)(2,1)S(1)} %get-tuple-element.48.refs_0_), channel_id=1, source_target_pairs={{0,2},{1,3},{2,0},{3,1},{4,6},{5,7},{6,4},{7,5},{8,10},{9,11},{10,... | collective-permute-start | bytes 589832 | tf_op jit(solution)/shard_map/ppermute | solution.py:558
  82.8 21.2 %collective-permute-start.16 = (bf16[16,6144]{1,0:T(8,128)(2,1)S(1)}, bf16[16,6144]{1,0:T(8,128)(2,1)S(1)}, u32[]{:S(2)}, u32[]{:S(2)}) collective-permute-start(bf16[16,6144]{1,0:T(8,128)(2,1)S(1)} %get-tuple-element.48.refs_0_), channel_id=1, source_target_pairs={{0,1},{1,0},{2,3},{3,2},{4,5},{5,4},{6,7},{7,6},{8,9},{9,8},{10,11... | collective-permute-start | bytes 589832 | tf_op jit(solution)/shard_map/ppermute | solution.py:452
  88.1 15.9 %collective-permute-start.19 = (bf16[16,6144]{1,0:T(8,128)(2,1)S(1)}, bf16[16,6144]{1,0:T(8,128)(2,1)S(1)}, u32[]{:S(2)}, u32[]{:S(2)}) collective-permute-start(bf16[16,6144]{1,0:T(8,128)(2,1)S(1)} %collective-permute-done.15.refs_3_), channel_id=1, source_target_pairs={{0,1},{1,0},{2,3},{3,2},{4,5},{5,4},{6,7},{7,6},{8,9},{9,8},{10,11... | collective-permute-start | bytes 589832 | tf_op jit(solution)/shard_map/ppermute | solution.py:452
  98.0 6.0 %collective-permute-start.18 = (bf16[16,6144]{1,0:T(8,128)(2,1)S(1)}, bf16[16,6144]{1,0:T(8,128)(2,1)S(1)}, u32[]{:S(2)}, u32[]{:S(2)}) collective-permute-start(bf16[16,6144]{1,0:T(8,128)(2,1)S(1)} %collective-permute-done.14.refs_2_), channel_id=1, source_target_pairs={{0,1},{1,0},{2,3},{3,2},{4,5},{5,4},{6,7},{7,6},{8,9},{9,8},{10,11... | collective-permute-start | bytes 589832 | tf_op jit(solution)/shard_map/ppermute | solution.py:452
  98.0 6.0 %collective-permute-start.17 = (bf16[16,6144]{1,0:T(8,128)(2,1)S(1)}, bf16[16,6144]{1,0:T(8,128)(2,1)S(1)}, u32[]{:S(2)}, u32[]{:S(2)}) collective-permute-start(bf16[16,6144]{1,0:T(8,128)(2,1)S(1)} %collective-permute-done.13.refs_1_), channel_id=1, source_target_pairs={{0,1},{1,0},{2,3},{3,2},{4,5},{5,4},{6,7},{7,6},{8,9},{9,8},{10,11... | collective-permute-start | bytes 589832 | tf_op jit(solution)/shard_map/ppermute | solution.py:452
  104.0 2.9 %copy-start = (f32[128,6144]{1,0:T(8,128)S(1)}, f32[128,6144]{1,0:T(8,128)}, u32[]{:S(2)}) copy-start(f32[128,6144]{1,0:T(8,128)} %intra_attention.1.refs_3_.intra_ref) | copy-start | bytes 9437188
  104.1 2.9 %copy-start.1 = (bf16[1,128,6144]{2,1,0:T(8,128)(2,1)S(1)}, bf16[1,128,6144]{2,1,0:T(8,128)(2,1)}, u32[]{:S(2)}) copy-start(bf16[1,128,6144]{2,1,0:T(8,128)(2,1)} %param.12) | copy-start | bytes 4718596
  104.1 2.9 %copy-start.2 = (bf16[1,128,6144]{2,1,0:T(8,128)(2,1)S(1)}, bf16[1,128,6144]{2,1,0:T(8,128)(2,1)}, u32[]{:S(2)}) copy-start(bf16[1,128,6144]{2,1,0:T(8,128)(2,1)} %param.11) | copy-start | bytes 4718596
  104.1 2.9 %copy-start.3 = (f32[1,128,48]{1,2,0:T(8,128)S(1)}, f32[1,128,48]{1,2,0:T(8,128)}, u32[]{:S(2)}) copy-start(f32[1,128,48]{1,2,0:T(8,128)} %param.15) | copy-start | bytes 73732
  106.9 7.7 %collective-permute-start.20 = (bf16[64,6144]{1,0:T(8,128)(2,1)S(1)}, bf16[64,6144]{1,0:T(8,128)(2,1)S(1)}, u32[]{:S(2)}, u32[]{:S(2)}) collective-permute-start(bf16[64,6144]{1,0:T(8,128)(2,1)S(1)} %get-tuple-element.52), channel_id=1, source_target_pairs={{0,1},{1,0},{2,3},{3,2},{4,5},{5,4},{6,7},{7,6},{8,9},{9,8},{10,11... | collective-permute-start | bytes 2359304 | tf_op jit(solution)/shard_map/ppermute | solution.py:452
  113.1 38.2 %collective-permute-start.12 = (bf16[128,6144]{1,0:T(8,128)(2,1)S(1)}, bf16[128,6144]{1,0:T(8,128)(2,1)S(1)}, u32[]{:S(2)}, u32[]{:S(2)}) collective-permute-start(bf16[128,6144]{1,0:T(8,128)(2,1)S(1)} %finish.1), channel_id=1, source_target_pairs={{0,8},{8,16},{16,24},{24,0},{1,9},{9,17},{17,25},{25,1},{2,10},{10... | collective-permute-start | bytes 4718600 | tf_op jit(solution)/shard_map/ppermute | solution.py:447
  114.6 19.2 %copy-start.10 = (f32[16,128]{1,0:T(8,128)S(1)}, f32[16,128]{1,0:T(8,128)}, u32[]{:S(2)}) copy-start(f32[16,128]{1,0:T(8,128)} %get-tuple-element.46.refs_1_) | copy-start | bytes 24580
  114.6 19.2 %copy-start.11 = (f32[16,128]{1,0:T(8,128)S(1)}, f32[16,128]{1,0:T(8,128)}, u32[]{:S(2)}) copy-start(f32[16,128]{1,0:T(8,128)} %get-tuple-element.47.refs_2_) | copy-start | bytes 24580
  114.9 9.8 %collective-permute-start.23 = (bf16[16,6144]{1,0:T(8,128)(2,1)S(1)}, bf16[16,6144]{1,0:T(8,128)(2,1)S(1)}, u32[]{:S(2)}, u32[]{:S(2)}) collective-permute-start(bf16[16,6144]{1,0:T(8,128)(2,1)S(1)} %get-tuple-element.76), channel_id=1, source_target_pairs={{0,6},{1,7},{2,4},{3,5},{4,2},{5,3},{6,0},{7,1},{8,14},{9,15},{10,... | collective-permute-start | bytes 589832 | tf_op jit(solution)/shard_map/ppermute | solution.py:569
  117.6 16.3 %collective-permute-start.22 = (bf16[16,6144]{1,0:T(8,128)(2,1)S(1)}, bf16[16,6144]{1,0:T(8,128)(2,1)S(1)}, u32[]{:S(2)}, u32[]{:S(2)}) collective-permute-start(bf16[16,6144]{1,0:T(8,128)(2,1)S(1)} %get-tuple-element.77), channel_id=1, source_target_pairs={{0,4},{1,5},{2,6},{3,7},{4,0},{5,1},{6,2},{7,3},{8,12},{9,13},{10,... | collective-permute-start | bytes 589832 | tf_op jit(solution)/shard_map/ppermute | solution.py:569
  117.6 16.3 %collective-permute-start.21 = (bf16[16,6144]{1,0:T(8,128)(2,1)S(1)}, bf16[16,6144]{1,0:T(8,128)(2,1)S(1)}, u32[]{:S(2)}, u32[]{:S(2)}) collective-permute-start(bf16[16,6144]{1,0:T(8,128)(2,1)S(1)} %get-tuple-element.78), channel_id=1, source_target_pairs={{0,2},{1,3},{2,0},{3,1},{4,6},{5,7},{6,4},{7,5},{8,10},{9,11},{10,... | collective-permute-start | bytes 589832 | tf_op jit(solution)/shard_map/ppermute | solution.py:569
  134.1 21.0 %collective-permute-start.24 = (bf16[16,6272]{1,0:T(8,128)(2,1)S(1)}, bf16[16,6272]{1,0:T(8,128)(2,1)S(1)}, u32[]{:S(2)}, u32[]{:S(2)}) collective-permute-start(bf16[16,6272]{1,0:T(8,128)(2,1)S(1)} %late_rows.1), channel_id=1, source_target_pairs={{0,8},{8,16},{16,24},{24,0},{1,9},{9,17},{17,25},{25,1},{2,10},{10... | collective-permute-start | bytes 602120 | tf_op jit(solution)/shard_map/ppermute | solution.py:447

commit v8 on v7

--- a/solution.py
+++ b/solution.py
@@ -289,10 +289,11 @@
     keeps, gots, refs = refs[:steps], refs[steps : 2 * steps], refs[2 * steps :]
     resid_ref, again_ref, early_ref, attn_ref, scale_ref = refs
     length, width = resid_ref.shape
-    growth = jnp.exp(cumul_rows(rate_ref))
+    growth = jnp.exp(cumul_rows(rate_ref)).T
     for head in range(width // HEAD):
-        across = jnp.broadcast_to(growth[head : head + 1, :], (length, length))
-        scale_ref[:, head * HEAD : (head + 1) * HEAD] = across.T
+        scale_ref[:, head * HEAD : (head + 1) * HEAD] = jnp.broadcast_to(
+            growth[:, head : head + 1], (length, HEAD)
+        )
 
     def use(cols, state):
         hi, lo = split(state)

time: 157 us -> 158 us (level)
  no operation moved by 1% of the time
where the time goes in v8:
time: 158 us; the launch traced here: 157 us
  waiting for transfers between devices  64 us (41%)
  starting transfers between devices  42.3 us (27%)
  Pallas kernels  36.8 us (23%)
  other arithmetic  9.17 us (6%)
  local copies, waits for them, and re-layouts  4.02 us (3%)
    ppermute x2, waiting for transfers between devices, passed_along(): return lax.ppermute(value, axis, pairs)  19.5 us
    ppermute x3, starting transfers between devices, layer(): lax.ppermute(outbox, 'ctx', [(i, i ^ 2 * d) for i in range(count)])  17.4 us
    ppermute x3, waiting for transfers between devices, layer(): lax.ppermute(outbox, 'ctx', [(i, i ^ 2 * d) for i in range(count)])  15.1 us
    ppermute x5, starting transfers between devices, chain_prefix(): before = lax.ppermute(gone, 'ctx', pairs)  15 us
    ppermute x5, waiting for transfers between devices, chain_prefix(): before = lax.ppermute(gone, 'ctx', pairs)  14.8 us
    ppermute x3, waiting for transfers between devices, layer(): lax.ppermute(pair[d], 'ctx', [(i, i ^ 2 * d) for i in range(count)])  14.5 us
    pallas_call x1, Pallas kernels, intra_attention(): pl.pallas_call(lambda *refs: intra_kernel(part * groups, *refs), in_specs...  6.49 us
    pallas_call x1, Pallas kernels, finish(): pl.pallas_call(lambda *refs: finish_kernel(CHUNKS, steps, *refs), in_spec...  6.26 us
  transfers between devices with their start and end apart: 25, of which 10 were waited for; matrix products, arithmetic and copies ran while one was open for 2% of the time, Pallas kernels for 17%

profile of v8, /device:TPU:0, one launch (start us, length us, event | category | flops | bytes accessed | tf_op | source)
XLA Modules:
  0.0 157.0 jit_solution(11422910807603176559)
XLA Ops:
  0.0 3.0 %half_state.2 = (f32[24,128,128]{2,1,0:T(8,128)}, f32[48,128]{1,0:T(8,128)}) custom-call(s32[1]{0:T(128)S(6)} %sub.47.half_ref, f32[48,128]{1,0:T(8,128)} %bitcast.23, bf16[128,6144]{1,0:T(8,128)(2,1)} %bitcast.28, bf16[128,6144]{1,0:T(8,128)(2,1)} %bitcast.31), custom_call_target="tpu_custom_call" | custom-call | tf_op jit(solution)/shard_map/half_state/pallas_call | solution.py:101
  3.0 0.6 collective-permute-start.1
  3.6 0.1 collective-permute-start
  3.6 3.0 %half_state.3 = (f32[24,128,128]{2,1,0:T(8,128)}, f32[48,128]{1,0:T(8,128)}) custom-call(s32[1]{0:T(128)} %bitcast.half_ref, f32[48,128]{1,0:T(8,128)} %bitcast.24, bf16[128,6144]{1,0:T(8,128)(2,1)} %bitcast.29, bf16[128,6144]{1,0:T(8,128)(2,1)} %bitcast.32), custom_call_target="tpu_custom_call" | custom-call | tf_op jit(solution)/shard_map/half_state/pallas_call | solution.py:101
  6.9 1.8 %add_convert_fusion.5 = f16[8,128,128]{2,1,0:T(8,128)(2,1)S(1)} fusion(f32[24,128,128]{2,1,0:T(8,128)S(1)} %collective-permute-done.1, s32[]{:T(128)S(6)} %select_n.265, f32[24,128,128]{2,1,0:T(8,128)} %get-tuple-element.30, f32[8,128]{1,0:T(8,128)S(1)} %get-tuple-element.93, pred[]{:T(512)S(6)} %eq.5), kind=kLoop, calls=%fused_computation.30 | loop fusion | flops 655360 | bytes 1314821 | tf_op jit(solution)/shard_map/convert_element_type | solution.py:482
  8.7 4.9 %collective-permute-start.2 = (f16[8,128,128]{2,1,0:T(8,128)(2,1)S(1)}, f16[8,128,128]{2,1,0:T(8,128)(2,1)S(1)}, u32[]{:S(2)}, u32[]{:S(2)}) collective-permute-start(f16[8,128,128]{2,1,0:T(8,128)(2,1)S(1)} %add_convert_fusion.5), channel_id=1, source_target_pairs={{0,2},{1,3},{8,10},{9,11},{16,18},{17,19},{24,26},{25,27}} | collective-permute-start | bytes 786440 | tf_op jit(solution)/shard_map/ppermute | solution.py:485
  13.6 5.8 %collective-permute-done.2 = f16[8,128,128]{2,1,0:T(8,128)(2,1)S(1)} collective-permute-done((f16[8,128,128]{2,1,0:T(8,128)(2,1)S(1)}, f16[8,128,128]{2,1,0:T(8,128)(2,1)S(1)}, u32[]{:S(2)}, u32[]{:S(2)}) %collective-permute-start.2) | collective-permute-done | bytes 262176 | tf_op jit(solution)/shard_map/ppermute | solution.py:485
  19.4 1.2 add_convert_fusion.4
  20.6 4.4 %collective-permute-start.3 = (f16[8,128,128]{2,1,0:T(8,128)(2,1)S(1)}, f16[8,128,128]{2,1,0:T(8,128)(2,1)S(1)}, u32[]{:S(2)}, u32[]{:S(2)}) collective-permute-start(f16[8,128,128]{2,1,0:T(8,128)(2,1)S(1)} %add_convert_fusion.4), channel_id=1, source_target_pairs={{0,2},{1,3},{2,4},{3,5},{8,10},{9,11},{10,12},{11,13},{16,18},{17,... | collective-permute-start | bytes 786440 | tf_op jit(solution)/shard_map/ppermute | solution.py:485
  25.0 4.9 %collective-permute-done.3 = f16[8,128,128]{2,1,0:T(8,128)(2,1)S(1)} collective-permute-done((f16[8,128,128]{2,1,0:T(8,128)(2,1)S(1)}, f16[8,128,128]{2,1,0:T(8,128)(2,1)S(1)}, u32[]{:S(2)}, u32[]{:S(2)}) %collective-permute-start.3) | collective-permute-done | bytes 262176 | tf_op jit(solution)/shard_map/ppermute | solution.py:485
  30.0 1.1 convert_select_fusion.6
  31.1 4.4 %collective-permute-start.4 = (f16[8,128,128]{2,1,0:T(8,128)(2,1)S(1)}, f16[8,128,128]{2,1,0:T(8,128)(2,1)S(1)}, u32[]{:S(2)}, u32[]{:S(2)}) collective-permute-start(f16[8,128,128]{2,1,0:T(8,128)(2,1)S(1)} %get-tuple-element.33), channel_id=1, source_target_pairs={{0,2},{1,3},{2,4},{3,5},{4,6},{5,7},{8,10},{9,11},{10,12},{11,13},... | collective-permute-start | bytes 786440 | tf_op jit(solution)/shard_map/ppermute | solution.py:485
  35.5 4.1 %collective-permute-done.4 = f16[8,128,128]{2,1,0:T(8,128)(2,1)S(1)} collective-permute-done((f16[8,128,128]{2,1,0:T(8,128)(2,1)S(1)}, f16[8,128,128]{2,1,0:T(8,128)(2,1)S(1)}, u32[]{:S(2)}, u32[]{:S(2)}) %collective-permute-start.4) | collective-permute-done | bytes 262176 | tf_op jit(solution)/shard_map/ppermute | solution.py:485
  39.5 1.1 convert_select_fusion.4
  40.6 0.7 collective-permute-start.5
  41.3 1.1 convert_select_fusion.2
  42.4 0.7 collective-permute-start.6
  43.1 0.5 collective-permute-start.9
  43.6 0.1 collective-permute-start.10
  43.7 2.6 %convert_select_fusion = (f32[8,128,128]{2,1,0:T(8,128)}, f32[8,128,128]{2,1,0:T(8,128)S(1)}, f32[8,128,128]{2,1,0:T(8,128)S(1)}, f32[8,128,128]{2,1,0:T(8,128)}) fusion(f16[8,128,128]{2,1,0:T(8,128)(2,1)S(1)} %collective-permute-done.6, f32[8,128]{1,0:T(8,128)S(1)} %get-tuple-element.80, pred[]{:T(512)S(6)} %eq.5, f32[24,128,128]{2,1,0:T(8,128)} %copy-done.12, ...), kind=kLoop, calls=%fused_computation.1 | loop fusion | flops 1572864 | bytes 4726793 | tf_op jit(solution)/shard_map/jit(_where)/select_n | solution.py:490
  46.3 0.4 collective-permute-start.11
  46.7 0.1 collective-permute-start.7
  46.8 6.5 %intra_attention.1.refs_3_.intra_ref = f32[128,6144]{1,0:T(8,128)} custom-call(f32[48,128]{1,0:T(8,128)} %bitcast.25, bf16[128,6144]{1,0:T(8,128)(2,1)} %bitcast.18, bf16[128,6144]{1,0:T(8,128)(2,1)} %bitcast.30, bf16[128,6144]{1,0:T(8,128)(2,1)} %bitcast.33), custom_call_target="tpu_custom_call" | custom-call | tf_op jit(solution)/shard_map/intra_attention/pallas_call | solution.py:166
  53.3 5.1 %select.7 = (f32[16,128]{1,0:T(8,128)}, f32[16,128]{1,0:T(8,128)}, f32[16,6144]{1,0:T(8,128)}, bf16[16,6144]{1,0:T(8,128)(2,1)}, f32[16,6144]{1,0:T(8,128)}, /*index=5*/f32[16,6144]{1,0:T(8,128)}) custom-call(s32[2,128]{1,0:T(2,128)} %bitcast.36, f32[2,128]{1,0:T(2,128)} %bitcast.37, f32[48,128]{1,0:T(8,128)} %bitcast.26, bf16[128,6144]{1,0:T(8,128)(2,1)} %bitcast.19, ...), custom_call_target="tpu_custom_call" | custom-call | tf_op jit(solution)/shard_map/select/pallas_call | solution.py:220
  58.5 1.0 copy-done.4
  59.5 1.0 copy-done.5
  60.5 1.0 copy-done.6
  61.5 0.9 copy-done.7
  62.4 3.0 %selected_rows.1 = (bf16[16,6144]{1,0:T(8,128)(2,1)S(1)}, f32[16,6144]{1,0:T(8,128)S(1)}) custom-call(s32[2]{0:T(128)S(1)} %pad_add_fusion.refs_0_, f32[16,6144]{1,0:T(8,128)S(1)} %copy-done.4, bf16[16,6144]{1,0:T(8,128)(2,1)S(1)} %copy-done.7, f32[16,6144]{1,0:T(8,128)S(1)} %copy-done.5, f32[16,6144]{1,0:T(8,128)S(1)} %copy-done.6, ...), custom_call_target="tpu_custom_call" | custom-call | tf_op jit(solution)/shard_map/selected_rows/pallas_call | solution.py:278
  65.4 16.8 %collective-permute-start.15 = (bf16[16,6144]{1,0:T(8,128)(2,1)S(1)}, bf16[16,6144]{1,0:T(8,128)(2,1)S(1)}, u32[]{:S(2)}, u32[]{:S(2)}) collective-permute-start(bf16[16,6144]{1,0:T(8,128)(2,1)S(1)} %get-tuple-element.48.refs_0_), channel_id=1, source_target_pairs={{0,6},{1,7},{2,4},{3,5},{4,2},{5,3},{6,0},{7,1},{8,14},{9,15},{10,... | collective-permute-start | bytes 589832 | tf_op jit(solution)/shard_map/ppermute | solution.py:559
  82.2 0.6 collective-permute-start.13
  82.9 5.3 %collective-permute-done.15.refs_3_ = bf16[16,6144]{1,0:T(8,128)(2,1)S(1)} collective-permute-done((bf16[16,6144]{1,0:T(8,128)(2,1)S(1)}, bf16[16,6144]{1,0:T(8,128)(2,1)S(1)}, u32[]{:S(2)}, u32[]{:S(2)}) %collective-permute-start.15) | collective-permute-done | bytes 196640 | tf_op jit(solution)/shard_map/ppermute | solution.py:559
  88.1 9.9 %collective-permute-done.14.refs_2_ = bf16[16,6144]{1,0:T(8,128)(2,1)S(1)} collective-permute-done((bf16[16,6144]{1,0:T(8,128)(2,1)S(1)}, bf16[16,6144]{1,0:T(8,128)(2,1)S(1)}, u32[]{:S(2)}, u32[]{:S(2)}) %collective-permute-start.14) | collective-permute-done | bytes 196640 | tf_op jit(solution)/shard_map/ppermute | solution.py:559
  98.0 0.5 collective-permute-start.17
  98.5 5.5 %fetch.1 = (bf16[6144,640]{1,0:T(8,128)(2,1)S(1)}, bf16[640,6144]{1,0:T(8,128)(2,1)S(1)}) custom-call(bf16[6144,640]{1,0:T(8,128)(2,1)} %bitcast.34, bf16[640,6144]{1,0:T(8,128)(2,1)} %bitcast.35), custom_call_target="tpu_custom_call" | custom-call | tf_op jit(solution)/shard_map/fetch/pallas_call | solution.py:402
  104.1 2.8 %expert_rows.1 = (bf16[64,6144]{1,0:T(8,128)(2,1)S(1)}, bf16[64,6144]{1,0:T(8,128)(2,1)S(1)}) custom-call(bf16[16,6144]{1,0:T(8,128)(2,1)S(1)} %get-tuple-element.48.refs_0_, bf16[16,6144]{1,0:T(8,128)(2,1)S(1)} %collective-permute-done.13.refs_1_, bf16[16,6144]{1,0:T(8,128)(2,1)S(1)} %collective-permute-done.14.refs_2_, ...), custom_call_target="tpu_custom_call" | custom-call | tf_op jit(solution)/shard_map/expert_rows/pallas_call | solution.py:434
  107.0 6.3 %finish.1 = bf16[128,6144]{1,0:T(8,128)(2,1)S(1)} custom-call(s32[2]{0:T(128)S(1)} %pad_add_fusion.refs_0_, f32[48,128]{1,0:T(8,128)S(1)} %bitcast.27, bf16[128,6144]{1,0:T(8,128)(2,1)S(1)} %bitcast.20, f32[128,6144]{1,0:T(8,128)S(1)} %copy-done, f32[8,128,128]{2,1,0:T(8,128)S(1)} %get-tuple-element.71.refs_4_.refs_5_, ...), custom_call_target="tpu_custom_call" | custom-call | tf_op jit(solution)/shard_map/finish/pallas_call | solution.py:321
  113.3 1.5 collective-permute-start.12
  114.8 0.2 add_convert_fusion
  115.1 2.7 %collective-permute-start.23 = (bf16[16,6144]{1,0:T(8,128)(2,1)S(1)}, bf16[16,6144]{1,0:T(8,128)(2,1)S(1)}, u32[]{:S(2)}, u32[]{:S(2)}) collective-permute-start(bf16[16,6144]{1,0:T(8,128)(2,1)S(1)} %get-tuple-element.76), channel_id=1, source_target_pairs={{0,6},{1,7},{2,4},{3,5},{4,2},{5,3},{6,0},{7,1},{8,14},{9,15},{10,... | collective-permute-start | bytes 589832 | tf_op jit(solution)/shard_map/ppermute | solution.py:570
  117.8 1.8 %collective-permute-start.21 = (bf16[16,6144]{1,0:T(8,128)(2,1)S(1)}, bf16[16,6144]{1,0:T(8,128)(2,1)S(1)}, u32[]{:S(2)}, u32[]{:S(2)}) collective-permute-start(bf16[16,6144]{1,0:T(8,128)(2,1)S(1)} %get-tuple-element.78), channel_id=1, source_target_pairs={{0,2},{1,3},{2,0},{3,1},{4,6},{5,7},{6,4},{7,5},{8,10},{9,11},{10,... | collective-permute-start | bytes 589832 | tf_op jit(solution)/shard_map/ppermute | solution.py:570
  119.5 5.3 %collective-permute-done.23.refs_6_ = bf16[16,6144]{1,0:T(8,128)(2,1)S(1)} collective-permute-done((bf16[16,6144]{1,0:T(8,128)(2,1)S(1)}, bf16[16,6144]{1,0:T(8,128)(2,1)S(1)}, u32[]{:S(2)}, u32[]{:S(2)}) %collective-permute-start.23) | collective-permute-done | bytes 196640 | tf_op jit(solution)/shard_map/ppermute | solution.py:570
  124.9 9.2 %collective-permute-done.22.refs_5_ = bf16[16,6144]{1,0:T(8,128)(2,1)S(1)} collective-permute-done((bf16[16,6144]{1,0:T(8,128)(2,1)S(1)}, bf16[16,6144]{1,0:T(8,128)(2,1)S(1)}, u32[]{:S(2)}, u32[]{:S(2)}) %collective-permute-start.22) | collective-permute-done | bytes 196640 | tf_op jit(solution)/shard_map/ppermute | solution.py:570
  134.1 0.2 late_rows.1
  134.3 1.5 collective-permute-start.24
  135.8 15.7 %collective-permute-done.12.early_ref = bf16[128,6144]{1,0:T(8,128)(2,1)S(1)} collective-permute-done((bf16[128,6144]{1,0:T(8,128)(2,1)S(1)}, bf16[128,6144]{1,0:T(8,128)(2,1)S(1)}, u32[]{:S(2)}, u32[]{:S(2)}) %collective-permute-start.12) | collective-permute-done | bytes 1572896 | tf_op jit(solution)/shard_map/ppermute | solution.py:448
  151.5 3.8 %collective-permute-done.24.late_ref = bf16[16,6272]{1,0:T(8,128)(2,1)S(1)} collective-permute-done((bf16[16,6272]{1,0:T(8,128)(2,1)S(1)}, bf16[16,6272]{1,0:T(8,128)(2,1)S(1)}, u32[]{:S(2)}, u32[]{:S(2)}) %collective-permute-start.24) | collective-permute-done | bytes 200736 | tf_op jit(solution)/shard_map/ppermute | solution.py:448
  155.3 1.5 merged.1
  (52 shorter events, 0.5 us)
Async XLA Ops:
  3.0 3.9 %collective-permute-start.1 = (f32[24,128,128]{2,1,0:T(8,128)}, f32[24,128,128]{2,1,0:T(8,128)S(1)}, u32[]{:S(2)}, u32[]{:S(2)}) collective-permute-start(f32[24,128,128]{2,1,0:T(8,128)} %get-tuple-element.31), channel_id=1, source_target_pairs={{0,1},{1,0},{2,3},{3,2},{4,5},{5,4},{6,7},{7,6},{8,9},{9,8},{10,11... | collective-permute-start | bytes 4718600 | tf_op jit(solution)/shard_map/ppermute | solution.py:453
  3.6 3.3 %collective-permute-start = (f32[48,128]{1,0:T(8,128)}, f32[48,128]{1,0:T(8,128)S(1)}, u32[]{:S(2)}, u32[]{:S(2)}) collective-permute-start(f32[48,128]{1,0:T(8,128)} %get-tuple-element.29), channel_id=1, source_target_pairs={{0,1},{1,0},{2,3},{3,2},{4,5},{5,4},{6,7},{7,6},{8,9},{9,8},{10,11... | collective-permute-start | bytes 73736 | tf_op jit(solution)/shard_map/ppermute | solution.py:453
  3.6 3.2 %copy-start.14 = (f32[48,128]{1,0:T(8,128)S(1)}, f32[48,128]{1,0:T(8,128)}, u32[]{:S(2)}) copy-start(f32[48,128]{1,0:T(8,128)} %get-tuple-element.29) | copy-start | bytes 73732
  6.8 23.2 %copy-start.13 = (f32[24,128,128]{2,1,0:T(8,128)S(1)}, f32[24,128,128]{2,1,0:T(8,128)}, u32[]{:S(2)}) copy-start(f32[24,128,128]{2,1,0:T(8,128)} %get-tuple-element.30) | copy-start | bytes 4718596
  6.9 34.4 %copy-start.12 = (f32[24,128,128]{2,1,0:T(8,128)}, f32[24,128,128]{2,1,0:T(8,128)S(1)}, u32[]{:S(2)}) copy-start(f32[24,128,128]{2,1,0:T(8,128)S(1)} %collective-permute-done.1) | copy-start | bytes 4718596
  8.7 10.7 %collective-permute-start.2 = (f16[8,128,128]{2,1,0:T(8,128)(2,1)S(1)}, f16[8,128,128]{2,1,0:T(8,128)(2,1)S(1)}, u32[]{:S(2)}, u32[]{:S(2)}) collective-permute-start(f16[8,128,128]{2,1,0:T(8,128)(2,1)S(1)} %add_convert_fusion.5), channel_id=1, source_target_pairs={{0,2},{1,3},{8,10},{9,11},{16,18},{17,19},{24,26},{25,27}} | collective-permute-start | bytes 786440 | tf_op jit(solution)/shard_map/ppermute | solution.py:485
  20.6 9.3 %collective-permute-start.3 = (f16[8,128,128]{2,1,0:T(8,128)(2,1)S(1)}, f16[8,128,128]{2,1,0:T(8,128)(2,1)S(1)}, u32[]{:S(2)}, u32[]{:S(2)}) collective-permute-start(f16[8,128,128]{2,1,0:T(8,128)(2,1)S(1)} %add_convert_fusion.4), channel_id=1, source_target_pairs={{0,2},{1,3},{2,4},{3,5},{8,10},{9,11},{10,12},{11,13},{16,18},{17,... | collective-permute-start | bytes 786440 | tf_op jit(solution)/shard_map/ppermute | solution.py:485
  31.1 8.5 %collective-permute-start.4 = (f16[8,128,128]{2,1,0:T(8,128)(2,1)S(1)}, f16[8,128,128]{2,1,0:T(8,128)(2,1)S(1)}, u32[]{:S(2)}, u32[]{:S(2)}) collective-permute-start(f16[8,128,128]{2,1,0:T(8,128)(2,1)S(1)} %get-tuple-element.33), channel_id=1, source_target_pairs={{0,2},{1,3},{2,4},{3,5},{4,6},{5,7},{8,10},{9,11},{10,12},{11,13},... | collective-permute-start | bytes 786440 | tf_op jit(solution)/shard_map/ppermute | solution.py:485
  40.6 0.7 collective-permute-start.5
  42.4 1.3 collective-permute-start.6
  43.1 15.4 %collective-permute-start.8 = (f32[8,128,128]{2,1,0:T(8,128)}, f32[8,128,128]{2,1,0:T(8,128)S(1)}, u32[]{:S(2)}, u32[]{:S(2)}) collective-permute-start(f32[8,128,128]{2,1,0:T(8,128)} %get-tuple-element.38), channel_id=1, source_target_pairs={{0,1},{1,0},{2,3},{3,2},{4,5},{5,4},{6,7},{7,6},{8,9},{9,8},{10,11... | collective-permute-start | bytes 1572872 | tf_op jit(solution)/shard_map/ppermute | solution.py:453
  43.1 15.3 %collective-permute-start.9 = (f32[8,128,128]{2,1,0:T(8,128)}, f32[8,128,128]{2,1,0:T(8,128)}, u32[]{:S(2)}, u32[]{:S(2)}) collective-permute-start(f32[8,128,128]{2,1,0:T(8,128)} %get-tuple-element.39), channel_id=1, source_target_pairs={{0,1},{1,0},{2,3},{3,2},{4,5},{5,4},{6,7},{7,6},{8,9},{9,8},{10,11... | collective-permute-start | bytes 1572872 | tf_op jit(solution)/shard_map/ppermute | solution.py:453
  43.6 14.8 %collective-permute-start.10 = (f32[8,128,128]{2,1,0:T(8,128)}, f32[8,128,128]{2,1,0:T(8,128)}, u32[]{:S(2)}, u32[]{:S(2)}) collective-permute-start(f32[8,128,128]{2,1,0:T(8,128)} %get-tuple-element.40), channel_id=1, source_target_pairs={{0,1},{1,0},{2,3},{3,2},{4,5},{5,4},{6,7},{7,6},{8,9},{9,8},{10,11... | collective-permute-start | bytes 1572872 | tf_op jit(solution)/shard_map/ppermute | solution.py:453
  46.3 12.2 %collective-permute-start.11 = (f32[8,128,128]{2,1,0:T(8,128)}, f32[8,128,128]{2,1,0:T(8,128)}, u32[]{:S(2)}, u32[]{:S(2)}) collective-permute-start(f32[8,128,128]{2,1,0:T(8,128)} %get-tuple-element.61), channel_id=1, source_target_pairs={{0,1},{1,0},{2,3},{3,2},{4,5},{5,4},{6,7},{7,6},{8,9},{9,8},{10,11... | collective-permute-start | bytes 1572872 | tf_op jit(solution)/shard_map/ppermute | solution.py:453
  46.7 11.8 %collective-permute-start.7 = (f32[8,128,128]{2,1,0:T(8,128)}, f32[8,128,128]{2,1,0:T(8,128)}, u32[]{:S(2)}, u32[]{:S(2)}) collective-permute-start(f32[8,128,128]{2,1,0:T(8,128)} %get-tuple-element.72), channel_id=1, source_target_pairs={{0,1},{1,0},{2,3},{3,2},{4,5},{5,4},{6,7},{7,6},{8,9},{9,8},{10,11... | collective-permute-start | bytes 1572872 | tf_op jit(solution)/shard_map/ppermute | solution.py:453
  53.3 5.2 %copy-start.8 = (f32[1,6144]{1,0:T(1,128)S(1)}, f32[1,6144]{1,0:T(1,128)}, u32[]{:S(2)}) copy-start(f32[1,6144]{1,0:T(1,128)} %refs_15_.3) | copy-start | bytes 73732
  53.3 5.2 %copy-start.9 = (f32[1,6144]{1,0:T(1,128)S(1)}, f32[1,6144]{1,0:T(1,128)}, u32[]{:S(2)}) copy-start(f32[1,6144]{1,0:T(1,128)} %refs_16_.1) | copy-start | bytes 73732
  58.5 1.0 copy-start.4
  59.5 1.0 copy-start.5
  60.5 1.0 copy-start.6
  61.5 0.9 copy-start.7
  65.4 22.7 %collective-permute-start.15 = (bf16[16,6144]{1,0:T(8,128)(2,1)S(1)}, bf16[16,6144]{1,0:T(8,128)(2,1)S(1)}, u32[]{:S(2)}, u32[]{:S(2)}) collective-permute-start(bf16[16,6144]{1,0:T(8,128)(2,1)S(1)} %get-tuple-element.48.refs_0_), channel_id=1, source_target_pairs={{0,6},{1,7},{2,4},{3,5},{4,2},{5,3},{6,0},{7,1},{8,14},{9,15},{10,... | collective-permute-start | bytes 589832 | tf_op jit(solution)/shard_map/ppermute | solution.py:559
  82.2 15.8 %collective-permute-start.14 = (bf16[16,6144]{1,0:T(8,128)(2,1)S(1)}, bf16[16,6144]{1,0:T(8,128)(2,1)S(1)}, u32[]{:S(2)}, u32[]{:S(2)}) collective-permute-start(bf16[16,6144]{1,0:T(8,128)(2,1)S(1)} %get-tuple-element.48.refs_0_), channel_id=1, source_target_pairs={{0,4},{1,5},{2,6},{3,7},{4,0},{5,1},{6,2},{7,3},{8,12},{9,13},{10,... | collective-permute-start | bytes 589832 | tf_op jit(solution)/shard_map/ppermute | solution.py:559
  82.2 15.8 %collective-permute-start.13 = (bf16[16,6144]{1,0:T(8,128)(2,1)S(1)}, bf16[16,6144]{1,0:T(8,128)(2,1)S(1)}, u32[]{:S(2)}, u32[]{:S(2)}) collective-permute-start(bf16[16,6144]{1,0:T(8,128)(2,1)S(1)} %get-tuple-element.48.refs_0_), channel_id=1, source_target_pairs={{0,2},{1,3},{2,0},{3,1},{4,6},{5,7},{6,4},{7,5},{8,10},{9,11},{10,... | collective-permute-start | bytes 589832 | tf_op jit(solution)/shard_map/ppermute | solution.py:559
  82.8 21.2 %collective-permute-start.16 = (bf16[16,6144]{1,0:T(8,128)(2,1)S(1)}, bf16[16,6144]{1,0:T(8,128)(2,1)S(1)}, u32[]{:S(2)}, u32[]{:S(2)}) collective-permute-start(bf16[16,6144]{1,0:T(8,128)(2,1)S(1)} %get-tuple-element.48.refs_0_), channel_id=1, source_target_pairs={{0,1},{1,0},{2,3},{3,2},{4,5},{5,4},{6,7},{7,6},{8,9},{9,8},{10,11... | collective-permute-start | bytes 589832 | tf_op jit(solution)/shard_map/ppermute | solution.py:453
  88.1 15.9 %collective-permute-start.19 = (bf16[16,6144]{1,0:T(8,128)(2,1)S(1)}, bf16[16,6144]{1,0:T(8,128)(2,1)S(1)}, u32[]{:S(2)}, u32[]{:S(2)}) collective-permute-start(bf16[16,6144]{1,0:T(8,128)(2,1)S(1)} %collective-permute-done.15.refs_3_), channel_id=1, source_target_pairs={{0,1},{1,0},{2,3},{3,2},{4,5},{5,4},{6,7},{7,6},{8,9},{9,8},{10,11... | collective-permute-start | bytes 589832 | tf_op jit(solution)/shard_map/ppermute | solution.py:453
  98.0 6.0 %collective-permute-start.18 = (bf16[16,6144]{1,0:T(8,128)(2,1)S(1)}, bf16[16,6144]{1,0:T(8,128)(2,1)S(1)}, u32[]{:S(2)}, u32[]{:S(2)}) collective-permute-start(bf16[16,6144]{1,0:T(8,128)(2,1)S(1)} %collective-permute-done.14.refs_2_), channel_id=1, source_target_pairs={{0,1},{1,0},{2,3},{3,2},{4,5},{5,4},{6,7},{7,6},{8,9},{9,8},{10,11... | collective-permute-start | bytes 589832 | tf_op jit(solution)/shard_map/ppermute | solution.py:453
  98.0 6.0 %collective-permute-start.17 = (bf16[16,6144]{1,0:T(8,128)(2,1)S(1)}, bf16[16,6144]{1,0:T(8,128)(2,1)S(1)}, u32[]{:S(2)}, u32[]{:S(2)}) collective-permute-start(bf16[16,6144]{1,0:T(8,128)(2,1)S(1)} %collective-permute-done.13.refs_1_), channel_id=1, source_target_pairs={{0,1},{1,0},{2,3},{3,2},{4,5},{5,4},{6,7},{7,6},{8,9},{9,8},{10,11... | collective-permute-start | bytes 589832 | tf_op jit(solution)/shard_map/ppermute | solution.py:453
  104.0 2.9 %copy-start = (f32[128,6144]{1,0:T(8,128)S(1)}, f32[128,6144]{1,0:T(8,128)}, u32[]{:S(2)}) copy-start(f32[128,6144]{1,0:T(8,128)} %intra_attention.1.refs_3_.intra_ref) | copy-start | bytes 9437188
  104.1 2.9 %copy-start.1 = (bf16[1,128,6144]{2,1,0:T(8,128)(2,1)S(1)}, bf16[1,128,6144]{2,1,0:T(8,128)(2,1)}, u32[]{:S(2)}) copy-start(bf16[1,128,6144]{2,1,0:T(8,128)(2,1)} %param.12) | copy-start | bytes 4718596
  104.1 2.9 %copy-start.2 = (bf16[1,128,6144]{2,1,0:T(8,128)(2,1)S(1)}, bf16[1,128,6144]{2,1,0:T(8,128)(2,1)}, u32[]{:S(2)}) copy-start(bf16[1,128,6144]{2,1,0:T(8,128)(2,1)} %param.11) | copy-start | bytes 4718596
  104.1 2.9 %copy-start.3 = (f32[1,128,48]{1,2,0:T(8,128)S(1)}, f32[1,128,48]{1,2,0:T(8,128)}, u32[]{:S(2)}) copy-start(f32[1,128,48]{1,2,0:T(8,128)} %param.15) | copy-start | bytes 73732
  106.9 7.9 %collective-permute-start.20 = (bf16[64,6144]{1,0:T(8,128)(2,1)S(1)}, bf16[64,6144]{1,0:T(8,128)(2,1)S(1)}, u32[]{:S(2)}, u32[]{:S(2)}) collective-permute-start(bf16[64,6144]{1,0:T(8,128)(2,1)S(1)} %get-tuple-element.52), channel_id=1, source_target_pairs={{0,1},{1,0},{2,3},{3,2},{4,5},{5,4},{6,7},{7,6},{8,9},{9,8},{10,11... | collective-permute-start | bytes 2359304 | tf_op jit(solution)/shard_map/ppermute | solution.py:453
  113.3 38.2 %collective-permute-start.12 = (bf16[128,6144]{1,0:T(8,128)(2,1)S(1)}, bf16[128,6144]{1,0:T(8,128)(2,1)S(1)}, u32[]{:S(2)}, u32[]{:S(2)}) collective-permute-start(bf16[128,6144]{1,0:T(8,128)(2,1)S(1)} %finish.1), channel_id=1, source_target_pairs={{0,8},{8,16},{16,24},{24,0},{1,9},{9,17},{17,25},{25,1},{2,10},{10... | collective-permute-start | bytes 4718600 | tf_op jit(solution)/shard_map/ppermute | solution.py:448
  114.8 19.2 %copy-start.10 = (f32[16,128]{1,0:T(8,128)S(1)}, f32[16,128]{1,0:T(8,128)}, u32[]{:S(2)}) copy-start(f32[16,128]{1,0:T(8,128)} %get-tuple-element.46.refs_1_) | copy-start | bytes 24580
  114.8 19.2 %copy-start.11 = (f32[16,128]{1,0:T(8,128)S(1)}, f32[16,128]{1,0:T(8,128)}, u32[]{:S(2)}) copy-start(f32[16,128]{1,0:T(8,128)} %get-tuple-element.47.refs_2_) | copy-start | bytes 24580
  115.1 9.8 %collective-permute-start.23 = (bf16[16,6144]{1,0:T(8,128)(2,1)S(1)}, bf16[16,6144]{1,0:T(8,128)(2,1)S(1)}, u32[]{:S(2)}, u32[]{:S(2)}) collective-permute-start(bf16[16,6144]{1,0:T(8,128)(2,1)S(1)} %get-tuple-element.76), channel_id=1, source_target_pairs={{0,6},{1,7},{2,4},{3,5},{4,2},{5,3},{6,0},{7,1},{8,14},{9,15},{10,... | collective-permute-start | bytes 589832 | tf_op jit(solution)/shard_map/ppermute | solution.py:570
  117.8 16.3 %collective-permute-start.22 = (bf16[16,6144]{1,0:T(8,128)(2,1)S(1)}, bf16[16,6144]{1,0:T(8,128)(2,1)S(1)}, u32[]{:S(2)}, u32[]{:S(2)}) collective-permute-start(bf16[16,6144]{1,0:T(8,128)(2,1)S(1)} %get-tuple-element.77), channel_id=1, source_target_pairs={{0,4},{1,5},{2,6},{3,7},{4,0},{5,1},{6,2},{7,3},{8,12},{9,13},{10,... | collective-permute-start | bytes 589832 | tf_op jit(solution)/shard_map/ppermute | solution.py:570
  117.8 16.3 %collective-permute-start.21 = (bf16[16,6144]{1,0:T(8,128)(2,1)S(1)}, bf16[16,6144]{1,0:T(8,128)(2,1)S(1)}, u32[]{:S(2)}, u32[]{:S(2)}) collective-permute-start(bf16[16,6144]{1,0:T(8,128)(2,1)S(1)} %get-tuple-element.78), channel_id=1, source_target_pairs={{0,2},{1,3},{2,0},{3,1},{4,6},{5,7},{6,4},{7,5},{8,10},{9,11},{10,... | collective-permute-start | bytes 589832 | tf_op jit(solution)/shard_map/ppermute | solution.py:570
  134.3 21.0 %collective-permute-start.24 = (bf16[16,6272]{1,0:T(8,128)(2,1)S(1)}, bf16[16,6272]{1,0:T(8,128)(2,1)S(1)}, u32[]{:S(2)}, u32[]{:S(2)}) collective-permute-start(bf16[16,6272]{1,0:T(8,128)(2,1)S(1)} %late_rows.1), channel_id=1, source_target_pairs={{0,8},{8,16},{16,24},{24,0},{1,9},{9,17},{17,25},{25,1},{2,10},{10... | collective-permute-start | bytes 602120 | tf_op jit(solution)/shard_map/ppermute | solution.py:448
